TPU v7x, 32 devices: a whole 2x2x4 slice. The times are simulated.
32 devices in a mesh: ctx: 16 (over z, y, core), tp: 2 (over x).
Axes of the slice: x: 2, y: 2, z: 4, core: 2. Of those that a mesh axis runs over, the one named last changes fastest.
Arguments:
- tokens: bfloat16 [6144, 2048], P(('ctx', 'tp')), may hold values from -6 to 6
- attn_gain: float32 [2048], replicated, may hold values from 0.5 to 1.5
- ffn_gain: float32 [2048], replicated, may hold values from 0.5 to 1.5
- query_norm_gain: float32 [64], replicated, may hold values from 0.5 to 1.5
- k_gain: float32 [64], replicated, may hold values from 0.5 to 1.5
- w_query: bfloat16 [2048, 2048], P('ctx', 'tp'), may hold values from -0.125 to 0.125
- key_projection: bfloat16 [2048, 512], P('ctx', 'tp'), may hold values from -0.125 to 0.125
- value_projection: bfloat16 [2048, 512], P('ctx', 'tp'), may hold values from -0.125 to 0.125
- w_out: bfloat16 [2048, 2048], P('tp', 'ctx'), may hold values from -2 to 2
- w_gate: bfloat16 [2048, 8192], P('ctx', 'tp'), may hold values from -0.125 to 0.125
- w_up: bfloat16 [2048, 8192], P('ctx', 'tp'), may hold values from -0.125 to 0.125
- w_down: bfloat16 [8192, 2048], P('tp', 'ctx'), may hold values from -0.0625 to 0.0625
- doc_start: int32 [6144], P('ctx'), may hold values from 0 to 6143, as said below
- cotangent: bfloat16 [6144, 2048], P(('ctx', 'tp')), may hold values from -9 to 9
Outputs:
- out_tokens: bfloat16 [6144, 2048], P(('ctx', 'tp'))
- d_tokens: float32 [6144, 2048], P(('ctx', 'tp'))
- d_attn_gain: float32 [2048], replicated
- d_ffn_gain: float32 [2048], replicated
- d_q_gain: float32 [64], replicated
- d_k_gain: float32 [64], replicated
- d_query: float32 [2048, 2048], P('ctx', 'tp')
- d_key: float32 [2048, 512], P('ctx', 'tp')
- d_value: float32 [2048, 512], P('ctx', 'tp')
- d_out: float32 [2048, 2048], P('tp', 'ctx')
- d_gate: float32 [2048, 8192], P('ctx', 'tp')
- d_up: float32 [2048, 8192], P('ctx', 'tp')
- d_down: float32 [8192, 2048], P('tp', 'ctx')
Inputs may be any that keep to these rules, and one draw needn't show every extreme that they name: `doc_start`: each token's value is the first position of its document; documents are runs of consecutive positions in order, of 144 to 2304 tokens (the last one may be cut shorter by the end), and one document holds exactly 2304 tokens.
All inputs are finite; a program needn't handle non-finite values.
Results may differ from a plain program's by a relative error of at most 0.022.
Values may be sent and summed in bfloat16 or wider, within the bound.
No kernel may reach another device: no remote copies, remote signals or barrier semaphores. Data moves between devices by JAX's collectives and lax.ppermute only.
A program may use at most 320 MiB of HBM per device.

v0:
```python
import jax
import jax.numpy as jnp
from jax import lax
from jax.sharding import PartitionSpec as P

WB = 6


epsilon = 1e-05
rope_base = 1000000.0
neg_large = -1e30


def shifted(value, axis, by):
    devices = lax.axis_size(axis)
    pairs = [(i, i + by) for i in range(devices) if 0 <= i + by < devices]
    return lax.ppermute(value, axis, pairs)


def rms_scale(values):
    return lax.rsqrt(jnp.mean(values * values, axis=-1, keepdims=True) + epsilon)


def feature_rms_norm(values, gain_vec):
    return values * rms_scale(values) * gain_vec


def rotary_embed_heads(values, cosine_table, sine_table):
    half_size = values.shape[-1] // 2
    first = values[..., :half_size]
    second = values[..., half_size:]
    return jnp.concatenate(
        [first * cosine_table - second * sine_table, second * cosine_table + first * sine_table],
        axis=-1,
    )


def rope_tables(relative, head_size):
    half_size = head_size // 2
    inv_freq = jnp.power(rope_base, -2.0 * jnp.arange(half_size, dtype=jnp.float32) / head_size)
    angles = relative.astype(jnp.float32)[:, None] * inv_freq[None, :]
    return (jnp.cos(angles), jnp.sin(angles))


def matrix_multiply(left, right):
    return jnp.dot(left, right, preferred_element_type=jnp.float32)


def gather_weights(w_query, key_projection, value_projection, w_out, w_gate, w_up, w_down):
    return (
        lax.all_gather(w_query, "ctx", axis=0, tiled=True),
        lax.all_gather(key_projection, "ctx", axis=0, tiled=True),
        lax.all_gather(value_projection, "ctx", axis=0, tiled=True),
        lax.all_gather(w_out, "ctx", axis=1, tiled=True),
        lax.all_gather(w_gate, "ctx", axis=0, tiled=True),
        lax.all_gather(w_up, "ctx", axis=0, tiled=True),
        lax.all_gather(w_down, "ctx", axis=1, tiled=True),
    )


def on_device(
    tokens,
    attn_gain,
    ffn_gain,
    query_norm_gain,
    k_gain,
    w_query,
    key_projection,
    value_projection,
    w_out,
    w_gate,
    w_up,
    w_down,
    doc_start,
    cotangent,
):
    block_len = doc_start.shape[0]
    head_size = query_norm_gain.shape[0]
    q_heads = w_query.shape[1] // head_size
    kv_heads = key_projection.shape[1] // head_size
    group_size = q_heads // kv_heads
    scale_factor = head_size ** (-0.5)
    ctx_index = lax.axis_index("ctx")
    wq_full, wk_full, wv_full, wo_full, wg_full, wu_full, wd_full = gather_weights(
        w_query, key_projection, value_projection, w_out, w_gate, w_up, w_down
    )
    x_float = tokens.astype(jnp.float32)
    normed_one, norm_one_back = jax.vjp(feature_rms_norm, x_float, attn_gain)
    first_operand = lax.all_gather(normed_one.astype(jnp.bfloat16), "tp", axis=0, tiled=True)
    positions = ctx_index * block_len + jnp.arange(block_len, dtype=jnp.int32)
    cosine_table, sine_table = rope_tables(positions - doc_start, head_size)
    cosine_table = cosine_table[:, None, :]
    sine_table = sine_table[:, None, :]

    def prepare(raw_heads, gain_vec):
        return rotary_embed_heads(feature_rms_norm(raw_heads, gain_vec), cosine_table, sine_table)

    query_unnormed = matrix_multiply(first_operand, wq_full).reshape(block_len, q_heads, head_size)
    key_unnormed = matrix_multiply(first_operand, wk_full).reshape(block_len, kv_heads, head_size)
    v_heads = (
        matrix_multiply(first_operand, wv_full)
        .astype(jnp.bfloat16)
        .reshape(block_len, kv_heads, head_size)
    )
    q_ready, q_back = jax.vjp(prepare, query_unnormed, query_norm_gain)
    k_ready, k_back = jax.vjp(prepare, key_unnormed, k_gain)
    q_bf = q_ready.astype(jnp.bfloat16).reshape(block_len, kv_heads, group_size, head_size)
    k_bf = k_ready.astype(jnp.bfloat16)

    def block_mask(source):
        key_pos = source * block_len + jnp.arange(block_len, dtype=jnp.int32)
        return (key_pos[None, :] >= doc_start[:, None]) & (key_pos[None, :] <= positions[:, None])

    def block_scores(k_block, allowed):
        raw_scores = jnp.einsum("qhgd,khd->qhgk", q_bf, k_block, preferred_element_type=jnp.float32)
        return jnp.where(allowed[:, None, None, :], raw_scores * scale_factor, neg_large)

    def forward_update(carry, k_block, v_block, allowed):
        run_max, run_total, run_acc = carry
        masked = block_scores(k_block, allowed)
        new_max = jnp.maximum(run_max, jnp.max(masked, axis=-1))
        exp_scores = jnp.exp(masked - new_max[..., None])
        factor = jnp.exp(run_max - new_max)
        new_total = run_total * factor + jnp.sum(exp_scores, axis=-1)
        new_acc = run_acc * factor[..., None] + jnp.einsum(
            "qhgk,khd->qhgd",
            exp_scores.astype(jnp.bfloat16),
            v_block,
            preferred_element_type=jnp.float32,
        )
        return (new_max, new_total, new_acc)

    def forward_step(carry, kv_pair, source):
        allowed = block_mask(source)
        return forward_update(carry, kv_pair[0], kv_pair[1], allowed)

    stat_shape = (block_len, kv_heads, group_size)
    state = (
        jnp.full(stat_shape, neg_large, jnp.float32),
        jnp.zeros(stat_shape, jnp.float32),
        jnp.zeros(stat_shape + (head_size,), jnp.float32),
    )
    kv_pair = jnp.stack([k_bf, v_heads])
    kept_pairs = [kv_pair]
    state = forward_step(state, kv_pair, ctx_index)
    for distance in range(1, WB + 1):
        kv_pair = shifted(kv_pair, "ctx", 1)
        kept_pairs.append(kv_pair)
        state = forward_step(state, kv_pair, ctx_index - distance)
    run_max, run_total, run_acc = state
    log_total = run_max + jnp.log(run_total)
    attn_float = run_acc / run_total[..., None]
    attn_bf = attn_float.astype(jnp.bfloat16).reshape(block_len, q_heads * head_size)
    attn_sum = lax.psum_scatter(
        matrix_multiply(attn_bf, wo_full).astype(jnp.bfloat16),
        "tp",
        scatter_dimension=0,
        tiled=True,
    ).astype(jnp.float32)
    resid = x_float + attn_sum
    normed_two, norm_two_back = jax.vjp(feature_rms_norm, resid, ffn_gain)
    a_two = lax.all_gather(normed_two.astype(jnp.bfloat16), "tp", axis=0, tiled=True)
    gate = matrix_multiply(a_two, wg_full)
    up_part = matrix_multiply(a_two, wu_full)
    hidden_float, act_back = jax.vjp(
        lambda gate_in, up_in: jax.nn.silu(gate_in) * up_in, gate, up_part
    )
    hidden = hidden_float.astype(jnp.bfloat16)
    ffn_total = lax.psum_scatter(
        matrix_multiply(hidden, wd_full).astype(jnp.bfloat16), "tp", scatter_dimension=0, tiled=True
    ).astype(jnp.float32)
    out_tokens = (resid + ffn_total).astype(jnp.bfloat16)
    wq_back, wk_back, wv_back, wo_back, wg_back, wu_back, wd_back = gather_weights(
        w_query, key_projection, value_projection, w_out, w_gate, w_up, w_down
    )
    grad_rows = lax.all_gather(cotangent, "tp", axis=0, tiled=True)
    d_hidden = matrix_multiply(grad_rows, wd_back.T)
    d_gate_float, d_up_float = act_back(d_hidden)
    d_gate_bf = d_gate_float.astype(jnp.bfloat16)
    d_up_bf = d_up_float.astype(jnp.bfloat16)
    d_normed_two = lax.psum_scatter(
        (matrix_multiply(d_gate_bf, wg_back.T) + matrix_multiply(d_up_bf, wu_back.T)).astype(
            jnp.bfloat16
        ),
        "tp",
        scatter_dimension=0,
        tiled=True,
    ).astype(jnp.float32)
    d_resid_norm, d_ffn_gain = norm_two_back(d_normed_two)
    d_resid = cotangent.astype(jnp.float32) + d_resid_norm
    resid_rows = lax.all_gather(d_resid.astype(jnp.bfloat16), "tp", axis=0, tiled=True)
    d_attn = (
        matrix_multiply(resid_rows, wo_back.T)
        .astype(jnp.bfloat16)
        .reshape(block_len, kv_heads, group_size, head_size)
    )
    delta = jnp.sum(d_attn.astype(jnp.float32) * attn_float, axis=-1)

    def backward_update(kv_pair, allowed):
        k_block = kv_pair[0]
        v_block = kv_pair[1]
        masked = block_scores(k_block, allowed)
        probs = jnp.exp(masked - log_total[..., None])
        d_probs = jnp.einsum("qhgd,khd->qhgk", d_attn, v_block, preferred_element_type=jnp.float32)
        d_scores = (probs * (d_probs - delta[..., None]) * scale_factor).astype(jnp.bfloat16)
        d_query_part = jnp.einsum(
            "qhgk,khd->qhgd", d_scores, k_block, preferred_element_type=jnp.float32
        )
        d_key_part = jnp.einsum(
            "qhgk,qhgd->khd", d_scores, q_bf, preferred_element_type=jnp.float32
        )
        d_value_part = jnp.einsum(
            "qhgk,qhgd->khd", probs.astype(jnp.bfloat16), d_attn, preferred_element_type=jnp.float32
        )
        return (d_query_part, jnp.stack([d_key_part, d_value_part]))

    def backward_step(kv_pair, source):
        allowed = block_mask(source)
        return backward_update(kv_pair, allowed)

    d_query_acc, key_grads = backward_step(kept_pairs[WB], ctx_index - WB)
    for distance in range(WB - 1, -1, -1):
        key_grads = shifted(key_grads.astype(jnp.bfloat16), "ctx", -1).astype(key_grads.dtype)
        query_part, fresh_grads = backward_step(kept_pairs[distance], ctx_index - distance)
        d_query_acc = d_query_acc + query_part
        key_grads = key_grads + fresh_grads
    d_q_raw, d_q_gain = q_back(d_query_acc.reshape(block_len, q_heads, head_size))
    d_k_raw, d_k_gain = k_back(key_grads[0])
    dq_bf = d_q_raw.astype(jnp.bfloat16).reshape(block_len, q_heads * head_size)
    dk_bf = d_k_raw.astype(jnp.bfloat16).reshape(block_len, kv_heads * head_size)
    dv_bf = key_grads[1].astype(jnp.bfloat16).reshape(block_len, kv_heads * head_size)
    part_q = matrix_multiply(dq_bf, wq_back.T)
    part_k = matrix_multiply(dk_bf, wk_back.T)
    part_v = matrix_multiply(dv_bf, wv_back.T)
    d_normed_one = lax.psum_scatter(
        (part_q + part_k + part_v).astype(jnp.bfloat16), "tp", scatter_dimension=0, tiled=True
    ).astype(jnp.float32)
    d_x_norm, d_attn_gain = norm_one_back(d_normed_one)
    d_tokens = d_resid + d_x_norm
    d_query_w = matrix_multiply(first_operand.T, dq_bf)
    d_key_w = matrix_multiply(first_operand.T, dk_bf)
    d_value_w = matrix_multiply(first_operand.T, dv_bf)
    d_out_w = matrix_multiply(attn_bf.T, resid_rows)
    d_gate_w = matrix_multiply(a_two.T, d_gate_bf)
    d_up_w = matrix_multiply(a_two.T, d_up_bf)
    d_down = matrix_multiply(hidden.T, grad_rows)
    grad_shards = (
        lax.psum_scatter(d_query_w, "ctx", scatter_dimension=0, tiled=True),
        lax.psum_scatter(d_key_w, "ctx", scatter_dimension=0, tiled=True),
        lax.psum_scatter(d_value_w, "ctx", scatter_dimension=0, tiled=True),
        lax.psum_scatter(d_out_w, "ctx", scatter_dimension=1, tiled=True),
        lax.psum_scatter(d_gate_w, "ctx", scatter_dimension=0, tiled=True),
        lax.psum_scatter(d_up_w, "ctx", scatter_dimension=0, tiled=True),
        lax.psum_scatter(d_down, "ctx", scatter_dimension=1, tiled=True),
    )
    gain_totals = lax.psum((d_attn_gain, d_ffn_gain, d_q_gain, d_k_gain), ("ctx", "tp"))
    return (
        out_tokens,
        d_tokens,
        gain_totals[0],
        gain_totals[1],
        gain_totals[2],
        gain_totals[3],
        grad_shards[0],
        grad_shards[1],
        grad_shards[2],
        grad_shards[3],
        grad_shards[4],
        grad_shards[5],
        grad_shards[6],
    )


def solution(mesh):
    return jax.shard_map(
        on_device,
        mesh=mesh,
        in_specs=(
            P(("ctx", "tp"), None),
            P(),
            P(),
            P(),
            P(),
            P("ctx", "tp"),
            P("ctx", "tp"),
            P("ctx", "tp"),
            P("tp", "ctx"),
            P("ctx", "tp"),
            P("ctx", "tp"),
            P("tp", "ctx"),
            P("ctx"),
            P(("ctx", "tp"), None),
        ),
        out_specs=(
            P(("ctx", "tp"), None),
            P(("ctx", "tp"), None),
            P(),
            P(),
            P(),
            P(),
            P("ctx", "tp"),
            P("ctx", "tp"),
            P("ctx", "tp"),
            P("tp", "ctx"),
            P("ctx", "tp"),
            P("ctx", "tp"),
            P("tp", "ctx"),
        ),
        check_vma=False,
    )
```

profile of v0, /device:TPU:0, one launch (start us, length us, event | category | flops | bytes accessed | tf_op | source)
XLA Modules:
  0.0 2458.5 jit_solution(16163992965003976624)
XLA Ops:
  15.2 27.0 %all-gather.12.cloned.1.call-done = bf16[384,2048]{1,0:T(8,128)(2,1)} async-done(((bf16[192,2048]{1,0:T(8,128)(2,1)}), bf16[384,2048]{1,0:T(8,128)(2,1)}) %all-gather.12.cloned.1.call-update) | async-done | bytes 1572880 | tf_op jit(solution)/shard_map/all_gather | solution.py:89
  42.1 40.1 %all-gather.14.cloned.1.call-done = bf16[2048,256]{1,0:T(8,128)(2,1)} async-done(((bf16[128,256]{1,0:T(8,128)(2,1)}), bf16[2048,256]{1,0:T(8,128)(2,1)}) %all-gather.14.cloned.1.call-update) | async-done | bytes 1048592 | tf_op jit(solution)/shard_map/all_gather | solution.py:52
  85.8 35.6 %all-gather.18.cloned.1.call-done = bf16[2048,256]{1,0:T(8,128)(2,1)} async-done(((bf16[128,256]{1,0:T(8,128)(2,1)}), bf16[2048,256]{1,0:T(8,128)(2,1)}) %all-gather.18.cloned.1.call-update) | async-done | bytes 1048592 | tf_op jit(solution)/shard_map/all_gather | solution.py:53
  128.1 5.6 collective-permute-start.1
  135.9 8.0 collective-permute-start.2
  145.2 10.3 collective-permute-start.3
  156.8 12.4 collective-permute-start.4
  170.4 8.1 collective-permute-start.5
  178.6 4.6 multiply_reduce_fusion.4
  187.7 5.8 fusion.49
  193.5 5.1 fusion.50
  198.6 6.0 fusion.51
  204.6 5.1 fusion.46
  209.8 6.6 fusion.52
  216.4 5.7 fusion.21
  222.1 5.8 fusion.33
  227.9 5.7 fusion.31
  233.6 5.6 fusion.29
  239.2 5.6 fusion.27
  249.0 7.2 fusion.65
  256.2 7.4 fusion.55
  263.7 7.3 fusion.57
  282.3 5.8 fusion.203
  288.1 5.5 convolution_convert_fusion
  293.6 38.9 %reduce-scatter.12.cloned.1.call-done = bf16[192,2048]{1,0:T(8,128)(2,1)} async-done(((bf16[384,2048]{1,0:T(8,128)(2,1)}), bf16[192,2048]{1,0:T(8,128)(2,1)}) %reduce-scatter.12.cloned.1.call-update) | async-done | bytes 786448 | tf_op jit(solution)/shard_map/reduce_scatter | solution.py:154
  339.7 24.1 all-gather.22.cloned.1.call-done
  363.7 129.3 %all-gather.26.cloned.1.call-done = bf16[2048,4096]{1,0:T(8,128)(2,1)} async-done(((bf16[128,4096]{1,0:T(8,128)(2,1)}), bf16[2048,4096]{1,0:T(8,128)(2,1)}) %all-gather.26.cloned.1.call-update) | async-done | bytes 16777232 | tf_op jit(solution)/shard_map/all_gather | solution.py:56
  493.1 12.3 fusion.205
  505.3 115.2 %all-gather.24.cloned.1.call-done = bf16[2048,4096]{1,0:T(8,128)(2,1)} async-done(((bf16[128,4096]{1,0:T(8,128)(2,1)}), bf16[2048,4096]{1,0:T(8,128)(2,1)}) %all-gather.24.cloned.1.call-update) | async-done | bytes 16777232 | tf_op jit(solution)/shard_map/all_gather | solution.py:55
  620.6 11.8 fusion.204
  632.4 15.1 all-gather.30.cloned.1.call-done
  647.4 132.8 %all-gather.28.cloned.1.call-done = bf16[4096,2048]{1,0:T(8,128)(2,1)} async-done(((bf16[4096,128]{1,0:T(8,128)(2,1)}), bf16[4096,2048]{1,0:T(8,128)(2,1)}) %all-gather.28.cloned.1.call-update) | async-done | bytes 16777232 | tf_op jit(solution)/shard_map/all_gather | solution.py:57
  780.2 17.7 multiply_convert_fusion
  797.9 12.3 fusion.206
  810.2 19.2 add_convert_fusion.1
  829.5 24.4 reduce-scatter.16.cloned.1.call-done
  859.1 27.3 %all-gather.32.cloned.1.call-done = bf16[384,2048]{1,0:T(8,128)(2,1)} async-done(((bf16[192,2048]{1,0:T(8,128)(2,1)}), bf16[384,2048]{1,0:T(8,128)(2,1)}) %all-gather.32.cloned.1.call-update) | async-done | bytes 1572880 | tf_op jit(solution)/shard_map/all_gather | solution.py:191
  886.4 4.5 convolution_convert_fusion.2
  891.3 6.1 fusion.143
  897.5 6.9 fusion.132
  924.4 6.0 fusion.20
  940.4 5.8 fusion.8
  946.2 5.8 fusion.11
  952.0 5.9 fusion.14
  957.8 7.4 fusion.17
  977.0 4.6 add_add_fusion.3
  992.3 5.5 collective-permute-done.8
  1000.8 6.2 collective-permute-done.9
  1010.6 5.8 collective-permute-done.10
  1021.5 4.1 collective-permute-done.11
  1028.9 12.1 convolution_convert_fusion.1
  1045.4 5.8 fusion.209
  1052.9 5.6 fusion.212
  1059.9 17.7 fusion.214
  1077.7 17.3 fusion.213
  1096.9 17.6 fusion.215
  1117.6 49.1 %all-reduce.4 = (f32[2048]{0:T(1024)}, f32[2048]{0:T(1024)}, f32[64]{0:T(128)}, f32[64]{0:T(128)}) all-reduce(f32[2048]{0:T(1024)S(1)} %get-tuple-element.17, f32[2048]{0:T(1024)S(1)} %copy-done.81, f32[64]{0:T(128)S(1)} %get-tuple-element.15, f32[64]{0:T(128)S(1)} %get-tuple-element.19), channel_id=1, replica_groups=mesh['ctx'=16,'tp'=2] {'ctx','tp'}, use_global_device_ids=true, to_apply=%region_28.29 | all-reduce | flops 4224 | bytes 33792 | tf_op jit(solution)/shard_map/psum | solution.py:256
  1166.8 4.1 fusion.105
  1170.9 53.0 %reduce-scatter.24.cloned.1.call-done = f32[128,256]{1,0:T(8,128)} async-done(((f32[2048,256]{1,0:T(8,128)}), f32[128,256]{1,0:T(8,128)}) %reduce-scatter.24.cloned.1.call-update) | async-done | bytes 131088 | tf_op jit(solution)/shard_map/reduce_scatter | solution.py:250
  1223.9 108.1 %reduce-scatter.20.cloned.1.call-done = f32[128,1024]{1,0:T(8,128)} async-done(((f32[2048,1024]{1,0:T(8,128)}), f32[128,1024]{1,0:T(8,128)}) %reduce-scatter.20.cloned.1.call-update) | async-done | bytes 524304 | tf_op jit(solution)/shard_map/reduce_scatter | solution.py:248
  1332.0 109.3 %reduce-scatter.26.cloned.1.call-done = f32[1024,128]{1,0:T(8,128)} async-done(((f32[1024,2048]{1,0:T(8,128)}), f32[1024,128]{1,0:T(8,128)}) %reduce-scatter.26.cloned.1.call-update) | async-done | bytes 524304 | tf_op jit(solution)/shard_map/reduce_scatter | solution.py:251
  1441.3 337.0 %reduce-scatter.30.cloned.1.call-done = f32[128,4096]{1,0:T(8,128)} async-done(((f32[2048,4096]{1,0:T(8,128)}), f32[128,4096]{1,0:T(8,128)}) %reduce-scatter.30.cloned.1.call-update) | async-done | bytes 2097168 | tf_op jit(solution)/shard_map/reduce_scatter | solution.py:253
  1778.3 336.5 %reduce-scatter.28.cloned.1.call-done = f32[128,4096]{1,0:T(8,128)} async-done(((f32[2048,4096]{1,0:T(8,128)}), f32[128,4096]{1,0:T(8,128)}) %reduce-scatter.28.cloned.1.call-update) | async-done | bytes 2097168 | tf_op jit(solution)/shard_map/reduce_scatter | solution.py:252
  2114.9 336.7 %reduce-scatter.32.cloned.1.call-done = f32[4096,128]{1,0:T(8,128)} async-done(((f32[4096,2048]{1,0:T(8,128)}), f32[4096,128]{1,0:T(8,128)}) %reduce-scatter.32.cloned.1.call-update) | async-done | bytes 2097168 | tf_op jit(solution)/shard_map/reduce_scatter | solution.py:254
  (403 shorter events, 135.4 us)
Async XLA Ops:
  7.2 78.4 %copy-start.91 = (f32[64]{0:T(128)S(1)}, f32[64]{0:T(128)}, u32[]{:S(2)}) copy-start(f32[64]{0:T(128)} %param.18) | copy-start | bytes 772
  7.2 35.0 %all-gather.12.cloned.1.call-start = ((), (), s32[]{:S(2)}) async-start(), calls=%async_computation.11 | async-start | bytes 2359296 | tf_op jit(solution)/shard_map/all_gather | solution.py:89
  12.1 157.2 %copy-start.90 = (s32[384]{0:T(512)S(1)}, s32[384]{0:T(512)}, u32[]{:S(2)}) copy-start(s32[384]{0:T(512)} %param.26) | copy-start | bytes 4612
  12.1 70.2 %all-gather.14.cloned.1.call-start = ((), (), s32[]{:S(2)}) async-start(), calls=%async_computation.12 | async-start | bytes 1114112 | tf_op jit(solution)/shard_map/all_gather | solution.py:52
  12.8 108.5 %all-gather.18.cloned.1.call-start = ((), (), s32[]{:S(2)}) async-start(), calls=%async_computation.14 | async-start | bytes 1114112 | tf_op jit(solution)/shard_map/all_gather | solution.py:53
  13.6 165.0 %all-gather.16.cloned.1.call-start = ((), (), s32[]{:S(2)}) async-start(), calls=%async_computation.13 | async-start | bytes 4456448 | tf_op jit(solution)/shard_map/all_gather | solution.py:51
  14.1 273.9 %all-gather.20.cloned.1.call-start = ((), (), s32[]{:S(2)}) async-start(), calls=%async_computation.15 | async-start | bytes 4456448 | tf_op jit(solution)/shard_map/all_gather | solution.py:54
  15.2 168.4 %copy-start.27 = (f32[384,32]{0,1:T(8,128)}, f32[384,32]{0,1:T(8,128)S(1)}, u32[]{:S(2)}) copy-start(f32[384,32]{0,1:T(8,128)S(1)} %get-tuple-element.61) | copy-start | bytes 147460
  15.2 168.4 %copy-start.29 = (f32[384,32]{0,1:T(8,128)}, f32[384,32]{0,1:T(8,128)S(1)}, u32[]{:S(2)}) copy-start(f32[384,32]{0,1:T(8,128)S(1)} %get-tuple-element.62) | copy-start | bytes 147460
  42.1 136.4 %copy-start = (bf16[384,2048]{1,0:T(8,128)(2,1)S(1)}, bf16[384,2048]{1,0:T(8,128)(2,1)}, u32[]{:S(2)}) copy-start(bf16[384,2048]{1,0:T(8,128)(2,1)} %all-gather.12.cloned.1.call-done) | copy-start | bytes 4718596
  85.7 118.9 %copy-start.31 = (bf16[384,4,32]{0,2,1:T(8,128)(2,1)}, bf16[384,4,32]{0,2,1:T(8,128)(2,1)S(1)}, u32[]{:S(2)}) copy-start(bf16[384,4,32]{0,2,1:T(8,128)(2,1)S(1)} %get-tuple-element.50) | copy-start | bytes 294916
  85.8 118.9 %copy-start.33 = (bf16[384,4,32]{0,2,1:T(8,128)(2,1)}, bf16[384,4,32]{0,2,1:T(8,128)(2,1)S(1)}, u32[]{:S(2)}) copy-start(bf16[384,4,32]{0,2,1:T(8,128)(2,1)S(1)} %get-tuple-element.51) | copy-start | bytes 294916
  123.8 125.2 %copy-start.35 = (bf16[384,256]{0,1:T(8,128)(2,1)}, bf16[384,256]{0,1:T(8,128)(2,1)S(1)}, u32[]{:S(2)}) copy-start(bf16[384,256]{0,1:T(8,128)(2,1)S(1)} %convolution_convert_fusion.3) | copy-start | bytes 589828
  123.9 3.5 collective-permute-start
  128.1 7.0 collective-permute-start.1
  135.9 9.3 collective-permute-start.2
  145.2 11.6 collective-permute-start.3
  155.5 177.0 %reduce-scatter.12.cloned.1.call-start = ((), (), s32[]{:S(2)}) async-start(), calls=%async_computation.16 | async-start | bytes 2359296 | tf_op jit(solution)/shard_map/reduce_scatter | solution.py:154
  156.8 26.3 %copy-start.73 = (bf16[2,384,4,64]{1,3,2,0:T(8,128)(2,1)}, bf16[2,384,4,64]{1,3,2,0:T(8,128)(2,1)S(1)}, u32[]{:S(2)}) copy-start(bf16[2,384,4,64]{1,3,2,0:T(8,128)(2,1)S(1)} %collective-permute-done.3) | copy-start | bytes 1179652
  156.8 13.6 collective-permute-start.4
  170.3 78.7 %copy-start.47 = (pred[384,384]{0,1:T(8,128)(4,1)}, pred[384,384]{0,1:T(8,128)(4,1)S(1)}, u32[]{:S(2)}) copy-start(pred[384,384]{0,1:T(8,128)(4,1)S(1)} %get-tuple-element.54) | copy-start | bytes 442372
  170.3 85.9 %copy-start.39 = (pred[384,384]{0,1:T(8,128)(4,1)}, pred[384,384]{0,1:T(8,128)(4,1)S(1)}, u32[]{:S(2)}) copy-start(pred[384,384]{0,1:T(8,128)(4,1)S(1)} %get-tuple-element.57) | copy-start | bytes 442372
  170.3 93.3 %copy-start.41 = (pred[384,384]{0,1:T(8,128)(4,1)}, pred[384,384]{0,1:T(8,128)(4,1)S(1)}, u32[]{:S(2)}) copy-start(pred[384,384]{0,1:T(8,128)(4,1)S(1)} %get-tuple-element.56) | copy-start | bytes 442372
  170.4 721.0 %copy-start.45 = (pred[384,384]{0,1:T(8,128)(4,1)}, pred[384,384]{0,1:T(8,128)(4,1)S(1)}, u32[]{:S(2)}) copy-start(pred[384,384]{0,1:T(8,128)(4,1)S(1)} %get-tuple-element.58) | copy-start | bytes 442372
  170.4 727.1 %copy-start.43 = (pred[384,384]{0,1:T(8,128)(4,1)}, pred[384,384]{0,1:T(8,128)(4,1)S(1)}, u32[]{:S(2)}) copy-start(pred[384,384]{0,1:T(8,128)(4,1)S(1)} %get-tuple-element.60) | copy-start | bytes 442372
  170.4 39.3 %collective-permute-start.5 = (bf16[2,384,4,64]{1,3,2,0:T(8,128)(2,1)}, bf16[2,384,4,64]{1,3,2,0:T(8,128)(2,1)}, u32[]{:S(2)}, u32[]{:S(2)}) collective-permute-start(bf16[2,384,4,64]{1,3,2,0:T(8,128)(2,1)} %collective-permute-done.4), channel_id=1, source_target_pairs={{0,2},{2,4},{4,6},{6,8},{8,10},{10,12},{12,14},{14,16},{16,18},{18... | collective-permute-start | bytes 1179656 | tf_op jit(solution)/shard_map/ppermute | solution.py:17
  186.1 92.1 %copy-start.17 = (f32[4,384,384,4]{2,1,3,0:T(8,128)}, f32[4,384,384,4]{2,1,3,0:T(8,128)S(1)}, u32[]{:S(2)}) copy-start(f32[4,384,384,4]{2,1,3,0:T(8,128)S(1)} %get-tuple-element.78) | copy-start | bytes 28311556
  187.7 87.0 %copy-start.18 = (f32[4,384,384,4]{2,1,3,0:T(8,128)}, f32[4,384,384,4]{2,1,3,0:T(8,128)S(1)}, u32[]{:S(2)}) copy-start(f32[4,384,384,4]{2,1,3,0:T(8,128)S(1)} %get-tuple-element.76) | copy-start | bytes 28311556
  288.1 44.5 %copy-start.2 = (bf16[192,2048]{1,0:T(8,128)(2,1)S(1)}, bf16[192,2048]{1,0:T(8,128)(2,1)}, u32[]{:S(2)}) copy-start(bf16[192,2048]{1,0:T(8,128)(2,1)} %param.14) | copy-start | bytes 2359300
  288.1 46.0 %copy-start.57 = (f32[2048]{0:T(1024)S(1)}, f32[2048]{0:T(1024)}, u32[]{:S(2)}) copy-start(f32[2048]{0:T(1024)} %param.16) | copy-start | bytes 24580
  293.6 70.2 %all-gather.22.cloned.1.call-start = ((), (), s32[]{:S(2)}) async-start(), calls=%async_computation.17 | async-start | bytes 2359296 | tf_op jit(solution)/shard_map/all_gather | solution.py:162
  334.0 522.3 %copy-start.82 = (f32[192]{0:T(256)}, f32[192]{0:T(256)S(1)}, u32[]{:S(2)}) copy-start(f32[192]{0:T(256)S(1)} %fusion.168) | copy-start | bytes 2308
  336.4 156.7 %all-gather.26.cloned.1.call-start = ((), (), s32[]{:S(2)}) async-start(), calls=%async_computation.19 | async-start | bytes 17825792 | tf_op jit(solution)/shard_map/all_gather | solution.py:56
  337.1 283.4 %all-gather.24.cloned.1.call-start = ((), (), s32[]{:S(2)}) async-start(), calls=%async_computation.18 | async-start | bytes 17825792 | tf_op jit(solution)/shard_map/all_gather | solution.py:55
  337.9 309.6 %all-gather.30.cloned.1.call-start = ((), (), s32[]{:S(2)}) async-start(), calls=%async_computation.22 | async-start | bytes 2359296 | tf_op jit(solution)/shard_map/all_gather | solution.py:176
  338.4 441.8 %all-gather.28.cloned.1.call-start = ((), (), s32[]{:S(2)}) async-start(), calls=%async_computation.20 | async-start | bytes 17825792 | tf_op jit(solution)/shard_map/all_gather | solution.py:57
  339.2 514.6 %reduce-scatter.16.cloned.1.call-start = ((), (), s32[]{:S(2)}) async-start(), calls=%async_computation.23 | async-start | bytes 2359296 | tf_op jit(solution)/shard_map/reduce_scatter | solution.py:181
  363.7 256.8 %copy-start.15 = (bf16[384,2048]{1,0:T(8,128)(2,1)S(1)}, bf16[384,2048]{1,0:T(8,128)(2,1)}, u32[]{:S(2)}) copy-start(bf16[384,2048]{1,0:T(8,128)(2,1)} %all-gather.22.cloned.1.call-done) | copy-start | bytes 4718596
  810.2 43.7 %copy-start.10 = (bf16[192,2048]{1,0:T(8,128)(2,1)S(1)}, bf16[192,2048]{1,0:T(8,128)(2,1)}, u32[]{:S(2)}) copy-start(bf16[192,2048]{1,0:T(8,128)(2,1)} %reduce-scatter.12.cloned.1.call-done) | copy-start | bytes 2359300
  810.2 46.1 %copy-start.19 = (bf16[192,2048]{1,0:T(8,128)(2,1)S(1)}, bf16[192,2048]{1,0:T(8,128)(2,1)}, u32[]{:S(2)}) copy-start(bf16[192,2048]{1,0:T(8,128)(2,1)} %param.27) | copy-start | bytes 2359300
  829.4 57.0 %all-gather.32.cloned.1.call-start = ((), (), s32[]{:S(2)}) async-start(), calls=%async_computation.24 | async-start | bytes 2359296 | tf_op jit(solution)/shard_map/all_gather | solution.py:191
  856.3 34.6 %copy-start.86 = (f32[192]{0:T(256)}, f32[192]{0:T(256)S(1)}, u32[]{:S(2)}) copy-start(f32[192]{0:T(256)S(1)} %multiply_multiply_fusion.5) | copy-start | bytes 2308
  859.1 255.5 %reduce-scatter.18.cloned.1.call-start = ((), (), s32[]{:S(2)}) async-start(), calls=%async_computation.25 | async-start | bytes 2359296 | tf_op jit(solution)/shard_map/reduce_scatter | solution.py:235
  934.9 48.2 %collective-permute-start.6 = (bf16[2,384,4,64]{1,3,2,0:T(8,128)(2,1)}, bf16[2,384,4,64]{1,3,2,0:T(8,128)(2,1)}, u32[]{:S(2)}, u32[]{:S(2)}) collective-permute-start(bf16[2,384,4,64]{1,3,2,0:T(8,128)(2,1)} %pad_maximum_fusion.2), channel_id=1, source_target_pairs={{2,0},{4,2},{6,4},{8,6},{10,8},{12,10},{14,12},{16,14},{18,16},{20... | collective-permute-start | bytes 1179656 | tf_op jit(solution)/shard_map/ppermute | solution.py:17
  984.3 4.4 collective-permute-start.7
  988.7 9.1 collective-permute-start.8
  997.9 9.1 collective-permute-start.9
  1007.2 9.2 collective-permute-start.10
  1016.5 9.1 collective-permute-start.11
  1028.8 137.9 %reduce-scatter.14.cloned.1.call-start = ((), (), s32[]{:S(2)}) async-start(), calls=%async_computation.21 | async-start | bytes 2359296 | tf_op jit(solution)/shard_map/reduce_scatter | solution.py:169
  1041.1 129.8 %reduce-scatter.22.cloned.1.call-start = ((), (), s32[]{:S(2)}) async-start(), calls=%async_computation.27 | async-start | bytes 2228224 | tf_op jit(solution)/shard_map/reduce_scatter | solution.py:249
  1043.2 180.7 %reduce-scatter.24.cloned.1.call-start = ((), (), s32[]{:S(2)}) async-start(), calls=%async_computation.28 | async-start | bytes 2228224 | tf_op jit(solution)/shard_map/reduce_scatter | solution.py:250
  1045.4 286.6 %reduce-scatter.20.cloned.1.call-start = ((), (), s32[]{:S(2)}) async-start(), calls=%async_computation.26 | async-start | bytes 8912896 | tf_op jit(solution)/shard_map/reduce_scatter | solution.py:248
  1051.2 390.0 %reduce-scatter.26.cloned.1.call-start = ((), (), s32[]{:S(2)}) async-start(), calls=%async_computation.29 | async-start | bytes 8912896 | tf_op jit(solution)/shard_map/reduce_scatter | solution.py:251
  1058.5 719.8 %reduce-scatter.30.cloned.1.call-start = ((), (), s32[]{:S(2)}) async-start(), calls=%async_computation.31 | async-start | bytes 35651584 | tf_op jit(solution)/shard_map/reduce_scatter | solution.py:253
  1077.7 1037.2 %reduce-scatter.28.cloned.1.call-start = ((), (), s32[]{:S(2)}) async-start(), calls=%async_computation.30 | async-start | bytes 35651584 | tf_op jit(solution)/shard_map/reduce_scatter | solution.py:252
  1095.0 1356.5 %reduce-scatter.32.cloned.1.call-start = ((), (), s32[]{:S(2)}) async-start(), calls=%async_computation.32 | async-start | bytes 35651584 | tf_op jit(solution)/shard_map/reduce_scatter | solution.py:254
  1114.5 52.2 %copy-start.89 = (f32[192]{0:T(256)S(1)}, f32[192]{0:T(256)}, u32[]{:S(2)}) copy-start(f32[192]{0:T(256)} %copy-done.88) | copy-start | bytes 2308
  1114.5 52.3 %copy-start.11 = (bf16[192,2048]{1,0:T(8,128)(2,1)S(1)}, bf16[192,2048]{1,0:T(8,128)(2,1)}, u32[]{:S(2)}) copy-start(bf16[192,2048]{1,0:T(8,128)(2,1)} %reduce-scatter.12.cloned.1.call-done) | copy-start | bytes 2359300
  1114.5 52.3 %copy-start.20 = (bf16[192,2048]{1,0:T(8,128)(2,1)S(1)}, bf16[192,2048]{1,0:T(8,128)(2,1)}, u32[]{:S(2)}) copy-start(bf16[192,2048]{1,0:T(8,128)(2,1)} %param.27) | copy-start | bytes 2359300
  1114.5 52.3 %copy-start.21 = (bf16[192,2048]{1,0:T(8,128)(2,1)S(1)}, bf16[192,2048]{1,0:T(8,128)(2,1)}, u32[]{:S(2)}) copy-start(bf16[192,2048]{1,0:T(8,128)(2,1)} %reduce-scatter.16.cloned.1.call-done) | copy-start | bytes 2359300
  1114.5 52.3 %copy-start.58 = (f32[2048]{0:T(1024)S(1)}, f32[2048]{0:T(1024)}, u32[]{:S(2)}) copy-start(f32[2048]{0:T(1024)} %param.16) | copy-start | bytes 24580
  1114.6 52.3 %copy-start.83 = (f32[192]{0:T(256)S(1)}, f32[192]{0:T(256)}, u32[]{:S(2)}) copy-start(f32[192]{0:T(256)} %copy-done.82) | copy-start | bytes 2308
  1114.6 52.3 %copy-start.87 = (f32[192]{0:T(256)S(1)}, f32[192]{0:T(256)}, u32[]{:S(2)}) copy-start(f32[192]{0:T(256)} %copy-done.86) | copy-start | bytes 2308
  (95 other events, 542.0 us)
Sparse Core Ops, SparseCore 0:
  12.2 29.8 all-gather.11
  44.3 37.9 all-gather.13
  84.5 36.8 all-gather.17
  123.4 54.1 all-gather.15
  179.6 54.2 all-gather.19
  293.7 38.8 reduce-scatter.11
  336.5 27.2 all-gather.21
  366.1 126.8 all-gather.25
  495.5 125.0 all-gather.23
  622.0 25.3 all-gather.29
  649.8 130.3 all-gather.27
  829.5 24.2 reduce-scatter.15
  859.2 27.2 all-gather.31
  1029.0 35.2 reduce-scatter.17
  1066.4 26.0 reduce-scatter.13
  1096.7 61.9 reduce-scatter.21
  1163.4 60.4 reduce-scatter.23
  1228.4 103.5 reduce-scatter.19
  1336.7 104.5 reduce-scatter.25
  1446.0 332.3 reduce-scatter.29
  1783.2 331.6 reduce-scatter.27
  2119.7 331.7 reduce-scatter.31
where the time goes:
time: 2460 us
  waiting for transfers between devices  1920 us (78%)
  matrix products  343 us (14%)
  other arithmetic  58.5 us (2%)
  starting transfers between devices  57.4 us (2%)
  blocking collectives  49.1 us (2%)
    reduce_scatter x1, waiting for transfers between devices, on_device(): lax.psum_scatter(d_up_w, 'ctx', scatter_dimension=0, tiled=True)  337 us
    reduce_scatter x1, waiting for transfers between devices, on_device(): lax.psum_scatter(d_down, 'ctx', scatter_dimension=1, tiled=True)  337 us
    reduce_scatter x1, waiting for transfers between devices, on_device(): lax.psum_scatter(d_gate_w, 'ctx', scatter_dimension=0, tiled=True)  337 us
    dot_general x21, matrix products, matrix_multiply(): return jnp.dot(left, right, preferred_element_type=jnp.float32)  177 us
    all_gather x1, waiting for transfers between devices, gather_weights(): lax.all_gather(w_down, 'ctx', axis=1, tiled=True)  133 us
    all_gather x1, waiting for transfers between devices, gather_weights(): lax.all_gather(w_up, 'ctx', axis=0, tiled=True)  129 us
    all_gather x1, waiting for transfers between devices, gather_weights(): lax.all_gather(w_gate, 'ctx', axis=0, tiled=True)  115 us
    reduce_scatter x1, waiting for transfers between devices, on_device(): lax.psum_scatter(d_out_w, 'ctx', scatter_dimension=1, tiled=True)  109 us
  transfers between devices with their start and end apart: 34, of which 26 were waited for; matrix products, arithmetic and copies ran while one was open for 11% of the time, Pallas kernels for 0%

commit v1 on v0

v1 whole, which is shorter than its diff:
```python
import functools
import math

import jax
import jax.numpy as jnp
from jax import lax
from jax.experimental import pallas as pl
from jax.experimental.pallas import tpu as pltpu
from jax.sharding import PartitionSpec as P

WB = 6
EPSILON = 1e-05
ROPE_BASE = 1000000.0
LOG2E = math.log2(math.e)

QUAD = 4
KEY_BLOCK = 256

F32 = jnp.float32
BF16 = jnp.bfloat16


def swap_ctx(value, bit):
    n = lax.axis_size("ctx")
    return lax.ppermute(value, "ctx", [(i, i ^ bit) for i in range(n)])


def swap_core(value):
    return swap_ctx(value, 1)


def swap_b(value):
    return swap_ctx(value, 2)


def swap_x(value):
    return lax.ppermute(value, "tp", [(0, 1), (1, 0)])


def line_move(value, by, sources):
    pairs = [(s * QUAD + q, (s + by) * QUAD + q) for s in sources for q in range(QUAD)]
    return lax.ppermute(value, "ctx", pairs)


def line_gather(own, line, n):
    up, down = [own], [own]
    for j in range(1, n):
        up.append(line_move(up[-1], 1, range(j - 1, n - 1)))
        down.append(line_move(down[-1], -1, range(1, n - j + 1)))
    slots = [own]
    for j in range(1, n):
        slots.append(jnp.where(line + j < n, down[j], up[n - j]))
    return slots


def add16(a, b):
    return (a.astype(F32) + b.astype(F32)).astype(BF16)


def line_scatter(slots, n):
    got_up = got_down = None
    for t in range(1, n):
        send_up, send_down = slots[n - t], slots[t]
        if got_up is not None:
            send_up, send_down = add16(send_up, got_up), add16(send_down, got_down)
        got_up = line_move(send_up, 1, range(0, t))
        got_down = line_move(send_down, -1, range(n - t, n))
    total = slots[0].astype(F32)
    if got_up is not None:
        total = total + got_up.astype(F32) + got_down.astype(F32)
    return total


def gather_rows(own):
    half = own.shape[0] // 2
    from_x, from_b = swap_x(own), swap_b(own)
    top, bottom = swap_x(from_b[:half]), swap_b(from_x[half:])
    near = [own, from_x, from_b, top, bottom]
    return jnp.concatenate(near + [swap_core(piece) for piece in near], axis=0)


def scatter_rows(near, far):
    r = near.shape[0] // 4
    half = r // 2

    def fold(block):
        rows = slice(block * r, (block + 1) * r)
        return add16(near[rows], swap_core(far[rows]))

    both, for_x, for_b, own = fold(3), fold(1), fold(2), fold(0)
    top, bottom = swap_x(both[:half]), swap_b(both[half:])
    x_top, b_bottom = swap_x(for_x[:half]), swap_b(for_b[half:])
    x_bottom = swap_x(add16(for_x[half:], bottom))
    b_top = swap_b(add16(for_b[:half], top))
    own = own.astype(F32)
    return jnp.concatenate(
        [
            own[:half] + x_top.astype(F32) + b_top.astype(F32),
            own[half:] + b_bottom.astype(F32) + x_bottom.astype(F32),
        ],
        axis=0,
    )


def spread(pieces):
    n = lax.axis_size("ctx")
    groups = [list(range(i, i + QUAD)) for i in range(0, n, QUAD)]
    return lax.all_to_all(pieces, "ctx", 0, 0, axis_index_groups=groups, tiled=True)


def sum_everywhere(value):
    bit = 1
    value = value + swap_x(value)
    while bit < lax.axis_size("ctx"):
        value = value + swap_ctx(value, bit)
        bit *= 2
    return value


def dot(a, b):
    return jnp.dot(a, b, preferred_element_type=F32)


def dot_nt(a, b):
    return lax.dot_general(a, b, (((1,), (1,)), ((), ())), preferred_element_type=F32)


def dot_tn(a, b):
    return lax.dot_general(a, b, (((0,), (0,)), ((), ())), preferred_element_type=F32)


def rms_scale(values):
    return lax.rsqrt(jnp.mean(values * values, axis=-1, keepdims=True) + EPSILON)


def norm_back(values, scale, gain, grad):
    unit = values * scale
    inner = grad * gain
    d_values = scale * (inner - unit * jnp.mean(inner * unit, axis=-1, keepdims=True))
    return d_values, jnp.sum(grad * unit, axis=0)


def swap_halves(u):
    h = u.shape[-1] // 2
    return jnp.concatenate([u[:, h:], u[:, :h]], axis=-1)


def prep_kernel(table, raw_ref, cos_ref, sin_ref, q_gain_ref, k_gain_ref, q_ref, kv_ref, *, heads, width):
    cos, sin = cos_ref[...], sin_ref[...]

    def ready(u, gain):
        u = u * rms_scale(u) * gain
        return (u * cos + swap_halves(u) * sin).astype(BF16)

    for h in range(heads):
        cols = slice(h * width, (h + 1) * width)
        q_ref[:, cols] = ready(raw_ref[:, cols], q_gain_ref[...])
    k0 = heads * width
    kv_ref[:, :width] = ready(raw_ref[:, k0 : k0 + width], k_gain_ref[...])
    kv_ref[:, width:] = raw_ref[:, k0 + width :].astype(BF16)


def prep_back_kernel(
    table, raw_ref, cos_ref, sin_ref, q_gain_ref, k_gain_ref, dq_ref, dkv_ref, out_ref, dg_ref, *, heads, width
):
    cos, sin = cos_ref[...], sin_ref[...]

    @pl.when(pl.program_id(0) == 0)
    def _():
        dg_ref[...] = jnp.zeros_like(dg_ref)

    def back(w, gain, grad):
        e = grad * cos - swap_halves(grad) * sin
        scale = rms_scale(w)
        unit = w * scale
        inner = e * gain
        dw = scale * (inner - unit * jnp.mean(inner * unit, axis=-1, keepdims=True))
        return dw.astype(BF16), jnp.sum(e * unit, axis=0, keepdims=True)

    total = jnp.zeros((1, width), F32)
    for h in range(heads):
        cols = slice(h * width, (h + 1) * width)
        dw, dg = back(raw_ref[:, cols], q_gain_ref[...], dq_ref[:, cols])
        out_ref[:, cols] = dw
        total = total + dg
    k0 = heads * width
    dw, dg = back(raw_ref[:, k0 : k0 + width], k_gain_ref[...], dkv_ref[:, :width])
    out_ref[:, k0 : k0 + width] = dw
    out_ref[:, k0 + width :] = dkv_ref[:, width:].astype(BF16)
    dg_ref[0:1, :] += total
    dg_ref[1:2, :] += dg


def stack_heads(block, heads, width):
    return jnp.concatenate([block[:, h * width : (h + 1) * width] for h in range(heads)], axis=0)


def attend_kernel(
    table, lo, hi, q_ref, start_ref, kv_ref, o_ref, of_ref, stat_ref, acc, total, *, heads, width, reach, bk
):
    t = pl.program_id(0)
    r = q_ref.shape[0]
    q = stack_heads(q_ref[...], heads, width)
    q = jnp.concatenate([q, jnp.zeros_like(q)], axis=-1)
    start = jnp.concatenate([start_ref[...]] * heads, axis=0)
    pos = reach + t * r + lax.broadcasted_iota(jnp.int32, (r, 1), 0)
    pos = jnp.concatenate([pos] * heads, axis=0)
    acc[...] = jnp.zeros_like(acc)
    total[...] = jnp.zeros_like(total)
    c = LOG2E / math.sqrt(width)

    def step(kb, carry):
        k0 = pl.multiple_of(kb * bk, bk)
        kv = kv_ref[pl.ds(k0, bk), :]
        s = dot_nt(q, kv)
        key = k0 + lax.broadcasted_iota(jnp.int32, (1, bk), 1)
        p = jnp.where((key >= start) & (key <= pos), jnp.exp2(s * c), 0.0)
        total[...] += jnp.sum(p, axis=-1, keepdims=True)
        acc[...] += dot(p.astype(BF16), kv)
        return carry

    lax.fori_loop(lo[t], hi[t], step, 0)
    o = acc[...][:, width:] / total[...]
    stat_ref[...] = jnp.log2(total[...])
    for h in range(heads):
        part = o[h * r : (h + 1) * r]
        of_ref[:, h * width : (h + 1) * width] = part
        o_ref[:, h * width : (h + 1) * width] = part.astype(BF16)


def attend_back_kernel(
    table, lo, hi, q_ref, do_ref, of_ref, stat_ref, start_ref, kv_ref, dq_ref, dkv_ref, acc, *, heads, width, reach, bk
):
    t = pl.program_id(0)
    r = q_ref.shape[0]

    @pl.when(t == 0)
    def _():
        dkv_ref[...] = jnp.zeros_like(dkv_ref)

    scale = 1.0 / math.sqrt(width)
    q = stack_heads(q_ref[...], heads, width)
    do = stack_heads(do_ref[...], heads, width)
    of = stack_heads(of_ref[...], heads, width)
    delta = jnp.sum(do.astype(F32) * of, axis=-1, keepdims=True)
    lane = lax.broadcasted_iota(jnp.int32, (heads * r, 2 * width), 1)
    rows = jnp.transpose(jnp.where(lane == 0, stat_ref[...], delta))
    stat, delta = rows[0:1, :], rows[1:2, :]
    q = jnp.concatenate([q, jnp.zeros_like(q)], axis=-1)
    q_scaled = (q.astype(F32) * scale).astype(BF16)
    do = jnp.concatenate([jnp.zeros_like(do), do], axis=-1)
    start = jnp.concatenate([start_ref[0]] * heads, axis=-1)
    pos = reach + t * r + lax.broadcasted_iota(jnp.int32, (1, r), 1)
    pos = jnp.concatenate([pos] * heads, axis=-1)
    acc[...] = jnp.zeros_like(acc)

    def step(kb, carry):
        k0 = pl.multiple_of(kb * bk, bk)
        kv = kv_ref[pl.ds(k0, bk), :]
        s = dot_nt(kv, q_scaled)
        dp = dot_nt(kv, do)
        key = k0 + lax.broadcasted_iota(jnp.int32, (bk, 1), 0)
        p = jnp.where((key >= start) & (key <= pos), jnp.exp2(s * LOG2E - stat), 0.0)
        ds = (p * (dp - delta)).astype(BF16)
        dkv_ref[pl.ds(k0, bk), :] += dot(ds, q_scaled) + dot(p.astype(BF16), do)
        acc[...] += dot_tn(ds, kv)
        return carry

    lax.fori_loop(lo[t], hi[t], step, 0)
    dq = acc[...][:, :width] * scale
    for h in range(heads):
        dq_ref[:, h * width : (h + 1) * width] = dq[h * r : (h + 1) * r]


def call(kernel, blocks, prefetch, ins, outs, scratch, args, flops, nbytes, transcendentals=0):
    return pl.pallas_call(
        kernel,
        out_shape=[jax.ShapeDtypeStruct(shape, dtype) for shape, dtype, _ in outs],
        grid_spec=pltpu.PrefetchScalarGridSpec(
            num_scalar_prefetch=prefetch,
            grid=(blocks,),
            in_specs=ins,
            out_specs=[spec for _, _, spec in outs],
            scratch_shapes=scratch,
        ),
        compiler_params=pltpu.CompilerParams(
            dimension_semantics=("arbitrary",), vmem_limit_bytes=48 * 1024 * 1024
        ),
        cost_estimate=pl.CostEstimate(
            flops=int(flops), bytes_accessed=int(nbytes), transcendentals=int(transcendentals)
        ),
    )(*args)


def on_device(
    tokens,
    attn_gain,
    ffn_gain,
    query_norm_gain,
    k_gain,
    w_query,
    key_projection,
    value_projection,
    w_out,
    w_gate,
    w_up,
    w_down,
    doc_start,
    cotangent,
):
    i, x = lax.axis_index("ctx"), lax.axis_index("tp")
    n = lax.axis_size("ctx") // QUAD
    line, b, core = i // QUAD, (i // 2) % 2, i % 2
    r, model = tokens.shape
    plane = 2 * QUAD * r
    width = query_norm_gain.shape[0]
    heads = w_query.shape[1] // QUAD // width
    qw = heads * width
    hidden = w_gate.shape[1] // QUAD
    step = model // n
    reach = WB * doc_start.shape[0]

    def rotated(v):
        return lax.dynamic_slice_in_dim(jnp.concatenate([v, v], axis=-1), line * step, model, v.ndim - 1)

    def unrotated(v):
        return lax.dynamic_slice_in_dim(jnp.concatenate([v, v], axis=-1), (n - line) * step, model, v.ndim - 1)

    def columns(j):
        return slice(j * step, (j + 1) * step)

    def by_quarter(w):
        return w.reshape(w.shape[0], QUAD, -1)

    qkv_shard = jnp.concatenate(
        [by_quarter(w_query), by_quarter(key_projection), by_quarter(value_projection)], axis=-1
    ).transpose(1, 0, 2)
    qkv_shard = spread(qkv_shard).reshape(step, -1)
    out_shard = spread(w_out.reshape(QUAD, qw, -1)).transpose(1, 0, 2).reshape(qw, step)
    gu_shard = jnp.concatenate([by_quarter(w_gate), by_quarter(w_up)], axis=-1).transpose(1, 0, 2)
    gu_shard = spread(gu_shard).reshape(step, -1)
    down_shard = spread(w_down.reshape(QUAD, hidden, -1)).transpose(1, 0, 2).reshape(hidden, step)
    w_qkv = jnp.concatenate(line_gather(qkv_shard, line, n), axis=0)
    w_o = jnp.concatenate(line_gather(out_shard, line, n), axis=1)
    w_gu = jnp.concatenate(line_gather(gu_shard, line, n), axis=0)
    w_d = jnp.concatenate(line_gather(down_shard, line, n), axis=1)

    near_core, near_b = swap_core(doc_start), swap_b(doc_start)
    far = swap_core(near_b)
    rows0 = [jnp.where(core == c, doc_start, near_core) for c in range(2)]
    rows1 = [jnp.where(core == c, near_b, far) for c in range(2)]
    starts = jnp.concatenate([jnp.where(b == y, rows0[c], rows1[c]) for y in range(2) for c in range(2)])
    first = line * plane
    relative = first + jnp.arange(plane, dtype=jnp.int32) - starts
    inv_freq = jnp.power(ROPE_BASE, -2.0 * jnp.arange(width // 2, dtype=F32) / width)
    angles = relative.astype(F32)[:, None] * inv_freq[None, :]
    cos, sin = jnp.cos(angles), jnp.sin(angles)
    cos = jnp.concatenate([cos, cos], axis=-1)
    sin = jnp.concatenate([-sin, sin], axis=-1)
    blocks = jnp.arange(2 * QUAD, dtype=jnp.int32)
    table = (
        ((((blocks >> 1) & 1) ^ core) << 2) | (((blocks >> 2) ^ b) << 1) | ((blocks & 1) ^ x)
    ).astype(jnp.int32)
    local_start = starts - (first - reach)
    lo = local_start[::r] // KEY_BLOCK
    hi = (reach + (blocks + 1) * r - 1) // KEY_BLOCK + 1
    nb = 2 * QUAD

    gain_1, gain_2 = rotated(attn_gain), rotated(ffn_gain)
    x_own = rotated(tokens).astype(F32)
    scale_1 = rms_scale(x_own)
    a_one = gather_rows((x_own * scale_1 * gain_1).astype(BF16))
    cot_own = rotated(cotangent)
    cot = gather_rows(cot_own)
    raw = dot(a_one, w_qkv)

    def here(cols):
        return pl.BlockSpec((r, cols), lambda t, *_: (t, 0))

    def moved(cols):
        return pl.BlockSpec((r, cols), lambda t, table, *_: (table[t], 0))

    def whole(shape):
        return pl.BlockSpec(shape, lambda t, *_: (0,) * len(shape))

    q_gain, key_gain = query_norm_gain[None, :], k_gain[None, :]
    q, kv = call(
        functools.partial(prep_kernel, heads=heads, width=width),
        nb,
        1,
        [moved(qw + 2 * width), here(width), here(width), whole((1, width)), whole((1, width))],
        [((plane, qw), BF16, here(qw)), ((plane, 2 * width), BF16, here(2 * width))],
        [],
        (table, raw, cos, sin, q_gain, key_gain),
        plane * (qw + width) * 10,
        plane * (qw + 2 * width) * 6,
    )
    spans = []
    left, distance = reach, 1
    while left > 0:
        spans.append((distance, min(left, plane)))
        left -= plane
        distance += 1
    halo = [line_move(kv[plane - rows :], d, range(0, max(n - d, 0))) for d, rows in spans]
    keys = jnp.concatenate(halo[::-1] + [kv], axis=0)
    nk = keys.shape[0]
    attn_flops = 2 * plane * heads * (plane // 2 + 2 * KEY_BLOCK) * width

    stacked = pl.BlockSpec((heads * r, 1), lambda t, *_: (t, 0))
    o, o_float, stat = call(
        functools.partial(attend_kernel, heads=heads, width=width, reach=reach, bk=KEY_BLOCK),
        nb,
        3,
        [here(qw), pl.BlockSpec((r, 1), lambda t, *_: (t, 0)), whole((nk, 2 * width))],
        [
            ((plane, qw), BF16, moved(qw)),
            ((plane, qw), F32, here(qw)),
            ((plane * heads, 1), F32, stacked),
        ],
        [pltpu.VMEM((heads * r, 2 * width), F32), pltpu.VMEM((heads * r, 1), F32)],
        (table, lo, hi, q, local_start[:, None], keys),
        8 * attn_flops,
        plane * qw * 8,
    )

    half = plane // 2
    attn_sum = scatter_rows(dot(o[:half], w_o).astype(BF16), dot(o[half:], w_o).astype(BF16))
    resid = x_own + attn_sum
    scale_2 = rms_scale(resid)
    a_two = gather_rows((resid * scale_2 * gain_2).astype(BF16))

    gate_up = dot(a_two, w_gu)
    gate, up = gate_up[:, :hidden], gate_up[:, hidden:]
    d_hid = dot_nt(cot, w_d)
    sig = jax.nn.sigmoid(gate)
    silu = gate * sig
    hid = (silu * up).astype(BF16)
    d_gate = (d_hid * up * sig * (1.0 + gate * (1.0 - sig))).astype(BF16)
    d_up = (d_hid * silu).astype(BF16)
    d_gu = jnp.concatenate([d_gate, d_up], axis=-1)
    d_two = scatter_rows(dot_nt(d_gu[:half], w_gu).astype(BF16), dot_nt(d_gu[half:], w_gu).astype(BF16))
    d_res, d_ffn_gain = norm_back(resid, scale_2, gain_2, d_two)
    d_h = cot_own.astype(F32) + d_res
    d_h_rows = gather_rows(d_h.astype(BF16))
    ffn_sum = scatter_rows(dot(hid[:half], w_d).astype(BF16), dot(hid[half:], w_d).astype(BF16))
    out_tokens = unrotated((resid + ffn_sum).astype(BF16))

    gu_grad = line_scatter([dot_tn(a_two[:, columns(j)], d_gu).astype(BF16) for j in range(n)], n)
    down_grad = line_scatter([dot_tn(hid, cot[:, columns(j)]).astype(BF16) for j in range(n)], n)

    d_o = dot_nt(d_h_rows, w_o).astype(BF16)
    dq, dkv = call(
        functools.partial(attend_back_kernel, heads=heads, width=width, reach=reach, bk=KEY_BLOCK),
        nb,
        3,
        [
            here(qw),
            moved(qw),
            here(qw),
            stacked,
            pl.BlockSpec((1, 1, r), lambda t, *_: (t, 0, 0)),
            whole((nk, 2 * width)),
        ],
        [((plane, qw), F32, here(qw)), ((nk, 2 * width), F32, whole((nk, 2 * width)))],
        [pltpu.VMEM((heads * r, 2 * width), F32)],
        (table, lo, hi, q, d_o, o_float, stat, local_start.reshape(nb, 1, r), keys),
        20 * attn_flops,
        plane * qw * 12,
    )
    dkv_own = dkv[nk - plane :]
    offset = nk - plane
    for d, rows in spans:
        back = line_move(dkv[offset - rows : offset].astype(BF16), -d, range(d, n)).astype(F32)
        offset -= rows
        dkv_own = dkv_own + jnp.concatenate([jnp.zeros((plane - rows, 2 * width), F32), back], axis=0)
    d_raw, d_head_gains = call(
        functools.partial(prep_back_kernel, heads=heads, width=width),
        nb,
        1,
        [
            moved(qw + 2 * width),
            here(width),
            here(width),
            whole((1, width)),
            whole((1, width)),
            here(qw),
            here(2 * width),
        ],
        [((plane, qw + 2 * width), BF16, moved(qw + 2 * width)), ((8, width), F32, whole((8, width)))],
        [],
        (table, raw, cos, sin, q_gain, key_gain, dq, dkv_own),
        plane * (qw + width) * 20,
        plane * (qw + 2 * width) * 10,
    )
    out_grad = line_scatter([dot_tn(o, d_h_rows[:, columns(j)]).astype(BF16) for j in range(n)], n)
    qkv_grad = line_scatter([dot_tn(a_one[:, columns(j)], d_raw).astype(BF16) for j in range(n)], n)
    d_one = scatter_rows(dot_nt(d_raw[:half], w_qkv).astype(BF16), dot_nt(d_raw[half:], w_qkv).astype(BF16))
    d_x, d_attn_gain = norm_back(x_own, scale_1, gain_1, d_one)
    d_tokens = unrotated(d_h + d_x)

    def columns_back(grad):
        return spread(grad.astype(BF16).reshape(QUAD, step // QUAD, -1)).transpose(1, 0, 2)

    def rows_back(grad):
        pieces = grad.astype(BF16).reshape(grad.shape[0], QUAD, -1).transpose(1, 0, 2)
        return spread(pieces).reshape(QUAD * grad.shape[0], -1).astype(F32)

    gu_back = columns_back(gu_grad)
    qkv_back = columns_back(qkv_grad)
    kk = step // QUAD

    def piece(v, start, size):
        return v[:, :, start : start + size].reshape(kk, -1).astype(F32)

    gains = sum_everywhere(
        jnp.concatenate([unrotated(d_attn_gain), unrotated(d_ffn_gain), d_head_gains[0], d_head_gains[1]])
    )
    return (
        out_tokens,
        d_tokens,
        gains[:model],
        gains[model : 2 * model],
        gains[2 * model : 2 * model + width],
        gains[2 * model + width :],
        piece(qkv_back, 0, qw),
        piece(qkv_back, qw, width),
        piece(qkv_back, qw + width, width),
        rows_back(out_grad),
        piece(gu_back, 0, hidden),
        piece(gu_back, hidden, hidden),
        rows_back(down_grad),
    )


def solution(mesh):
    return jax.shard_map(
        on_device,
        mesh=mesh,
        in_specs=(
            P(("ctx", "tp"), None),
            P(),
            P(),
            P(),
            P(),
            P("ctx", "tp"),
            P("ctx", "tp"),
            P("ctx", "tp"),
            P("tp", "ctx"),
            P("ctx", "tp"),
            P("ctx", "tp"),
            P("tp", "ctx"),
            P("ctx"),
            P(("ctx", "tp"), None),
        ),
        out_specs=(
            P(("ctx", "tp"), None),
            P(("ctx", "tp"), None),
            P(),
            P(),
            P(),
            P(),
            P("ctx", "tp"),
            P("ctx", "tp"),
            P("ctx", "tp"),
            P("tp", "ctx"),
            P("ctx", "tp"),
            P("ctx", "tp"),
            P("tp", "ctx"),
        ),
        check_vma=False,
    )
```

time: 2460 us -> 1030 us (0.42)
  waiting for transfers between devices: 1920 us -> 369 us
  starting transfers between devices: 57.4 us -> 282 us
  matrix products: 343 us -> 151 us
  Pallas kernels: 0 us -> 74.1 us
  local copies, waits for them, and re-layouts: 10.8 us -> 67.9 us
  blocking collectives: 49.1 us -> 0 us
    reduce_scatter x11 -> x0, waiting for transfers between devices: 1340 us -> none  [the longest x1 337 us: on_device(): lax.psum_scatter(d_up_w, 'ctx', scatter_dimension=0, tiled=True)]
    all_gather x11 -> x0, waiting for transfers between devices: 546 us -> none  [the longest x1 133 us: gather_weights(): lax.all_gather(w_down, 'ctx', axis=1, tiled=True)]
    ppermute x12 -> x136, waiting for transfers between devices: 27.9 us -> 364 us  [the longest x52 243 us: line_move(): return lax.ppermute(value, 'ctx', pairs)]
    ppermute x12 -> x136, starting transfers between devices: 55.4 us -> 250 us  [the longest x52 185 us: line_move(): return lax.ppermute(value, 'ctx', pairs)]
    dot_general x63 -> x28, matrix products: 343 us -> 151 us  [the longest x16 62.4 us: dot_tn(): lax.dot_general(a, b, (((0,), (0,)), ((), ())), preferred_element_type=F32)]
    pallas_call x0 -> x4, Pallas kernels: none -> 74.1 us  [call(): pl.pallas_call(kernel, out_shape=[jax.ShapeDtypeStruct(shape, dtype) for...]
    psum x1 -> x0, blocking collectives: 49.1 us -> none  [on_device(): lax.psum((d_attn_gain, d_ffn_gain, d_q_gain, d_k_gain), ('ctx', 'tp'))]
    reduce_sum x14 -> x4, other arithmetic: 40.9 us -> 3.25 us  [the longest x2 1.99 us: rms_scale(): jnp.mean(values * values, axis=-1, keepdims=True) + EPSILON]
  transfers between devices with their start and end apart: 34 -> 144, of which waited for: 26 -> 48; matrix products, arithmetic and copies ran while one was open for 11% -> 19% of each run, Pallas kernels for 0% -> 7%
where the time goes in v1:
time: 1030 us; the launch traced here: 1020 us
  waiting for transfers between devices  369 us (36%)
  starting transfers between devices  282 us (27%)
  matrix products  151 us (15%)
  Pallas kernels  74.1 us (7%)
  other arithmetic  70.3 us (7%)
  local copies, waits for them, and re-layouts  67.9 us (7%)
    ppermute x52, waiting for transfers between devices, line_move(): return lax.ppermute(value, 'ctx', pairs)  243 us
    ppermute x52, starting transfers between devices, line_move(): return lax.ppermute(value, 'ctx', pairs)  185 us
    ppermute x63, waiting for transfers between devices, swap_ctx(): return lax.ppermute(value, 'ctx', [(i, i ^ bit) for i in range(n)])  86.1 us
    pallas_call x4, Pallas kernels, call(): pl.pallas_call(kernel, out_shape=[jax.ShapeDtypeStruct(shape, dtype) for...  74.1 us
    dot_general x16, matrix products, dot_tn(): lax.dot_general(a, b, (((0,), (0,)), ((), ())), preferred_element_type=F32)  62.4 us
    dot_general x6, matrix products, dot_nt(): lax.dot_general(a, b, (((1,), (1,)), ((), ())), preferred_element_type=F32)  46.5 us
    dot_general x6, matrix products, dot(): return jnp.dot(a, b, preferred_element_type=F32)  42.2 us
    ppermute x63, starting transfers between devices, swap_ctx(): return lax.ppermute(value, 'ctx', [(i, i ^ bit) for i in range(n)])  42.2 us
  transfers between devices with their start and end apart: 144, of which 48 were waited for; matrix products, arithmetic and copies ran while one was open for 19% of the time, Pallas kernels for 7%

profile of v1, /device:TPU:0, one launch (start us, length us, event | category | flops | bytes accessed | tf_op | source)
XLA Modules:
  0.0 1018.5 jit_solution(15384854858453333579)
XLA Ops:
  24.3 4.3 fusion.142
  30.6 4.1 all-to-all-start
  34.9 4.2 collective-permute-start.21
  40.4 4.1 collective-permute-done.21
  53.0 4.3 all-to-all-start.3
  58.5 4.6 collective-permute-start.13
  72.0 5.1 collective-permute-done.12
  95.8 5.2 collective-permute-done.6
  107.2 9.6 collective-permute-done.17
  122.8 5.5 fusion.151.raw_ref
  128.4 9.3 shard_map.237
  140.3 4.2 collective-permute-start.18
  144.6 7.2 collective-permute-done.18
  152.0 19.0 %shard_map.238 = (bf16[1536,256]{1,0:T(8,128)(2,1)S(1)}, f32[1536,256]{1,0:T(8,128)S(1)}, f32[6144,1]{1,0:T(8,128)}) custom-call(s32[8]{0:T(128)S(1)} %xor_or_fusion.table, s32[8]{0:T(128)S(1)} %get-tuple-element.179.lo, s32[8]{0:T(128)S(1)} %get-tuple-element.180.hi, bf16[1536,256]{1,0:T(8,128)(2,1)S(1)} %get-tuple-element.22.q_ref, ...), custom_call_target="tpu_custom_call" | custom-call | flops 8053063680 | bytes 3145728 | tf_op jit(solution)/shard_map/pallas_call | solution.py:276
  177.1 4.4 all-to-all-start.2
  190.2 14.0 %collective-permute-start.52 = (bf16[1024,512]{0,1:T(8,128)(2,1)S(1)}, bf16[1024,512]{0,1:T(8,128)(2,1)}, u32[]{:S(2)}, u32[]{:S(2)}) collective-permute-start(bf16[1024,512]{0,1:T(8,128)(2,1)S(1)} %bitcast.93), channel_id=1, source_target_pairs={{0,8},{2,10},{4,12},{6,14},{8,16},{10,18},{12,20},{14,22},{16,24},... | collective-permute-start | bytes 3145736 | tf_op jit(solution)/shard_map/ppermute | solution.py:42
  206.1 3.9 add_convert_fusion.19
  213.4 12.5 %collective-permute-done.52 = bf16[1024,512]{0,1:T(8,128)(2,1)} collective-permute-done((bf16[1024,512]{0,1:T(8,128)(2,1)S(1)}, bf16[1024,512]{0,1:T(8,128)(2,1)}, u32[]{:S(2)}, u32[]{:S(2)}) %collective-permute-start.52) | collective-permute-done | bytes 1048608 | tf_op jit(solution)/shard_map/ppermute | solution.py:42
  233.3 3.9 copy.119
  239.5 6.2 collective-permute-start.46
  249.0 7.3 collective-permute-done.34
  272.3 5.5 collective-permute-done.32
  280.5 9.4 collective-permute-done.46
  294.1 15.8 %collective-permute-done.45 = bf16[512,2048]{1,0:T(8,128)(2,1)S(1)} collective-permute-done((bf16[512,2048]{1,0:T(8,128)(2,1)S(1)}, bf16[512,2048]{1,0:T(8,128)(2,1)S(1)}, u32[]{:S(2)}, u32[]{:S(2)}) %collective-permute-start.45) | collective-permute-done | bytes 2097184 | tf_op jit(solution)/shard_map/ppermute | solution.py:42
  316.4 15.9 %collective-permute-done.56 = bf16[1024,512]{0,1:T(8,128)(2,1)S(1)} collective-permute-done((bf16[1024,512]{0,1:T(8,128)(2,1)}, bf16[1024,512]{0,1:T(8,128)(2,1)S(1)}, u32[]{:S(2)}, u32[]{:S(2)}) %collective-permute-start.56) | collective-permute-done | bytes 1048608 | tf_op jit(solution)/shard_map/ppermute | solution.py:42
  335.9 4.2 collective-permute-done.38
  343.5 30.9 %collective-permute-done.49 = bf16[512,2048]{1,0:T(8,128)(2,1)S(1)} collective-permute-done((bf16[512,2048]{1,0:T(8,128)(2,1)S(1)}, bf16[512,2048]{1,0:T(8,128)(2,1)S(1)}, u32[]{:S(2)}, u32[]{:S(2)}) %collective-permute-start.49) | collective-permute-done | bytes 2097184 | tf_op jit(solution)/shard_map/ppermute | solution.py:42
  379.2 41.8 %collective-permute-done.50 = bf16[512,2048]{1,0:T(8,128)(2,1)S(1)} collective-permute-done((bf16[512,2048]{1,0:T(8,128)(2,1)S(1)}, bf16[512,2048]{1,0:T(8,128)(2,1)S(1)}, u32[]{:S(2)}, u32[]{:S(2)}) %collective-permute-start.50) | collective-permute-done | bytes 2097184 | tf_op jit(solution)/shard_map/ppermute | solution.py:42
  421.2 19.7 %fusion.153 = f32[1536,2048]{1,0:T(8,128)} fusion(bf16[1536,2048]{1,0:T(8,128)(2,1)} %copy-done.69, bf16[512,2048]{1,0:T(8,128)(2,1)S(1)} %broadcast_select_fusion, bf16[512,2048]{1,0:T(8,128)(2,1)S(1)} %broadcast_select_fusion.1, bf16[512,2048]{1,0:T(8,128)(2,1)S(1)} %broadcast_select_fusion.2, bf16[512,2048]{1,0:T(8,128)(2,1)S(1)} %bitcast.84), kind=kOutput, calls=%fused_computation.304 | convolution fusion | flops 12918456320 | bytes 27262976 | tf_op jit(solution)/shard_map/dot_general | solution.py:121
  441.0 17.1 %multiply_convert_fusion = (bf16[1536,1024]{1,0:T(8,128)(2,1)}, bf16[1536,1024]{1,0:T(8,128)(2,1)}, bf16[1536,1024]{1,0:T(8,128)(2,1)}) fusion(f32[1536,2048]{1,0:T(8,128)} %fusion.153, bf16[1536,2048]{1,0:T(8,128)(2,1)} %constant_dynamic-update-slice_fusion.23, bf16[1024,512]{0,1:T(8,128)(2,1)} %broadcast_select_fusion.3, ...), kind=kOutput, calls=%fused_computation.6 | convolution fusion | flops 6482821120 | bytes 32505856 | tf_op jit(solution)/shard_map/dot_general | solution.py:125
  458.1 8.2 convolution_convert_fusion.10
  466.4 6.3 convolution_convert_fusion.8
  472.7 10.5 %convolution_convert_fusion.1 = bf16[768,2048]{1,0:T(8,128)(2,1)S(1)} fusion(bf16[1536,1024]{1,0:T(8,128)(2,1)} %get-tuple-element.101, bf16[1536,1024]{1,0:T(8,128)(2,1)} %get-tuple-element.100, bf16[512,2048]{1,0:T(8,128)(2,1)} %copy-done.28, bf16[512,2048]{1,0:T(8,128)(2,1)S(1)} %broadcast_select_fusion.1, bf16[512,2048]{1,0:T(8,128)(2,1)} %copy-done.27, ...), kind=kOutput, calls=%fused_computation.20 | convolution fusion | flops 6483869696 | bytes 17825792 | tf_op jit(solution)/shard_map/dot_general | solution.py:125
  483.2 11.7 %convolution_convert_fusion = bf16[768,2048]{1,0:T(8,128)(2,1)S(1)} fusion(bf16[1536,1024]{1,0:T(8,128)(2,1)} %get-tuple-element.101, bf16[1536,1024]{1,0:T(8,128)(2,1)} %get-tuple-element.100, bf16[512,2048]{1,0:T(8,128)(2,1)} %copy-done.28, bf16[512,2048]{1,0:T(8,128)(2,1)} %copy-done.26, bf16[512,2048]{1,0:T(8,128)(2,1)} %copy-done.27, ...), kind=kOutput, calls=%fused_computation.19 | convolution fusion | flops 6483869696 | bytes 17825792 | tf_op jit(solution)/shard_map/dot_general | solution.py:125
  494.9 6.2 convolution_convert_fusion.4
  501.2 7.5 convolution_convert_fusion.5
  528.4 17.0 %collective-permute-done.130 = bf16[1024,512]{0,1:T(8,128)(2,1)S(1)} collective-permute-done((bf16[1024,512]{0,1:T(8,128)(2,1)S(1)}, bf16[1024,512]{0,1:T(8,128)(2,1)S(1)}, u32[]{:S(2)}, u32[]{:S(2)}) %collective-permute-start.130) | collective-permute-done | bytes 1048608 | tf_op jit(solution)/shard_map/ppermute | solution.py:42
  550.8 4.3 collective-permute-done.84
  560.4 6.7 collective-permute-done.65
  570.6 4.9 collective-permute-done.82
  579.9 4.4 collective-permute-done.59
  585.1 4.5 collective-permute-start.131
  595.7 16.4 %collective-permute-done.131 = bf16[1024,512]{0,1:T(8,128)(2,1)S(1)} collective-permute-done((bf16[1024,512]{0,1:T(8,128)(2,1)S(1)}, bf16[1024,512]{0,1:T(8,128)(2,1)S(1)}, u32[]{:S(2)}, u32[]{:S(2)}) %collective-permute-start.131) | collective-permute-done | bytes 1048608 | tf_op jit(solution)/shard_map/ppermute | solution.py:42
  614.8 4.5 collective-permute-start.132
  619.3 9.3 fusion.1
  633.1 7.4 collective-permute-done.88
  642.5 36.8 %collective-permute-start.125 = (bf16[512,2048]{1,0:T(8,128)(2,1)}, bf16[512,2048]{1,0:T(8,128)(2,1)}, u32[]{:S(2)}, u32[]{:S(2)}) collective-permute-start(bf16[512,2048]{1,0:T(8,128)(2,1)} %get-tuple-element.137), channel_id=1, source_target_pairs={{0,8},{2,10},{4,12},{6,14},{8,16},{10,18},{12,20},{14,22},{1,9},{3... | collective-permute-start | bytes 6291464 | tf_op jit(solution)/shard_map/ppermute | solution.py:42
  687.2 3.8 collective-permute-start.118
  691.1 32.3 %shard_map.239 = (f32[1536,256]{1,0:T(8,128)S(1)}, f32[3840,128]{1,0:T(8,128)}) custom-call(s32[8]{0:T(128)S(1)} %xor_or_fusion.table, s32[8]{0:T(128)S(1)} %get-tuple-element.179.lo, s32[8]{0:T(128)S(1)} %get-tuple-element.180.hi, bf16[1536,256]{1,0:T(8,128)(2,1)S(1)} %copy-done.13, bf16[1536,256]{1,0:T(8,128)(2,1)S(1)} %convolution_convert_fusion.12.do_ref, ...), custom_call_target="tpu_custom_call" | custom-call | flops 20132659200 | bytes 4718592 | tf_op jit(solution)/shard_map/pallas_call | solution.py:276
  728.1 4.4 add_convert_fusion.3
  732.4 4.2 all-to-all-start.7
  741.5 10.5 %collective-permute-start.119 = (bf16[256,512]{1,0:T(8,128)(2,1)S(1)}, bf16[256,512]{1,0:T(8,128)(2,1)S(1)}, u32[]{:S(2)}, u32[]{:S(2)}) collective-permute-start(bf16[256,512]{1,0:T(8,128)(2,1)S(1)} %get-tuple-element.160), channel_id=1, source_target_pairs={{0,8},{2,10},{4,12},{6,14},{8,16},{10,18},{12,20},{14,22},{1,9},{3... | collective-permute-start | bytes 786440 | tf_op jit(solution)/shard_map/ppermute | solution.py:42
  752.7 6.2 collective-permute-done.96
  760.3 13.5 %shard_map.240 = (bf16[1536,384]{1,0:T(8,128)(2,1)S(1)}, f32[8,64]{1,0:T(8,128)S(1)}) custom-call(s32[8]{0:T(128)S(1)} %xor_or_fusion.table, f32[1536,384]{1,0:T(8,128)} %copy-done, f32[1536,64]{1,0:T(8,128)S(1)} %get-tuple-element.183.cos_ref, f32[1536,64]{1,0:T(8,128)S(1)} %get-tuple-element.184.sin_ref, f32[1,64]{1,0:T(1,128)S(1)} %bitcast.74, ...), custom_call_target="tpu_custom_call" | custom-call | flops 9830400 | bytes 5898240 | tf_op jit(solution)/shard_map/pallas_call | solution.py:276
  791.0 5.3 collective-permute-done.120
  803.0 3.8 collective-permute-start.113
  820.0 4.7 add_convert_fusion.2
  826.0 39.2 %collective-permute-start.126 = (bf16[512,2048]{1,0:T(8,128)(2,1)}, bf16[512,2048]{1,0:T(8,128)(2,1)}, u32[]{:S(2)}, u32[]{:S(2)}) collective-permute-start(bf16[512,2048]{1,0:T(8,128)(2,1)} %add_convert_fusion.2), channel_id=1, source_target_pairs={{0,8},{2,10},{4,12},{6,14},{8,16},{10,18},{12,20},{14,22},{16,24},... | collective-permute-start | bytes 6291464 | tf_op jit(solution)/shard_map/ppermute | solution.py:42
  880.7 37.1 %collective-permute-done.114 = bf16[512,384]{1,0:T(8,128)(2,1)S(1)} collective-permute-done((bf16[512,384]{1,0:T(8,128)(2,1)S(1)}, bf16[512,384]{1,0:T(8,128)(2,1)S(1)}, u32[]{:S(2)}, u32[]{:S(2)}) %collective-permute-start.114) | collective-permute-done | bytes 393248 | tf_op jit(solution)/shard_map/ppermute | solution.py:42
  931.8 12.0 %collective-permute-done.105 = bf16[96,2048]{1,0:T(8,128)(2,1)S(1)} collective-permute-done((bf16[96,2048]{1,0:T(8,128)(2,1)}, bf16[96,2048]{1,0:T(8,128)(2,1)S(1)}, u32[]{:S(2)}, u32[]{:S(2)}) %collective-permute-start.105) | collective-permute-done | bytes 393248 | tf_op jit(solution)/shard_map/ppermute | solution.py:25
  945.5 9.1 collective-permute-done.103
  962.6 9.6 add_convert_fusion
  972.2 4.5 all-to-all-start.6
  981.2 21.5 %collective-permute-done.109 = f32[4224]{0:T(1024)S(1)} collective-permute-done((f32[4224]{0:T(1024)S(1)}, f32[4224]{0:T(1024)S(1)}, u32[]{:S(2)}, u32[]{:S(2)}) %collective-permute-start.109) | collective-permute-done | bytes 16928 | tf_op jit(solution)/shard_map/ppermute | solution.py:25
  (600 shorter events, 323.3 us)
Async XLA Ops:
  8.0 58.2 %collective-permute-start.4 = (bf16[192,2048]{1,0:T(8,128)(2,1)}, bf16[192,2048]{1,0:T(8,128)(2,1)}, u32[]{:S(2)}, u32[]{:S(2)}) collective-permute-start(bf16[192,2048]{1,0:T(8,128)(2,1)} %get-tuple-element.97), channel_id=1, source_target_pairs={{0,4},{2,6},{4,0},{6,2},{8,12},{10,14},{12,8},{14,10},{16,20},{18,... | collective-permute-start | bytes 2359304 | tf_op jit(solution)/shard_map/ppermute | solution.py:25
  8.1 69.7 %collective-permute-start.3 = (bf16[192,2048]{1,0:T(8,128)(2,1)}, bf16[192,2048]{1,0:T(8,128)(2,1)}, u32[]{:S(2)}, u32[]{:S(2)}) collective-permute-start(bf16[192,2048]{1,0:T(8,128)(2,1)} %get-tuple-element.97), channel_id=1, source_target_pairs={{0,1},{1,0},{2,3},{3,2},{4,5},{5,4},{6,7},{7,6},{8,9},{9,8},{10,11... | collective-permute-start | bytes 2359304 | tf_op jit(solution)/shard_map/ppermute | solution.py:37
  53.0 124.1 %all-to-all-start.3 = ((bf16[4,1024,128]{2,1,0:T(8,128)(2,1)}), bf16[4,1024,128]{2,1,0:T(8,128)(2,1)}, u32[]{:S(2)}, u32[]{:S(2)}) async-start(bf16[4,1024,128]{2,1,0:T(8,128)(2,1)} %bitcast.91), calls=%async_computation.3 | async-start | bytes 2097152 | tf_op jit(solution)/shard_map/all_to_all | solution.py:108
  72.0 30.5 %collective-permute-start.7 = (bf16[192,2048]{1,0:T(8,128)(2,1)}, bf16[192,2048]{1,0:T(8,128)(2,1)S(1)}, u32[]{:S(2)}, u32[]{:S(2)}) collective-permute-start(bf16[192,2048]{1,0:T(8,128)(2,1)} %get-tuple-element.97), channel_id=1, source_target_pairs={{0,2},{2,0},{4,6},{6,4},{8,10},{10,8},{12,14},{14,12},{16,18},{18,... | collective-permute-start | bytes 2359304 | tf_op jit(solution)/shard_map/ppermute | solution.py:25
  88.8 50.4 %collective-permute-start.23 = (bf16[256,512]{0,1:T(8,128)(2,1)}, bf16[256,512]{0,1:T(8,128)(2,1)S(1)}, u32[]{:S(2)}, u32[]{:S(2)}) collective-permute-start(bf16[256,512]{0,1:T(8,128)(2,1)} %collective-permute-done.22), channel_id=1, source_target_pairs={{16,24},{18,26},{20,28},{22,30},{17,25},{19,27},{21,29},{23,31}} | collective-permute-start | bytes 786440 | tf_op jit(solution)/shard_map/ppermute | solution.py:42
  92.3 26.8 %collective-permute-start.9 = (bf16[192,2048]{1,0:T(8,128)(2,1)}, bf16[192,2048]{1,0:T(8,128)(2,1)S(1)}, u32[]{:S(2)}, u32[]{:S(2)}) collective-permute-start(bf16[192,2048]{1,0:T(8,128)(2,1)} %collective-permute-done.4), channel_id=1, source_target_pairs={{0,2},{2,0},{4,6},{6,4},{8,10},{10,8},{12,14},{14,12},{16,18},{18,... | collective-permute-start | bytes 2359304 | tf_op jit(solution)/shard_map/ppermute | solution.py:25
  104.8 39.7 %collective-permute-start.25 = (bf16[256,512]{0,1:T(8,128)(2,1)}, bf16[256,512]{0,1:T(8,128)(2,1)S(1)}, u32[]{:S(2)}, u32[]{:S(2)}) collective-permute-start(bf16[256,512]{0,1:T(8,128)(2,1)} %collective-permute-done.24), channel_id=1, source_target_pairs={{8,0},{10,2},{12,4},{14,6},{9,1},{11,3},{13,5},{15,7}} | collective-permute-start | bytes 786440 | tf_op jit(solution)/shard_map/ppermute | solution.py:42
  116.8 57.7 %collective-permute-start.69 = (bf16[96,2048]{1,0:T(8,128)(2,1)S(1)}, bf16[96,2048]{1,0:T(8,128)(2,1)}, u32[]{:S(2)}, u32[]{:S(2)}) collective-permute-start(bf16[96,2048]{1,0:T(8,128)(2,1)S(1)} %slice.498), channel_id=1, source_target_pairs={{0,1},{1,0},{2,3},{3,2},{4,5},{5,4},{6,7},{7,6},{8,9},{9,8},{10,11... | collective-permute-start | bytes 1179656 | tf_op jit(solution)/shard_map/ppermute | solution.py:37
  120.6 65.0 %collective-permute-start.70 = (bf16[96,2048]{1,0:T(8,128)(2,1)}, bf16[96,2048]{1,0:T(8,128)(2,1)}, u32[]{:S(2)}, u32[]{:S(2)}) collective-permute-start(bf16[96,2048]{1,0:T(8,128)(2,1)} %slice.499), channel_id=1, source_target_pairs={{0,4},{2,6},{4,0},{6,2},{8,12},{10,14},{12,8},{14,10},{16,20},{18,... | collective-permute-start | bytes 1179656 | tf_op jit(solution)/shard_map/ppermute | solution.py:25
  173.9 30.3 %collective-permute-start.30 = (bf16[192,2048]{1,0:T(8,128)(2,1)}, bf16[192,2048]{1,0:T(8,128)(2,1)}, u32[]{:S(2)}, u32[]{:S(2)}) collective-permute-start(bf16[192,2048]{1,0:T(8,128)(2,1)} %get-tuple-element.132), channel_id=1, source_target_pairs={{0,2},{2,0},{4,6},{6,4},{8,10},{10,8},{12,14},{14,12},{16,18},{18,... | collective-permute-start | bytes 2359304 | tf_op jit(solution)/shard_map/ppermute | solution.py:25
  174.4 31.1 %collective-permute-start.27 = (bf16[192,2048]{1,0:T(8,128)(2,1)}, bf16[192,2048]{1,0:T(8,128)(2,1)}, u32[]{:S(2)}, u32[]{:S(2)}) collective-permute-start(bf16[192,2048]{1,0:T(8,128)(2,1)} %get-tuple-element.133), channel_id=1, source_target_pairs={{0,2},{2,0},{4,6},{6,4},{8,10},{10,8},{12,14},{14,12},{16,18},{18,... | collective-permute-start | bytes 2359304 | tf_op jit(solution)/shard_map/ppermute | solution.py:25
  174.4 31.2 %collective-permute-start.26 = (bf16[192,2048]{1,0:T(8,128)(2,1)}, bf16[192,2048]{1,0:T(8,128)(2,1)}, u32[]{:S(2)}, u32[]{:S(2)}) collective-permute-start(bf16[192,2048]{1,0:T(8,128)(2,1)} %get-tuple-element.134), channel_id=1, source_target_pairs={{0,2},{2,0},{4,6},{6,4},{8,10},{10,8},{12,14},{14,12},{16,18},{18,... | collective-permute-start | bytes 2359304 | tf_op jit(solution)/shard_map/ppermute | solution.py:25
  177.1 56.2 %all-to-all-start.2 = ((bf16[4,128,2048]{1,2,0:T(8,128)(2,1)}), bf16[4,128,2048]{1,2,0:T(8,128)(2,1)}, u32[]{:S(2)}, u32[]{:S(2)}) async-start(bf16[4,128,2048]{1,2,0:T(8,128)(2,1)} %maximum_bitcast_fusion), calls=%async_computation.2 | async-start | bytes 4194304 | tf_op jit(solution)/shard_map/all_to_all | solution.py:108
  185.6 25.3 %collective-permute-start.71 = (bf16[192,2048]{1,0:T(8,128)(2,1)}, bf16[192,2048]{1,0:T(8,128)(2,1)S(1)}, u32[]{:S(2)}, u32[]{:S(2)}) collective-permute-start(bf16[192,2048]{1,0:T(8,128)(2,1)} %get-tuple-element.91), channel_id=1, source_target_pairs={{0,2},{2,0},{4,6},{6,4},{8,10},{10,8},{12,14},{14,12},{16,18},{18,... | collective-permute-start | bytes 2359304 | tf_op jit(solution)/shard_map/ppermute | solution.py:25
  190.2 35.7 %collective-permute-start.52 = (bf16[1024,512]{0,1:T(8,128)(2,1)S(1)}, bf16[1024,512]{0,1:T(8,128)(2,1)}, u32[]{:S(2)}, u32[]{:S(2)}) collective-permute-start(bf16[1024,512]{0,1:T(8,128)(2,1)S(1)} %bitcast.93), channel_id=1, source_target_pairs={{0,8},{2,10},{4,12},{6,14},{8,16},{10,18},{12,20},{14,22},{16,24},... | collective-permute-start | bytes 3145736 | tf_op jit(solution)/shard_map/ppermute | solution.py:42
  204.2 26.8 %collective-permute-start.51 = (bf16[1024,512]{0,1:T(8,128)(2,1)S(1)}, bf16[1024,512]{0,1:T(8,128)(2,1)}, u32[]{:S(2)}, u32[]{:S(2)}) collective-permute-start(bf16[1024,512]{0,1:T(8,128)(2,1)S(1)} %bitcast.94), channel_id=1, source_target_pairs={{8,0},{10,2},{12,4},{14,6},{16,8},{18,10},{20,12},{22,14},{24,16},... | collective-permute-start | bytes 3145736 | tf_op jit(solution)/shard_map/ppermute | solution.py:42
  205.6 33.8 %collective-permute-start.74 = (bf16[96,2048]{1,0:T(8,128)(2,1)}, bf16[96,2048]{1,0:T(8,128)(2,1)}, u32[]{:S(2)}, u32[]{:S(2)}) collective-permute-start(bf16[96,2048]{1,0:T(8,128)(2,1)} %collective-permute-done.69), channel_id=1, source_target_pairs={{0,2},{2,0},{4,6},{6,4},{8,10},{10,8},{12,14},{14,12},{16,18},{18,... | collective-permute-start | bytes 1179656 | tf_op jit(solution)/shard_map/ppermute | solution.py:25
  210.9 34.8 %collective-permute-start.31 = (bf16[96,2048]{1,0:T(8,128)(2,1)}, bf16[96,2048]{1,0:T(8,128)(2,1)}, u32[]{:S(2)}, u32[]{:S(2)}) collective-permute-start(bf16[96,2048]{1,0:T(8,128)(2,1)} %get-tuple-element.158), channel_id=1, source_target_pairs={{0,1},{1,0},{2,3},{3,2},{4,5},{5,4},{6,7},{7,6},{8,9},{9,8},{10,11... | collective-permute-start | bytes 1179656 | tf_op jit(solution)/shard_map/ppermute | solution.py:37
  213.4 45.5 %collective-permute-start.73 = (bf16[192,2048]{1,0:T(8,128)(2,1)}, bf16[192,2048]{1,0:T(8,128)(2,1)}, u32[]{:S(2)}, u32[]{:S(2)}) collective-permute-start(bf16[192,2048]{1,0:T(8,128)(2,1)} %collective-permute-done.68), channel_id=1, source_target_pairs={{0,2},{2,0},{4,6},{6,4},{8,10},{10,8},{12,14},{14,12},{16,18},{18,... | collective-permute-start | bytes 2359304 | tf_op jit(solution)/shard_map/ppermute | solution.py:25
  225.9 34.3 %collective-permute-start.53 = (bf16[1024,512]{0,1:T(8,128)(2,1)}, bf16[1024,512]{0,1:T(8,128)(2,1)}, u32[]{:S(2)}, u32[]{:S(2)}) collective-permute-start(bf16[1024,512]{0,1:T(8,128)(2,1)} %collective-permute-done.52), channel_id=1, source_target_pairs={{8,16},{10,18},{12,20},{14,22},{16,24},{18,26},{20,28},{22,30},{9,... | collective-permute-start | bytes 3145736 | tf_op jit(solution)/shard_map/ppermute | solution.py:42
  231.1 30.9 %collective-permute-start.55 = (bf16[1024,512]{0,1:T(8,128)(2,1)}, bf16[1024,512]{0,1:T(8,128)(2,1)}, u32[]{:S(2)}, u32[]{:S(2)}) collective-permute-start(bf16[1024,512]{0,1:T(8,128)(2,1)} %collective-permute-done.51), channel_id=1, source_target_pairs={{8,0},{10,2},{12,4},{14,6},{16,8},{18,10},{20,12},{22,14},{9,1},{1... | collective-permute-start | bytes 3145736 | tf_op jit(solution)/shard_map/ppermute | solution.py:42
  239.5 50.4 %collective-permute-start.46 = (bf16[512,2048]{1,0:T(8,128)(2,1)}, bf16[512,2048]{1,0:T(8,128)(2,1)S(1)}, u32[]{:S(2)}, u32[]{:S(2)}) collective-permute-start(bf16[512,2048]{1,0:T(8,128)(2,1)} %bitcast.80), channel_id=1, source_target_pairs={{0,8},{2,10},{4,12},{6,14},{8,16},{10,18},{12,20},{14,22},{16,24},... | collective-permute-start | bytes 6291464 | tf_op jit(solution)/shard_map/ppermute | solution.py:42
  258.9 51.0 %collective-permute-start.45 = (bf16[512,2048]{1,0:T(8,128)(2,1)S(1)}, bf16[512,2048]{1,0:T(8,128)(2,1)S(1)}, u32[]{:S(2)}, u32[]{:S(2)}) collective-permute-start(bf16[512,2048]{1,0:T(8,128)(2,1)S(1)} %bitcast.83), channel_id=1, source_target_pairs={{8,0},{10,2},{12,4},{14,6},{16,8},{18,10},{20,12},{22,14},{24,16},... | collective-permute-start | bytes 6291464 | tf_op jit(solution)/shard_map/ppermute | solution.py:42
  277.8 32.6 %collective-permute-start.54 = (bf16[1024,512]{0,1:T(8,128)(2,1)}, bf16[1024,512]{0,1:T(8,128)(2,1)S(1)}, u32[]{:S(2)}, u32[]{:S(2)}) collective-permute-start(bf16[1024,512]{0,1:T(8,128)(2,1)} %collective-permute-done.53), channel_id=1, source_target_pairs={{16,24},{18,26},{20,28},{22,30},{17,25},{19,27},{21,29},{23,31}} | collective-permute-start | bytes 3145736 | tf_op jit(solution)/shard_map/ppermute | solution.py:42
  278.5 53.8 %collective-permute-start.56 = (bf16[1024,512]{0,1:T(8,128)(2,1)}, bf16[1024,512]{0,1:T(8,128)(2,1)S(1)}, u32[]{:S(2)}, u32[]{:S(2)}) collective-permute-start(bf16[1024,512]{0,1:T(8,128)(2,1)} %collective-permute-done.55), channel_id=1, source_target_pairs={{8,0},{10,2},{12,4},{14,6},{9,1},{11,3},{13,5},{15,7}} | collective-permute-start | bytes 3145736 | tf_op jit(solution)/shard_map/ppermute | solution.py:42
  289.9 52.0 %collective-permute-start.47 = (bf16[512,2048]{1,0:T(8,128)(2,1)S(1)}, bf16[512,2048]{1,0:T(8,128)(2,1)S(1)}, u32[]{:S(2)}, u32[]{:S(2)}) collective-permute-start(bf16[512,2048]{1,0:T(8,128)(2,1)S(1)} %collective-permute-done.46), channel_id=1, source_target_pairs={{8,16},{10,18},{12,20},{14,22},{16,24},{18,26},{20,28},{22,30},{9,... | collective-permute-start | bytes 6291464 | tf_op jit(solution)/shard_map/ppermute | solution.py:42
  290.9 25.5 %collective-permute-start.37 = (bf16[192,2048]{1,0:T(8,128)(2,1)S(1)}, bf16[192,2048]{1,0:T(8,128)(2,1)S(1)}, u32[]{:S(2)}, u32[]{:S(2)}) collective-permute-start(bf16[192,2048]{1,0:T(8,128)(2,1)S(1)} %get-tuple-element.93), channel_id=1, source_target_pairs={{0,4},{2,6},{4,0},{6,2},{8,12},{10,14},{12,8},{14,10},{16,20},{18,... | collective-permute-start | bytes 2359304 | tf_op jit(solution)/shard_map/ppermute | solution.py:25
  310.4 64.0 %collective-permute-start.49 = (bf16[512,2048]{1,0:T(8,128)(2,1)S(1)}, bf16[512,2048]{1,0:T(8,128)(2,1)S(1)}, u32[]{:S(2)}, u32[]{:S(2)}) collective-permute-start(bf16[512,2048]{1,0:T(8,128)(2,1)S(1)} %collective-permute-done.45), channel_id=1, source_target_pairs={{8,0},{10,2},{12,4},{14,6},{16,8},{18,10},{20,12},{22,14},{9,1},{1... | collective-permute-start | bytes 6291464 | tf_op jit(solution)/shard_map/ppermute | solution.py:42
  316.4 26.3 %collective-permute-start.40 = (bf16[192,2048]{1,0:T(8,128)(2,1)S(1)}, bf16[192,2048]{1,0:T(8,128)(2,1)S(1)}, u32[]{:S(2)}, u32[]{:S(2)}) collective-permute-start(bf16[192,2048]{1,0:T(8,128)(2,1)S(1)} %get-tuple-element.93), channel_id=1, source_target_pairs={{0,2},{2,0},{4,6},{6,4},{8,10},{10,8},{12,14},{14,12},{16,18},{18,... | collective-permute-start | bytes 2359304 | tf_op jit(solution)/shard_map/ppermute | solution.py:25
  341.9 34.2 %collective-permute-start.42 = (bf16[192,2048]{1,0:T(8,128)(2,1)S(1)}, bf16[192,2048]{1,0:T(8,128)(2,1)S(1)}, u32[]{:S(2)}, u32[]{:S(2)}) collective-permute-start(bf16[192,2048]{1,0:T(8,128)(2,1)S(1)} %collective-permute-done.37), channel_id=1, source_target_pairs={{0,2},{2,0},{4,6},{6,4},{8,10},{10,8},{12,14},{14,12},{16,18},{18,... | collective-permute-start | bytes 2359304 | tf_op jit(solution)/shard_map/ppermute | solution.py:25
  341.9 37.1 %collective-permute-start.48 = (bf16[512,2048]{1,0:T(8,128)(2,1)S(1)}, bf16[512,2048]{1,0:T(8,128)(2,1)S(1)}, u32[]{:S(2)}, u32[]{:S(2)}) collective-permute-start(bf16[512,2048]{1,0:T(8,128)(2,1)S(1)} %collective-permute-done.47), channel_id=1, source_target_pairs={{16,24},{18,26},{20,28},{22,30},{17,25},{19,27},{21,29},{23,31}} | collective-permute-start | bytes 6291464 | tf_op jit(solution)/shard_map/ppermute | solution.py:42
  342.8 33.4 %collective-permute-start.43 = (bf16[96,2048]{1,0:T(8,128)(2,1)S(1)}, bf16[96,2048]{1,0:T(8,128)(2,1)S(1)}, u32[]{:S(2)}, u32[]{:S(2)}) collective-permute-start(bf16[96,2048]{1,0:T(8,128)(2,1)S(1)} %collective-permute-done.38), channel_id=1, source_target_pairs={{0,2},{2,0},{4,6},{6,4},{8,10},{10,8},{12,14},{14,12},{16,18},{18,... | collective-permute-start | bytes 1179656 | tf_op jit(solution)/shard_map/ppermute | solution.py:25
  343.4 32.8 %collective-permute-start.44 = (bf16[96,2048]{1,0:T(8,128)(2,1)S(1)}, bf16[96,2048]{1,0:T(8,128)(2,1)S(1)}, u32[]{:S(2)}, u32[]{:S(2)}) collective-permute-start(bf16[96,2048]{1,0:T(8,128)(2,1)S(1)} %collective-permute-done.39), channel_id=1, source_target_pairs={{0,2},{2,0},{4,6},{6,4},{8,10},{10,8},{12,14},{14,12},{16,18},{18,... | collective-permute-start | bytes 1179656 | tf_op jit(solution)/shard_map/ppermute | solution.py:25
  374.4 46.6 %collective-permute-start.50 = (bf16[512,2048]{1,0:T(8,128)(2,1)S(1)}, bf16[512,2048]{1,0:T(8,128)(2,1)S(1)}, u32[]{:S(2)}, u32[]{:S(2)}) collective-permute-start(bf16[512,2048]{1,0:T(8,128)(2,1)S(1)} %collective-permute-done.49), channel_id=1, source_target_pairs={{8,0},{10,2},{12,4},{14,6},{9,1},{11,3},{13,5},{15,7}} | collective-permute-start | bytes 6291464 | tf_op jit(solution)/shard_map/ppermute | solution.py:42
  522.0 92.8 %collective-permute-start.124 = (bf16[512,2048]{1,0:T(8,128)(2,1)S(1)}, bf16[512,2048]{1,0:T(8,128)(2,1)S(1)}, u32[]{:S(2)}, u32[]{:S(2)}) collective-permute-start(bf16[512,2048]{1,0:T(8,128)(2,1)S(1)} %copy-done.23), channel_id=1, source_target_pairs={{0,8},{2,10},{4,12},{6,14},{1,9},{3,11},{5,13},{7,15}} | collective-permute-start | bytes 6291464 | tf_op jit(solution)/shard_map/ppermute | solution.py:42
  523.4 44.3 %collective-permute-start.78 = (bf16[96,2048]{1,0:T(8,128)(2,1)S(1)}, bf16[96,2048]{1,0:T(8,128)(2,1)S(1)}, u32[]{:S(2)}, u32[]{:S(2)}) collective-permute-start(bf16[96,2048]{1,0:T(8,128)(2,1)S(1)} %slice.509), channel_id=1, source_target_pairs={{0,1},{1,0},{2,3},{3,2},{4,5},{5,4},{6,7},{7,6},{8,9},{9,8},{10,11... | collective-permute-start | bytes 1179656 | tf_op jit(solution)/shard_map/ppermute | solution.py:37
  524.0 45.3 %collective-permute-start.83 = (bf16[96,2048]{1,0:T(8,128)(2,1)S(1)}, bf16[96,2048]{1,0:T(8,128)(2,1)S(1)}, u32[]{:S(2)}, u32[]{:S(2)}) collective-permute-start(bf16[96,2048]{1,0:T(8,128)(2,1)S(1)} %slice.517), channel_id=1, source_target_pairs={{0,4},{2,6},{4,0},{6,2},{8,12},{10,14},{12,8},{14,10},{16,20},{18,... | collective-permute-start | bytes 1179656 | tf_op jit(solution)/shard_map/ppermute | solution.py:25
  584.3 35.0 %collective-permute-start.127 = (bf16[512,2048]{1,0:T(8,128)(2,1)S(1)}, bf16[512,2048]{1,0:T(8,128)(2,1)S(1)}, u32[]{:S(2)}, u32[]{:S(2)}) collective-permute-start(bf16[512,2048]{1,0:T(8,128)(2,1)S(1)} %copy-done.25), channel_id=1, source_target_pairs={{24,16},{26,18},{28,20},{30,22},{25,17},{27,19},{29,21},{31,23}} | collective-permute-start | bytes 6291464 | tf_op jit(solution)/shard_map/ppermute | solution.py:42
  585.1 27.0 %collective-permute-start.131 = (bf16[1024,512]{0,1:T(8,128)(2,1)S(1)}, bf16[1024,512]{0,1:T(8,128)(2,1)S(1)}, u32[]{:S(2)}, u32[]{:S(2)}) collective-permute-start(bf16[1024,512]{0,1:T(8,128)(2,1)S(1)} %get-tuple-element.148), channel_id=1, source_target_pairs={{0,8},{2,10},{4,12},{6,14},{8,16},{10,18},{12,20},{14,22},{1,9},{3... | collective-permute-start | bytes 3145736 | tf_op jit(solution)/shard_map/ppermute | solution.py:42
  594.3 48.2 %collective-permute-start.90 = (bf16[192,2048]{1,0:T(8,128)(2,1)S(1)}, bf16[192,2048]{1,0:T(8,128)(2,1)S(1)}, u32[]{:S(2)}, u32[]{:S(2)}) collective-permute-start(bf16[192,2048]{1,0:T(8,128)(2,1)S(1)} %get-tuple-element.88), channel_id=1, source_target_pairs={{0,2},{2,0},{4,6},{6,4},{8,10},{10,8},{12,14},{14,12},{16,18},{18,... | collective-permute-start | bytes 2359304 | tf_op jit(solution)/shard_map/ppermute | solution.py:25
  614.8 112.0 %collective-permute-start.132 = (bf16[1024,512]{0,1:T(8,128)(2,1)S(1)}, bf16[1024,512]{0,1:T(8,128)(2,1)S(1)}, u32[]{:S(2)}, u32[]{:S(2)}) collective-permute-start(bf16[1024,512]{0,1:T(8,128)(2,1)S(1)} %add_convert_fusion.5), channel_id=1, source_target_pairs={{0,8},{2,10},{4,12},{6,14},{8,16},{10,18},{12,20},{14,22},{16,24},... | collective-permute-start | bytes 3145736 | tf_op jit(solution)/shard_map/ppermute | solution.py:42
  633.0 46.5 %collective-permute-start.91 = (bf16[192,2048]{1,0:T(8,128)(2,1)S(1)}, bf16[192,2048]{1,0:T(8,128)(2,1)S(1)}, u32[]{:S(2)}, u32[]{:S(2)}) collective-permute-start(bf16[192,2048]{1,0:T(8,128)(2,1)S(1)} %collective-permute-done.86), channel_id=1, source_target_pairs={{0,2},{2,0},{4,6},{6,4},{8,10},{10,8},{12,14},{14,12},{16,18},{18,... | collective-permute-start | bytes 2359304 | tf_op jit(solution)/shard_map/ppermute | solution.py:25
  640.6 39.2 %collective-permute-start.92 = (bf16[192,2048]{1,0:T(8,128)(2,1)S(1)}, bf16[192,2048]{1,0:T(8,128)(2,1)S(1)}, u32[]{:S(2)}, u32[]{:S(2)}) collective-permute-start(bf16[192,2048]{1,0:T(8,128)(2,1)S(1)} %collective-permute-done.87), channel_id=1, source_target_pairs={{0,2},{2,0},{4,6},{6,4},{8,10},{10,8},{12,14},{14,12},{16,18},{18,... | collective-permute-start | bytes 2359304 | tf_op jit(solution)/shard_map/ppermute | solution.py:25
  641.2 86.9 %collective-permute-start.135 = (bf16[1024,512]{0,1:T(8,128)(2,1)S(1)}, bf16[1024,512]{0,1:T(8,128)(2,1)S(1)}, u32[]{:S(2)}, u32[]{:S(2)}) collective-permute-start(bf16[1024,512]{0,1:T(8,128)(2,1)S(1)} %add_convert_fusion.4), channel_id=1, source_target_pairs={{8,0},{10,2},{12,4},{14,6},{16,8},{18,10},{20,12},{22,14},{24,16},... | collective-permute-start | bytes 3145736 | tf_op jit(solution)/shard_map/ppermute | solution.py:42
  642.5 176.2 %collective-permute-start.125 = (bf16[512,2048]{1,0:T(8,128)(2,1)}, bf16[512,2048]{1,0:T(8,128)(2,1)}, u32[]{:S(2)}, u32[]{:S(2)}) collective-permute-start(bf16[512,2048]{1,0:T(8,128)(2,1)} %get-tuple-element.137), channel_id=1, source_target_pairs={{0,8},{2,10},{4,12},{6,14},{8,16},{10,18},{12,20},{14,22},{1,9},{3... | collective-permute-start | bytes 6291464 | tf_op jit(solution)/shard_map/ppermute | solution.py:42
  685.8 53.1 %collective-permute-start.121 = (bf16[256,512]{1,0:T(8,128)(2,1)}, bf16[256,512]{1,0:T(8,128)(2,1)}, u32[]{:S(2)}, u32[]{:S(2)}) collective-permute-start(bf16[256,512]{1,0:T(8,128)(2,1)} %fusion.106), channel_id=1, source_target_pairs={{24,16},{26,18},{28,20},{30,22},{25,17},{27,19},{29,21},{31,23}} | collective-permute-start | bytes 786440 | tf_op jit(solution)/shard_map/ppermute | solution.py:42
  687.2 51.8 %collective-permute-start.118 = (bf16[256,512]{1,0:T(8,128)(2,1)S(1)}, bf16[256,512]{1,0:T(8,128)(2,1)}, u32[]{:S(2)}, u32[]{:S(2)}) collective-permute-start(bf16[256,512]{1,0:T(8,128)(2,1)S(1)} %fusion.115), channel_id=1, source_target_pairs={{0,8},{2,10},{4,12},{6,14},{1,9},{3,11},{5,13},{7,15}} | collective-permute-start | bytes 786440 | tf_op jit(solution)/shard_map/ppermute | solution.py:42
  726.8 32.1 %collective-permute-start.95 = (bf16[1536,128]{1,0:T(8,128)(2,1)}, bf16[1536,128]{1,0:T(8,128)(2,1)}, u32[]{:S(2)}, u32[]{:S(2)}) collective-permute-start(bf16[1536,128]{1,0:T(8,128)(2,1)} %slice.522), channel_id=1, source_target_pairs={{8,0},{10,2},{12,4},{14,6},{16,8},{18,10},{20,12},{22,14},{24,16},... | collective-permute-start | bytes 1179656 | tf_op jit(solution)/shard_map/ppermute | solution.py:42
  732.4 75.8 %all-to-all-start.7 = ((bf16[4,1024,128]{1,2,0:T(8,128)(2,1)}), bf16[4,1024,128]{1,2,0:T(8,128)(2,1)}, u32[]{:S(2)}, u32[]{:S(2)}) async-start(bf16[4,1024,128]{1,2,0:T(8,128)(2,1)} %bitcast.97), calls=%async_computation.7 | async-start | bytes 2097152 | tf_op jit(solution)/shard_map/all_to_all | solution.py:108
  741.5 42.0 %collective-permute-start.119 = (bf16[256,512]{1,0:T(8,128)(2,1)S(1)}, bf16[256,512]{1,0:T(8,128)(2,1)S(1)}, u32[]{:S(2)}, u32[]{:S(2)}) collective-permute-start(bf16[256,512]{1,0:T(8,128)(2,1)S(1)} %get-tuple-element.160), channel_id=1, source_target_pairs={{0,8},{2,10},{4,12},{6,14},{8,16},{10,18},{12,20},{14,22},{1,9},{3... | collective-permute-start | bytes 786440 | tf_op jit(solution)/shard_map/ppermute | solution.py:42
  752.0 33.9 %collective-permute-start.122 = (bf16[256,512]{1,0:T(8,128)(2,1)S(1)}, bf16[256,512]{1,0:T(8,128)(2,1)S(1)}, u32[]{:S(2)}, u32[]{:S(2)}) collective-permute-start(bf16[256,512]{1,0:T(8,128)(2,1)S(1)} %get-tuple-element.161), channel_id=1, source_target_pairs={{16,8},{18,10},{20,12},{22,14},{24,16},{26,18},{28,20},{30,22},{17... | collective-permute-start | bytes 786440 | tf_op jit(solution)/shard_map/ppermute | solution.py:42
  796.3 78.1 %collective-permute-start.128 = (bf16[512,2048]{1,0:T(8,128)(2,1)}, bf16[512,2048]{1,0:T(8,128)(2,1)}, u32[]{:S(2)}, u32[]{:S(2)}) collective-permute-start(bf16[512,2048]{1,0:T(8,128)(2,1)} %get-tuple-element.138), channel_id=1, source_target_pairs={{16,8},{18,10},{20,12},{22,14},{24,16},{26,18},{28,20},{30,22},{17... | collective-permute-start | bytes 6291464 | tf_op jit(solution)/shard_map/ppermute | solution.py:42
  798.3 27.7 %collective-permute-start.100 = (bf16[192,2048]{1,0:T(8,128)(2,1)}, bf16[192,2048]{1,0:T(8,128)(2,1)}, u32[]{:S(2)}, u32[]{:S(2)}) collective-permute-start(bf16[192,2048]{1,0:T(8,128)(2,1)} %get-tuple-element.107), channel_id=1, source_target_pairs={{0,2},{2,0},{4,6},{6,4},{8,10},{10,8},{12,14},{14,12},{16,18},{18,... | collective-permute-start | bytes 2359304 | tf_op jit(solution)/shard_map/ppermute | solution.py:25
  818.7 46.5 %collective-permute-start.101 = (bf16[192,2048]{1,0:T(8,128)(2,1)S(1)}, bf16[192,2048]{1,0:T(8,128)(2,1)S(1)}, u32[]{:S(2)}, u32[]{:S(2)}) collective-permute-start(bf16[192,2048]{1,0:T(8,128)(2,1)S(1)} %get-tuple-element.108), channel_id=1, source_target_pairs={{0,2},{2,0},{4,6},{6,4},{8,10},{10,8},{12,14},{14,12},{16,18},{18,... | collective-permute-start | bytes 2359304 | tf_op jit(solution)/shard_map/ppermute | solution.py:25
  818.7 47.8 %collective-permute-start.98 = (bf16[192,2048]{1,0:T(8,128)(2,1)S(1)}, bf16[192,2048]{1,0:T(8,128)(2,1)S(1)}, u32[]{:S(2)}, u32[]{:S(2)}) collective-permute-start(bf16[192,2048]{1,0:T(8,128)(2,1)S(1)} %get-tuple-element.109), channel_id=1, source_target_pairs={{0,2},{2,0},{4,6},{6,4},{8,10},{10,8},{12,14},{14,12},{16,18},{18,... | collective-permute-start | bytes 2359304 | tf_op jit(solution)/shard_map/ppermute | solution.py:25
  819.5 48.3 %collective-permute-start.97 = (bf16[192,2048]{1,0:T(8,128)(2,1)S(1)}, bf16[192,2048]{1,0:T(8,128)(2,1)S(1)}, u32[]{:S(2)}, u32[]{:S(2)}) collective-permute-start(bf16[192,2048]{1,0:T(8,128)(2,1)S(1)} %get-tuple-element.110), channel_id=1, source_target_pairs={{0,2},{2,0},{4,6},{6,4},{8,10},{10,8},{12,14},{14,12},{16,18},{18,... | collective-permute-start | bytes 2359304 | tf_op jit(solution)/shard_map/ppermute | solution.py:25
  826.0 136.6 %collective-permute-start.126 = (bf16[512,2048]{1,0:T(8,128)(2,1)}, bf16[512,2048]{1,0:T(8,128)(2,1)}, u32[]{:S(2)}, u32[]{:S(2)}) collective-permute-start(bf16[512,2048]{1,0:T(8,128)(2,1)} %add_convert_fusion.2), channel_id=1, source_target_pairs={{0,8},{2,10},{4,12},{6,14},{8,16},{10,18},{12,20},{14,22},{16,24},... | collective-permute-start | bytes 6291464 | tf_op jit(solution)/shard_map/ppermute | solution.py:42
  865.2 52.7 %collective-permute-start.114 = (bf16[512,384]{1,0:T(8,128)(2,1)S(1)}, bf16[512,384]{1,0:T(8,128)(2,1)S(1)}, u32[]{:S(2)}, u32[]{:S(2)}) collective-permute-start(bf16[512,384]{1,0:T(8,128)(2,1)S(1)} %add_convert_fusion.24), channel_id=1, source_target_pairs={{0,8},{2,10},{4,12},{6,14},{8,16},{10,18},{12,20},{14,22},{16,24},... | collective-permute-start | bytes 1179656 | tf_op jit(solution)/shard_map/ppermute | solution.py:42
  866.5 53.4 %collective-permute-start.117 = (bf16[512,384]{1,0:T(8,128)(2,1)S(1)}, bf16[512,384]{1,0:T(8,128)(2,1)S(1)}, u32[]{:S(2)}, u32[]{:S(2)}) collective-permute-start(bf16[512,384]{1,0:T(8,128)(2,1)S(1)} %add_convert_fusion.22), channel_id=1, source_target_pairs={{8,0},{10,2},{12,4},{14,6},{16,8},{18,10},{20,12},{22,14},{24,16},... | collective-permute-start | bytes 1179656 | tf_op jit(solution)/shard_map/ppermute | solution.py:42
  872.3 55.6 %collective-permute-start.102 = (bf16[96,2048]{1,0:T(8,128)(2,1)}, bf16[96,2048]{1,0:T(8,128)(2,1)}, u32[]{:S(2)}, u32[]{:S(2)}) collective-permute-start(bf16[96,2048]{1,0:T(8,128)(2,1)} %get-tuple-element.152), channel_id=1, source_target_pairs={{0,1},{1,0},{2,3},{3,2},{4,5},{5,4},{6,7},{7,6},{8,9},{9,8},{10,11... | collective-permute-start | bytes 1179656 | tf_op jit(solution)/shard_map/ppermute | solution.py:37
  877.9 84.7 %collective-permute-start.129 = (bf16[512,2048]{1,0:T(8,128)(2,1)}, bf16[512,2048]{1,0:T(8,128)(2,1)}, u32[]{:S(2)}, u32[]{:S(2)}) collective-permute-start(bf16[512,2048]{1,0:T(8,128)(2,1)} %add_convert_fusion.1), channel_id=1, source_target_pairs={{8,0},{10,2},{12,4},{14,6},{16,8},{18,10},{20,12},{22,14},{24,16},... | collective-permute-start | bytes 6291464 | tf_op jit(solution)/shard_map/ppermute | solution.py:42
  917.9 27.2 %collective-permute-start.99 = (bf16[96,2048]{1,0:T(8,128)(2,1)}, bf16[96,2048]{1,0:T(8,128)(2,1)}, u32[]{:S(2)}, u32[]{:S(2)}) collective-permute-start(bf16[96,2048]{1,0:T(8,128)(2,1)} %slice.529), channel_id=1, source_target_pairs={{0,1},{1,0},{2,3},{3,2},{4,5},{5,4},{6,7},{7,6},{8,9},{9,8},{10,11... | collective-permute-start | bytes 1179656 | tf_op jit(solution)/shard_map/ppermute | solution.py:37
  919.9 25.6 %collective-permute-start.104 = (bf16[96,2048]{1,0:T(8,128)(2,1)}, bf16[96,2048]{1,0:T(8,128)(2,1)}, u32[]{:S(2)}, u32[]{:S(2)}) collective-permute-start(bf16[96,2048]{1,0:T(8,128)(2,1)} %slice.537), channel_id=1, source_target_pairs={{0,4},{2,6},{4,0},{6,2},{8,12},{10,14},{12,8},{14,10},{16,20},{18,... | collective-permute-start | bytes 1179656 | tf_op jit(solution)/shard_map/ppermute | solution.py:25
  972.2 40.9 %all-to-all-start.6 = ((bf16[4,128,2048]{2,1,0:T(8,128)(2,1)}), bf16[4,128,2048]{2,1,0:T(8,128)(2,1)}, u32[]{:S(2)}, u32[]{:S(2)}) async-start(bf16[4,128,2048]{2,1,0:T(8,128)(2,1)} %bitcast.85), calls=%async_computation.6 | async-start | bytes 4194304 | tf_op jit(solution)/shard_map/all_to_all | solution.py:108
  (163 other events, 2987.0 us)

commit v2 on v1

--- a/solution.py
+++ b/solution.py
@@ -14,7 +14,7 @@
 LOG2E = math.log2(math.e)
 
 QUAD = 4
-KEY_BLOCK = 256
+KEY_BLOCK = 384
 
 F32 = jnp.float32
 BF16 = jnp.bfloat16
@@ -42,64 +42,91 @@
     return lax.ppermute(value, "ctx", pairs)
 
 
-def line_gather(own, line, n):
-    up, down = [own], [own]
-    for j in range(1, n):
-        up.append(line_move(up[-1], 1, range(j - 1, n - 1)))
-        down.append(line_move(down[-1], -1, range(1, n - j + 1)))
-    slots = [own]
-    for j in range(1, n):
-        slots.append(jnp.where(line + j < n, down[j], up[n - j]))
-    return slots
+def line_groups(n):
+    return [[p * QUAD + q for p in range(n)] for q in range(QUAD)]
+
+
+def line_gather(own, n):
+    return lax.all_gather(own, "ctx", axis=0, axis_index_groups=line_groups(n), tiled=True)
+
+
+def line_scatter(partial, n):
+    return lax.psum_scatter(partial, "ctx", scatter_dimension=0, axis_index_groups=line_groups(n), tiled=True)
+
+
+def line_move(value, by, sources):
+    pairs = [(s * QUAD + q, (s + by) * QUAD + q) for s in sources for q in range(QUAD)]
+    return lax.ppermute(value, "ctx", pairs)
+
+
+def tie(*values):
+    return lax.optimization_barrier(values)
 
 
 def add16(a, b):
     return (a.astype(F32) + b.astype(F32)).astype(BF16)
 
 
-def line_scatter(slots, n):
-    got_up = got_down = None
-    for t in range(1, n):
-        send_up, send_down = slots[n - t], slots[t]
-        if got_up is not None:
-            send_up, send_down = add16(send_up, got_up), add16(send_down, got_down)
-        got_up = line_move(send_up, 1, range(0, t))
-        got_down = line_move(send_down, -1, range(n - t, n))
-    total = slots[0].astype(F32)
-    if got_up is not None:
-        total = total + got_up.astype(F32) + got_down.astype(F32)
-    return total
-
-
-def gather_rows(own):
-    half = own.shape[0] // 2
-    from_x, from_b = swap_x(own), swap_b(own)
-    top, bottom = swap_x(from_b[:half]), swap_b(from_x[half:])
-    near = [own, from_x, from_b, top, bottom]
-    return jnp.concatenate(near + [swap_core(piece) for piece in near], axis=0)
-
-
-def scatter_rows(near, far):
-    r = near.shape[0] // 4
-    half = r // 2
-
-    def fold(block):
-        rows = slice(block * r, (block + 1) * r)
-        return add16(near[rows], swap_core(far[rows]))
-
-    both, for_x, for_b, own = fold(3), fold(1), fold(2), fold(0)
-    top, bottom = swap_x(both[:half]), swap_b(both[half:])
-    x_top, b_bottom = swap_x(for_x[:half]), swap_b(for_b[half:])
-    x_bottom = swap_x(add16(for_x[half:], bottom))
-    b_top = swap_b(add16(for_b[:half], top))
-    own = own.astype(F32)
-    return jnp.concatenate(
-        [
-            own[:half] + x_top.astype(F32) + b_top.astype(F32),
-            own[half:] + b_bottom.astype(F32) + x_bottom.astype(F32),
-        ],
-        axis=0,
-    )
+class Rows:
+    def __init__(self, own):
+        self.own, self.half = own, own.shape[0] // 2
+        self.first = (swap_x(own), swap_b(own))
+
+    def second(self):
+        from_x, from_b = self.first
+        self.last = (swap_x(from_b[: self.half]), swap_b(from_x[self.half :]))
+
+    def third(self):
+        near = [self.own, *self.first, *self.last]
+        return jnp.concatenate(near + [swap_core(piece) for piece in near], axis=0)
+
+
+def gather_rows(own, beside=None):
+    rows = Rows(own)
+    if beside is not None:
+        rows.first, beside = tie(rows.first, beside)
+    rows.second()
+    return rows.third() if beside is None else (rows.third(), beside)
+
+
+class Sums:
+    def __init__(self, near, far):
+        r = near.shape[0] // 4
+        self.half = r // 2
+
+        def fold(block):
+            rows = slice(block * r, (block + 1) * r)
+            return add16(near[rows], swap_core(far[rows]))
+
+        self.parts = (fold(3), fold(1), fold(2), fold(0))
+
+    def second(self):
+        both, for_x, for_b, _ = self.parts
+        half = self.half
+        self.got = (swap_x(both[:half]), swap_b(both[half:]), swap_x(for_x[:half]), swap_b(for_b[half:]))
+
+    def third(self):
+        _, for_x, for_b, own = self.parts
+        top, bottom, x_top, b_bottom = self.got
+        half = self.half
+        x_bottom = swap_x(add16(for_x[half:], bottom))
+        b_top = swap_b(add16(for_b[:half], top))
+        own = own.astype(F32)
+        return jnp.concatenate(
+            [
+                own[:half] + x_top.astype(F32) + b_top.astype(F32),
+                own[half:] + b_bottom.astype(F32) + x_bottom.astype(F32),
+            ],
+            axis=0,
+        )
+
+
+def scatter_rows(near, far, beside=None):
+    sums = Sums(near, far)
+    sums.second()
+    if beside is not None:
+        sums.got, beside = tie(sums.got, beside)
+    return sums.third() if beside is None else (sums.third(), beside)
 
 
 def spread(pieces):
@@ -196,32 +223,36 @@
 
 
 def attend_kernel(
-    table, lo, hi, q_ref, start_ref, kv_ref, o_ref, of_ref, stat_ref, acc, total, *, heads, width, reach, bk
+    table, lo, hi, q_ref, start_ref, kv_ref, o_ref, of_ref, stat_ref, acc, ones_v, *, heads, width, reach, bk
 ):
     t = pl.program_id(0)
     r = q_ref.shape[0]
+
+    @pl.when(t == 0)
+    def _():
+        lane = lax.broadcasted_iota(jnp.int32, kv_ref.shape, 1)
+        ones_v[...] = jnp.where(lane < width, jnp.ones((), BF16), kv_ref[...])
+
     q = stack_heads(q_ref[...], heads, width)
     q = jnp.concatenate([q, jnp.zeros_like(q)], axis=-1)
     start = jnp.concatenate([start_ref[...]] * heads, axis=0)
     pos = reach + t * r + lax.broadcasted_iota(jnp.int32, (r, 1), 0)
     pos = jnp.concatenate([pos] * heads, axis=0)
     acc[...] = jnp.zeros_like(acc)
-    total[...] = jnp.zeros_like(total)
     c = LOG2E / math.sqrt(width)
 
     def step(kb, carry):
         k0 = pl.multiple_of(kb * bk, bk)
-        kv = kv_ref[pl.ds(k0, bk), :]
-        s = dot_nt(q, kv)
+        s = dot_nt(q, kv_ref[pl.ds(k0, bk), :])
         key = k0 + lax.broadcasted_iota(jnp.int32, (1, bk), 1)
         p = jnp.where((key >= start) & (key <= pos), jnp.exp2(s * c), 0.0)
-        total[...] += jnp.sum(p, axis=-1, keepdims=True)
-        acc[...] += dot(p.astype(BF16), kv)
+        acc[...] += dot(p.astype(BF16), ones_v[pl.ds(k0, bk), :])
         return carry
 
     lax.fori_loop(lo[t], hi[t], step, 0)
-    o = acc[...][:, width:] / total[...]
-    stat_ref[...] = jnp.log2(total[...])
+    total = acc[:, :1]
+    o = acc[:, width:] / total
+    stat_ref[...] = jnp.log2(total)
     for h in range(heads):
         part = o[h * r : (h + 1) * r]
         of_ref[:, h * width : (h + 1) * width] = part
@@ -270,6 +301,113 @@
     dq = acc[...][:, :width] * scale
     for h in range(heads):
         dq_ref[:, h * width : (h + 1) * width] = dq[h * r : (h + 1) * r]
+
+
+def feed_kernel(a_ref, c_ref, w_ref, *refs, hb, more):
+    prev, (hid_ref, dgu_ref, near_ref, far_ref) = refs[:more], refs[more:]
+    t = pl.program_id(0)
+    half = pl.num_programs(0) // 2
+    a, c = a_ref[...], c_ref[...]
+    gate, up = dot(a, w_ref[:, :hb]), dot(a, w_ref[:, hb : 2 * hb])
+    d_hid = dot(c, w_ref[:, 2 * hb :])
+    sig = jax.nn.sigmoid(gate)
+    silu = gate * sig
+    hid_ref[...] = (silu * up).astype(BF16)
+    dgu_ref[:, :hb] = (d_hid * up * (sig * (1.0 + gate * (1.0 - sig)))).astype(BF16)
+    dgu_ref[:, hb:] = (d_hid * silu).astype(BF16)
+    back = dot_nt(dgu_ref[...], w_ref[:, : 2 * hb])
+
+    @pl.when(t < half)
+    def _():
+        near_ref[...] = (back + prev[0][...].astype(F32) if prev else back).astype(BF16)
+
+    @pl.when(t >= half)
+    def _():
+        far_ref[...] = (back + prev[1][...].astype(F32) if prev else back).astype(BF16)
+
+
+def feed_forward(a, c, w, prev, rows=256):
+    total, model = a.shape
+    hb = w.shape[1] // 3
+    blocks = total // rows
+    half = blocks // 2
+    row = lambda cols: pl.BlockSpec((rows, cols), lambda t: (t, 0))
+    near = pl.BlockSpec((rows, model), lambda t: (jnp.minimum(t, half - 1), 0))
+    far = pl.BlockSpec((rows, model), lambda t: (jnp.maximum(t - half, 0), 0))
+    whole = pl.BlockSpec((model, 3 * hb), lambda t: (0, 0), pipeline_mode=pl.Buffered(1))
+    part = ((total // 2, model), BF16)
+    return call(
+        functools.partial(feed_kernel, hb=hb, more=len(prev)),
+        blocks,
+        0,
+        [row(model), row(model), whole] + [near, far][: len(prev)],
+        [((total, hb), BF16, row(hb)), ((total, 2 * hb), BF16, row(2 * hb)), (*part, near), (*part, far)],
+        [],
+        (a, c, w, *prev),
+        10 * total * model * hb,
+        2 * total * (3 * model + 3 * hb) + 6 * model * hb,
+        total * hb,
+    )
+
+
+def pack_kernel(*refs, flip, widths):
+    ins, outs = refs[: len(flip)], refs[len(flip) :]
+    for quarter in range(QUAD):
+        for o, out_ref in enumerate(outs):
+            at = 0
+            for ref, turned, width in zip(ins, flip, widths):
+                part = width // len(outs)
+                cut = slice(quarter * width + o * part, quarter * width + (o + 1) * part)
+                out_ref[quarter, :, at : at + part] = jnp.transpose(ref[cut, :]) if turned else ref[:, cut]
+                at += part
+
+
+def whole_block(v):
+    return pl.BlockSpec(v.shape, lambda t: (0,) * len(v.shape))
+
+
+def packed(weights, flip, outs):
+    rows = weights[0].shape[0]
+    widths = [(w.shape[0] if f else w.shape[1]) // QUAD for w, f in zip(weights, flip)]
+    shape = jax.ShapeDtypeStruct((QUAD, rows, sum(widths) // outs), BF16)
+    return call(
+        functools.partial(pack_kernel, flip=flip, widths=widths),
+        1,
+        0,
+        [whole_block(w) for w in weights],
+        [(shape.shape, BF16, whole_block(shape))] * outs,
+        [],
+        tuple(weights),
+        1,
+        4 * outs * math.prod(shape.shape),
+    )
+
+
+def weights_kernel(a_ref, b_ref, c_ref, d_ref, out_ref):
+    cols = b_ref.shape[1]
+    out_ref[:, :cols] = dot_tn(a_ref[...], b_ref[...]).astype(BF16)
+    out_ref[:, cols:] = dot_tn(c_ref[...], d_ref[...]).astype(BF16)
+
+
+def weight_grads(a, b, c, d, rows=512):
+    total, model = a.shape
+    cut = pl.BlockSpec((total, rows), lambda t: (0, t))
+
+    def whole(v):
+        return pl.BlockSpec(v.shape, lambda t: (0, 0), pipeline_mode=pl.Buffered(1))
+
+    cols = b.shape[1] + d.shape[1]
+    return call(
+        weights_kernel,
+        model // rows,
+        0,
+        [cut, whole(b), cut, whole(d)],
+        [((model, cols), BF16, pl.BlockSpec((rows, cols), lambda t: (t, 0)))],
+        [],
+        (a, b, c, d),
+        2 * total * model * cols,
+        2 * (2 * total * model + (total + model) * cols),
+    )[0]
 
 
 def call(kernel, blocks, prefetch, ins, outs, scratch, args, flops, nbytes, transcendentals=0):
@@ -320,30 +458,14 @@
     step = model // n
     reach = WB * doc_start.shape[0]
 
-    def rotated(v):
-        return lax.dynamic_slice_in_dim(jnp.concatenate([v, v], axis=-1), line * step, model, v.ndim - 1)
-
-    def unrotated(v):
-        return lax.dynamic_slice_in_dim(jnp.concatenate([v, v], axis=-1), (n - line) * step, model, v.ndim - 1)
-
-    def columns(j):
-        return slice(j * step, (j + 1) * step)
-
-    def by_quarter(w):
-        return w.reshape(w.shape[0], QUAD, -1)
-
-    qkv_shard = jnp.concatenate(
-        [by_quarter(w_query), by_quarter(key_projection), by_quarter(value_projection)], axis=-1
-    ).transpose(1, 0, 2)
-    qkv_shard = spread(qkv_shard).reshape(step, -1)
-    out_shard = spread(w_out.reshape(QUAD, qw, -1)).transpose(1, 0, 2).reshape(qw, step)
-    gu_shard = jnp.concatenate([by_quarter(w_gate), by_quarter(w_up)], axis=-1).transpose(1, 0, 2)
-    gu_shard = spread(gu_shard).reshape(step, -1)
-    down_shard = spread(w_down.reshape(QUAD, hidden, -1)).transpose(1, 0, 2).reshape(hidden, step)
-    w_qkv = jnp.concatenate(line_gather(qkv_shard, line, n), axis=0)
-    w_o = jnp.concatenate(line_gather(out_shard, line, n), axis=1)
-    w_gu = jnp.concatenate(line_gather(gu_shard, line, n), axis=0)
-    w_d = jnp.concatenate(line_gather(down_shard, line, n), axis=1)
+    (sent,) = packed((w_query, key_projection, value_projection, w_out), (0, 0, 0, 1), 1)
+    sent, tokens = tie(spread(sent), tokens)
+    w_attn = line_gather(sent.reshape(step, -1), n)
+    w_qkv, w_o = w_attn[:, : qw + 2 * width], w_attn[:, qw + 2 * width :]
+
+    hid_block = hidden // 2
+    sent, w_gate = tie(sent, w_gate)
+    ffn_pieces = packed((w_gate, w_up, w_down), (0, 0, 1), 2)
 
     near_core, near_b = swap_core(doc_start), swap_b(doc_start)
     far = swap_core(near_b)
@@ -366,12 +488,13 @@
     hi = (reach + (blocks + 1) * r - 1) // KEY_BLOCK + 1
     nb = 2 * QUAD
 
-    gain_1, gain_2 = rotated(attn_gain), rotated(ffn_gain)
-    x_own = rotated(tokens).astype(F32)
+    gain_1, gain_2 = attn_gain, ffn_gain
+    x_own = tokens.astype(F32)
     scale_1 = rms_scale(x_own)
-    a_one = gather_rows((x_own * scale_1 * gain_1).astype(BF16))
-    cot_own = rotated(cotangent)
-    cot = gather_rows(cot_own)
+    a_one, pieces_0 = tie(gather_rows((x_own * scale_1 * gain_1).astype(BF16)), ffn_pieces[0])
+    sent_0, cot_own = tie(spread(pieces_0), cotangent)
+    w_ffn_0 = line_gather(sent_0.reshape(step, -1), n)
+    cot = Rows(cot_own)
     raw = dot(a_one, w_qkv)
 
     def here(cols):
@@ -403,6 +526,9 @@
         distance += 1
     halo = [line_move(kv[plane - rows :], d, range(0, max(n - d, 0))) for d, rows in spans]
     keys = jnp.concatenate(halo[::-1] + [kv], axis=0)
+    keys, cot.first = tie(keys, cot.first)
+    cot.second()
+    q, pieces_1 = tie(q, ffn_pieces[1])
     nk = keys.shape[0]
     attn_flops = 2 * plane * heads * (plane // 2 + 2 * KEY_BLOCK) * width
 
@@ -417,38 +543,47 @@
             ((plane, qw), F32, here(qw)),
             ((plane * heads, 1), F32, stacked),
         ],
-        [pltpu.VMEM((heads * r, 2 * width), F32), pltpu.VMEM((heads * r, 1), F32)],
+        [pltpu.VMEM((heads * r, 2 * width), F32), pltpu.VMEM((nk, 2 * width), BF16)],
         (table, lo, hi, q, local_start[:, None], keys),
         8 * attn_flops,
         plane * qw * 8,
     )
 
     half = plane // 2
-    attn_sum = scatter_rows(dot(o[:half], w_o).astype(BF16), dot(o[half:], w_o).astype(BF16))
+    o, sent_1 = tie(o, spread(pieces_1))
+    w_ffn_1 = line_gather(sent_1.reshape(step, -1), n)
+    keys, cot.last = tie(keys, cot.last)
+    attn_sum, cot = scatter_rows(
+        dot_nt(o[:half], w_o).astype(BF16), dot_nt(o[half:], w_o).astype(BF16), cot.third()
+    )
     resid = x_own + attn_sum
     scale_2 = rms_scale(resid)
     a_two = gather_rows((resid * scale_2 * gain_2).astype(BF16))
 
-    gate_up = dot(a_two, w_gu)
-    gate, up = gate_up[:, :hidden], gate_up[:, hidden:]
-    d_hid = dot_nt(cot, w_d)
-    sig = jax.nn.sigmoid(gate)
-    silu = gate * sig
-    hid = (silu * up).astype(BF16)
-    d_gate = (d_hid * up * sig * (1.0 + gate * (1.0 - sig))).astype(BF16)
-    d_up = (d_hid * silu).astype(BF16)
-    d_gu = jnp.concatenate([d_gate, d_up], axis=-1)
-    d_two = scatter_rows(dot_nt(d_gu[:half], w_gu).astype(BF16), dot_nt(d_gu[half:], w_gu).astype(BF16))
+    hid_0, d_gu_0, near, far = feed_forward(a_two, cot, w_ffn_0, ())
+    ffn_grad_0 = weight_grads(a_two, d_gu_0, cot, hid_0)
+    w_ffn_1, _ = tie(w_ffn_1, ffn_grad_0)
+    ffn_grad_0 = line_scatter(ffn_grad_0, n)
+    hid_1, d_gu_1, near, far = feed_forward(a_two, cot, w_ffn_1, (near, far))
+    d_two, ffn_grad_1 = scatter_rows(near, far, weight_grads(a_two, d_gu_1, cot, hid_1))
+    ffn_grad_1 = line_scatter(ffn_grad_1, n)
     d_res, d_ffn_gain = norm_back(resid, scale_2, gain_2, d_two)
-    d_h = cot_own.astype(F32) + d_res
-    d_h_rows = gather_rows(d_h.astype(BF16))
-    ffn_sum = scatter_rows(dot(hid[:half], w_d).astype(BF16), dot(hid[half:], w_d).astype(BF16))
-    out_tokens = unrotated((resid + ffn_sum).astype(BF16))
-
-    gu_grad = line_scatter([dot_tn(a_two[:, columns(j)], d_gu).astype(BF16) for j in range(n)], n)
-    down_grad = line_scatter([dot_tn(hid, cot[:, columns(j)]).astype(BF16) for j in range(n)], n)
-
-    d_o = dot_nt(d_h_rows, w_o).astype(BF16)
+    d_h = cotangent.astype(F32) + d_res
+
+    def down_rows(cut):
+        return (dot_nt(hid_0[cut], w_ffn_0[:, 2 * hid_block :]) + dot_nt(hid_1[cut], w_ffn_1[:, 2 * hid_block :])).astype(BF16)
+
+    d_h_rows, down = gather_rows(
+        d_h.astype(BF16), (down_rows(slice(0, half)), down_rows(slice(half, plane)))
+    )
+    ffn_sum = Sums(*down)
+
+    def home(grad):
+        return spread(grad.reshape(QUAD, step // QUAD, -1)).transpose(1, 0, 2)
+
+    d_o = dot(d_h_rows, w_o).astype(BF16)
+    d_o, ffn_sum.parts = tie(d_o, ffn_sum.parts)
+    ffn_sum.second()
     dq, dkv = call(
         functools.partial(attend_back_kernel, heads=heads, width=width, reach=reach, bk=KEY_BLOCK),
         nb,
@@ -467,6 +602,9 @@
         20 * attn_flops,
         plane * qw * 12,
     )
+    dq, ffn_sum.got, ffn_grad_0 = tie(dq, ffn_sum.got, ffn_grad_0)
+    back_0 = home(ffn_grad_0)
+    out_tokens = (resid + ffn_sum.third()).astype(BF16)
     dkv_own = dkv[nk - plane :]
     offset = nk - plane
     for d, rows in spans:
@@ -492,29 +630,25 @@
         plane * (qw + width) * 20,
         plane * (qw + 2 * width) * 10,
     )
-    out_grad = line_scatter([dot_tn(o, d_h_rows[:, columns(j)]).astype(BF16) for j in range(n)], n)
-    qkv_grad = line_scatter([dot_tn(a_one[:, columns(j)], d_raw).astype(BF16) for j in range(n)], n)
-    d_one = scatter_rows(dot_nt(d_raw[:half], w_qkv).astype(BF16), dot_nt(d_raw[half:], w_qkv).astype(BF16))
+    attn_grad, ffn_grad_1 = tie(weight_grads(a_one, d_raw, d_h_rows, o), ffn_grad_1)
+    attn_grad, back_0 = tie(attn_grad, back_0)
+    attn_grad = line_scatter(attn_grad, n)
+    back_1 = home(ffn_grad_1)
+    attn_back = home(attn_grad)
+    d_one, back_1 = scatter_rows(
+        dot_nt(d_raw[:half], w_qkv).astype(BF16), dot_nt(d_raw[half:], w_qkv).astype(BF16), back_1
+    )
     d_x, d_attn_gain = norm_back(x_own, scale_1, gain_1, d_one)
-    d_tokens = unrotated(d_h + d_x)
-
-    def columns_back(grad):
-        return spread(grad.astype(BF16).reshape(QUAD, step // QUAD, -1)).transpose(1, 0, 2)
-
-    def rows_back(grad):
-        pieces = grad.astype(BF16).reshape(grad.shape[0], QUAD, -1).transpose(1, 0, 2)
-        return spread(pieces).reshape(QUAD * grad.shape[0], -1).astype(F32)
-
-    gu_back = columns_back(gu_grad)
-    qkv_back = columns_back(qkv_grad)
-    kk = step // QUAD
-
-    def piece(v, start, size):
-        return v[:, :, start : start + size].reshape(kk, -1).astype(F32)
-
-    gains = sum_everywhere(
-        jnp.concatenate([unrotated(d_attn_gain), unrotated(d_ffn_gain), d_head_gains[0], d_head_gains[1]])
-    )
+    d_tokens = d_h + d_x
+
+    def piece(start, size):
+        return attn_back[:, :, start : start + size].reshape(step // QUAD, -1).astype(F32)
+
+    def joined(start):
+        cols = [v[:, :, start : start + hid_block] for v in (back_0, back_1)]
+        return jnp.concatenate(cols, axis=-1).reshape(step // QUAD, -1).astype(F32)
+
+    gains = sum_everywhere(jnp.concatenate([d_attn_gain, d_ffn_gain, d_head_gains[0], d_head_gains[1]]))
     return (
         out_tokens,
         d_tokens,
@@ -522,13 +656,13 @@
         gains[model : 2 * model],
         gains[2 * model : 2 * model + width],
         gains[2 * model + width :],
-        piece(qkv_back, 0, qw),
-        piece(qkv_back, qw, width),
-        piece(qkv_back, qw + width, width),
-        rows_back(out_grad),
-        piece(gu_back, 0, hidden),
-        piece(gu_back, hidden, hidden),
-        rows_back(down_grad),
+        piece(0, qw),
+        piece(qw, width),
+        piece(qw + width, width),
+        piece(qw + 2 * width, qw).T,
+        joined(0),
+        joined(hid_block),
+        joined(2 * hid_block).T,
     )
 
 

time: 1030 us -> 716 us (0.70)
  starting transfers between devices: 282 us -> 103 us
  waiting for transfers between devices: 369 us -> 231 us
  matrix products: 151 us -> 39.5 us
  Pallas kernels: 74.1 us -> 147 us
  blocking collectives: 0 us -> 37.9 us
  other arithmetic: 70.3 us -> 54.5 us
  between operations: 3.77 us -> 16.1 us
    ppermute x52 -> x4, waiting for transfers between devices: 243 us -> 56.7 us  [line_move(): return lax.ppermute(value, 'ctx', pairs)]
    ppermute x52 -> x4, starting transfers between devices: 185 us -> 10.6 us  [line_move(): return lax.ppermute(value, 'ctx', pairs)]
    pallas_call x4 -> x11, Pallas kernels: 74.1 us -> 147 us  [call(): pl.pallas_call(kernel, out_shape=[jax.ShapeDtypeStruct(shape, dtype) for...]
    dot_general x16 -> x0, matrix products: 62.4 us -> none  [dot_tn(): lax.dot_general(a, b, (((0,), (0,)), ((), ())), preferred_element_type=F32)]
    all_to_all x0 -> x2, blocking collectives: none -> 37.9 us  [spread(): lax.all_to_all(pieces, 'ctx', 0, 0, axis_index_groups=groups, tiled=True)]
    dot_general x6 -> x2, matrix products: 42.2 us -> 9.37 us  [dot(): return jnp.dot(a, b, preferred_element_type=F32)]
    all_gather x0 -> x3, waiting for transfers between devices: none -> 31.8 us  [line_gather(): lax.all_gather(own, 'ctx', axis=0, axis_index_groups=line_groups(n), tile...]
    dot_general x6 -> x8, matrix products: 46.5 us -> 30.2 us  [dot_nt(): lax.dot_general(a, b, (((1,), (1,)), ((), ())), preferred_element_type=F32)]
  transfers between devices with their start and end apart: 144 -> 98, of which waited for: 48 -> 36; matrix products, arithmetic and copies ran while one was open for 19% -> 22% of each run, Pallas kernels for 7% -> 21%
where the time goes in v2:
time: 716 us; the launch traced here: 707 us
  waiting for transfers between devices  231 us (32%)
  Pallas kernels  147 us (21%)
  starting transfers between devices  103 us (14%)
  local copies, waits for them, and re-layouts  77.6 us (11%)
  other arithmetic  54.5 us (8%)
  matrix products  39.5 us (6%)
  blocking collectives  37.9 us (5%)
  between operations  16.1 us (2%)
    pallas_call x11, Pallas kernels, call(): pl.pallas_call(kernel, out_shape=[jax.ShapeDtypeStruct(shape, dtype) for...  147 us
    ppermute x63, waiting for transfers between devices, swap_ctx(): return lax.ppermute(value, 'ctx', [(i, i ^ bit) for i in range(n)])  101 us
    ppermute x4, waiting for transfers between devices, line_move(): return lax.ppermute(value, 'ctx', pairs)  56.7 us
    unnamed x188, local copies, waits for them, and re-layouts  47.4 us
    ppermute x63, starting transfers between devices, swap_ctx(): return lax.ppermute(value, 'ctx', [(i, i ^ bit) for i in range(n)])  40.9 us
    all_to_all x2, blocking collectives, spread(): lax.all_to_all(pieces, 'ctx', 0, 0, axis_index_groups=groups, tiled=True)  37.9 us
    ppermute x21, waiting for transfers between devices, swap_x(): return lax.ppermute(value, 'tp', [(0, 1), (1, 0)])  35.3 us
    all_gather x3, waiting for transfers between devices, line_gather(): lax.all_gather(own, 'ctx', axis=0, axis_index_groups=line_groups(n), tile...  31.8 us
  transfers between devices with their start and end apart: 98, of which 36 were waited for; matrix products, arithmetic and copies ran while one was open for 22% of the time, Pallas kernels for 21%

profile of v2, /device:TPU:0, one launch (start us, length us, event | category | flops | bytes accessed | tf_op | source)
XLA Modules:
  0.0 707.0 jit_solution(1856642302340285006)
XLA Ops:
  11.0 14.5 %all_to_all.30 = bf16[4,128,640]{2,1,0:T(8,128)(2,1)} all-to-all(bf16[4,128,640]{2,1,0:T(8,128)(2,1)S(1)} %shard_map.237), channel_id=1, replica_groups={{0,2,4,6},{8,10,12,14},{16,18,20,22},{24,26,28,30},{1,3,5,7},{9,11,13,1..., dimensions={0} | all-to-all | bytes 1310720 | tf_op jit(solution)/shard_map/all_to_all | solution.py:135
  31.3 15.2 %collective-permute-done.4 = bf16[192,2048]{1,0:T(8,128)(2,1)} collective-permute-done((bf16[192,2048]{1,0:T(8,128)(2,1)}, bf16[192,2048]{1,0:T(8,128)(2,1)}, u32[]{:S(2)}, u32[]{:S(2)}) %collective-permute-start.4) | collective-permute-done | bytes 786464 | tf_op jit(solution)/shard_map/ppermute | solution.py:25
  65.1 23.4 %all_to_all.31 = bf16[4,128,1536]{2,1,0:T(8,128)(2,1)} all-to-all(bf16[4,128,1536]{2,1,0:T(8,128)(2,1)S(1)} %get-tuple-element.93), channel_id=1, replica_groups={{0,2,4,6},{8,10,12,14},{16,18,20,22},{24,26,28,30},{1,3,5,7},{9,11,13,1..., dimensions={0} | all-to-all | bytes 3145728 | tf_op jit(solution)/shard_map/all_to_all | solution.py:135
  89.1 3.2 collective-permute-done.1
  93.9 2.8 fusion.44
  99.1 6.1 fusion.20.raw_ref
  105.2 9.4 %shard_map.239 = (bf16[1536,256]{1,0:T(8,128)(2,1)S(1)}, bf16[1536,128]{1,0:T(8,128)(2,1)S(1)}) custom-call(s32[8]{0:T(128)S(1)} %xor_or_fusion.table, f32[1536,384]{1,0:T(8,128)S(1)} %fusion.20.raw_ref, f32[1536,64]{1,0:T(8,128)S(1)} %get-tuple-element.280.cos_ref, f32[1536,64]{1,0:T(8,128)S(1)} %get-tuple-element.281.sin_ref, f32[1,64]{1,0:T(1,128)S(1)} %bitcast.40, ...), custom_call_target="tpu_custom_call" | custom-call | flops 4915200 | bytes 3538944 | tf_op jit(solution)/shard_map/pallas_call | solution.py:414
  114.6 3.6 collective-permute-start.13
  118.3 4.4 collective-permute-start.12
  124.9 4.3 all-to-all-start.2
  129.6 14.5 %collective-permute-done.12 = bf16[768,128]{1,0:T(8,128)(2,1)S(1)} collective-permute-done((bf16[768,128]{1,0:T(8,128)(2,1)S(1)}, bf16[768,128]{1,0:T(8,128)(2,1)S(1)}, u32[]{:S(2)}, u32[]{:S(2)}) %collective-permute-start.12) | collective-permute-done | bytes 196640 | tf_op jit(solution)/shard_map/ppermute | solution.py:59
  150.0 12.0 %shard_map.240 = (bf16[1536,256]{1,0:T(8,128)(2,1)S(1)}, f32[1536,256]{1,0:T(8,128)S(1)}, f32[6144,1]{1,0:T(8,128)}) custom-call(s32[8]{0:T(128)S(1)} %xor_or_fusion.table, s32[8]{0:T(128)S(1)} %get-tuple-element.282.lo, s32[8]{0:T(128)S(1)} %get-tuple-element.283.hi, bf16[1536,256]{1,0:T(8,128)(2,1)S(1)} %copy-done.22, s32[1536,1]{1,0:T(8,128)S(1)} %copy-done.12, ...), custom_call_target="tpu_custom_call" | custom-call | flops 9663676416 | bytes 3145728 | tf_op jit(solution)/shard_map/pallas_call | solution.py:414
  161.9 2.7 constant_dynamic-update-slice_fusion.18
  170.5 2.3 convolution_convert_fusion.2
  177.8 2.1 constant_dynamic-update-slice_fusion.12
  180.0 2.3 convolution_convert_fusion.3
  182.9 2.9 add_convert_fusion.14
  191.6 6.4 collective-permute-done.21
  198.5 7.2 %collective-permute-done.19 = bf16[96,2048]{1,0:T(8,128)(2,1)S(1)} collective-permute-done((bf16[96,2048]{1,0:T(8,128)(2,1)S(1)}, bf16[96,2048]{1,0:T(8,128)(2,1)S(1)}, u32[]{:S(2)}, u32[]{:S(2)}) %collective-permute-start.19) | collective-permute-done | bytes 393248 | tf_op jit(solution)/shard_map/ppermute | solution.py:25
  207.9 8.1 %collective-permute-done.31 = bf16[96,2048]{1,0:T(8,128)(2,1)S(1)} collective-permute-done((bf16[96,2048]{1,0:T(8,128)(2,1)S(1)}, bf16[96,2048]{1,0:T(8,128)(2,1)S(1)}, u32[]{:S(2)}, u32[]{:S(2)}) %collective-permute-start.31) | collective-permute-done | bytes 393248 | tf_op jit(solution)/shard_map/ppermute | solution.py:25
  221.9 14.3 %collective-permute-done.34 = bf16[192,2048]{1,0:T(8,128)(2,1)S(1)} collective-permute-done((bf16[192,2048]{1,0:T(8,128)(2,1)S(1)}, bf16[192,2048]{1,0:T(8,128)(2,1)S(1)}, u32[]{:S(2)}, u32[]{:S(2)}) %collective-permute-start.34) | collective-permute-done | bytes 786464 | tf_op jit(solution)/shard_map/ppermute | solution.py:25
  241.7 4.1 collective-permute-done.35
  252.4 23.8 %shard_map.241 = (bf16[1536,512]{1,0:T(8,128)(2,1)S(1)}, bf16[1536,1024]{1,0:T(8,128)(2,1)S(1)}, bf16[768,2048]{1,0:T(8,128)(2,1)}, bf16[768,2048]{1,0:T(8,128)(2,1)}) custom-call(bf16[1536,2048]{1,0:T(8,128)(2,1)} %constant_dynamic-update-slice_fusion.20.a_ref, bf16[1536,2048]{1,0:T(8,128)(2,1)} %constant_dynamic-update-slice_fusion.10.c_ref, ...), custom_call_target="tpu_custom_call" | custom-call | flops 16106127360 | bytes 29884416 | tf_op jit(solution)/shard_map/pallas_call | solution.py:414
  276.2 13.6 %shard_map.242 = bf16[2048,1536]{1,0:T(8,128)(2,1)} custom-call(bf16[1536,2048]{1,0:T(8,128)(2,1)} %constant_dynamic-update-slice_fusion.20.a_ref, bf16[1536,1024]{1,0:T(8,128)(2,1)S(1)} %get-tuple-element.110.b_ref, bf16[1536,2048]{1,0:T(8,128)(2,1)} %constant_dynamic-update-slice_fusion.10.c_ref, bf16[1536,512]{1,0:T(8,128)(2,1)S(1)} %get-tuple-element.111.d_ref), custom_call_target="tpu_custom_call" | custom-call | flops 9663676416 | bytes 23592960 | tf_op jit(solution)/shard_map/pallas_call | solution.py:414
  291.0 12.0 %reduce-scatter.6.cloned.1.call-start = ((), (), s32[]{:S(2)}) async-start(), calls=%async_computation.13 | async-start | bytes 7864320 | tf_op jit(solution)/shard_map/reduce_scatter | solution.py:54
  303.4 31.8 %all-gather.6.cloned.1.call-done.w_ref = bf16[2048,1536]{1,0:T(8,128)(2,1)} async-done(((bf16[512,1536]{1,0:T(8,128)(2,1)}), bf16[2048,1536]{1,0:T(8,128)(2,1)}) %all-gather.6.cloned.1.call-update) | async-done | bytes 6291472 | tf_op jit(solution)/shard_map/all_gather | solution.py:50
  335.1 25.4 %shard_map.243 = (bf16[1536,512]{1,0:T(8,128)(2,1)S(1)}, bf16[1536,1024]{1,0:T(8,128)(2,1)S(1)}, bf16[768,2048]{1,0:T(8,128)(2,1)}, bf16[768,2048]{1,0:T(8,128)(2,1)}) custom-call(bf16[1536,2048]{1,0:T(8,128)(2,1)} %constant_dynamic-update-slice_fusion.20.a_ref, bf16[1536,2048]{1,0:T(8,128)(2,1)} %constant_dynamic-update-slice_fusion.10.c_ref, ...), custom_call_target="tpu_custom_call" | custom-call | flops 16106127360 | bytes 29884416 | tf_op jit(solution)/shard_map/pallas_call | solution.py:414
  360.5 4.3 fusion.50
  365.8 13.6 %shard_map.244 = bf16[2048,1536]{1,0:T(8,128)(2,1)} custom-call(bf16[1536,2048]{1,0:T(8,128)(2,1)} %constant_dynamic-update-slice_fusion.20.a_ref, bf16[1536,1024]{1,0:T(8,128)(2,1)S(1)} %get-tuple-element.117.b_ref, bf16[1536,2048]{1,0:T(8,128)(2,1)} %constant_dynamic-update-slice_fusion.10.c_ref, bf16[1536,512]{1,0:T(8,128)(2,1)S(1)} %get-tuple-element.118.d_ref), custom_call_target="tpu_custom_call" | custom-call | flops 9663676416 | bytes 23592960 | tf_op jit(solution)/shard_map/pallas_call | solution.py:414
  379.5 5.2 add_convert_fusion.10
  389.0 6.1 fusion.6
  398.3 7.2 %collective-permute-done.45 = bf16[96,2048]{1,0:T(8,128)(2,1)S(1)} collective-permute-done((bf16[96,2048]{1,0:T(8,128)(2,1)S(1)}, bf16[96,2048]{1,0:T(8,128)(2,1)S(1)}, u32[]{:S(2)}, u32[]{:S(2)}) %collective-permute-start.45) | collective-permute-done | bytes 393248 | tf_op jit(solution)/shard_map/ppermute | solution.py:25
  409.3 5.7 add_convert_fusion
  421.5 2.9 constant_dynamic-update-slice_fusion.39
  425.6 3.4 fusion.8
  429.0 3.5 add_convert_fusion.1
  432.6 9.1 %collective-permute-done.53 = bf16[192,2048]{1,0:T(8,128)(2,1)S(1)} collective-permute-done((bf16[192,2048]{1,0:T(8,128)(2,1)S(1)}, bf16[192,2048]{1,0:T(8,128)(2,1)S(1)}, u32[]{:S(2)}, u32[]{:S(2)}) %collective-permute-start.53) | collective-permute-done | bytes 786464 | tf_op jit(solution)/shard_map/ppermute | solution.py:25
  445.2 8.5 %collective-permute-done.54 = bf16[96,2048]{1,0:T(8,128)(2,1)S(1)} collective-permute-done((bf16[96,2048]{1,0:T(8,128)(2,1)S(1)}, bf16[96,2048]{1,0:T(8,128)(2,1)S(1)}, u32[]{:S(2)}, u32[]{:S(2)}) %collective-permute-start.54) | collective-permute-done | bytes 393248 | tf_op jit(solution)/shard_map/ppermute | solution.py:37
  455.6 3.2 collective-permute-done.59
  459.4 2.7 copy-done.33
  462.1 3.3 convolution_convert_fusion.4.do_ref
  467.0 25.0 %shard_map.245 = (f32[1536,256]{1,0:T(8,128)S(1)}, f32[3840,128]{1,0:T(8,128)}) custom-call(s32[8]{0:T(128)S(1)} %xor_or_fusion.table, s32[8]{0:T(128)S(1)} %get-tuple-element.282.lo, s32[8]{0:T(128)S(1)} %get-tuple-element.283.hi, bf16[1536,256]{1,0:T(8,128)(2,1)S(1)} %copy-done.23, bf16[1536,256]{1,0:T(8,128)(2,1)S(1)} %convolution_convert_fusion.4.do_ref, ...), custom_call_target="tpu_custom_call" | custom-call | flops 24159191040 | bytes 4718592 | tf_op jit(solution)/shard_map/pallas_call | solution.py:414
  492.0 2.2 convert.15
  501.1 22.6 %collective-permute-done.72 = bf16[768,128]{1,0:T(8,128)(2,1)S(1)} collective-permute-done((bf16[768,128]{1,0:T(8,128)(2,1)S(1)}, bf16[768,128]{1,0:T(8,128)(2,1)S(1)}, u32[]{:S(2)}, u32[]{:S(2)}) %collective-permute-start.72) | collective-permute-done | bytes 196640 | tf_op jit(solution)/shard_map/ppermute | solution.py:59
  525.1 19.6 %collective-permute-done.71 = bf16[1536,128]{1,0:T(8,128)(2,1)S(1)} collective-permute-done((bf16[1536,128]{1,0:T(8,128)(2,1)S(1)}, bf16[1536,128]{1,0:T(8,128)(2,1)S(1)}, u32[]{:S(2)}, u32[]{:S(2)}) %collective-permute-start.71) | collective-permute-done | bytes 393248 | tf_op jit(solution)/shard_map/ppermute | solution.py:59
  546.0 4.4 all-to-all-start.4
  557.8 13.4 %shard_map.246 = (bf16[1536,384]{1,0:T(8,128)(2,1)S(1)}, f32[8,64]{1,0:T(8,128)S(1)}) custom-call(s32[8]{0:T(128)S(1)} %xor_or_fusion.table, f32[1536,384]{1,0:T(8,128)} %copy-done, f32[1536,64]{1,0:T(8,128)S(1)} %get-tuple-element.280.cos_ref, f32[1536,64]{1,0:T(8,128)S(1)} %get-tuple-element.281.sin_ref, f32[1,64]{1,0:T(1,128)S(1)} %bitcast.41, ...), custom_call_target="tpu_custom_call" | custom-call | flops 9830400 | bytes 5898240 | tf_op jit(solution)/shard_map/pallas_call | solution.py:414
  575.3 9.4 %shard_map.247 = bf16[2048,640]{1,0:T(8,128)(2,1)} custom-call(bf16[1536,2048]{1,0:T(8,128)(2,1)} %constant_dynamic-update-slice_fusion.a_ref, bf16[1536,384]{1,0:T(8,128)(2,1)S(1)} %get-tuple-element.142.b_ref, bf16[1536,2048]{1,0:T(8,128)(2,1)} %copy-done.33, bf16[1536,256]{1,0:T(8,128)(2,1)S(1)} %get-tuple-element.98.d_ref), custom_call_target="tpu_custom_call" | custom-call | flops 4026531840 | bytes 17170432 | tf_op jit(solution)/shard_map/pallas_call | solution.py:414
  585.2 5.1 convolution_convert_fusion.1
  591.7 2.7 fusion.31
  594.4 3.8 all-to-all-start.3
  599.1 4.1 add_convert_fusion.2
  608.7 6.6 collective-permute-done.78
  615.3 11.8 %collective-permute-done.80 = bf16[96,2048]{1,0:T(8,128)(2,1)S(1)} collective-permute-done((bf16[96,2048]{1,0:T(8,128)(2,1)S(1)}, bf16[96,2048]{1,0:T(8,128)(2,1)S(1)}, u32[]{:S(2)}, u32[]{:S(2)}) %collective-permute-start.80) | collective-permute-done | bytes 393248 | tf_op jit(solution)/shard_map/ppermute | solution.py:25
  627.1 7.9 %collective-permute-done.76 = bf16[96,2048]{1,0:T(8,128)(2,1)S(1)} collective-permute-done((bf16[96,2048]{1,0:T(8,128)(2,1)S(1)}, bf16[96,2048]{1,0:T(8,128)(2,1)S(1)}, u32[]{:S(2)}, u32[]{:S(2)}) %collective-permute-start.76) | collective-permute-done | bytes 393248 | tf_op jit(solution)/shard_map/ppermute | solution.py:25
  639.4 2.5 fusion.52
  643.1 4.7 collective-permute-done.81
  655.3 2.7 convert_bitcast_fusion
  662.8 3.3 copy.64
  667.6 9.9 %collective-permute-start.86 = (f32[4224]{0:T(1024)S(1)}, f32[4224]{0:T(1024)S(1)}, u32[]{:S(2)}, u32[]{:S(2)}) collective-permute-start(f32[4224]{0:T(1024)S(1)} %add.277), channel_id=1, source_target_pairs={{0,8},{2,10},{4,12},{6,14},{8,0},{10,2},{12,4},{14,6},{16,24},{18,... | collective-permute-start | bytes 50696 | tf_op jit(solution)/shard_map/ppermute | solution.py:25
  680.3 2.2 copy.56
  682.5 3.5 all-to-all-start.5
  686.0 3.0 fusion.14
  690.2 6.0 all-to-all-done.5
  (457 shorter events, 163.4 us)
Async XLA Ops:
  7.2 91.9 %all-gather.4.cloned.1.call-start = ((), (), s32[]{:S(2)}) async-start(), calls=%async_computation.9 | async-start | bytes 3276800 | tf_op jit(solution)/shard_map/all_gather | solution.py:50
  27.3 19.2 %collective-permute-start.4 = (bf16[192,2048]{1,0:T(8,128)(2,1)}, bf16[192,2048]{1,0:T(8,128)(2,1)}, u32[]{:S(2)}, u32[]{:S(2)}) collective-permute-start(bf16[192,2048]{1,0:T(8,128)(2,1)} %get-tuple-element.206), channel_id=1, source_target_pairs={{0,4},{2,6},{4,0},{6,2},{8,12},{10,14},{12,8},{14,10},{16,20},{18,... | collective-permute-start | bytes 2359304 | tf_op jit(solution)/shard_map/ppermute | solution.py:25
  27.6 21.9 %collective-permute-start.3 = (bf16[192,2048]{1,0:T(8,128)(2,1)}, bf16[192,2048]{1,0:T(8,128)(2,1)}, u32[]{:S(2)}, u32[]{:S(2)}) collective-permute-start(bf16[192,2048]{1,0:T(8,128)(2,1)} %get-tuple-element.206), channel_id=1, source_target_pairs={{0,1},{1,0},{2,3},{3,2},{4,5},{5,4},{6,7},{7,6},{8,9},{9,8},{10,11... | collective-permute-start | bytes 2359304 | tf_op jit(solution)/shard_map/ppermute | solution.py:37
  29.5 222.9 %all-gather.8.cloned.1.call-start = ((), (), s32[]{:S(2)}) async-start(), calls=%async_computation.11 | async-start | bytes 7864320 | tf_op jit(solution)/shard_map/all_gather | solution.py:50
  29.6 31.1 %collective-permute-start.7 = (bf16[192,2048]{1,0:T(8,128)(2,1)}, bf16[192,2048]{1,0:T(8,128)(2,1)S(1)}, u32[]{:S(2)}, u32[]{:S(2)}) collective-permute-start(bf16[192,2048]{1,0:T(8,128)(2,1)} %get-tuple-element.206), channel_id=1, source_target_pairs={{0,2},{2,0},{4,6},{6,4},{8,10},{10,8},{12,14},{14,12},{16,18},{18,... | collective-permute-start | bytes 2359304 | tf_op jit(solution)/shard_map/ppermute | solution.py:25
  51.4 11.2 %collective-permute-start.9 = (bf16[192,2048]{1,0:T(8,128)(2,1)}, bf16[192,2048]{1,0:T(8,128)(2,1)S(1)}, u32[]{:S(2)}, u32[]{:S(2)}) collective-permute-start(bf16[192,2048]{1,0:T(8,128)(2,1)} %collective-permute-done.4), channel_id=1, source_target_pairs={{0,2},{2,0},{4,6},{6,4},{8,10},{10,8},{12,14},{14,12},{16,18},{18,... | collective-permute-start | bytes 2359304 | tf_op jit(solution)/shard_map/ppermute | solution.py:25
  98.2 45.9 %collective-permute-start.15 = (bf16[192,2048]{1,0:T(8,128)(2,1)}, bf16[192,2048]{1,0:T(8,128)(2,1)}, u32[]{:S(2)}, u32[]{:S(2)}) collective-permute-start(bf16[192,2048]{1,0:T(8,128)(2,1)} %param.27), channel_id=1, source_target_pairs={{0,4},{2,6},{4,0},{6,2},{8,12},{10,14},{12,8},{14,10},{16,20},{18,... | collective-permute-start | bytes 2359304 | tf_op jit(solution)/shard_map/ppermute | solution.py:25
  98.6 45.6 %collective-permute-start.14 = (bf16[192,2048]{1,0:T(8,128)(2,1)}, bf16[192,2048]{1,0:T(8,128)(2,1)}, u32[]{:S(2)}, u32[]{:S(2)}) collective-permute-start(bf16[192,2048]{1,0:T(8,128)(2,1)} %param.27), channel_id=1, source_target_pairs={{0,1},{1,0},{2,3},{3,2},{4,5},{5,4},{6,7},{7,6},{8,9},{9,8},{10,11... | collective-permute-start | bytes 2359304 | tf_op jit(solution)/shard_map/ppermute | solution.py:37
  114.6 29.5 %collective-permute-start.13 = (bf16[1536,128]{1,0:T(8,128)(2,1)S(1)}, bf16[1536,128]{1,0:T(8,128)(2,1)S(1)}, u32[]{:S(2)}, u32[]{:S(2)}) collective-permute-start(bf16[1536,128]{1,0:T(8,128)(2,1)S(1)} %get-tuple-element.92), channel_id=1, source_target_pairs={{0,8},{2,10},{4,12},{6,14},{8,16},{10,18},{12,20},{14,22},{16,24},... | collective-permute-start | bytes 1179656 | tf_op jit(solution)/shard_map/ppermute | solution.py:59
  118.2 50.2 %collective-permute-start.26 = (bf16[192,2048]{1,0:T(8,128)(2,1)}, bf16[192,2048]{1,0:T(8,128)(2,1)}, u32[]{:S(2)}, u32[]{:S(2)}) collective-permute-start(bf16[192,2048]{1,0:T(8,128)(2,1)} %param.27), channel_id=1, source_target_pairs={{0,2},{2,0},{4,6},{6,4},{8,10},{10,8},{12,14},{14,12},{16,18},{18,... | collective-permute-start | bytes 2359304 | tf_op jit(solution)/shard_map/ppermute | solution.py:25
  118.3 25.7 %collective-permute-start.12 = (bf16[768,128]{1,0:T(8,128)(2,1)S(1)}, bf16[768,128]{1,0:T(8,128)(2,1)S(1)}, u32[]{:S(2)}, u32[]{:S(2)}) collective-permute-start(bf16[768,128]{1,0:T(8,128)(2,1)S(1)} %slice.323), channel_id=1, source_target_pairs={{0,16},{2,18},{4,20},{6,22},{8,24},{10,26},{12,28},{14,30},{1,17},... | collective-permute-start | bytes 589832 | tf_op jit(solution)/shard_map/ppermute | solution.py:59
  124.9 45.6 %all-to-all-start.2 = ((bf16[4,128,1536]{2,1,0:T(8,128)(2,1)}), bf16[4,128,1536]{2,1,0:T(8,128)(2,1)}, u32[]{:S(2)}, u32[]{:S(2)}) async-start(bf16[4,128,1536]{2,1,0:T(8,128)(2,1)} %get-tuple-element.97), calls=%async_computation.2 | async-start | bytes 3145728 | tf_op jit(solution)/shard_map/all_to_all | solution.py:135
  129.2 205.9 %all-gather.6.cloned.1.call-start = ((), (), s32[]{:S(2)}) async-start(), calls=%async_computation.10 | async-start | bytes 7864320 | tf_op jit(solution)/shard_map/all_gather | solution.py:50
  145.2 29.9 %collective-permute-start.27 = (bf16[192,2048]{1,0:T(8,128)(2,1)}, bf16[192,2048]{1,0:T(8,128)(2,1)}, u32[]{:S(2)}, u32[]{:S(2)}) collective-permute-start(bf16[192,2048]{1,0:T(8,128)(2,1)} %collective-permute-done.14), channel_id=1, source_target_pairs={{0,2},{2,0},{4,6},{6,4},{8,10},{10,8},{12,14},{14,12},{16,18},{18,... | collective-permute-start | bytes 2359304 | tf_op jit(solution)/shard_map/ppermute | solution.py:25
  146.3 31.5 %collective-permute-start.28 = (bf16[192,2048]{1,0:T(8,128)(2,1)}, bf16[192,2048]{1,0:T(8,128)(2,1)}, u32[]{:S(2)}, u32[]{:S(2)}) collective-permute-start(bf16[192,2048]{1,0:T(8,128)(2,1)} %collective-permute-done.15), channel_id=1, source_target_pairs={{0,2},{2,0},{4,6},{6,4},{8,10},{10,8},{12,14},{14,12},{16,18},{18,... | collective-permute-start | bytes 2359304 | tf_op jit(solution)/shard_map/ppermute | solution.py:25
  146.9 19.9 %collective-permute-start.24 = (bf16[96,2048]{1,0:T(8,128)(2,1)S(1)}, bf16[96,2048]{1,0:T(8,128)(2,1)S(1)}, u32[]{:S(2)}, u32[]{:S(2)}) collective-permute-start(bf16[96,2048]{1,0:T(8,128)(2,1)S(1)} %slice.340), channel_id=1, source_target_pairs={{0,1},{1,0},{2,3},{3,2},{4,5},{5,4},{6,7},{7,6},{8,9},{9,8},{10,11... | collective-permute-start | bytes 1179656 | tf_op jit(solution)/shard_map/ppermute | solution.py:37
  148.4 18.4 %collective-permute-start.25 = (bf16[96,2048]{1,0:T(8,128)(2,1)S(1)}, bf16[96,2048]{1,0:T(8,128)(2,1)S(1)}, u32[]{:S(2)}, u32[]{:S(2)}) collective-permute-start(bf16[96,2048]{1,0:T(8,128)(2,1)S(1)} %slice.341), channel_id=1, source_target_pairs={{0,4},{2,6},{4,0},{6,2},{8,12},{10,14},{12,8},{14,10},{16,20},{18,... | collective-permute-start | bytes 1179656 | tf_op jit(solution)/shard_map/ppermute | solution.py:25
  175.1 370.9 %reduce-scatter.4.cloned.1.call-start = ((), (), s32[]{:S(2)}) async-start(), calls=%async_computation.12 | async-start | bytes 7864320 | tf_op jit(solution)/shard_map/reduce_scatter | solution.py:54
  185.9 12.0 %collective-permute-start.21 = (bf16[96,2048]{1,0:T(8,128)(2,1)S(1)}, bf16[96,2048]{1,0:T(8,128)(2,1)S(1)}, u32[]{:S(2)}, u32[]{:S(2)}) collective-permute-start(bf16[96,2048]{1,0:T(8,128)(2,1)S(1)} %slice.437), channel_id=1, source_target_pairs={{0,1},{1,0},{2,3},{3,2},{4,5},{5,4},{6,7},{7,6},{8,9},{9,8},{10,11... | collective-permute-start | bytes 1179656 | tf_op jit(solution)/shard_map/ppermute | solution.py:37
  186.5 12.0 %collective-permute-start.23 = (bf16[96,2048]{1,0:T(8,128)(2,1)S(1)}, bf16[96,2048]{1,0:T(8,128)(2,1)S(1)}, u32[]{:S(2)}, u32[]{:S(2)}) collective-permute-start(bf16[96,2048]{1,0:T(8,128)(2,1)S(1)} %slice.440), channel_id=1, source_target_pairs={{0,4},{2,6},{4,0},{6,2},{8,12},{10,14},{12,8},{14,10},{16,20},{18,... | collective-permute-start | bytes 1179656 | tf_op jit(solution)/shard_map/ppermute | solution.py:25
  186.9 18.8 %collective-permute-start.19 = (bf16[96,2048]{1,0:T(8,128)(2,1)S(1)}, bf16[96,2048]{1,0:T(8,128)(2,1)S(1)}, u32[]{:S(2)}, u32[]{:S(2)}) collective-permute-start(bf16[96,2048]{1,0:T(8,128)(2,1)S(1)} %get-tuple-element.259), channel_id=1, source_target_pairs={{0,4},{2,6},{4,0},{6,2},{8,12},{10,14},{12,8},{14,10},{16,20},{18,... | collective-permute-start | bytes 1179656 | tf_op jit(solution)/shard_map/ppermute | solution.py:25
  188.5 17.2 %collective-permute-start.18 = (bf16[96,2048]{1,0:T(8,128)(2,1)S(1)}, bf16[96,2048]{1,0:T(8,128)(2,1)S(1)}, u32[]{:S(2)}, u32[]{:S(2)}) collective-permute-start(bf16[96,2048]{1,0:T(8,128)(2,1)S(1)} %get-tuple-element.260), channel_id=1, source_target_pairs={{0,1},{1,0},{2,3},{3,2},{4,5},{5,4},{6,7},{7,6},{8,9},{9,8},{10,11... | collective-permute-start | bytes 1179656 | tf_op jit(solution)/shard_map/ppermute | solution.py:37
  218.8 17.4 %collective-permute-start.34 = (bf16[192,2048]{1,0:T(8,128)(2,1)S(1)}, bf16[192,2048]{1,0:T(8,128)(2,1)S(1)}, u32[]{:S(2)}, u32[]{:S(2)}) collective-permute-start(bf16[192,2048]{1,0:T(8,128)(2,1)S(1)} %get-tuple-element.202), channel_id=1, source_target_pairs={{0,4},{2,6},{4,0},{6,2},{8,12},{10,14},{12,8},{14,10},{16,20},{18,... | collective-permute-start | bytes 2359304 | tf_op jit(solution)/shard_map/ppermute | solution.py:25
  220.5 18.2 %collective-permute-start.33 = (bf16[192,2048]{1,0:T(8,128)(2,1)S(1)}, bf16[192,2048]{1,0:T(8,128)(2,1)S(1)}, u32[]{:S(2)}, u32[]{:S(2)}) collective-permute-start(bf16[192,2048]{1,0:T(8,128)(2,1)S(1)} %get-tuple-element.202), channel_id=1, source_target_pairs={{0,1},{1,0},{2,3},{3,2},{4,5},{5,4},{6,7},{7,6},{8,9},{9,8},{10,11... | collective-permute-start | bytes 2359304 | tf_op jit(solution)/shard_map/ppermute | solution.py:37
  221.9 26.0 %collective-permute-start.37 = (bf16[192,2048]{1,0:T(8,128)(2,1)S(1)}, bf16[192,2048]{1,0:T(8,128)(2,1)S(1)}, u32[]{:S(2)}, u32[]{:S(2)}) collective-permute-start(bf16[192,2048]{1,0:T(8,128)(2,1)S(1)} %get-tuple-element.202), channel_id=1, source_target_pairs={{0,2},{2,0},{4,6},{6,4},{8,10},{10,8},{12,14},{14,12},{16,18},{18,... | collective-permute-start | bytes 2359304 | tf_op jit(solution)/shard_map/ppermute | solution.py:25
  291.0 299.3 %reduce-scatter.6.cloned.1.call-start = ((), (), s32[]{:S(2)}) async-start(), calls=%async_computation.13 | async-start | bytes 7864320 | tf_op jit(solution)/shard_map/reduce_scatter | solution.py:54
  364.8 14.6 %collective-permute-start.48 = (bf16[192,2048]{1,0:T(8,128)(2,1)}, bf16[192,2048]{1,0:T(8,128)(2,1)}, u32[]{:S(2)}, u32[]{:S(2)}) collective-permute-start(bf16[192,2048]{1,0:T(8,128)(2,1)} %get-tuple-element.227), channel_id=1, source_target_pairs={{0,2},{2,0},{4,6},{6,4},{8,10},{10,8},{12,14},{14,12},{16,18},{18,... | collective-permute-start | bytes 2359304 | tf_op jit(solution)/shard_map/ppermute | solution.py:25
  364.9 14.6 %collective-permute-start.46 = (bf16[192,2048]{1,0:T(8,128)(2,1)}, bf16[192,2048]{1,0:T(8,128)(2,1)}, u32[]{:S(2)}, u32[]{:S(2)}) collective-permute-start(bf16[192,2048]{1,0:T(8,128)(2,1)} %get-tuple-element.228), channel_id=1, source_target_pairs={{0,2},{2,0},{4,6},{6,4},{8,10},{10,8},{12,14},{14,12},{16,18},{18,... | collective-permute-start | bytes 2359304 | tf_op jit(solution)/shard_map/ppermute | solution.py:25
  365.3 14.1 %collective-permute-start.43 = (bf16[192,2048]{1,0:T(8,128)(2,1)}, bf16[192,2048]{1,0:T(8,128)(2,1)}, u32[]{:S(2)}, u32[]{:S(2)}) collective-permute-start(bf16[192,2048]{1,0:T(8,128)(2,1)} %get-tuple-element.229), channel_id=1, source_target_pairs={{0,2},{2,0},{4,6},{6,4},{8,10},{10,8},{12,14},{14,12},{16,18},{18,... | collective-permute-start | bytes 2359304 | tf_op jit(solution)/shard_map/ppermute | solution.py:25
  365.4 14.1 %collective-permute-start.42 = (bf16[192,2048]{1,0:T(8,128)(2,1)}, bf16[192,2048]{1,0:T(8,128)(2,1)}, u32[]{:S(2)}, u32[]{:S(2)}) collective-permute-start(bf16[192,2048]{1,0:T(8,128)(2,1)} %get-tuple-element.230), channel_id=1, source_target_pairs={{0,2},{2,0},{4,6},{6,4},{8,10},{10,8},{12,14},{14,12},{16,18},{18,... | collective-permute-start | bytes 2359304 | tf_op jit(solution)/shard_map/ppermute | solution.py:25
  384.8 12.0 %collective-permute-start.47 = (bf16[96,2048]{1,0:T(8,128)(2,1)S(1)}, bf16[96,2048]{1,0:T(8,128)(2,1)S(1)}, u32[]{:S(2)}, u32[]{:S(2)}) collective-permute-start(bf16[96,2048]{1,0:T(8,128)(2,1)S(1)} %slice.449), channel_id=1, source_target_pairs={{0,1},{1,0},{2,3},{3,2},{4,5},{5,4},{6,7},{7,6},{8,9},{9,8},{10,11... | collective-permute-start | bytes 1179656 | tf_op jit(solution)/shard_map/ppermute | solution.py:37
  386.3 12.0 %collective-permute-start.49 = (bf16[96,2048]{1,0:T(8,128)(2,1)S(1)}, bf16[96,2048]{1,0:T(8,128)(2,1)S(1)}, u32[]{:S(2)}, u32[]{:S(2)}) collective-permute-start(bf16[96,2048]{1,0:T(8,128)(2,1)S(1)} %slice.450), channel_id=1, source_target_pairs={{0,4},{2,6},{4,0},{6,2},{8,12},{10,14},{12,8},{14,10},{16,20},{18,... | collective-permute-start | bytes 1179656 | tf_op jit(solution)/shard_map/ppermute | solution.py:25
  387.9 17.7 %collective-permute-start.45 = (bf16[96,2048]{1,0:T(8,128)(2,1)S(1)}, bf16[96,2048]{1,0:T(8,128)(2,1)S(1)}, u32[]{:S(2)}, u32[]{:S(2)}) collective-permute-start(bf16[96,2048]{1,0:T(8,128)(2,1)S(1)} %get-tuple-element.257), channel_id=1, source_target_pairs={{0,4},{2,6},{4,0},{6,2},{8,12},{10,14},{12,8},{14,10},{16,20},{18,... | collective-permute-start | bytes 1179656 | tf_op jit(solution)/shard_map/ppermute | solution.py:25
  388.5 17.1 %collective-permute-start.44 = (bf16[96,2048]{1,0:T(8,128)(2,1)S(1)}, bf16[96,2048]{1,0:T(8,128)(2,1)S(1)}, u32[]{:S(2)}, u32[]{:S(2)}) collective-permute-start(bf16[96,2048]{1,0:T(8,128)(2,1)S(1)} %get-tuple-element.258), channel_id=1, source_target_pairs={{0,1},{1,0},{2,3},{3,2},{4,5},{5,4},{6,7},{7,6},{8,9},{9,8},{10,11... | collective-permute-start | bytes 1179656 | tf_op jit(solution)/shard_map/ppermute | solution.py:37
  424.4 17.2 %collective-permute-start.53 = (bf16[192,2048]{1,0:T(8,128)(2,1)S(1)}, bf16[192,2048]{1,0:T(8,128)(2,1)S(1)}, u32[]{:S(2)}, u32[]{:S(2)}) collective-permute-start(bf16[192,2048]{1,0:T(8,128)(2,1)S(1)} %get-tuple-element.199), channel_id=1, source_target_pairs={{0,4},{2,6},{4,0},{6,2},{8,12},{10,14},{12,8},{14,10},{16,20},{18,... | collective-permute-start | bytes 2359304 | tf_op jit(solution)/shard_map/ppermute | solution.py:25
  425.0 16.9 %collective-permute-start.52 = (bf16[192,2048]{1,0:T(8,128)(2,1)S(1)}, bf16[192,2048]{1,0:T(8,128)(2,1)S(1)}, u32[]{:S(2)}, u32[]{:S(2)}) collective-permute-start(bf16[192,2048]{1,0:T(8,128)(2,1)S(1)} %get-tuple-element.199), channel_id=1, source_target_pairs={{0,1},{1,0},{2,3},{3,2},{4,5},{5,4},{6,7},{7,6},{8,9},{9,8},{10,11... | collective-permute-start | bytes 2359304 | tf_op jit(solution)/shard_map/ppermute | solution.py:37
  432.5 21.9 %collective-permute-start.56 = (bf16[192,2048]{1,0:T(8,128)(2,1)S(1)}, bf16[192,2048]{1,0:T(8,128)(2,1)S(1)}, u32[]{:S(2)}, u32[]{:S(2)}) collective-permute-start(bf16[192,2048]{1,0:T(8,128)(2,1)S(1)} %get-tuple-element.199), channel_id=1, source_target_pairs={{0,2},{2,0},{4,6},{6,4},{8,10},{10,8},{12,14},{14,12},{16,18},{18,... | collective-permute-start | bytes 2359304 | tf_op jit(solution)/shard_map/ppermute | solution.py:25
  441.9 12.8 %collective-permute-start.57 = (bf16[192,2048]{1,0:T(8,128)(2,1)S(1)}, bf16[192,2048]{1,0:T(8,128)(2,1)S(1)}, u32[]{:S(2)}, u32[]{:S(2)}) collective-permute-start(bf16[192,2048]{1,0:T(8,128)(2,1)S(1)} %collective-permute-done.52), channel_id=1, source_target_pairs={{0,2},{2,0},{4,6},{6,4},{8,10},{10,8},{12,14},{14,12},{16,18},{18,... | collective-permute-start | bytes 2359304 | tf_op jit(solution)/shard_map/ppermute | solution.py:25
  442.1 13.1 %collective-permute-start.58 = (bf16[192,2048]{1,0:T(8,128)(2,1)S(1)}, bf16[192,2048]{1,0:T(8,128)(2,1)S(1)}, u32[]{:S(2)}, u32[]{:S(2)}) collective-permute-start(bf16[192,2048]{1,0:T(8,128)(2,1)S(1)} %collective-permute-done.53), channel_id=1, source_target_pairs={{0,2},{2,0},{4,6},{6,4},{8,10},{10,8},{12,14},{14,12},{16,18},{18,... | collective-permute-start | bytes 2359304 | tf_op jit(solution)/shard_map/ppermute | solution.py:25
  442.6 11.1 %collective-permute-start.54 = (bf16[96,2048]{1,0:T(8,128)(2,1)S(1)}, bf16[96,2048]{1,0:T(8,128)(2,1)S(1)}, u32[]{:S(2)}, u32[]{:S(2)}) collective-permute-start(bf16[96,2048]{1,0:T(8,128)(2,1)S(1)} %slice.369), channel_id=1, source_target_pairs={{0,1},{1,0},{2,3},{3,2},{4,5},{5,4},{6,7},{7,6},{8,9},{9,8},{10,11... | collective-permute-start | bytes 1179656 | tf_op jit(solution)/shard_map/ppermute | solution.py:37
  453.7 11.7 %collective-permute-start.64 = (bf16[192,2048]{1,0:T(8,128)(2,1)S(1)}, bf16[192,2048]{1,0:T(8,128)(2,1)S(1)}, u32[]{:S(2)}, u32[]{:S(2)}) collective-permute-start(bf16[192,2048]{1,0:T(8,128)(2,1)S(1)} %get-tuple-element.219), channel_id=1, source_target_pairs={{0,2},{2,0},{4,6},{6,4},{8,10},{10,8},{12,14},{14,12},{16,18},{18,... | collective-permute-start | bytes 2359304 | tf_op jit(solution)/shard_map/ppermute | solution.py:25
  454.1 11.3 %collective-permute-start.63 = (bf16[192,2048]{1,0:T(8,128)(2,1)S(1)}, bf16[192,2048]{1,0:T(8,128)(2,1)S(1)}, u32[]{:S(2)}, u32[]{:S(2)}) collective-permute-start(bf16[192,2048]{1,0:T(8,128)(2,1)S(1)} %get-tuple-element.220), channel_id=1, source_target_pairs={{0,2},{2,0},{4,6},{6,4},{8,10},{10,8},{12,14},{14,12},{16,18},{18,... | collective-permute-start | bytes 2359304 | tf_op jit(solution)/shard_map/ppermute | solution.py:25
  454.4 11.0 %collective-permute-start.62 = (bf16[192,2048]{1,0:T(8,128)(2,1)S(1)}, bf16[192,2048]{1,0:T(8,128)(2,1)S(1)}, u32[]{:S(2)}, u32[]{:S(2)}) collective-permute-start(bf16[192,2048]{1,0:T(8,128)(2,1)S(1)} %get-tuple-element.221), channel_id=1, source_target_pairs={{0,2},{2,0},{4,6},{6,4},{8,10},{10,8},{12,14},{14,12},{16,18},{18,... | collective-permute-start | bytes 2359304 | tf_op jit(solution)/shard_map/ppermute | solution.py:25
  494.4 51.5 %collective-permute-start.68 = (bf16[96,2048]{1,0:T(8,128)(2,1)S(1)}, bf16[96,2048]{1,0:T(8,128)(2,1)S(1)}, u32[]{:S(2)}, u32[]{:S(2)}) collective-permute-start(bf16[96,2048]{1,0:T(8,128)(2,1)S(1)} %slice.383), channel_id=1, source_target_pairs={{0,4},{2,6},{4,0},{6,2},{8,12},{10,14},{12,8},{14,10},{16,20},{18,... | collective-permute-start | bytes 1179656 | tf_op jit(solution)/shard_map/ppermute | solution.py:25
  495.9 50.0 %collective-permute-start.67 = (bf16[96,2048]{1,0:T(8,128)(2,1)S(1)}, bf16[96,2048]{1,0:T(8,128)(2,1)}, u32[]{:S(2)}, u32[]{:S(2)}) collective-permute-start(bf16[96,2048]{1,0:T(8,128)(2,1)S(1)} %slice.382), channel_id=1, source_target_pairs={{0,1},{1,0},{2,3},{3,2},{4,5},{5,4},{6,7},{7,6},{8,9},{9,8},{10,11... | collective-permute-start | bytes 1179656 | tf_op jit(solution)/shard_map/ppermute | solution.py:37
  496.6 27.2 %collective-permute-start.72 = (bf16[768,128]{1,0:T(8,128)(2,1)S(1)}, bf16[768,128]{1,0:T(8,128)(2,1)S(1)}, u32[]{:S(2)}, u32[]{:S(2)}) collective-permute-start(bf16[768,128]{1,0:T(8,128)(2,1)S(1)} %slice.458), channel_id=1, source_target_pairs={{16,0},{18,2},{20,4},{22,6},{24,8},{26,10},{28,12},{30,14},{17,1},... | collective-permute-start | bytes 589832 | tf_op jit(solution)/shard_map/ppermute | solution.py:59
  497.9 46.8 %collective-permute-start.71 = (bf16[1536,128]{1,0:T(8,128)(2,1)S(1)}, bf16[1536,128]{1,0:T(8,128)(2,1)S(1)}, u32[]{:S(2)}, u32[]{:S(2)}) collective-permute-start(bf16[1536,128]{1,0:T(8,128)(2,1)S(1)} %slice.457), channel_id=1, source_target_pairs={{8,0},{10,2},{12,4},{14,6},{16,8},{18,10},{20,12},{22,14},{24,16},... | collective-permute-start | bytes 1179656 | tf_op jit(solution)/shard_map/ppermute | solution.py:59
  500.6 45.4 %collective-permute-start.66 = (bf16[96,2048]{1,0:T(8,128)(2,1)S(1)}, bf16[96,2048]{1,0:T(8,128)(2,1)}, u32[]{:S(2)}, u32[]{:S(2)}) collective-permute-start(bf16[96,2048]{1,0:T(8,128)(2,1)S(1)} %get-tuple-element.255), channel_id=1, source_target_pairs={{0,4},{2,6},{4,0},{6,2},{8,12},{10,14},{12,8},{14,10},{16,20},{18,... | collective-permute-start | bytes 1179656 | tf_op jit(solution)/shard_map/ppermute | solution.py:25
  523.8 22.2 %collective-permute-start.65 = (bf16[96,2048]{1,0:T(8,128)(2,1)S(1)}, bf16[96,2048]{1,0:T(8,128)(2,1)}, u32[]{:S(2)}, u32[]{:S(2)}) collective-permute-start(bf16[96,2048]{1,0:T(8,128)(2,1)S(1)} %get-tuple-element.256), channel_id=1, source_target_pairs={{0,1},{1,0},{2,3},{3,2},{4,5},{5,4},{6,7},{7,6},{8,9},{9,8},{10,11... | collective-permute-start | bytes 1179656 | tf_op jit(solution)/shard_map/ppermute | solution.py:37
  546.0 44.3 %all-to-all-start.4 = ((bf16[4,128,1536]{2,1,0:T(8,128)(2,1)}), bf16[4,128,1536]{2,1,0:T(8,128)(2,1)}, u32[]{:S(2)}, u32[]{:S(2)}) async-start(bf16[4,128,1536]{2,1,0:T(8,128)(2,1)} %bitcast.52), calls=%async_computation.6 | async-start | bytes 3145728 | tf_op jit(solution)/shard_map/all_to_all | solution.py:135
  550.4 129.9 %reduce-scatter.8.cloned.1.call-start = ((), (), s32[]{:S(2)}) async-start(), calls=%async_computation.14 | async-start | bytes 3276800 | tf_op jit(solution)/shard_map/reduce_scatter | solution.py:54
  552.5 32.2 %collective-permute-start.69 = (bf16[96,2048]{1,0:T(8,128)(2,1)}, bf16[96,2048]{1,0:T(8,128)(2,1)}, u32[]{:S(2)}, u32[]{:S(2)}) collective-permute-start(bf16[96,2048]{1,0:T(8,128)(2,1)} %add_convert_fusion.21), channel_id=1, source_target_pairs={{0,4},{2,6},{4,0},{6,2},{8,12},{10,14},{12,8},{14,10},{16,20},{18,... | collective-permute-start | bytes 1179656 | tf_op jit(solution)/shard_map/ppermute | solution.py:25
  556.4 34.5 %collective-permute-start.70 = (bf16[96,2048]{1,0:T(8,128)(2,1)}, bf16[96,2048]{1,0:T(8,128)(2,1)}, u32[]{:S(2)}, u32[]{:S(2)}) collective-permute-start(bf16[96,2048]{1,0:T(8,128)(2,1)} %add_convert_fusion.20), channel_id=1, source_target_pairs={{0,1},{1,0},{2,3},{3,2},{4,5},{5,4},{6,7},{7,6},{8,9},{9,8},{10,11... | collective-permute-start | bytes 1179656 | tf_op jit(solution)/shard_map/ppermute | solution.py:37
  574.8 23.4 %collective-permute-start.79 = (bf16[192,2048]{1,0:T(8,128)(2,1)}, bf16[192,2048]{1,0:T(8,128)(2,1)S(1)}, u32[]{:S(2)}, u32[]{:S(2)}) collective-permute-start(bf16[192,2048]{1,0:T(8,128)(2,1)} %get-tuple-element.211), channel_id=1, source_target_pairs={{0,2},{2,0},{4,6},{6,4},{8,10},{10,8},{12,14},{14,12},{16,18},{18,... | collective-permute-start | bytes 2359304 | tf_op jit(solution)/shard_map/ppermute | solution.py:25
  574.8 23.4 %collective-permute-start.77 = (bf16[192,2048]{1,0:T(8,128)(2,1)}, bf16[192,2048]{1,0:T(8,128)(2,1)}, u32[]{:S(2)}, u32[]{:S(2)}) collective-permute-start(bf16[192,2048]{1,0:T(8,128)(2,1)} %get-tuple-element.212), channel_id=1, source_target_pairs={{0,2},{2,0},{4,6},{6,4},{8,10},{10,8},{12,14},{14,12},{16,18},{18,... | collective-permute-start | bytes 2359304 | tf_op jit(solution)/shard_map/ppermute | solution.py:25
  575.3 22.9 %collective-permute-start.74 = (bf16[192,2048]{1,0:T(8,128)(2,1)}, bf16[192,2048]{1,0:T(8,128)(2,1)}, u32[]{:S(2)}, u32[]{:S(2)}) collective-permute-start(bf16[192,2048]{1,0:T(8,128)(2,1)} %get-tuple-element.213), channel_id=1, source_target_pairs={{0,2},{2,0},{4,6},{6,4},{8,10},{10,8},{12,14},{14,12},{16,18},{18,... | collective-permute-start | bytes 2359304 | tf_op jit(solution)/shard_map/ppermute | solution.py:25
  584.7 14.4 %collective-permute-start.73 = (bf16[192,2048]{1,0:T(8,128)(2,1)}, bf16[192,2048]{1,0:T(8,128)(2,1)}, u32[]{:S(2)}, u32[]{:S(2)}) collective-permute-start(bf16[192,2048]{1,0:T(8,128)(2,1)} %get-tuple-element.214), channel_id=1, source_target_pairs={{0,2},{2,0},{4,6},{6,4},{8,10},{10,8},{12,14},{14,12},{16,18},{18,... | collective-permute-start | bytes 2359304 | tf_op jit(solution)/shard_map/ppermute | solution.py:25
  594.4 41.5 %all-to-all-start.3 = ((bf16[4,128,1536]{2,1,0:T(8,128)(2,1)}), bf16[4,128,1536]{2,1,0:T(8,128)(2,1)S(1)}, u32[]{:S(2)}, u32[]{:S(2)}) async-start(bf16[4,128,1536]{2,1,0:T(8,128)(2,1)} %bitcast.5), calls=%async_computation.5 | async-start | bytes 3145728 | tf_op jit(solution)/shard_map/all_to_all | solution.py:135
  603.3 12.0 %collective-permute-start.78 = (bf16[96,2048]{1,0:T(8,128)(2,1)S(1)}, bf16[96,2048]{1,0:T(8,128)(2,1)S(1)}, u32[]{:S(2)}, u32[]{:S(2)}) collective-permute-start(bf16[96,2048]{1,0:T(8,128)(2,1)S(1)} %slice.468), channel_id=1, source_target_pairs={{0,1},{1,0},{2,3},{3,2},{4,5},{5,4},{6,7},{7,6},{8,9},{9,8},{10,11... | collective-permute-start | bytes 1179656 | tf_op jit(solution)/shard_map/ppermute | solution.py:37
  604.0 23.1 %collective-permute-start.80 = (bf16[96,2048]{1,0:T(8,128)(2,1)S(1)}, bf16[96,2048]{1,0:T(8,128)(2,1)S(1)}, u32[]{:S(2)}, u32[]{:S(2)}) collective-permute-start(bf16[96,2048]{1,0:T(8,128)(2,1)S(1)} %slice.471), channel_id=1, source_target_pairs={{0,4},{2,6},{4,0},{6,2},{8,12},{10,14},{12,8},{14,10},{16,20},{18,... | collective-permute-start | bytes 1179656 | tf_op jit(solution)/shard_map/ppermute | solution.py:25
  606.1 29.0 %collective-permute-start.76 = (bf16[96,2048]{1,0:T(8,128)(2,1)S(1)}, bf16[96,2048]{1,0:T(8,128)(2,1)S(1)}, u32[]{:S(2)}, u32[]{:S(2)}) collective-permute-start(bf16[96,2048]{1,0:T(8,128)(2,1)S(1)} %get-tuple-element.253), channel_id=1, source_target_pairs={{0,4},{2,6},{4,0},{6,2},{8,12},{10,14},{12,8},{14,10},{16,20},{18,... | collective-permute-start | bytes 1179656 | tf_op jit(solution)/shard_map/ppermute | solution.py:25
  606.2 29.7 %collective-permute-start.75 = (bf16[96,2048]{1,0:T(8,128)(2,1)S(1)}, bf16[96,2048]{1,0:T(8,128)(2,1)}, u32[]{:S(2)}, u32[]{:S(2)}) collective-permute-start(bf16[96,2048]{1,0:T(8,128)(2,1)S(1)} %get-tuple-element.254), channel_id=1, source_target_pairs={{0,1},{1,0},{2,3},{3,2},{4,5},{5,4},{6,7},{7,6},{8,9},{9,8},{10,11... | collective-permute-start | bytes 1179656 | tf_op jit(solution)/shard_map/ppermute | solution.py:37
  667.6 11.7 %collective-permute-start.86 = (f32[4224]{0:T(1024)S(1)}, f32[4224]{0:T(1024)S(1)}, u32[]{:S(2)}, u32[]{:S(2)}) collective-permute-start(f32[4224]{0:T(1024)S(1)} %add.277), channel_id=1, source_target_pairs={{0,8},{2,10},{4,12},{6,14},{8,0},{10,2},{12,4},{14,6},{16,24},{18,... | collective-permute-start | bytes 50696 | tf_op jit(solution)/shard_map/ppermute | solution.py:25
  682.5 13.7 %all-to-all-start.5 = ((bf16[4,128,640]{1,2,0:T(8,128)(2,1)}), bf16[4,128,640]{1,2,0:T(8,128)(2,1)S(1)}, u32[]{:S(2)}, u32[]{:S(2)}) async-start(bf16[4,128,640]{1,2,0:T(8,128)(2,1)} %copy.56), calls=%async_computation.8 | async-start | bytes 1310720 | tf_op jit(solution)/shard_map/all_to_all | solution.py:135
  (110 other events, 785.5 us)
Sparse Core Ops, SparseCore 0:
  29.7 55.2 all-gather.3
  88.7 123.0 all-gather.7
  213.4 121.7 all-gather.5
  337.3 108.9 reduce-scatter.3
  448.5 123.8 reduce-scatter.5
  590.5 57.7 reduce-scatter.7

commit v3 on v2

v3 whole, which is shorter than its diff:
```python
import functools
import math

import jax
import jax.numpy as jnp
from jax import lax
from jax.experimental import pallas as pl
from jax.experimental.pallas import tpu as pltpu
from jax.sharding import PartitionSpec as P

WB = 6
EPSILON = 1e-05
ROPE_BASE = 1000000.0
LOG2E = math.log2(math.e)

QUAD = 4
KEY_BLOCK = 384
FIRST_BLOCK = 4

F32 = jnp.float32
BF16 = jnp.bfloat16


def swap_ctx(value, bit):
    n = lax.axis_size("ctx")
    return lax.ppermute(value, "ctx", [(i, i ^ bit) for i in range(n)])


def swap_core(value):
    return swap_ctx(value, 1)


def swap_b(value):
    return swap_ctx(value, 2)


def swap_x(value):
    return lax.ppermute(value, "tp", [(0, 1), (1, 0)])


def line_move(value, by, sources):
    pairs = [(s * QUAD + q, (s + by) * QUAD + q) for s in sources for q in range(QUAD)]
    return lax.ppermute(value, "ctx", pairs)


def line_groups(n):
    return [[p * QUAD + q for p in range(n)] for q in range(QUAD)]


def line_gather(own, n):
    return lax.all_gather(own, "ctx", axis=0, axis_index_groups=line_groups(n), tiled=True)


def line_scatter(partial, n):
    return lax.psum_scatter(partial, "ctx", scatter_dimension=0, axis_index_groups=line_groups(n), tiled=True)


def line_move(value, by, sources):
    pairs = [(s * QUAD + q, (s + by) * QUAD + q) for s in sources for q in range(QUAD)]
    return lax.ppermute(value, "ctx", pairs)


def tie(*values):
    return lax.optimization_barrier(values)


def add16(a, b):
    return (a.astype(F32) + b.astype(F32)).astype(BF16)


def swap_both(value):
    n = lax.axis_size("ctx")
    return lax.ppermute(value, ("ctx", "tp"), [(2 * i + x, 2 * (i ^ 2) + 1 - x) for i in range(n) for x in range(2)])


class Rows:
    def __init__(self, own):
        self.own, self.half = own, own.shape[0] // 2
        self.first = (swap_x(own), swap_b(own))

    def second(self):
        from_x, from_b = self.first
        self.last = (swap_x(from_b[: self.half]), swap_b(from_x[self.half :]))

    def third(self):
        near = [self.own, *self.first, *self.last]
        return near + [swap_core(piece) for piece in near]


def gather_rows(own, beside=None):
    rows = Rows(own)
    if beside is not None:
        rows.first, beside = tie(rows.first, beside)
    rows.second()
    return rows.third() if beside is None else (rows.third(), beside)


class Sums:
    def __init__(self, near, far):
        r = near.shape[0] // 4
        self.half = r // 2

        def fold(block):
            return add16(near[block * r : (block + 1) * r], swap_core(far[block]))

        self.parts = (fold(3), fold(1), fold(2), fold(0))

    def second(self):
        both, for_x, for_b, _ = self.parts
        half = self.half
        self.got = (swap_x(both[:half]), swap_b(both[half:]), swap_x(for_x[:half]), swap_b(for_b[half:]))

    def third(self):
        _, for_x, for_b, own = self.parts
        top, bottom, x_top, b_bottom = self.got
        half = self.half
        x_bottom = swap_x(add16(for_x[half:], bottom))
        b_top = swap_b(add16(for_b[:half], top))
        own = own.astype(F32)
        return jnp.concatenate(
            [
                own[:half] + x_top.astype(F32) + b_top.astype(F32),
                own[half:] + b_bottom.astype(F32) + x_bottom.astype(F32),
            ],
            axis=0,
        )


def scatter_rows(near, far, beside=None):
    sums = Sums(near, far)
    sums.second()
    if beside is not None:
        sums.got, beside = tie(sums.got, beside)
    return sums.third() if beside is None else (sums.third(), beside)


def blocks_of(rows):
    r = rows.shape[0] // 4
    return [rows[k * r : (k + 1) * r] for k in range(4)]


def spread(pieces, axis=0):
    n = lax.axis_size("ctx")
    groups = [list(range(i, i + QUAD)) for i in range(0, n, QUAD)]
    return lax.all_to_all(pieces, "ctx", axis, axis, axis_index_groups=groups, tiled=True)


def sum_over_ctx(value):
    bit = 1
    while bit < lax.axis_size("ctx"):
        value = value + swap_ctx(value, bit)
        bit *= 2
    return value


def dot(a, b):
    return jnp.dot(a, b, preferred_element_type=F32)


def dot_nt(a, b):
    return lax.dot_general(a, b, (((1,), (1,)), ((), ())), preferred_element_type=F32)


def dot_tn(a, b):
    return lax.dot_general(a, b, (((0,), (0,)), ((), ())), preferred_element_type=F32)


def rms_scale(values):
    return lax.rsqrt(jnp.mean(values * values, axis=-1, keepdims=True) + EPSILON)


def norm_back(values, scale, gain, grad):
    unit = values * scale
    inner = grad * gain
    d_values = scale * (inner - unit * jnp.mean(inner * unit, axis=-1, keepdims=True))
    return d_values, jnp.sum(grad * unit, axis=0)


def pick(refs, block, out_ref, at):
    r = refs[0].shape[0]
    for k in range(8):
        index = k // 4 * (len(refs) // 2) + k % 4

        @pl.when(block == k)
        def _():
            if k % 4 < 3 or len(refs) == 8:
                out_ref[at : at + r, :] = refs[index][...]
            else:
                out_ref[at : at + r // 2, :] = refs[index][...]
                out_ref[at + r // 2 : at + r, :] = refs[index + 1][...]


class Heads:
    def __init__(self, width, cos, sin):
        self.width, self.cos, self.sin = width, cos, sin
        lanes = 2 * width
        row = lax.broadcasted_iota(jnp.int32, (lanes, lanes), 0)
        col = lax.broadcasted_iota(jnp.int32, (lanes, lanes), 1)
        self.same = jnp.where(row // width == col // width, 1.0 / width, 0.0).astype(BF16)

    def mean(self, u):
        high = u.astype(BF16)
        low = (u - high.astype(F32)).astype(BF16)
        return dot(high, self.same) + dot(low, self.same)

    def swapped(self, u):
        half = self.width // 2
        lane = lax.broadcasted_iota(jnp.int32, u.shape, 1)
        return jnp.where((lane & half) == 0, pltpu.roll(u, 2 * self.width - half, 1), pltpu.roll(u, half, 1))

    def ready(self, u, gain):
        u = u * lax.rsqrt(self.mean(u * u) + EPSILON) * gain
        return u * self.cos + self.swapped(u) * self.sin

    def back(self, w, gain, grad):
        e = grad * self.cos - self.swapped(grad) * self.sin
        scale = lax.rsqrt(self.mean(w * w) + EPSILON)
        unit = w * scale
        inner = e * gain
        return scale * (inner - unit * self.mean(inner * unit)), jnp.sum(e * unit, axis=0, keepdims=True)


def project_kernel(table, *refs, heads, width):
    pieces, (w_ref, cos_ref, sin_ref, q_gain_ref, k_gain_ref, rows_ref, raw_ref, q_ref, kv_ref) = refs[:-9], refs[-9:]
    pick(pieces, pl.program_id(0), rows_ref, 0)
    raw = dot(rows_ref[...], w_ref[...])
    raw_ref[...] = raw
    math_of = Heads(width, cos_ref[...], sin_ref[...])
    lanes = 2 * width
    for c in range(heads // 2):
        cols = slice(c * lanes, (c + 1) * lanes)
        q_ref[:, cols] = math_of.ready(raw[:, cols], q_gain_ref[...]).astype(BF16)
    last = raw[:, heads * width :]
    lane = lax.broadcasted_iota(jnp.int32, last.shape, 1)
    kv_ref[...] = jnp.where(lane < width, math_of.ready(last, k_gain_ref[...]), last).astype(BF16)


def prep_back_kernel(
    table, raw_ref, cos_ref, sin_ref, q_gain_ref, k_gain_ref, dq_ref, dkv_ref, *refs, heads, width, plane
):
    halo, (out_ref, dg_ref) = refs[:-2], refs[-2:]
    t = pl.program_id(0)

    @pl.when(t == 0)
    def _():
        dg_ref[...] = jnp.zeros_like(dg_ref)

    math_of = Heads(width, cos_ref[...], sin_ref[...])
    lanes = 2 * width
    total = jnp.zeros((1, lanes), F32)
    for c in range(heads // 2):
        cols = slice(c * lanes, (c + 1) * lanes)
        dw, dg = math_of.back(raw_ref[:, cols], q_gain_ref[...], dq_ref[:, cols])
        out_ref[:, cols] = dw.astype(BF16)
        total = total + dg
    grad = dkv_ref[...]
    r = grad.shape[0]
    for ref in halo:
        missing = plane // r - ref.shape[0] // r
        at = pl.multiple_of(jnp.maximum(t - missing, 0) * r, r)
        grad = grad + jnp.where(t >= missing, ref[pl.ds(at, r), :].astype(F32), 0.0)
    dw, dg = math_of.back(raw_ref[:, heads * width :], k_gain_ref[...], grad)
    lane = lax.broadcasted_iota(jnp.int32, grad.shape, 1)
    out_ref[:, heads * width :] = jnp.where(lane < width, dw, grad).astype(BF16)
    dg_ref[0:1, :] += total
    dg_ref[1:2, :] += dg


def rows_dot_kernel(*refs):
    pieces, (w_ref, rows_ref, out_ref) = refs[:10], refs[10:]
    pick(pieces, pl.program_id(0), rows_ref, 0)
    out_ref[...] = dot(rows_ref[...], w_ref[...]).astype(BF16)


def stack_heads(block, heads, width):
    return jnp.concatenate([block[:, h * width : (h + 1) * width] for h in range(heads)], axis=0)


def attend_kernel(table, lo, hi, q_ref, start_ref, kv_ref, *refs, heads, width, base, bk, last):
    ones_v = refs[-1]
    if last:
        acc_in, o_ref, of_ref, stat_ref, acc = refs[:5]
    else:
        acc = refs[0]
    t = pl.program_id(0)
    r = q_ref.shape[0]

    @pl.when(t == 0)
    def _():
        lane = lax.broadcasted_iota(jnp.int32, kv_ref.shape, 1)
        ones_v[...] = jnp.where(lane < width, jnp.ones((), BF16), kv_ref[...])

    q = stack_heads(q_ref[...], heads, width)
    q = jnp.concatenate([q, jnp.zeros_like(q)], axis=-1)
    start = jnp.concatenate([start_ref[...]] * heads, axis=0)
    pos = base + t * r + lax.broadcasted_iota(jnp.int32, (r, 1), 0)
    pos = jnp.concatenate([pos] * heads, axis=0)
    acc[...] = acc_in[...] if last else jnp.zeros_like(acc)
    c = LOG2E / math.sqrt(width)

    def step(kb, carry):
        k0 = pl.multiple_of(kb * bk, bk)
        s = dot_nt(q, kv_ref[pl.ds(k0, bk), :])
        key = k0 + lax.broadcasted_iota(jnp.int32, (1, bk), 1)
        p = jnp.where((key >= start) & (key <= pos), jnp.exp2(s * c), 0.0)
        acc[...] += dot(p.astype(BF16), ones_v[pl.ds(k0, bk), :])
        return carry

    lax.fori_loop(lo[t], hi[t], step, 0)
    if last:
        total = acc[:, :1]
        o = acc[:, width:] / total
        stat_ref[...] = jnp.log2(total)
        for h in range(heads):
            part = o[h * r : (h + 1) * r]
            of_ref[:, h * width : (h + 1) * width] = part
            o_ref[:, h * width : (h + 1) * width] = part.astype(BF16)


def attend_back_kernel(
    table, lo, hi, q_ref, do_ref, of_ref, stat_ref, start_ref, kv_ref, *refs, heads, width, base, bk, last
):
    if last:
        acc_in, dq_ref, dkv, acc = refs
    else:
        acc, dkv_refs, dkv = refs[0], refs[1:-1], refs[-1]
    t = pl.program_id(0)
    r = q_ref.shape[0]

    @pl.when(t == 0)
    def _():
        dkv[...] = jnp.zeros_like(dkv)

    scale = 1.0 / math.sqrt(width)
    q = stack_heads(q_ref[...], heads, width)
    do = stack_heads(do_ref[...], heads, width)
    of = stack_heads(of_ref[...], heads, width)
    delta = jnp.sum(do.astype(F32) * of, axis=-1, keepdims=True)
    lane = lax.broadcasted_iota(jnp.int32, (heads * r, 2 * width), 1)
    rows = jnp.transpose(jnp.where(lane == 0, stat_ref[...], delta))
    stat, delta = rows[0:1, :], rows[1:2, :]
    q = jnp.concatenate([q, jnp.zeros_like(q)], axis=-1)
    q_scaled = (q.astype(F32) * scale).astype(BF16)
    do = jnp.concatenate([jnp.zeros_like(do), do], axis=-1)
    start = jnp.concatenate([start_ref[0]] * heads, axis=-1)
    pos = base + t * r + lax.broadcasted_iota(jnp.int32, (1, r), 1)
    pos = jnp.concatenate([pos] * heads, axis=-1)
    acc[...] = acc_in[...] if last else jnp.zeros_like(acc)

    def step(kb, carry):
        k0 = pl.multiple_of(kb * bk, bk)
        kv = kv_ref[pl.ds(k0, bk), :]
        s = dot_nt(kv, q_scaled)
        dp = dot_nt(kv, do)
        key = k0 + lax.broadcasted_iota(jnp.int32, (bk, 1), 0)
        p = jnp.where((key >= start) & (key <= pos), jnp.exp2(s * LOG2E - stat), 0.0)
        ds = (p * (dp - delta)).astype(BF16)
        dkv[pl.ds(k0, bk), :] += dot(ds, q_scaled) + dot(p.astype(BF16), do)
        acc[...] += dot_tn(ds, kv)
        return carry

    lax.fori_loop(lo[t], hi[t], step, 0)
    if last:
        dq = acc[...][:, :width] * scale
        for h in range(heads):
            dq_ref[:, h * width : (h + 1) * width] = dq[h * r : (h + 1) * r]
    else:

        @pl.when(t == pl.num_programs(0) - 1)
        def _():
            at = 0
            for ref in dkv_refs:
                ref[...] = dkv[at : at + ref.shape[0], :].astype(BF16)
                at += ref.shape[0]


def feed_first_kernel(*refs, hb):
    pieces, (c_ref, w_ref, hid_ref, dgu_ref, back_ref, rows_ref) = refs[:10], refs[10:]
    t = pl.program_id(0)
    r = pieces[0].shape[0]
    pick(pieces, 2 * t, rows_ref, 0)
    pick(pieces, 2 * t + 1, rows_ref, r)
    back_ref[...] = feed(rows_ref, c_ref, w_ref, hid_ref, dgu_ref, hb).astype(BF16)


def feed_last_kernel(a_ref, c_ref, w_ref, prev_ref, hid_ref, dgu_ref, near_ref, *far_refs, hb):
    t = pl.program_id(0)
    back = feed(a_ref, c_ref, w_ref, hid_ref, dgu_ref, hb) + prev_ref[...].astype(F32)
    split_store(back, t, near_ref, far_refs)


def feed(a_ref, c_ref, w_ref, hid_ref, dgu_ref, hb):
    a, c = a_ref[...], c_ref[...]
    gate, up = dot(a, w_ref[:, :hb]), dot(a, w_ref[:, hb : 2 * hb])
    d_hid = dot(c, w_ref[:, 2 * hb :])
    sig = jax.nn.sigmoid(gate)
    silu = gate * sig
    hid_ref[...] = (silu * up).astype(BF16)
    dgu_ref[:, :hb] = (d_hid * up * (sig * (1.0 + gate * (1.0 - sig)))).astype(BF16)
    dgu_ref[:, hb:] = (d_hid * silu).astype(BF16)
    return dot_nt(dgu_ref[...], w_ref[:, : 2 * hb])


def down_kernel(h0_ref, h1_ref, w0_ref, w1_ref, near_ref, *far_refs):
    t = pl.program_id(0)
    y = sum(dot_nt(h[...], w[:, 2 * h.shape[1] :]) for h, w in ((h0_ref, w0_ref), (h1_ref, w1_ref)))
    split_store(y, t, near_ref, far_refs)


def split_store(value, t, near_ref, far_refs):
    r = far_refs[0].shape[0]

    @pl.when(t < 2)
    def _():
        near_ref[...] = value.astype(BF16)

    for k, ref in enumerate(far_refs):

        @pl.when(t == 2 + k // 2)
        def _():
            ref[...] = value[k % 2 * r : (k % 2 + 1) * r].astype(BF16)


def split_outs(total, model):
    far = pl.BlockSpec((total // 8, model), lambda t: (0, 0))
    near = pl.BlockSpec((total // 4, model), lambda t: (jnp.minimum(t, 1), 0))
    return [((total // 2, model), BF16, near)] + [((total // 8, model), BF16, far)] * 4


def split_dot_kernel(a_ref, w_ref, near_ref, *far_refs):
    split_store(dot_nt(a_ref[...], w_ref[...]), pl.program_id(0), near_ref, far_refs)


def split_dot(a, w):
    total, cols = a.shape
    model = w.shape[0]
    near, *far = call(
        split_dot_kernel,
        4,
        0,
        [pl.BlockSpec((total // 4, cols), lambda t: (t, 0)), whole_block(w)],
        split_outs(total, model),
        [],
        (a, w),
        2 * total * model * cols,
        2 * total * (model + cols),
    )
    return near, far


def down_rows(h0, h1, w0, w1):
    total, hb = h0.shape[0], (h0.shape[1] + h1.shape[1]) // 2
    model = w0.shape[0]

    def row(h):
        return pl.BlockSpec((total // 4, h.shape[1]), lambda t: (t, 0))

    near, *far = call(
        down_kernel,
        4,
        0,
        [row(h0), row(h1), whole_block(w0), whole_block(w1)],
        split_outs(total, model),
        [],
        (h0, h1, w0, w1),
        4 * total * model * hb,
        2 * total * (model + 2 * hb) + 12 * model * hb,
    )
    return near, far


def whole_block(v):
    return pl.BlockSpec(v.shape, lambda t, *_: (0,) * len(v.shape), pipeline_mode=pl.Buffered(1))


def feed_forward(a, c, w, prev=None):
    total, model = c.shape
    rows = total // 4
    hb = w.shape[1] // 3

    def row(cols):
        return pl.BlockSpec((rows, cols), lambda t: (t, 0))

    outs = [((total, hb), BF16, row(hb)), ((total, 2 * hb), BF16, row(2 * hb))]
    if prev is None:
        kernel, args = feed_first_kernel, (*a, c, w)
        ins = [whole_block(piece) for piece in a] + [row(model), whole_block(w)]
        outs += [((total, model), BF16, row(model))] * 2
    else:
        kernel, args = feed_last_kernel, (a, c, w, prev)
        ins = [row(model), row(model), whole_block(w), row(model)]
        outs += split_outs(total, model)
    return call(
        functools.partial(kernel, hb=hb),
        4,
        0,
        ins,
        outs,
        [],
        args,
        12 * total * model * hb,
        2 * total * (4 * model + 3 * hb) + 6 * model * hb,
        total * hb,
    )


def pack_kernel(*refs, flip, widths, cuts):
    ins, outs = refs[: len(flip)], refs[len(flip) :]
    for quarter in range(QUAD):
        for out_ref, (low, high) in zip(outs, cuts):
            at = 0
            for ref, turned, width in zip(ins, flip, widths):
                start, end = low * width // high[1], high[0] * width // high[1]
                cut = slice(quarter * width + start, quarter * width + end)
                out_ref[quarter, :, at : at + end - start] = jnp.transpose(ref[cut, :]) if turned else ref[:, cut]
                at += end - start


def packed(weights, flip, cuts):
    rows = weights[0].shape[flip[0]]
    widths = [(w.shape[0] if f else w.shape[1]) // QUAD for w, f in zip(weights, flip)]
    shapes = [
        jax.ShapeDtypeStruct((QUAD, rows, sum((high - low) * w // of for w in widths)), BF16)
        for low, (high, of) in cuts
    ]
    return call(
        functools.partial(pack_kernel, flip=flip, widths=widths, cuts=cuts),
        1,
        0,
        [whole_block(w) for w in weights],
        [(shape.shape, BF16, whole_block(shape)) for shape in shapes],
        [],
        tuple(weights),
        1,
        sum(4 * math.prod(shape.shape) for shape in shapes),
    )


def weights_kernel(a_ref, b_ref, c_ref, d_ref, *refs):
    out_ref = refs[-1]
    cols = b_ref.shape[1]
    first = dot_tn(a_ref[...], b_ref[...])
    out_ref[:, :cols] = first.astype(BF16)
    out_ref[:, cols:] = dot_tn(c_ref[...], d_ref[...]).astype(BF16)
    if len(refs) > 1:
        w_ref, sums_ref = refs[:2]
        sums_ref[...] = jnp.sum(first * w_ref[...].astype(F32), axis=1, keepdims=True)


def weight_grads(a, b, c, d, w=None, rows=512):
    total, model = a.shape
    cut = pl.BlockSpec((total, rows), lambda t: (0, t))

    def whole(v):
        return pl.BlockSpec(v.shape, lambda t: (0, 0), pipeline_mode=pl.Buffered(1))

    def tall(cols):
        return pl.BlockSpec((rows, cols), lambda t: (t, 0))

    cols = b.shape[1] + d.shape[1]
    more = [] if w is None else [w]
    return call(
        weights_kernel,
        model // rows,
        0,
        [cut, whole(b), cut, whole(d)] + [tall(v.shape[1]) for v in more],
        [((model, 1), F32, tall(1))] * len(more) + [((model, cols), BF16, tall(cols))],
        [],
        (a, b, c, d, *more),
        2 * total * model * cols,
        2 * (2 * total * model + (total + model) * cols),
    )


def call(kernel, blocks, prefetch, ins, outs, scratch, args, flops, nbytes, transcendentals=0):
    return pl.pallas_call(
        kernel,
        out_shape=[jax.ShapeDtypeStruct(shape, dtype) for shape, dtype, _ in outs],
        grid_spec=pltpu.PrefetchScalarGridSpec(
            num_scalar_prefetch=prefetch,
            grid=(blocks,),
            in_specs=ins,
            out_specs=[spec for _, _, spec in outs],
            scratch_shapes=scratch,
        ),
        compiler_params=pltpu.CompilerParams(
            dimension_semantics=("arbitrary",), vmem_limit_bytes=56 * 1024 * 1024
        ),
        cost_estimate=pl.CostEstimate(
            flops=int(flops), bytes_accessed=int(nbytes), transcendentals=int(transcendentals)
        ),
    )(*args)


def on_device(
    tokens,
    attn_gain,
    ffn_gain,
    query_norm_gain,
    k_gain,
    w_query,
    key_projection,
    value_projection,
    w_out,
    w_gate,
    w_up,
    w_down,
    doc_start,
    cotangent,
):
    i, x = lax.axis_index("ctx"), lax.axis_index("tp")
    n = lax.axis_size("ctx") // QUAD
    line, b, core = i // QUAD, (i // 2) % 2, i % 2
    r, model = tokens.shape
    plane = 2 * QUAD * r
    width = query_norm_gain.shape[0]
    heads = w_query.shape[1] // QUAD // width
    qw = heads * width
    hidden = w_gate.shape[1] // QUAD
    step = model // n
    reach = WB * doc_start.shape[0]

    (sent,) = packed((w_query, key_projection, value_projection, w_out), (0, 0, 0, 1), [(0, (1, 1))])
    sent, tokens = tie(spread(sent), tokens)
    w_attn = line_gather(sent.reshape(step, -1), n)
    w_qkv, w_o = w_attn[:, : qw + 2 * width], w_attn[:, qw + 2 * width :]
    x_own = tokens.astype(F32)
    scale_1 = rms_scale(x_own)

    cut = FIRST_BLOCK
    ffn_pieces = packed((w_gate, w_up, w_down), (0, 0, 1), [(0, (cut, 8)), (cut, (8, 8))])
    a_own = (x_own * scale_1 * attn_gain).astype(BF16)
    a_near = (swap_x(a_own), swap_b(a_own), swap_both(a_own))

    near_core, near_b = swap_core(doc_start), swap_b(doc_start)
    far = swap_core(near_b)
    rows0 = [jnp.where(core == c, doc_start, near_core) for c in range(2)]
    rows1 = [jnp.where(core == c, near_b, far) for c in range(2)]
    starts = jnp.concatenate([jnp.where(b == y, rows0[c], rows1[c]) for y in range(2) for c in range(2)])
    first = line * plane
    relative = first + jnp.arange(plane, dtype=jnp.int32) - starts
    inv_freq = jnp.power(ROPE_BASE, -2.0 * jnp.arange(width // 2, dtype=F32) / width)
    angles = relative.astype(F32)[:, None] * inv_freq[None, :]
    cos, sin = jnp.cos(angles), jnp.sin(angles)
    cos = jnp.concatenate([cos] * 4, axis=-1)
    sin = jnp.concatenate([-sin, sin] * 2, axis=-1)
    sent_0 = spread(ffn_pieces[0])
    w_ffn_0 = line_gather(sent_0.reshape(step, -1), n)
    a_near, cos, sin, pieces_1, _ = tie(a_near, cos, sin, ffn_pieces[1], sent_0)
    sent_1 = spread(pieces_1)
    a_pieces = [a_own, *a_near]
    a_pieces = a_pieces + [swap_core(piece) for piece in a_pieces]

    blocks = jnp.arange(2 * QUAD, dtype=jnp.int32)
    table = (
        ((((blocks >> 1) & 1) ^ core) << 2) | (((blocks >> 2) ^ b) << 1) | ((blocks & 1) ^ x)
    ).astype(jnp.int32)
    inverse = (
        ((((blocks >> 1) & 1) ^ b) << 2) | (((blocks >> 2) ^ core) << 1) | ((blocks & 1) ^ x)
    ).astype(jnp.int32)
    nb = 2 * QUAD

    def key_range(base, keys):
        local = starts - (first - base)
        low = jnp.clip(local[::r] // KEY_BLOCK, 0, keys // KEY_BLOCK)
        high = jnp.clip((base + (blocks + 1) * r - 1) // KEY_BLOCK + 1, low, keys // KEY_BLOCK)
        return local, low, high

    own_part, halo_part = key_range(0, plane), key_range(reach, reach)

    gain_1, gain_2 = attn_gain, ffn_gain

    def here(cols):
        return pl.BlockSpec((r, cols), lambda t, *_: (t, 0))

    def moved(cols):
        return pl.BlockSpec((r, cols), lambda t, table, *_: (table[t], 0))

    lanes = 2 * width
    two = lambda gain: jnp.concatenate([gain, gain])[None, :]
    q_gain, key_gain = two(query_norm_gain), two(k_gain)
    a_one, raw, q, kv = call(
        functools.partial(project_kernel, heads=heads, width=width),
        nb,
        1,
        [whole_block(piece) for piece in a_pieces]
        + [whole_block(w_qkv), moved(lanes), moved(lanes), whole_block(q_gain), whole_block(key_gain)],
        [
            ((plane, model), BF16, here(model)),
            ((plane, qw + lanes), F32, here(qw + lanes)),
            ((plane, qw), BF16, moved(qw)),
            ((plane, lanes), BF16, moved(lanes)),
        ],
        [],
        (inverse, *a_pieces, w_qkv, cos, sin, q_gain, key_gain),
        2 * plane * model * (qw + lanes),
        plane * (4 * model + 10 * qw),
    )
    q, kv, sent_1, cot_own = tie(q, kv, sent_1, cotangent)
    w_ffn_1 = line_gather(sent_1.reshape(step, -1), n)
    spans = []
    left, distance = reach, 1
    while left > 0:
        spans.append((distance, min(left, plane)))
        left -= plane
        distance += 1
    halo = [line_move(kv[plane - rows :], d, range(0, max(n - d, 0))) for d, rows in spans]
    attn_flops = plane * heads * (plane // 2 + 2 * KEY_BLOCK) * width
    stacked = pl.BlockSpec((heads * r, 1), lambda t, *_: (t, 0))
    sums = ((plane * heads, lanes), F32, pl.BlockSpec((heads * r, lanes), lambda t, *_: (t, 0)))

    def attend(part, base, keys, *acc):
        local, low, high = part
        outs = [((plane, qw), BF16, moved(qw)), ((plane, qw), F32, here(qw)), ((plane * heads, 1), F32, stacked)]
        return call(
            functools.partial(attend_kernel, heads=heads, width=width, base=base, bk=KEY_BLOCK, last=len(acc)),
            nb,
            3,
            [here(qw), pl.BlockSpec((r, 1), lambda t, *_: (t, 0)), whole_block(keys)] + [sums[2]] * len(acc),
            outs if acc else [sums],
            [pltpu.VMEM((heads * r, lanes), F32)] * len(acc) + [pltpu.VMEM(keys.shape, BF16)],
            (table, low, high, q, local[:, None], keys, *acc),
            8 * attn_flops,
            plane * qw * 10,
        )

    (acc,) = attend(own_part, 0, kv)
    cot = Rows(cot_own)
    acc, halo, cot.first = tie(acc, halo, cot.first)
    cot.second()
    halo_keys = jnp.concatenate(halo[::-1], axis=0)
    o, o_float, stat = attend(halo_part, reach, halo_keys, acc)

    half = plane // 2
    o, cot.last = tie(o, cot.last)

    attn_sum, cot = scatter_rows(*split_dot(o, w_o), jnp.concatenate(cot.third(), axis=0))
    resid = x_own + attn_sum
    scale_2 = rms_scale(resid)
    a_pieces = gather_rows((resid * scale_2 * gain_2).astype(BF16))

    hid_0, d_gu_0, back, a_two = feed_forward(a_pieces, cot, w_ffn_0)
    (ffn_grad_0,) = weight_grads(a_two, d_gu_0, cot, hid_0)
    w_ffn_1, _ = tie(w_ffn_1, ffn_grad_0)
    ffn_grad_0 = line_scatter(ffn_grad_0, n)
    hid_1, d_gu_1, near, *far = feed_forward(a_two, cot, w_ffn_1, back)
    d_two, ffn_grad_1 = scatter_rows(near, far, weight_grads(a_two, d_gu_1, cot, hid_1)[0])
    ffn_grad_1 = line_scatter(ffn_grad_1, n)
    d_res, d_ffn_gain = norm_back(resid, scale_2, gain_2, d_two)
    d_h = cotangent.astype(F32) + d_res

    h_pieces, down = gather_rows(d_h.astype(BF16), down_rows(hid_0, hid_1, w_ffn_0, w_ffn_1))
    ffn_sum = Sums(*down)

    def home(grad):
        return spread(grad.reshape(QUAD, step // QUAD, -1)).transpose(1, 0, 2)

    d_h_rows, d_o = call(
        rows_dot_kernel,
        nb,
        0,
        [whole_block(piece) for piece in h_pieces] + [whole_block(w_o)],
        [((plane, model), BF16, here(model)), ((plane, qw), BF16, here(qw))],
        [],
        (*h_pieces, w_o),
        2 * plane * model * qw,
        4 * plane * model,
    )
    d_o, ffn_sum.parts = tie(d_o, ffn_sum.parts)
    ffn_sum.second()

    def attend_back(part, base, keys, *acc):
        local, low, high = part
        if acc:
            outs = [((plane, qw), F32, here(qw)), (keys.shape, F32, pl.BlockSpec(keys.shape, lambda t, *_: (0, 0)))]
            scratch = pltpu.VMEM((heads * r, lanes), F32)
        else:
            outs = [sums] + [
                ((rows, lanes), BF16, pl.BlockSpec((rows, lanes), lambda t, *_: (0, 0))) for _, rows in spans[::-1]
            ]
            scratch = pltpu.VMEM(keys.shape, F32)
        return call(
            functools.partial(
                attend_back_kernel, heads=heads, width=width, base=base, bk=KEY_BLOCK, last=len(acc)
            ),
            nb,
            3,
            [
                here(qw),
                moved(qw),
                here(qw),
                stacked,
                pl.BlockSpec((1, 1, r), lambda t, *_: (t, 0, 0)),
                whole_block(keys),
            ]
            + [sums[2]] * len(acc),
            outs,
            [scratch],
            (table, low, high, q, d_o, o_float, stat, local.reshape(nb, 1, r), keys, *acc),
            20 * attn_flops,
            plane * qw * 12,
        )

    acc, *halo_grads = attend_back(halo_part, reach, halo_keys)
    acc, halo_grads, ffn_sum.got, ffn_grad_0 = tie(acc, halo_grads, ffn_sum.got, ffn_grad_0)
    back_0 = home(ffn_grad_0)
    returned = [line_move(g, -d, range(d, n)) for g, (d, _) in zip(halo_grads[::-1], spans)]
    dq, dkv = attend_back(own_part, 0, kv, acc)
    dq, back_0, returned = tie(dq, back_0, returned)
    d_raw, d_head_gains = call(
        functools.partial(prep_back_kernel, heads=heads, width=width, plane=plane),
        nb,
        1,
        [moved(qw + lanes), here(lanes), here(lanes), whole_block(q_gain), whole_block(key_gain), here(qw), here(lanes)]
        + [whole_block(g) for g in returned],
        [
            ((plane, qw + lanes), BF16, moved(qw + lanes)),
            ((8, lanes), F32, pl.BlockSpec((8, lanes), lambda t, *_: (0, 0))),
        ],
        [],
        (table, raw, cos, sin, q_gain, key_gain, dq, dkv, *returned),
        plane * (qw + width) * 20,
        plane * (qw + 2 * width) * 10,
    )
    one = split_dot(d_raw, w_qkv)
    d_raw, one = tie(d_raw, one)
    one = Sums(*one)
    gain_sums, attn_grad = weight_grads(a_one, d_raw, d_h_rows, o, w_qkv)
    attn_grad = line_scatter(attn_grad, n)
    out_tokens = (resid + ffn_sum.third()).astype(BF16)
    back_1 = home(ffn_grad_1)

    def joined(part):
        cols = [jnp.split(v, 3, axis=-1)[part] for v in (back_0, back_1)]
        return jnp.concatenate(cols, axis=-1).reshape(step // QUAD, -1).astype(F32)

    ffn_outs = (joined(0), joined(1), joined(2).T)
    one.second()
    one.got, ffn_outs, gain_sums = tie(one.got, ffn_outs, gain_sums)
    d_attn_gain = gain_sums[:, 0] / gain_1
    d_q_gain = d_head_gains[0, :width] + d_head_gains[0, width:]
    gains = sum_over_ctx(jnp.concatenate([d_attn_gain, d_ffn_gain, d_q_gain, d_head_gains[1, :width]]))
    d_x, _ = norm_back(x_own, scale_1, gain_1, one.third())
    d_tokens = d_h + d_x

    attn_back = home(attn_grad)
    attn_back, gains = tie(attn_back, gains)
    gains = gains + swap_x(gains)

    def piece(start, size):
        return attn_back[:, :, start : start + size].reshape(step // QUAD, -1).astype(F32)

    return (
        out_tokens,
        d_tokens,
        gains[:model],
        gains[model : 2 * model],
        gains[2 * model : 2 * model + width],
        gains[2 * model + width :],
        piece(0, qw),
        piece(qw, width),
        piece(qw + width, width),
        piece(qw + 2 * width, qw).T,
        *ffn_outs,
    )


def solution(mesh):
    return jax.shard_map(
        on_device,
        mesh=mesh,
        in_specs=(
            P(("ctx", "tp"), None),
            P(),
            P(),
            P(),
            P(),
            P("ctx", "tp"),
            P("ctx", "tp"),
            P("ctx", "tp"),
            P("tp", "ctx"),
            P("ctx", "tp"),
            P("ctx", "tp"),
            P("tp", "ctx"),
            P("ctx"),
            P(("ctx", "tp"), None),
        ),
        out_specs=(
            P(("ctx", "tp"), None),
            P(("ctx", "tp"), None),
            P(),
            P(),
            P(),
            P(),
            P("ctx", "tp"),
            P("ctx", "tp"),
            P("ctx", "tp"),
            P("tp", "ctx"),
            P("ctx", "tp"),
            P("ctx", "tp"),
            P("tp", "ctx"),
        ),
        check_vma=False,
    )
```

time: 716 us -> 678 us (0.947)
  Pallas kernels: 147 us -> 225 us
  waiting for transfers between devices: 231 us -> 179 us
  matrix products: 39.5 us -> 0 us
  starting transfers between devices: 103 us -> 88.3 us
  local copies, waits for them, and re-layouts: 77.6 us -> 63 us
    pallas_call x11 -> x17, Pallas kernels: 147 us -> 225 us  [call(): pl.pallas_call(kernel, out_shape=[jax.ShapeDtypeStruct(shape, dtype) for...]
    ppermute x4, waiting for transfers between devices: 56.7 us -> 12.5 us  [line_move(): return lax.ppermute(value, 'ctx', pairs)]
    dot_general x10 -> x0, matrix products: 39.5 us -> none  [the longest x8 30.2 us: dot_nt(): lax.dot_general(a, b, (((1,), (1,)), ((), ())), preferred_element_type=F32)]
    unnamed x188 -> x128, local copies, waits for them, and re-layouts: 47.4 us -> 24.4 us
    ppermute x63 -> x61, waiting for transfers between devices: 101 us -> 88 us  [swap_ctx(): return lax.ppermute(value, 'ctx', [(i, i ^ bit) for i in range(n)])]
    ppermute x0 -> x1, waiting for transfers between devices: none -> 12.3 us  [swap_both(): lax.ppermute(value, ('ctx', 'tp'), [(2 * i + x, 2 * (i ^ 2) + 1 - x) for...]
    ppermute x21 -> x20, waiting for transfers between devices: 35.3 us -> 23.1 us  [swap_x(): return lax.ppermute(value, 'tp', [(0, 1), (1, 0)])]
    reduce_scatter x3, starting transfers between devices: 12.1 us -> 0.3 us  [line_scatter(): lax.psum_scatter(partial, 'ctx', scatter_dimension=0, axis_index_groups=l...]
  transfers between devices with their start and end apart: 98 -> 96, of which waited for: 36 -> 37; matrix products, arithmetic and copies ran while one was open for 22% -> 16% of each run, Pallas kernels for 21% -> 33%
where the time goes in v3:
time: 678 us; the launch traced here: 668 us
  Pallas kernels  225 us (33%)
  waiting for transfers between devices  179 us (26%)
  starting transfers between devices  88.3 us (13%)
  local copies, waits for them, and re-layouts  63 us (9%)
  other arithmetic  57 us (8%)
  blocking collectives  39.6 us (6%)
  between operations  15.4 us (2%)
    pallas_call x17, Pallas kernels, call(): pl.pallas_call(kernel, out_shape=[jax.ShapeDtypeStruct(shape, dtype) for...  225 us
    ppermute x61, waiting for transfers between devices, swap_ctx(): return lax.ppermute(value, 'ctx', [(i, i ^ bit) for i in range(n)])  88 us
    all_to_all x2, blocking collectives, spread(): lax.all_to_all(pieces, 'ctx', axis, axis, axis_index_groups=groups, tiled...  39.6 us
    ppermute x61, starting transfers between devices, swap_ctx(): return lax.ppermute(value, 'ctx', [(i, i ^ bit) for i in range(n)])  37.9 us
    all_gather x3, waiting for transfers between devices, line_gather(): lax.all_gather(own, 'ctx', axis=0, axis_index_groups=line_groups(n), tile...  27.1 us
    unnamed x128, local copies, waits for them, and re-layouts  24.4 us
    ppermute x20, waiting for transfers between devices, swap_x(): return lax.ppermute(value, 'tp', [(0, 1), (1, 0)])  23.1 us
    convert_element_type x12, other arithmetic, add16(): return (a.astype(F32) + b.astype(F32)).astype(BF16)  22.5 us
  transfers between devices with their start and end apart: 96, of which 37 were waited for; matrix products, arithmetic and copies ran while one was open for 16% of the time, Pallas kernels for 33%

profile of v3, /device:TPU:0, one launch (start us, length us, event | category | flops | bytes accessed | tf_op | source)
XLA Modules:
  0.0 668.1 jit_solution(5846502442853726484)
XLA Ops:
  7.2 2.1 shard_map.237
  9.4 15.1 %all_to_all.30 = bf16[4,128,640]{2,1,0:T(8,128)(2,1)} all-to-all(bf16[4,128,640]{2,1,0:T(8,128)(2,1)} %shard_map.237), channel_id=1, replica_groups={{0,2,4,6},{8,10,12,14},{16,18,20,22},{24,26,28,30},{1,3,5,7},{9,11,13,1..., dimensions={0} | all-to-all | bytes 1310720 | tf_op jit(solution)/shard_map/all_to_all | solution.py:145
  24.6 3.9 shard_map.238
  28.4 24.5 %all_to_all.31 = bf16[4,128,1536]{2,1,0:T(8,128)(2,1)} all-to-all(bf16[4,128,1536]{2,1,0:T(8,128)(2,1)} %get-tuple-element.132), channel_id=1, replica_groups={{0,2,4,6},{8,10,12,14},{16,18,20,22},{24,26,28,30},{1,3,5,7},{9,11,13,1..., dimensions={0} | all-to-all | bytes 3145728 | tf_op jit(solution)/shard_map/all_to_all | solution.py:145
  59.5 2.2 collective-permute-start.5
  63.3 2.8 fusion.21
  66.1 2.5 pad_maximum_fusion.1
  68.6 12.3 %collective-permute-done.5.refs_3_ = bf16[192,2048]{1,0:T(8,128)(2,1)S(1)} collective-permute-done((bf16[192,2048]{1,0:T(8,128)(2,1)S(1)}, bf16[192,2048]{1,0:T(8,128)(2,1)S(1)}, u32[]{:S(2)}, u32[]{:S(2)}) %collective-permute-start.5) | collective-permute-done | bytes 786464 | tf_op jit(solution)/shard_map/ppermute | solution.py:73
  80.9 16.0 %collective-permute-done.4.refs_2_ = bf16[192,2048]{1,0:T(8,128)(2,1)S(1)} collective-permute-done((bf16[192,2048]{1,0:T(8,128)(2,1)S(1)}, bf16[192,2048]{1,0:T(8,128)(2,1)S(1)}, u32[]{:S(2)}, u32[]{:S(2)}) %collective-permute-start.4) | collective-permute-done | bytes 786464 | tf_op jit(solution)/shard_map/ppermute | solution.py:26
  98.0 3.6 all-to-all-start.2
  104.5 2.4 broadcast_subtract_fusion
  107.0 2.7 slice.280.refs_8_.w_ref.refs_0_
  109.7 14.2 %shard_map.239 = (bf16[1536,2048]{1,0:T(8,128)(2,1)}, f32[1536,384]{1,0:T(8,128)}, bf16[1536,256]{1,0:T(8,128)(2,1)}, bf16[1536,128]{1,0:T(8,128)(2,1)}) custom-call(s32[8]{0:T(128)} %or_or_fusion.table, bf16[192,2048]{1,0:T(8,128)(2,1)} %copy-done.6, bf16[192,2048]{1,0:T(8,128)(2,1)} %copy-done.19, bf16[192,2048]{1,0:T(8,128)(2,1)} %copy-done.18, ...), custom_call_target="tpu_custom_call" | custom-call | flops 2415919104 | bytes 16515072 | tf_op jit(solution)/shard_map/pallas_call | solution.py:576
  129.3 3.5 collective-permute-start.10
  132.9 5.1 collective-permute-start.11
  138.3 14.0 %shard_map.240.refs_0_ = f32[6144,128]{1,0:T(8,128)} custom-call(s32[8]{0:T(128)} %or_or_fusion.1.table, s32[8]{0:T(128)} %get-tuple-element.293.lo, s32[8]{0:T(128)} %get-tuple-element.292.hi, bf16[1536,256]{1,0:T(8,128)(2,1)} %get-tuple-element.142.q_ref, s32[1536,1]{1,0:T(8,128)} %get-tuple-element.334.start_ref, bf16[1536,128]{1,0:T(8,128)(2,1)} %get-tuple-element.143.kv_ref), custom_call_target="tpu_custom_call" | custom-call | flops 4831838208 | bytes 3932160 | tf_op jit(solution)/shard_map/pallas_call | solution.py:576
  152.2 2.3 slice.281.w_ref.refs_10_
  154.6 4.5 collective-permute-done.11
  167.0 2.6 copy-done.31
  170.4 9.2 %shard_map.241 = (bf16[1536,256]{1,0:T(8,128)(2,1)}, f32[1536,256]{1,0:T(8,128)}, f32[6144,1]{1,0:T(8,128)}) custom-call(s32[8]{0:T(128)} %or_or_fusion.1.table, s32[8]{0:T(128)} %get-tuple-element.295.lo, s32[8]{0:T(128)} %get-tuple-element.294.hi, bf16[1536,256]{1,0:T(8,128)(2,1)} %get-tuple-element.142.q_ref, s32[1536,1]{1,0:T(8,128)} %get-tuple-element.335.start_ref, ...), custom_call_target="tpu_custom_call" | custom-call | flops 4831838208 | bytes 3932160 | tf_op jit(solution)/shard_map/pallas_call | solution.py:576
  179.5 7.2 %shard_map.242 = (bf16[768,2048]{1,0:T(8,128)(2,1)}, bf16[192,2048]{1,0:T(8,128)(2,1)}, bf16[192,2048]{1,0:T(8,128)(2,1)}, bf16[192,2048]{1,0:T(8,128)(2,1)}, bf16[192,2048]{1,0:T(8,128)(2,1)}) custom-call(bf16[1536,256]{1,0:T(8,128)(2,1)} %get-tuple-element.151.a_ref.d_ref, bf16[2048,256]{1,0:T(8,128)(2,1)} %slice.281.w_ref.refs_10_), custom_call_target="tpu_custom_call" | custom-call | flops 1610612736 | bytes 7077888 | tf_op jit(solution)/shard_map/pallas_call | solution.py:576
  201.2 6.3 collective-permute-done.21
  208.3 7.2 %collective-permute-done.19 = bf16[96,2048]{1,0:T(8,128)(2,1)S(1)} collective-permute-done((bf16[96,2048]{1,0:T(8,128)(2,1)S(1)}, bf16[96,2048]{1,0:T(8,128)(2,1)S(1)}, u32[]{:S(2)}, u32[]{:S(2)}) %collective-permute-start.19) | collective-permute-done | bytes 393248 | tf_op jit(solution)/shard_map/ppermute | solution.py:26
  218.8 6.9 %collective-permute-done.29 = bf16[96,2048]{1,0:T(8,128)(2,1)S(1)} collective-permute-done((bf16[96,2048]{1,0:T(8,128)(2,1)S(1)}, bf16[96,2048]{1,0:T(8,128)(2,1)S(1)}, u32[]{:S(2)}, u32[]{:S(2)}) %collective-permute-start.29) | collective-permute-done | bytes 393248 | tf_op jit(solution)/shard_map/ppermute | solution.py:26
  230.1 15.5 %collective-permute-done.32.refs_2_ = bf16[192,2048]{1,0:T(8,128)(2,1)S(1)} collective-permute-done((bf16[192,2048]{1,0:T(8,128)(2,1)S(1)}, bf16[192,2048]{1,0:T(8,128)(2,1)S(1)}, u32[]{:S(2)}, u32[]{:S(2)}) %collective-permute-start.32) | collective-permute-done | bytes 786464 | tf_op jit(solution)/shard_map/ppermute | solution.py:26
  248.7 5.5 collective-permute-done.33.refs_3_
  254.2 4.4 collective-permute-done.34.refs_4_
  261.1 24.8 %shard_map.243 = (bf16[1536,512]{1,0:T(8,128)(2,1)}, bf16[1536,1024]{1,0:T(8,128)(2,1)}, bf16[1536,2048]{1,0:T(8,128)(2,1)}, bf16[1536,2048]{1,0:T(8,128)(2,1)}) custom-call(bf16[192,2048]{1,0:T(8,128)(2,1)} %copy-done.23, bf16[192,2048]{1,0:T(8,128)(2,1)} %copy-done.28, bf16[192,2048]{1,0:T(8,128)(2,1)} %copy-done.27, bf16[96,2048]{1,0:T(8,128)(2,1)} %copy-done.51, ...), custom_call_target="tpu_custom_call" | custom-call | flops 19327352832 | bytes 36175872 | tf_op jit(solution)/shard_map/pallas_call | solution.py:576
  286.0 15.5 %shard_map.244 = bf16[2048,1536]{1,0:T(8,128)(2,1)} custom-call(bf16[1536,2048]{1,0:T(8,128)(2,1)} %get-tuple-element.164.a_ref, bf16[1536,1024]{1,0:T(8,128)(2,1)} %get-tuple-element.166.b_ref, bf16[1536,2048]{1,0:T(8,128)(2,1)} %constant_dynamic-update-slice_fusion.2.refs_10_.c_ref, bf16[1536,512]{1,0:T(8,128)(2,1)} %get-tuple-element.167.d_ref.h0_ref), custom_call_target="tpu_custom_call" | custom-call | flops 9663676416 | bytes 23592960 | tf_op jit(solution)/shard_map/pallas_call | solution.py:576
  301.6 27.1 %all-gather.8.cloned.1.call-done.w_ref.w1_ref = bf16[2048,1536]{1,0:T(8,128)(2,1)} async-done(((bf16[512,1536]{1,0:T(8,128)(2,1)}), bf16[2048,1536]{1,0:T(8,128)(2,1)}) %all-gather.8.cloned.1.call-update) | async-done | bytes 6291472 | tf_op jit(solution)/shard_map/all_gather | solution.py:51
  328.6 25.7 %shard_map.245 = (bf16[1536,512]{1,0:T(8,128)(2,1)}, bf16[1536,1024]{1,0:T(8,128)(2,1)}, bf16[768,2048]{1,0:T(8,128)(2,1)}, bf16[192,2048]{1,0:T(8,128)(2,1)}, b...) custom-call(bf16[1536,2048]{1,0:T(8,128)(2,1)} %get-tuple-element.164.a_ref, ...), custom_call_target="tpu_custom_call" | custom-call | flops 19327352832 | bytes 36175872 | tf_op jit(solution)/shard_map/pallas_call | solution.py:576
  360.2 4.2 add_convert_fusion.8
  371.1 15.0 %shard_map.246 = bf16[2048,1536]{1,0:T(8,128)(2,1)} custom-call(bf16[1536,2048]{1,0:T(8,128)(2,1)} %get-tuple-element.164.a_ref, bf16[1536,1024]{1,0:T(8,128)(2,1)} %get-tuple-element.175.b_ref, bf16[1536,2048]{1,0:T(8,128)(2,1)} %constant_dynamic-update-slice_fusion.2.refs_10_.c_ref, bf16[1536,512]{1,0:T(8,128)(2,1)} %get-tuple-element.176.d_ref.h1_ref), custom_call_target="tpu_custom_call" | custom-call | flops 9663676416 | bytes 23592960 | tf_op jit(solution)/shard_map/pallas_call | solution.py:576
  391.8 8.0 %collective-permute-done.48 = bf16[96,2048]{1,0:T(8,128)(2,1)S(1)} collective-permute-done((bf16[96,2048]{1,0:T(8,128)(2,1)S(1)}, bf16[96,2048]{1,0:T(8,128)(2,1)S(1)}, u32[]{:S(2)}, u32[]{:S(2)}) %collective-permute-start.48) | collective-permute-done | bytes 393248 | tf_op jit(solution)/shard_map/ppermute | solution.py:26
  406.2 15.3 %shard_map.247 = (bf16[768,2048]{1,0:T(8,128)(2,1)}, bf16[192,2048]{1,0:T(8,128)(2,1)}, bf16[192,2048]{1,0:T(8,128)(2,1)}, bf16[192,2048]{1,0:T(8,128)(2,1)}, bf16[192,2048]{1,0:T(8,128)(2,1)}) custom-call(bf16[1536,512]{1,0:T(8,128)(2,1)} %get-tuple-element.167.d_ref.h0_ref, bf16[1536,512]{1,0:T(8,128)(2,1)} %get-tuple-element.176.d_ref.h1_ref, ...), custom_call_target="tpu_custom_call" | custom-call | flops 6442450944 | bytes 22020096 | tf_op jit(solution)/shard_map/pallas_call | solution.py:576
  427.0 7.2 %collective-permute-done.52.refs_3_ = bf16[96,2048]{1,0:T(8,128)(2,1)S(1)} collective-permute-done((bf16[96,2048]{1,0:T(8,128)(2,1)S(1)}, bf16[96,2048]{1,0:T(8,128)(2,1)S(1)}, u32[]{:S(2)}, u32[]{:S(2)}) %collective-permute-start.52) | collective-permute-done | bytes 393248 | tf_op jit(solution)/shard_map/ppermute | solution.py:38
  434.2 2.3 collective-permute-done.53.refs_4_
  445.5 8.6 %shard_map.248 = (bf16[1536,2048]{1,0:T(8,128)(2,1)}, bf16[1536,256]{1,0:T(8,128)(2,1)}) custom-call(bf16[192,2048]{1,0:T(8,128)(2,1)} %copy-done.11, bf16[192,2048]{1,0:T(8,128)(2,1)} %collective-permute-done.50.refs_1_, bf16[192,2048]{1,0:T(8,128)(2,1)} %collective-permute-done.51.refs_2_, bf16[96,2048]{1,0:T(8,128)(2,1)} %copy-done.24, ...), custom_call_target="tpu_custom_call" | custom-call | flops 1610612736 | bytes 12582912 | tf_op jit(solution)/shard_map/pallas_call | solution.py:576
  455.8 2.9 add_convert_fusion.4
  463.1 10.8 %shard_map.249 = (f32[6144,128]{1,0:T(8,128)}, bf16[768,128]{1,0:T(8,128)(2,1)}, bf16[1536,128]{1,0:T(8,128)(2,1)}) custom-call(s32[8]{0:T(128)} %or_or_fusion.1.table, s32[8]{0:T(128)} %get-tuple-element.295.lo, s32[8]{0:T(128)} %get-tuple-element.294.hi, bf16[1536,256]{1,0:T(8,128)(2,1)} %get-tuple-element.142.q_ref, ...), custom_call_target="tpu_custom_call" | custom-call | flops 12079595520 | bytes 4718592 | tf_op jit(solution)/shard_map/pallas_call | solution.py:576
  475.3 3.0 collective-permute-done.64
  479.3 4.3 all-to-all-start.3
  492.2 30.6 %shard_map.250 = (f32[1536,256]{1,0:T(8,128)}, f32[1536,128]{1,0:T(8,128)}) custom-call(s32[8]{0:T(128)} %or_or_fusion.1.table, s32[8]{0:T(128)} %get-tuple-element.293.lo, s32[8]{0:T(128)} %get-tuple-element.292.hi, bf16[1536,256]{1,0:T(8,128)(2,1)} %get-tuple-element.142.q_ref, bf16[1536,256]{1,0:T(8,128)(2,1)} %get-tuple-element.195.do_ref, ...), custom_call_target="tpu_custom_call" | custom-call | flops 12079595520 | bytes 4718592 | tf_op jit(solution)/shard_map/pallas_call | solution.py:576
  522.8 8.0 %collective-permute-done.69.refs_0_ = bf16[1536,128]{1,0:T(8,128)(2,1)S(1)} collective-permute-done((bf16[1536,128]{1,0:T(8,128)(2,1)S(1)}, bf16[1536,128]{1,0:T(8,128)(2,1)S(1)}, u32[]{:S(2)}, u32[]{:S(2)}) %collective-permute-start.69) | collective-permute-done | bytes 393248 | tf_op jit(solution)/shard_map/ppermute | solution.py:60
  531.6 9.1 %shard_map.251 = (bf16[1536,384]{1,0:T(8,128)(2,1)}, f32[8,128]{1,0:T(8,128)}) custom-call(s32[8]{0:T(128)} %or_or_fusion.1.table, f32[1536,384]{1,0:T(8,128)} %get-tuple-element.208.raw_ref, f32[1536,128]{1,0:T(8,128)} %get-tuple-element.137.refs_9_.cos_ref, f32[1536,128]{1,0:T(8,128)} %get-tuple-element.138.refs_10_.sin_ref, ...), custom_call_target="tpu_custom_call" | custom-call | flops 9830400 | bytes 5898240 | tf_op jit(solution)/shard_map/pallas_call | solution.py:576
  540.6 8.5 %shard_map.252 = (bf16[768,2048]{1,0:T(8,128)(2,1)}, bf16[192,2048]{1,0:T(8,128)(2,1)}, bf16[192,2048]{1,0:T(8,128)(2,1)}, bf16[192,2048]{1,0:T(8,128)(2,1)}, bf16[192,2048]{1,0:T(8,128)(2,1)}) custom-call(bf16[1536,384]{1,0:T(8,128)(2,1)} %get-tuple-element.232.a_ref.b_ref, bf16[2048,384]{1,0:T(8,128)(2,1)} %slice.280.refs_8_.w_ref.refs_0_), custom_call_target="tpu_custom_call" | custom-call | flops 2415919104 | bytes 7471104 | tf_op jit(solution)/shard_map/pallas_call | solution.py:576
  550.2 11.0 %shard_map.253 = (f32[2048,1]{1,0:T(8,128)}, bf16[2048,640]{1,0:T(8,128)(2,1)}) custom-call(bf16[1536,2048]{1,0:T(8,128)(2,1)} %get-tuple-element.231.a_ref, bf16[1536,384]{1,0:T(8,128)(2,1)} %get-tuple-element.232.a_ref.b_ref, bf16[1536,2048]{1,0:T(8,128)(2,1)} %get-tuple-element.233.c_ref, bf16[1536,256]{1,0:T(8,128)(2,1)} %get-tuple-element.151.a_ref.d_ref, ...), custom_call_target="tpu_custom_call" | custom-call | flops 4026531840 | bytes 17170432 | tf_op jit(solution)/shard_map/pallas_call | solution.py:576
  561.2 2.6 fusion.27
  563.7 2.1 reduce-scatter.6.cloned.1.call-done
  565.9 4.6 all-to-all-start.4
  573.4 5.2 add_convert_fusion
  584.0 7.0 %all-to-all-done.4 = bf16[4,128,1536]{2,1,0:T(8,128)(2,1)} async-done(((bf16[4,128,1536]{2,1,0:T(8,128)(2,1)}), bf16[4,128,1536]{2,1,0:T(8,128)(2,1)}, u32[]{:S(2)}, u32[]{:S(2)}) %all-to-all-start.4) | async-done | bytes 1572896 | tf_op jit(solution)/shard_map/all_to_all | solution.py:145
  591.1 2.5 fusion.28
  596.7 2.9 copy.61
  604.3 3.1 collective-permute-done.74
  607.4 2.2 reduce
  616.0 2.3 collective-permute-done.82
  618.3 8.2 %collective-permute-start.83 = (f32[4224]{0:T(1024)S(1)}, f32[4224]{0:T(1024)S(1)}, u32[]{:S(2)}, u32[]{:S(2)}) collective-permute-start(f32[4224]{0:T(1024)S(1)} %add.278), channel_id=1, source_target_pairs={{0,8},{2,10},{4,12},{6,14},{8,0},{10,2},{12,4},{14,6},{16,24},{18,... | collective-permute-start | bytes 50696 | tf_op jit(solution)/shard_map/ppermute | solution.py:26
  630.3 3.2 collective-permute-done.84
  633.5 4.1 collective-permute-done.79
  639.6 2.2 copy.62
  641.8 3.5 all-to-all-start.5
  645.3 3.0 fusion.7
  648.2 7.2 %all-to-all-done.5 = bf16[4,128,640]{1,2,0:T(8,128)(2,1)S(1)} async-done(((bf16[4,128,640]{1,2,0:T(8,128)(2,1)}), bf16[4,128,640]{1,2,0:T(8,128)(2,1)S(1)}, u32[]{:S(2)}, u32[]{:S(2)}) %all-to-all-start.5) | async-done | bytes 655392 | tf_op jit(solution)/shard_map/all_to_all | solution.py:145
  (385 shorter events, 146.6 us)
Async XLA Ops:
  7.2 99.8 %all-gather.4.cloned.1.call-start = ((), (), s32[]{:S(2)}) async-start(), calls=%async_computation.9 | async-start | bytes 3276800 | tf_op jit(solution)/shard_map/all_gather | solution.py:51
  24.5 236.6 %all-gather.6.cloned.1.call-start = ((), (), s32[]{:S(2)}) async-start(), calls=%async_computation.10 | async-start | bytes 7864320 | tf_op jit(solution)/shard_map/all_gather | solution.py:51
  59.5 21.4 %collective-permute-start.5 = (bf16[192,2048]{1,0:T(8,128)(2,1)S(1)}, bf16[192,2048]{1,0:T(8,128)(2,1)S(1)}, u32[]{:S(2)}, u32[]{:S(2)}) collective-permute-start(bf16[192,2048]{1,0:T(8,128)(2,1)S(1)} %fusion.3.refs_0_), channel_id=1, source_target_pairs={{0,5},{1,4},{2,7},{3,6},{4,1},{5,0},{6,3},{7,2},{8,13},{9,12},{10,... | collective-permute-start | bytes 2359304 | tf_op jit(solution)/shard_map/ppermute | solution.py:73
  61.6 35.3 %collective-permute-start.4 = (bf16[192,2048]{1,0:T(8,128)(2,1)S(1)}, bf16[192,2048]{1,0:T(8,128)(2,1)S(1)}, u32[]{:S(2)}, u32[]{:S(2)}) collective-permute-start(bf16[192,2048]{1,0:T(8,128)(2,1)S(1)} %fusion.3.refs_0_), channel_id=1, source_target_pairs={{0,4},{2,6},{4,0},{6,2},{8,12},{10,14},{12,8},{14,10},{16,20},{18,... | collective-permute-start | bytes 2359304 | tf_op jit(solution)/shard_map/ppermute | solution.py:26
  63.3 33.6 %collective-permute-start.3 = (bf16[192,2048]{1,0:T(8,128)(2,1)S(1)}, bf16[192,2048]{1,0:T(8,128)(2,1)S(1)}, u32[]{:S(2)}, u32[]{:S(2)}) collective-permute-start(bf16[192,2048]{1,0:T(8,128)(2,1)S(1)} %fusion.3.refs_0_), channel_id=1, source_target_pairs={{0,1},{1,0},{2,3},{3,2},{4,5},{5,4},{6,7},{7,6},{8,9},{9,8},{10,11... | collective-permute-start | bytes 2359304 | tf_op jit(solution)/shard_map/ppermute | solution.py:38
  68.6 41.1 %collective-permute-start.6 = (bf16[192,2048]{1,0:T(8,128)(2,1)S(1)}, bf16[192,2048]{1,0:T(8,128)(2,1)}, u32[]{:S(2)}, u32[]{:S(2)}) collective-permute-start(bf16[192,2048]{1,0:T(8,128)(2,1)S(1)} %fusion.3.refs_0_), channel_id=1, source_target_pairs={{0,2},{2,0},{4,6},{6,4},{8,10},{10,8},{12,14},{14,12},{16,18},{18,... | collective-permute-start | bytes 2359304 | tf_op jit(solution)/shard_map/ppermute | solution.py:26
  98.0 25.9 %all-to-all-start.2 = ((bf16[4,128,1536]{2,1,0:T(8,128)(2,1)}), bf16[4,128,1536]{2,1,0:T(8,128)(2,1)S(1)}, u32[]{:S(2)}, u32[]{:S(2)}) async-start(bf16[4,128,1536]{2,1,0:T(8,128)(2,1)} %get-tuple-element.141), calls=%async_computation.2 | async-start | bytes 3145728 | tf_op jit(solution)/shard_map/all_to_all | solution.py:145
  101.6 227.0 %all-gather.8.cloned.1.call-start = ((), (), s32[]{:S(2)}) async-start(), calls=%async_computation.11 | async-start | bytes 7864320 | tf_op jit(solution)/shard_map/all_gather | solution.py:51
  124.0 35.1 %collective-permute-start.13 = (bf16[192,2048]{1,0:T(8,128)(2,1)S(1)}, bf16[192,2048]{1,0:T(8,128)(2,1)}, u32[]{:S(2)}, u32[]{:S(2)}) collective-permute-start(bf16[192,2048]{1,0:T(8,128)(2,1)S(1)} %copy-done.12), channel_id=1, source_target_pairs={{0,4},{2,6},{4,0},{6,2},{8,12},{10,14},{12,8},{14,10},{16,20},{18,... | collective-permute-start | bytes 2359304 | tf_op jit(solution)/shard_map/ppermute | solution.py:26
  125.7 33.3 %collective-permute-start.12 = (bf16[192,2048]{1,0:T(8,128)(2,1)S(1)}, bf16[192,2048]{1,0:T(8,128)(2,1)}, u32[]{:S(2)}, u32[]{:S(2)}) collective-permute-start(bf16[192,2048]{1,0:T(8,128)(2,1)S(1)} %copy-done.12), channel_id=1, source_target_pairs={{0,1},{1,0},{2,3},{3,2},{4,5},{5,4},{6,7},{7,6},{8,9},{9,8},{10,11... | collective-permute-start | bytes 2359304 | tf_op jit(solution)/shard_map/ppermute | solution.py:38
  129.3 29.7 %collective-permute-start.10 = (bf16[1536,128]{1,0:T(8,128)(2,1)}, bf16[1536,128]{1,0:T(8,128)(2,1)S(1)}, u32[]{:S(2)}, u32[]{:S(2)}) collective-permute-start(bf16[1536,128]{1,0:T(8,128)(2,1)} %get-tuple-element.143.kv_ref), channel_id=1, source_target_pairs={{0,8},{2,10},{4,12},{6,14},{8,16},{10,18},{12,20},{14,22},{16,24},... | collective-permute-start | bytes 1179656 | tf_op jit(solution)/shard_map/ppermute | solution.py:60
  132.9 55.1 %collective-permute-start.24 = (bf16[192,2048]{1,0:T(8,128)(2,1)S(1)}, bf16[192,2048]{1,0:T(8,128)(2,1)}, u32[]{:S(2)}, u32[]{:S(2)}) collective-permute-start(bf16[192,2048]{1,0:T(8,128)(2,1)S(1)} %copy-done.12), channel_id=1, source_target_pairs={{0,2},{2,0},{4,6},{6,4},{8,10},{10,8},{12,14},{14,12},{16,18},{18,... | collective-permute-start | bytes 2359304 | tf_op jit(solution)/shard_map/ppermute | solution.py:26
  132.9 26.1 %collective-permute-start.11 = (bf16[768,128]{1,0:T(8,128)(2,1)}, bf16[768,128]{1,0:T(8,128)(2,1)}, u32[]{:S(2)}, u32[]{:S(2)}) collective-permute-start(bf16[768,128]{1,0:T(8,128)(2,1)} %slice.213), channel_id=1, source_target_pairs={{0,16},{2,18},{4,20},{6,22},{8,24},{10,26},{12,28},{14,30},{1,17},... | collective-permute-start | bytes 589832 | tf_op jit(solution)/shard_map/ppermute | solution.py:60
  138.0 341.3 %reduce-scatter.4.cloned.1.call-start = ((), (), s32[]{:S(2)}) async-start(), calls=%async_computation.12 | async-start | bytes 7864320 | tf_op jit(solution)/shard_map/reduce_scatter | solution.py:55
  160.1 32.2 %collective-permute-start.26 = (bf16[192,2048]{1,0:T(8,128)(2,1)}, bf16[192,2048]{1,0:T(8,128)(2,1)S(1)}, u32[]{:S(2)}, u32[]{:S(2)}) collective-permute-start(bf16[192,2048]{1,0:T(8,128)(2,1)} %collective-permute-done.13), channel_id=1, source_target_pairs={{0,2},{2,0},{4,6},{6,4},{8,10},{10,8},{12,14},{14,12},{16,18},{18,... | collective-permute-start | bytes 2359304 | tf_op jit(solution)/shard_map/ppermute | solution.py:26
  161.2 26.9 %collective-permute-start.25 = (bf16[192,2048]{1,0:T(8,128)(2,1)}, bf16[192,2048]{1,0:T(8,128)(2,1)S(1)}, u32[]{:S(2)}, u32[]{:S(2)}) collective-permute-start(bf16[192,2048]{1,0:T(8,128)(2,1)} %collective-permute-done.12), channel_id=1, source_target_pairs={{0,2},{2,0},{4,6},{6,4},{8,10},{10,8},{12,14},{14,12},{16,18},{18,... | collective-permute-start | bytes 2359304 | tf_op jit(solution)/shard_map/ppermute | solution.py:26
  162.7 16.8 %collective-permute-start.15 = (bf16[96,2048]{1,0:T(8,128)(2,1)S(1)}, bf16[96,2048]{1,0:T(8,128)(2,1)S(1)}, u32[]{:S(2)}, u32[]{:S(2)}) collective-permute-start(bf16[96,2048]{1,0:T(8,128)(2,1)S(1)} %slice.215), channel_id=1, source_target_pairs={{0,4},{2,6},{4,0},{6,2},{8,12},{10,14},{12,8},{14,10},{16,20},{18,... | collective-permute-start | bytes 1179656 | tf_op jit(solution)/shard_map/ppermute | solution.py:26
  163.1 16.4 %collective-permute-start.14 = (bf16[96,2048]{1,0:T(8,128)(2,1)S(1)}, bf16[96,2048]{1,0:T(8,128)(2,1)S(1)}, u32[]{:S(2)}, u32[]{:S(2)}) collective-permute-start(bf16[96,2048]{1,0:T(8,128)(2,1)S(1)} %slice.214), channel_id=1, source_target_pairs={{0,1},{1,0},{2,3},{3,2},{4,5},{5,4},{6,7},{7,6},{8,9},{9,8},{10,11... | collective-permute-start | bytes 1179656 | tf_op jit(solution)/shard_map/ppermute | solution.py:38
  195.5 12.0 %collective-permute-start.21 = (bf16[96,2048]{1,0:T(8,128)(2,1)S(1)}, bf16[96,2048]{1,0:T(8,128)(2,1)S(1)}, u32[]{:S(2)}, u32[]{:S(2)}) collective-permute-start(bf16[96,2048]{1,0:T(8,128)(2,1)S(1)} %slice.285), channel_id=1, source_target_pairs={{0,1},{1,0},{2,3},{3,2},{4,5},{5,4},{6,7},{7,6},{8,9},{9,8},{10,11... | collective-permute-start | bytes 1179656 | tf_op jit(solution)/shard_map/ppermute | solution.py:38
  196.3 12.0 %collective-permute-start.23 = (bf16[96,2048]{1,0:T(8,128)(2,1)S(1)}, bf16[96,2048]{1,0:T(8,128)(2,1)S(1)}, u32[]{:S(2)}, u32[]{:S(2)}) collective-permute-start(bf16[96,2048]{1,0:T(8,128)(2,1)S(1)} %slice.286), channel_id=1, source_target_pairs={{0,4},{2,6},{4,0},{6,2},{8,12},{10,14},{12,8},{14,10},{16,20},{18,... | collective-permute-start | bytes 1179656 | tf_op jit(solution)/shard_map/ppermute | solution.py:26
  197.9 17.6 %collective-permute-start.19 = (bf16[96,2048]{1,0:T(8,128)(2,1)S(1)}, bf16[96,2048]{1,0:T(8,128)(2,1)S(1)}, u32[]{:S(2)}, u32[]{:S(2)}) collective-permute-start(bf16[96,2048]{1,0:T(8,128)(2,1)S(1)} %get-tuple-element.332), channel_id=1, source_target_pairs={{0,4},{2,6},{4,0},{6,2},{8,12},{10,14},{12,8},{14,10},{16,20},{18,... | collective-permute-start | bytes 1179656 | tf_op jit(solution)/shard_map/ppermute | solution.py:26
  198.3 17.2 %collective-permute-start.18 = (bf16[96,2048]{1,0:T(8,128)(2,1)S(1)}, bf16[96,2048]{1,0:T(8,128)(2,1)S(1)}, u32[]{:S(2)}, u32[]{:S(2)}) collective-permute-start(bf16[96,2048]{1,0:T(8,128)(2,1)S(1)} %get-tuple-element.333), channel_id=1, source_target_pairs={{0,1},{1,0},{2,3},{3,2},{4,5},{5,4},{6,7},{7,6},{8,9},{9,8},{10,11... | collective-permute-start | bytes 1179656 | tf_op jit(solution)/shard_map/ppermute | solution.py:38
  228.3 17.2 %collective-permute-start.32 = (bf16[192,2048]{1,0:T(8,128)(2,1)S(1)}, bf16[192,2048]{1,0:T(8,128)(2,1)S(1)}, u32[]{:S(2)}, u32[]{:S(2)}) collective-permute-start(bf16[192,2048]{1,0:T(8,128)(2,1)S(1)} %multiply_convert_fusion.refs_0_), channel_id=1, source_target_pairs={{0,4},{2,6},{4,0},{6,2},{8,12},{10,14},{12,8},{14,10},{16,20},{18,... | collective-permute-start | bytes 2359304 | tf_op jit(solution)/shard_map/ppermute | solution.py:26
  228.7 18.3 %collective-permute-start.31 = (bf16[192,2048]{1,0:T(8,128)(2,1)S(1)}, bf16[192,2048]{1,0:T(8,128)(2,1)S(1)}, u32[]{:S(2)}, u32[]{:S(2)}) collective-permute-start(bf16[192,2048]{1,0:T(8,128)(2,1)S(1)} %multiply_convert_fusion.refs_0_), channel_id=1, source_target_pairs={{0,1},{1,0},{2,3},{3,2},{4,5},{5,4},{6,7},{7,6},{8,9},{9,8},{10,11... | collective-permute-start | bytes 2359304 | tf_op jit(solution)/shard_map/ppermute | solution.py:38
  230.1 28.6 %collective-permute-start.35 = (bf16[192,2048]{1,0:T(8,128)(2,1)S(1)}, bf16[192,2048]{1,0:T(8,128)(2,1)S(1)}, u32[]{:S(2)}, u32[]{:S(2)}) collective-permute-start(bf16[192,2048]{1,0:T(8,128)(2,1)S(1)} %multiply_convert_fusion.refs_0_), channel_id=1, source_target_pairs={{0,2},{2,0},{4,6},{6,4},{8,10},{10,8},{12,14},{14,12},{16,18},{18,... | collective-permute-start | bytes 2359304 | tf_op jit(solution)/shard_map/ppermute | solution.py:26
  247.0 11.7 %collective-permute-start.37 = (bf16[192,2048]{1,0:T(8,128)(2,1)S(1)}, bf16[192,2048]{1,0:T(8,128)(2,1)S(1)}, u32[]{:S(2)}, u32[]{:S(2)}) collective-permute-start(bf16[192,2048]{1,0:T(8,128)(2,1)S(1)} %collective-permute-done.32.refs_2_), channel_id=1, source_target_pairs={{0,2},{2,0},{4,6},{6,4},{8,10},{10,8},{12,14},{14,12},{16,18},{18,... | collective-permute-start | bytes 2359304 | tf_op jit(solution)/shard_map/ppermute | solution.py:26
  247.0 11.6 %collective-permute-start.34 = (bf16[96,2048]{1,0:T(8,128)(2,1)S(1)}, bf16[96,2048]{1,0:T(8,128)(2,1)S(1)}, u32[]{:S(2)}, u32[]{:S(2)}) collective-permute-start(bf16[96,2048]{1,0:T(8,128)(2,1)S(1)} %slice.291), channel_id=1, source_target_pairs={{0,4},{2,6},{4,0},{6,2},{8,12},{10,14},{12,8},{14,10},{16,20},{18,... | collective-permute-start | bytes 1179656 | tf_op jit(solution)/shard_map/ppermute | solution.py:26
  248.7 12.4 %collective-permute-start.36 = (bf16[192,2048]{1,0:T(8,128)(2,1)S(1)}, bf16[192,2048]{1,0:T(8,128)(2,1)}, u32[]{:S(2)}, u32[]{:S(2)}) collective-permute-start(bf16[192,2048]{1,0:T(8,128)(2,1)S(1)} %collective-permute-done.31.refs_1_), channel_id=1, source_target_pairs={{0,2},{2,0},{4,6},{6,4},{8,10},{10,8},{12,14},{14,12},{16,18},{18,... | collective-permute-start | bytes 2359304 | tf_op jit(solution)/shard_map/ppermute | solution.py:26
  301.5 264.3 %reduce-scatter.6.cloned.1.call-start = ((), (), s32[]{:S(2)}) async-start(), calls=%async_computation.13 | async-start | bytes 7864320 | tf_op jit(solution)/shard_map/reduce_scatter | solution.py:55
  366.1 20.0 %collective-permute-start.45 = (bf16[96,2048]{1,0:T(8,128)(2,1)}, bf16[96,2048]{1,0:T(8,128)(2,1)S(1)}, u32[]{:S(2)}, u32[]{:S(2)}) collective-permute-start(bf16[96,2048]{1,0:T(8,128)(2,1)} %slice.295), channel_id=1, source_target_pairs={{0,1},{1,0},{2,3},{3,2},{4,5},{5,4},{6,7},{7,6},{8,9},{9,8},{10,11... | collective-permute-start | bytes 1179656 | tf_op jit(solution)/shard_map/ppermute | solution.py:38
  367.5 18.6 %collective-permute-start.47 = (bf16[96,2048]{1,0:T(8,128)(2,1)}, bf16[96,2048]{1,0:T(8,128)(2,1)}, u32[]{:S(2)}, u32[]{:S(2)}) collective-permute-start(bf16[96,2048]{1,0:T(8,128)(2,1)} %slice.296), channel_id=1, source_target_pairs={{0,4},{2,6},{4,0},{6,2},{8,12},{10,14},{12,8},{14,10},{16,20},{18,... | collective-permute-start | bytes 1179656 | tf_op jit(solution)/shard_map/ppermute | solution.py:26
  369.9 17.2 %collective-permute-start.43 = (bf16[96,2048]{1,0:T(8,128)(2,1)}, bf16[96,2048]{1,0:T(8,128)(2,1)}, u32[]{:S(2)}, u32[]{:S(2)}) collective-permute-start(bf16[96,2048]{1,0:T(8,128)(2,1)} %get-tuple-element.330), channel_id=1, source_target_pairs={{0,4},{2,6},{4,0},{6,2},{8,12},{10,14},{12,8},{14,10},{16,20},{18,... | collective-permute-start | bytes 1179656 | tf_op jit(solution)/shard_map/ppermute | solution.py:26
  370.5 16.7 %collective-permute-start.42 = (bf16[96,2048]{1,0:T(8,128)(2,1)}, bf16[96,2048]{1,0:T(8,128)(2,1)}, u32[]{:S(2)}, u32[]{:S(2)}) collective-permute-start(bf16[96,2048]{1,0:T(8,128)(2,1)} %get-tuple-element.331), channel_id=1, source_target_pairs={{0,1},{1,0},{2,3},{3,2},{4,5},{5,4},{6,7},{7,6},{8,9},{9,8},{10,11... | collective-permute-start | bytes 1179656 | tf_op jit(solution)/shard_map/ppermute | solution.py:38
  405.0 17.5 %collective-permute-start.51 = (bf16[192,2048]{1,0:T(8,128)(2,1)S(1)}, bf16[192,2048]{1,0:T(8,128)(2,1)}, u32[]{:S(2)}, u32[]{:S(2)}) collective-permute-start(bf16[192,2048]{1,0:T(8,128)(2,1)S(1)} %get-tuple-element.288.refs_0_), channel_id=1, source_target_pairs={{0,4},{2,6},{4,0},{6,2},{8,12},{10,14},{12,8},{14,10},{16,20},{18,... | collective-permute-start | bytes 2359304 | tf_op jit(solution)/shard_map/ppermute | solution.py:26
  405.6 17.2 %collective-permute-start.50 = (bf16[192,2048]{1,0:T(8,128)(2,1)S(1)}, bf16[192,2048]{1,0:T(8,128)(2,1)}, u32[]{:S(2)}, u32[]{:S(2)}) collective-permute-start(bf16[192,2048]{1,0:T(8,128)(2,1)S(1)} %get-tuple-element.288.refs_0_), channel_id=1, source_target_pairs={{0,1},{1,0},{2,3},{3,2},{4,5},{5,4},{6,7},{7,6},{8,9},{9,8},{10,11... | collective-permute-start | bytes 2359304 | tf_op jit(solution)/shard_map/ppermute | solution.py:38
  421.5 19.6 %collective-permute-start.54 = (bf16[192,2048]{1,0:T(8,128)(2,1)S(1)}, bf16[192,2048]{1,0:T(8,128)(2,1)}, u32[]{:S(2)}, u32[]{:S(2)}) collective-permute-start(bf16[192,2048]{1,0:T(8,128)(2,1)S(1)} %get-tuple-element.288.refs_0_), channel_id=1, source_target_pairs={{0,2},{2,0},{4,6},{6,4},{8,10},{10,8},{12,14},{14,12},{16,18},{18,... | collective-permute-start | bytes 2359304 | tf_op jit(solution)/shard_map/ppermute | solution.py:26
  423.8 10.4 %collective-permute-start.52 = (bf16[96,2048]{1,0:T(8,128)(2,1)S(1)}, bf16[96,2048]{1,0:T(8,128)(2,1)S(1)}, u32[]{:S(2)}, u32[]{:S(2)}) collective-permute-start(bf16[96,2048]{1,0:T(8,128)(2,1)S(1)} %slice.243), channel_id=1, source_target_pairs={{0,1},{1,0},{2,3},{3,2},{4,5},{5,4},{6,7},{7,6},{8,9},{9,8},{10,11... | collective-permute-start | bytes 1179656 | tf_op jit(solution)/shard_map/ppermute | solution.py:38
  425.5 11.1 %collective-permute-start.53 = (bf16[96,2048]{1,0:T(8,128)(2,1)S(1)}, bf16[96,2048]{1,0:T(8,128)(2,1)}, u32[]{:S(2)}, u32[]{:S(2)}) collective-permute-start(bf16[96,2048]{1,0:T(8,128)(2,1)S(1)} %slice.244), channel_id=1, source_target_pairs={{0,4},{2,6},{4,0},{6,2},{8,12},{10,14},{12,8},{14,10},{16,20},{18,... | collective-permute-start | bytes 1179656 | tf_op jit(solution)/shard_map/ppermute | solution.py:26
  427.0 14.7 %collective-permute-start.55 = (bf16[192,2048]{1,0:T(8,128)(2,1)}, bf16[192,2048]{1,0:T(8,128)(2,1)}, u32[]{:S(2)}, u32[]{:S(2)}) collective-permute-start(bf16[192,2048]{1,0:T(8,128)(2,1)} %collective-permute-done.50.refs_1_), channel_id=1, source_target_pairs={{0,2},{2,0},{4,6},{6,4},{8,10},{10,8},{12,14},{14,12},{16,18},{18,... | collective-permute-start | bytes 2359304 | tf_op jit(solution)/shard_map/ppermute | solution.py:26
  441.1 13.0 %collective-permute-start.59 = (bf16[192,2048]{1,0:T(8,128)(2,1)}, bf16[192,2048]{1,0:T(8,128)(2,1)S(1)}, u32[]{:S(2)}, u32[]{:S(2)}) collective-permute-start(bf16[192,2048]{1,0:T(8,128)(2,1)} %get-tuple-element.190), channel_id=1, source_target_pairs={{0,2},{2,0},{4,6},{6,4},{8,10},{10,8},{12,14},{14,12},{16,18},{18,... | collective-permute-start | bytes 2359304 | tf_op jit(solution)/shard_map/ppermute | solution.py:26
  441.1 13.0 %collective-permute-start.60 = (bf16[192,2048]{1,0:T(8,128)(2,1)}, bf16[192,2048]{1,0:T(8,128)(2,1)S(1)}, u32[]{:S(2)}, u32[]{:S(2)}) collective-permute-start(bf16[192,2048]{1,0:T(8,128)(2,1)} %get-tuple-element.191), channel_id=1, source_target_pairs={{0,2},{2,0},{4,6},{6,4},{8,10},{10,8},{12,14},{14,12},{16,18},{18,... | collective-permute-start | bytes 2359304 | tf_op jit(solution)/shard_map/ppermute | solution.py:26
  441.6 12.5 %collective-permute-start.61 = (bf16[192,2048]{1,0:T(8,128)(2,1)}, bf16[192,2048]{1,0:T(8,128)(2,1)S(1)}, u32[]{:S(2)}, u32[]{:S(2)}) collective-permute-start(bf16[192,2048]{1,0:T(8,128)(2,1)} %get-tuple-element.192), channel_id=1, source_target_pairs={{0,2},{2,0},{4,6},{6,4},{8,10},{10,8},{12,14},{14,12},{16,18},{18,... | collective-permute-start | bytes 2359304 | tf_op jit(solution)/shard_map/ppermute | solution.py:26
  441.7 14.2 %collective-permute-start.62 = (bf16[192,2048]{1,0:T(8,128)(2,1)}, bf16[192,2048]{1,0:T(8,128)(2,1)}, u32[]{:S(2)}, u32[]{:S(2)}) collective-permute-start(bf16[192,2048]{1,0:T(8,128)(2,1)} %get-tuple-element.193), channel_id=1, source_target_pairs={{0,2},{2,0},{4,6},{6,4},{8,10},{10,8},{12,14},{14,12},{16,18},{18,... | collective-permute-start | bytes 2359304 | tf_op jit(solution)/shard_map/ppermute | solution.py:26
  458.9 16.4 %collective-permute-start.66 = (bf16[96,2048]{1,0:T(8,128)(2,1)S(1)}, bf16[96,2048]{1,0:T(8,128)(2,1)S(1)}, u32[]{:S(2)}, u32[]{:S(2)}) collective-permute-start(bf16[96,2048]{1,0:T(8,128)(2,1)S(1)} %slice.253), channel_id=1, source_target_pairs={{0,4},{2,6},{4,0},{6,2},{8,12},{10,14},{12,8},{14,10},{16,20},{18,... | collective-permute-start | bytes 1179656 | tf_op jit(solution)/shard_map/ppermute | solution.py:26
  460.0 15.2 %collective-permute-start.65 = (bf16[96,2048]{1,0:T(8,128)(2,1)S(1)}, bf16[96,2048]{1,0:T(8,128)(2,1)}, u32[]{:S(2)}, u32[]{:S(2)}) collective-permute-start(bf16[96,2048]{1,0:T(8,128)(2,1)S(1)} %slice.252), channel_id=1, source_target_pairs={{0,1},{1,0},{2,3},{3,2},{4,5},{5,4},{6,7},{7,6},{8,9},{9,8},{10,11... | collective-permute-start | bytes 1179656 | tf_op jit(solution)/shard_map/ppermute | solution.py:38
  460.6 17.7 %collective-permute-start.64 = (bf16[96,2048]{1,0:T(8,128)(2,1)S(1)}, bf16[96,2048]{1,0:T(8,128)(2,1)}, u32[]{:S(2)}, u32[]{:S(2)}) collective-permute-start(bf16[96,2048]{1,0:T(8,128)(2,1)S(1)} %get-tuple-element.328), channel_id=1, source_target_pairs={{0,4},{2,6},{4,0},{6,2},{8,12},{10,14},{12,8},{14,10},{16,20},{18,... | collective-permute-start | bytes 1179656 | tf_op jit(solution)/shard_map/ppermute | solution.py:26
  461.2 18.1 %collective-permute-start.63 = (bf16[96,2048]{1,0:T(8,128)(2,1)S(1)}, bf16[96,2048]{1,0:T(8,128)(2,1)}, u32[]{:S(2)}, u32[]{:S(2)}) collective-permute-start(bf16[96,2048]{1,0:T(8,128)(2,1)S(1)} %get-tuple-element.329), channel_id=1, source_target_pairs={{0,1},{1,0},{2,3},{3,2},{4,5},{5,4},{6,7},{7,6},{8,9},{9,8},{10,11... | collective-permute-start | bytes 1179656 | tf_op jit(solution)/shard_map/ppermute | solution.py:38
  479.3 51.5 %all-to-all-start.3 = ((bf16[4,128,1536]{2,1,0:T(8,128)(2,1)}), bf16[4,128,1536]{2,1,0:T(8,128)(2,1)}, u32[]{:S(2)}, u32[]{:S(2)}) async-start(bf16[4,128,1536]{2,1,0:T(8,128)(2,1)} %bitcast.52), calls=%async_computation.4 | async-start | bytes 3145728 | tf_op jit(solution)/shard_map/all_to_all | solution.py:145
  483.7 155.9 %reduce-scatter.8.cloned.1.call-start = ((), (), s32[]{:S(2)}) async-start(), calls=%async_computation.14 | async-start | bytes 3276800 | tf_op jit(solution)/shard_map/reduce_scatter | solution.py:55
  487.6 35.2 %collective-permute-start.70 = (bf16[768,128]{1,0:T(8,128)(2,1)S(1)}, bf16[768,128]{1,0:T(8,128)(2,1)S(1)}, u32[]{:S(2)}, u32[]{:S(2)}) collective-permute-start(bf16[768,128]{1,0:T(8,128)(2,1)S(1)} %copy-done.55), channel_id=1, source_target_pairs={{16,0},{18,2},{20,4},{22,6},{24,8},{26,10},{28,12},{30,14},{17,1},... | collective-permute-start | bytes 589832 | tf_op jit(solution)/shard_map/ppermute | solution.py:60
  488.9 123.4 %collective-permute-start.67 = (bf16[96,2048]{1,0:T(8,128)(2,1)}, bf16[96,2048]{1,0:T(8,128)(2,1)}, u32[]{:S(2)}, u32[]{:S(2)}) collective-permute-start(bf16[96,2048]{1,0:T(8,128)(2,1)} %add_convert_fusion.19), channel_id=1, source_target_pairs={{0,4},{2,6},{4,0},{6,2},{8,12},{10,14},{12,8},{14,10},{16,20},{18,... | collective-permute-start | bytes 1179656 | tf_op jit(solution)/shard_map/ppermute | solution.py:26
  490.9 39.9 %collective-permute-start.69 = (bf16[1536,128]{1,0:T(8,128)(2,1)S(1)}, bf16[1536,128]{1,0:T(8,128)(2,1)S(1)}, u32[]{:S(2)}, u32[]{:S(2)}) collective-permute-start(bf16[1536,128]{1,0:T(8,128)(2,1)S(1)} %copy-done.50), channel_id=1, source_target_pairs={{8,0},{10,2},{12,4},{14,6},{16,8},{18,10},{20,12},{22,14},{24,16},... | collective-permute-start | bytes 1179656 | tf_op jit(solution)/shard_map/ppermute | solution.py:60
  549.1 22.7 %collective-permute-start.71 = (bf16[192,2048]{1,0:T(8,128)(2,1)}, bf16[192,2048]{1,0:T(8,128)(2,1)S(1)}, u32[]{:S(2)}, u32[]{:S(2)}) collective-permute-start(bf16[192,2048]{1,0:T(8,128)(2,1)} %get-tuple-element.225), channel_id=1, source_target_pairs={{0,2},{2,0},{4,6},{6,4},{8,10},{10,8},{12,14},{14,12},{16,18},{18,... | collective-permute-start | bytes 2359304 | tf_op jit(solution)/shard_map/ppermute | solution.py:26
  549.1 24.2 %collective-permute-start.72 = (bf16[192,2048]{1,0:T(8,128)(2,1)}, bf16[192,2048]{1,0:T(8,128)(2,1)}, u32[]{:S(2)}, u32[]{:S(2)}) collective-permute-start(bf16[192,2048]{1,0:T(8,128)(2,1)} %get-tuple-element.226), channel_id=1, source_target_pairs={{0,2},{2,0},{4,6},{6,4},{8,10},{10,8},{12,14},{14,12},{16,18},{18,... | collective-permute-start | bytes 2359304 | tf_op jit(solution)/shard_map/ppermute | solution.py:26
  549.6 23.7 %collective-permute-start.75 = (bf16[192,2048]{1,0:T(8,128)(2,1)}, bf16[192,2048]{1,0:T(8,128)(2,1)}, u32[]{:S(2)}, u32[]{:S(2)}) collective-permute-start(bf16[192,2048]{1,0:T(8,128)(2,1)} %get-tuple-element.227), channel_id=1, source_target_pairs={{0,2},{2,0},{4,6},{6,4},{8,10},{10,8},{12,14},{14,12},{16,18},{18,... | collective-permute-start | bytes 2359304 | tf_op jit(solution)/shard_map/ppermute | solution.py:26
  549.7 23.7 %collective-permute-start.77 = (bf16[192,2048]{1,0:T(8,128)(2,1)}, bf16[192,2048]{1,0:T(8,128)(2,1)}, u32[]{:S(2)}, u32[]{:S(2)}) collective-permute-start(bf16[192,2048]{1,0:T(8,128)(2,1)} %get-tuple-element.228), channel_id=1, source_target_pairs={{0,2},{2,0},{4,6},{6,4},{8,10},{10,8},{12,14},{14,12},{16,18},{18,... | collective-permute-start | bytes 2359304 | tf_op jit(solution)/shard_map/ppermute | solution.py:26
  565.9 25.2 %all-to-all-start.4 = ((bf16[4,128,1536]{2,1,0:T(8,128)(2,1)}), bf16[4,128,1536]{2,1,0:T(8,128)(2,1)}, u32[]{:S(2)}, u32[]{:S(2)}) async-start(bf16[4,128,1536]{2,1,0:T(8,128)(2,1)} %bitcast.51), calls=%async_computation.6 | async-start | bytes 3145728 | tf_op jit(solution)/shard_map/all_to_all | solution.py:145
  571.8 40.5 %collective-permute-start.68 = (bf16[96,2048]{1,0:T(8,128)(2,1)}, bf16[96,2048]{1,0:T(8,128)(2,1)}, u32[]{:S(2)}, u32[]{:S(2)}) collective-permute-start(bf16[96,2048]{1,0:T(8,128)(2,1)} %add_convert_fusion.18), channel_id=1, source_target_pairs={{0,1},{1,0},{2,3},{3,2},{4,5},{5,4},{6,7},{7,6},{8,9},{9,8},{10,11... | collective-permute-start | bytes 1179656 | tf_op jit(solution)/shard_map/ppermute | solution.py:38
  579.4 14.2 %collective-permute-start.76 = (bf16[96,2048]{1,0:T(8,128)(2,1)}, bf16[96,2048]{1,0:T(8,128)(2,1)}, u32[]{:S(2)}, u32[]{:S(2)}) collective-permute-start(bf16[96,2048]{1,0:T(8,128)(2,1)} %slice.305), channel_id=1, source_target_pairs={{0,1},{1,0},{2,3},{3,2},{4,5},{5,4},{6,7},{7,6},{8,9},{9,8},{10,11... | collective-permute-start | bytes 1179656 | tf_op jit(solution)/shard_map/ppermute | solution.py:38
  582.0 22.3 %collective-permute-start.78 = (bf16[96,2048]{1,0:T(8,128)(2,1)}, bf16[96,2048]{1,0:T(8,128)(2,1)}, u32[]{:S(2)}, u32[]{:S(2)}) collective-permute-start(bf16[96,2048]{1,0:T(8,128)(2,1)} %slice.306), channel_id=1, source_target_pairs={{0,4},{2,6},{4,0},{6,2},{8,12},{10,14},{12,8},{14,10},{16,20},{18,... | collective-permute-start | bytes 1179656 | tf_op jit(solution)/shard_map/ppermute | solution.py:26
  584.0 23.5 %collective-permute-start.74 = (bf16[96,2048]{1,0:T(8,128)(2,1)}, bf16[96,2048]{1,0:T(8,128)(2,1)}, u32[]{:S(2)}, u32[]{:S(2)}) collective-permute-start(bf16[96,2048]{1,0:T(8,128)(2,1)} %get-tuple-element.326), channel_id=1, source_target_pairs={{0,4},{2,6},{4,0},{6,2},{8,12},{10,14},{12,8},{14,10},{16,20},{18,... | collective-permute-start | bytes 1179656 | tf_op jit(solution)/shard_map/ppermute | solution.py:26
  593.6 13.8 %collective-permute-start.73 = (bf16[96,2048]{1,0:T(8,128)(2,1)}, bf16[96,2048]{1,0:T(8,128)(2,1)}, u32[]{:S(2)}, u32[]{:S(2)}) collective-permute-start(bf16[96,2048]{1,0:T(8,128)(2,1)} %get-tuple-element.327), channel_id=1, source_target_pairs={{0,1},{1,0},{2,3},{3,2},{4,5},{5,4},{6,7},{7,6},{8,9},{9,8},{10,11... | collective-permute-start | bytes 1179656 | tf_op jit(solution)/shard_map/ppermute | solution.py:38
  618.3 10.5 %collective-permute-start.83 = (f32[4224]{0:T(1024)S(1)}, f32[4224]{0:T(1024)S(1)}, u32[]{:S(2)}, u32[]{:S(2)}) collective-permute-start(f32[4224]{0:T(1024)S(1)} %add.278), channel_id=1, source_target_pairs={{0,8},{2,10},{4,12},{6,14},{8,0},{10,2},{12,4},{14,6},{16,24},{18,... | collective-permute-start | bytes 50696 | tf_op jit(solution)/shard_map/ppermute | solution.py:26
  641.8 13.7 %all-to-all-start.5 = ((bf16[4,128,640]{1,2,0:T(8,128)(2,1)}), bf16[4,128,640]{1,2,0:T(8,128)(2,1)S(1)}, u32[]{:S(2)}, u32[]{:S(2)}) async-start(bf16[4,128,640]{1,2,0:T(8,128)(2,1)} %copy.62), calls=%async_computation.8 | async-start | bytes 1310720 | tf_op jit(solution)/shard_map/all_to_all | solution.py:145
  (88 other events, 526.7 us)
Sparse Core Ops, SparseCore 0:
  24.6 55.9 all-gather.3
  82.2 122.4 all-gather.5
  206.8 121.7 all-gather.7
  330.8 108.9 reduce-scatter.3
  442.0 123.8 reduce-scatter.5
  568.0 55.4 reduce-scatter.7

commit v4 on v3

--- a/solution.py
+++ b/solution.py
@@ -126,6 +126,15 @@
         )
 
 
+    def second_x(self):
+        self.got = swap_x(self.parts[0])
+
+    def third_x(self, beside):
+        _, for_x, for_b, own = self.parts
+        for_b, for_x, beside = tie(add16(for_b, self.got), for_x, beside)
+        return own.astype(F32) + swap_x(for_x).astype(F32) + swap_b(for_b).astype(F32), beside
+
+
 def scatter_rows(near, far, beside=None):
     sums = Sums(near, far)
     sums.second()
@@ -145,9 +154,8 @@
     return lax.all_to_all(pieces, "ctx", axis, axis, axis_index_groups=groups, tiled=True)
 
 
-def sum_over_ctx(value):
-    bit = 1
-    while bit < lax.axis_size("ctx"):
+def sum_over_ctx(value, bit, end):
+    while bit < end:
         value = value + swap_ctx(value, bit)
         bit *= 2
     return value
@@ -536,6 +544,37 @@
     )
 
 
+def unpack_kernel(*refs, flip, cuts):
+    blocks, outs = refs[: len(cuts)], refs[len(cuts) :]
+    for block, (low, high) in zip(blocks, cuts):
+        at = 0
+        for ref, turned in zip(outs, flip):
+            width = (ref.shape[0] if turned else ref.shape[1]) // QUAD
+            start, end = low * width // high[1], high[0] * width // high[1]
+            for quarter in range(QUAD):
+                part = block[quarter, :, at : at + end - start].astype(F32)
+                cut = slice(quarter * width + start, quarter * width + end)
+                if turned:
+                    ref[cut, :] = jnp.transpose(part)
+                else:
+                    ref[:, cut] = part
+            at += end - start
+
+
+def unpacked(blocks, shapes, flip, cuts):
+    return call(
+        functools.partial(unpack_kernel, flip=flip, cuts=cuts),
+        1,
+        0,
+        [whole_block(v) for v in blocks],
+        [(shape, F32, whole_block(jax.ShapeDtypeStruct(shape, F32))) for shape in shapes],
+        [],
+        tuple(blocks),
+        1,
+        sum(6 * math.prod(v.shape) for v in blocks),
+    )
+
+
 def weights_kernel(a_ref, b_ref, c_ref, d_ref, *refs):
     out_ref = refs[-1]
     cols = b_ref.shape[1]
@@ -544,7 +583,11 @@
     out_ref[:, cols:] = dot_tn(c_ref[...], d_ref[...]).astype(BF16)
     if len(refs) > 1:
         w_ref, sums_ref = refs[:2]
-        sums_ref[...] = jnp.sum(first * w_ref[...].astype(F32), axis=1, keepdims=True)
+        both = first * w_ref[...].astype(F32)
+        high = both.astype(BF16)
+        low = (both - high.astype(F32)).astype(BF16)
+        ones = jnp.ones((sums_ref.shape[0], cols), BF16)
+        sums_ref[...] = dot_nt(ones, high) + dot_nt(ones, low)
 
 
 def weight_grads(a, b, c, d, w=None, rows=512):
@@ -564,7 +607,7 @@
         model // rows,
         0,
         [cut, whole(b), cut, whole(d)] + [tall(v.shape[1]) for v in more],
-        [((model, 1), F32, tall(1))] * len(more) + [((model, cols), BF16, tall(cols))],
+        [((8, model), F32, pl.BlockSpec((8, rows), lambda t: (0, t)))] * len(more) + [((model, cols), BF16, tall(cols))],
         [],
         (a, b, c, d, *more),
         2 * total * model * cols,
@@ -628,7 +671,8 @@
     scale_1 = rms_scale(x_own)
 
     cut = FIRST_BLOCK
-    ffn_pieces = packed((w_gate, w_up, w_down), (0, 0, 1), [(0, (cut, 8)), (cut, (8, 8))])
+    ffn_cuts = [(0, (cut, 8)), (cut, (8, 8))]
+    ffn_pieces = packed((w_gate, w_up, w_down), (0, 0, 1), ffn_cuts)
     a_own = (x_own * scale_1 * attn_gain).astype(BF16)
     a_near = (swap_x(a_own), swap_b(a_own), swap_both(a_own))
 
@@ -753,7 +797,7 @@
     ffn_sum = Sums(*down)
 
     def home(grad):
-        return spread(grad.reshape(QUAD, step // QUAD, -1)).transpose(1, 0, 2)
+        return spread(grad.reshape(QUAD, step // QUAD, -1))
 
     d_h_rows, d_o = call(
         rows_dot_kernel,
@@ -826,30 +870,32 @@
     d_raw, one = tie(d_raw, one)
     one = Sums(*one)
     gain_sums, attn_grad = weight_grads(a_one, d_raw, d_h_rows, o, w_qkv)
+    gain_sums = gain_sums[0]
     attn_grad = line_scatter(attn_grad, n)
+    gain_sums, ffn_grad_1 = tie(gain_sums, ffn_grad_1)
+    one.second_x()
+    back_1 = home(ffn_grad_1)
+    d_one, back_1 = one.third_x(back_1)
+    ffn_outs = unpacked((back_0, back_1), [v.shape for v in (w_gate, w_up, w_down)], (0, 0, 1), ffn_cuts)
+    d_one, ffn_outs, gain_sums, ffn_sum.got = tie(d_one, ffn_outs, gain_sums, ffn_sum.got)
+    d_attn_gain = gain_sums / gain_1
+    d_q_gain = d_head_gains[0, :width] + d_head_gains[0, width:]
+    gains = jnp.concatenate([d_attn_gain, d_ffn_gain, d_q_gain, d_head_gains[1, :width]])
+    gains = sum_over_ctx(gains + swap_x(gains), 1, QUAD)
+    d_x, _ = norm_back(x_own, scale_1, gain_1, d_one)
+    d_tokens = d_h + d_x
     out_tokens = (resid + ffn_sum.third()).astype(BF16)
-    back_1 = home(ffn_grad_1)
-
-    def joined(part):
-        cols = [jnp.split(v, 3, axis=-1)[part] for v in (back_0, back_1)]
-        return jnp.concatenate(cols, axis=-1).reshape(step // QUAD, -1).astype(F32)
-
-    ffn_outs = (joined(0), joined(1), joined(2).T)
-    one.second()
-    one.got, ffn_outs, gain_sums = tie(one.got, ffn_outs, gain_sums)
-    d_attn_gain = gain_sums[:, 0] / gain_1
-    d_q_gain = d_head_gains[0, :width] + d_head_gains[0, width:]
-    gains = sum_over_ctx(jnp.concatenate([d_attn_gain, d_ffn_gain, d_q_gain, d_head_gains[1, :width]]))
-    d_x, _ = norm_back(x_own, scale_1, gain_1, one.third())
-    d_tokens = d_h + d_x
-
+
+    attn_grad, back_1 = tie(attn_grad, back_1)
     attn_back = home(attn_grad)
     attn_back, gains = tie(attn_back, gains)
-    gains = gains + swap_x(gains)
-
-    def piece(start, size):
-        return attn_back[:, :, start : start + size].reshape(step // QUAD, -1).astype(F32)
-
+    gains = sum_over_ctx(gains, QUAD, QUAD * n)
+    attn_outs = unpacked(
+        [attn_back],
+        [v.shape for v in (w_query, key_projection, value_projection, w_out)],
+        (0, 0, 0, 1),
+        [(0, (1, 1))],
+    )
     return (
         out_tokens,
         d_tokens,
@@ -857,10 +903,7 @@
         gains[model : 2 * model],
         gains[2 * model : 2 * model + width],
         gains[2 * model + width :],
-        piece(0, qw),
-        piece(qw, width),
-        piece(qw + width, width),
-        piece(qw + 2 * width, qw).T,
+        *attn_outs,
         *ffn_outs,
     )
 

time: 678 us -> 678 us (level)
  local copies, waits for them, and re-layouts: 63 us -> 44.2 us
  waiting for transfers between devices: 179 us -> 193 us
  Pallas kernels: 225 us -> 233 us
    ppermute x20 -> x19, waiting for transfers between devices: 23.1 us -> 43 us  [swap_x(): return lax.ppermute(value, 'tp', [(0, 1), (1, 0)])]
    all_to_all x4, waiting for transfers between devices: 14.3 us -> 5.19 us  [spread(): lax.all_to_all(pieces, 'ctx', axis, axis, axis_index_groups=groups, tiled...]
    pallas_call x17 -> x19, Pallas kernels: 225 us -> 233 us  [call(): pl.pallas_call(kernel, out_shape=[jax.ShapeDtypeStruct(shape, dtype) for...]
    ppermute x61 -> x59, starting transfers between devices: 37.9 us -> 44.3 us  [swap_ctx(): return lax.ppermute(value, 'ctx', [(i, i ^ bit) for i in range(n)])]
    unnamed x128 -> x107, local copies, waits for them, and re-layouts: 24.4 us -> 19.7 us
    ppermute x61 -> x59, waiting for transfers between devices: 88 us -> 85.2 us  [swap_ctx(): return lax.ppermute(value, 'ctx', [(i, i ^ bit) for i in range(n)])]
    ppermute x20 -> x19, starting transfers between devices: 20.6 us -> 20 us  [swap_x(): return lax.ppermute(value, 'tp', [(0, 1), (1, 0)])]
    convert_element_type x12 -> x11, other arithmetic: 22.5 us -> 22.3 us  [add16(): return (a.astype(F32) + b.astype(F32)).astype(BF16)]
  transfers between devices with their start and end apart: 96 -> 93, of which waited for: 37 -> 37; matrix products, arithmetic and copies ran while one was open for 16% -> 13% of each run, Pallas kernels for 33% -> 34%
where the time goes in v4:
time: 678 us; the launch traced here: 672 us
  Pallas kernels  233 us (34%)
  waiting for transfers between devices  193 us (28%)
  starting transfers between devices  94.1 us (14%)
  other arithmetic  52.7 us (8%)
  local copies, waits for them, and re-layouts  44.2 us (7%)
  blocking collectives  39.6 us (6%)
  between operations  15.3 us (2%)
    pallas_call x19, Pallas kernels, call(): pl.pallas_call(kernel, out_shape=[jax.ShapeDtypeStruct(shape, dtype) for...  233 us
    ppermute x59, waiting for transfers between devices, swap_ctx(): return lax.ppermute(value, 'ctx', [(i, i ^ bit) for i in range(n)])  85.2 us
    ppermute x59, starting transfers between devices, swap_ctx(): return lax.ppermute(value, 'ctx', [(i, i ^ bit) for i in range(n)])  44.3 us
    ppermute x19, waiting for transfers between devices, swap_x(): return lax.ppermute(value, 'tp', [(0, 1), (1, 0)])  43 us
    all_to_all x2, blocking collectives, spread(): lax.all_to_all(pieces, 'ctx', axis, axis, axis_index_groups=groups, tiled...  39.6 us
    all_gather x3, waiting for transfers between devices, line_gather(): lax.all_gather(own, 'ctx', axis=0, axis_index_groups=line_groups(n), tile...  27.5 us
    convert_element_type x11, other arithmetic, add16(): return (a.astype(F32) + b.astype(F32)).astype(BF16)  22.3 us
    ppermute x19, starting transfers between devices, swap_x(): return lax.ppermute(value, 'tp', [(0, 1), (1, 0)])  20 us
  transfers between devices with their start and end apart: 93, of which 37 were waited for; matrix products, arithmetic and copies ran while one was open for 13% of the time, Pallas kernels for 34%

profile of v4, /device:TPU:0, one launch (start us, length us, event | category | flops | bytes accessed | tf_op | source)
XLA Modules:
  0.0 671.7 jit_solution(14615509770834616468)
XLA Ops:
  7.2 2.1 shard_map.237
  9.4 15.1 %all_to_all.30 = bf16[4,128,640]{2,1,0:T(8,128)(2,1)} all-to-all(bf16[4,128,640]{2,1,0:T(8,128)(2,1)} %shard_map.237), channel_id=1, replica_groups={{0,2,4,6},{8,10,12,14},{16,18,20,22},{24,26,28,30},{1,3,5,7},{9,11,13,1..., dimensions={0} | all-to-all | bytes 1310720 | tf_op jit(solution)/shard_map/all_to_all | solution.py:154
  24.6 3.9 shard_map.238
  28.4 24.5 %all_to_all.31 = bf16[4,128,1536]{2,1,0:T(8,128)(2,1)} all-to-all(bf16[4,128,1536]{2,1,0:T(8,128)(2,1)} %get-tuple-element.146), channel_id=1, replica_groups={{0,2,4,6},{8,10,12,14},{16,18,20,22},{24,26,28,30},{1,3,5,7},{9,11,13,1..., dimensions={0} | all-to-all | bytes 3145728 | tf_op jit(solution)/shard_map/all_to_all | solution.py:154
  59.0 2.1 collective-permute-start.5
  62.8 2.8 fusion.18
  65.6 2.5 pad_maximum_fusion.1
  68.1 12.2 %collective-permute-done.5.refs_3_ = bf16[192,2048]{1,0:T(8,128)(2,1)S(1)} collective-permute-done((bf16[192,2048]{1,0:T(8,128)(2,1)S(1)}, bf16[192,2048]{1,0:T(8,128)(2,1)S(1)}, u32[]{:S(2)}, u32[]{:S(2)}) %collective-permute-start.5) | collective-permute-done | bytes 786464 | tf_op jit(solution)/shard_map/ppermute | solution.py:73
  80.4 16.0 %collective-permute-done.4.refs_2_ = bf16[192,2048]{1,0:T(8,128)(2,1)S(1)} collective-permute-done((bf16[192,2048]{1,0:T(8,128)(2,1)S(1)}, bf16[192,2048]{1,0:T(8,128)(2,1)S(1)}, u32[]{:S(2)}, u32[]{:S(2)}) %collective-permute-start.4) | collective-permute-done | bytes 786464 | tf_op jit(solution)/shard_map/ppermute | solution.py:26
  97.5 3.6 all-to-all-start.2
  104.1 2.4 broadcast_subtract_fusion
  106.5 2.7 slice.236.refs_8_.w_ref.refs_0_
  109.2 14.2 %shard_map.239 = (bf16[1536,2048]{1,0:T(8,128)(2,1)}, f32[1536,384]{1,0:T(8,128)}, bf16[1536,256]{1,0:T(8,128)(2,1)}, bf16[1536,128]{1,0:T(8,128)(2,1)}) custom-call(s32[8]{0:T(128)} %or_or_fusion.table, bf16[192,2048]{1,0:T(8,128)(2,1)} %copy-done.5, bf16[192,2048]{1,0:T(8,128)(2,1)} %copy-done.15, bf16[192,2048]{1,0:T(8,128)(2,1)} %copy-done.14, ...), custom_call_target="tpu_custom_call" | custom-call | flops 2415919104 | bytes 16515072 | tf_op jit(solution)/shard_map/pallas_call | solution.py:619
  128.9 3.5 collective-permute-start.10
  132.5 5.1 collective-permute-start.11
  137.8 14.0 %shard_map.240.refs_0_ = f32[6144,128]{1,0:T(8,128)} custom-call(s32[8]{0:T(128)} %or_or_fusion.1.table, s32[8]{0:T(128)} %get-tuple-element.282.lo, s32[8]{0:T(128)} %get-tuple-element.281.hi, bf16[1536,256]{1,0:T(8,128)(2,1)} %get-tuple-element.156.q_ref, s32[1536,1]{1,0:T(8,128)} %get-tuple-element.311.start_ref, bf16[1536,128]{1,0:T(8,128)(2,1)} %get-tuple-element.157.kv_ref), custom_call_target="tpu_custom_call" | custom-call | flops 4831838208 | bytes 3932160 | tf_op jit(solution)/shard_map/pallas_call | solution.py:619
  151.8 2.3 slice.237.w_ref.refs_10_
  154.1 4.4 collective-permute-done.11
  166.5 2.5 copy-done.23
  169.8 9.2 %shard_map.241 = (bf16[1536,256]{1,0:T(8,128)(2,1)}, f32[1536,256]{1,0:T(8,128)}, f32[6144,1]{1,0:T(8,128)}) custom-call(s32[8]{0:T(128)} %or_or_fusion.1.table, s32[8]{0:T(128)} %get-tuple-element.284.lo, s32[8]{0:T(128)} %get-tuple-element.283.hi, bf16[1536,256]{1,0:T(8,128)(2,1)} %get-tuple-element.156.q_ref, s32[1536,1]{1,0:T(8,128)} %get-tuple-element.312.start_ref, ...), custom_call_target="tpu_custom_call" | custom-call | flops 4831838208 | bytes 3932160 | tf_op jit(solution)/shard_map/pallas_call | solution.py:619
  179.0 7.2 %shard_map.242 = (bf16[768,2048]{1,0:T(8,128)(2,1)}, bf16[192,2048]{1,0:T(8,128)(2,1)}, bf16[192,2048]{1,0:T(8,128)(2,1)}, bf16[192,2048]{1,0:T(8,128)(2,1)}, bf16[192,2048]{1,0:T(8,128)(2,1)}) custom-call(bf16[1536,256]{1,0:T(8,128)(2,1)} %get-tuple-element.165.a_ref.d_ref, bf16[2048,256]{1,0:T(8,128)(2,1)} %slice.237.w_ref.refs_10_), custom_call_target="tpu_custom_call" | custom-call | flops 1610612736 | bytes 7077888 | tf_op jit(solution)/shard_map/pallas_call | solution.py:619
  188.8 2.1 constant_dynamic-update-slice_fusion.6
  200.7 6.3 collective-permute-done.21
  207.8 7.2 %collective-permute-done.19 = bf16[96,2048]{1,0:T(8,128)(2,1)S(1)} collective-permute-done((bf16[96,2048]{1,0:T(8,128)(2,1)S(1)}, bf16[96,2048]{1,0:T(8,128)(2,1)S(1)}, u32[]{:S(2)}, u32[]{:S(2)}) %collective-permute-start.19) | collective-permute-done | bytes 393248 | tf_op jit(solution)/shard_map/ppermute | solution.py:26
  218.3 6.9 %collective-permute-done.29 = bf16[96,2048]{1,0:T(8,128)(2,1)S(1)} collective-permute-done((bf16[96,2048]{1,0:T(8,128)(2,1)S(1)}, bf16[96,2048]{1,0:T(8,128)(2,1)S(1)}, u32[]{:S(2)}, u32[]{:S(2)}) %collective-permute-start.29) | collective-permute-done | bytes 393248 | tf_op jit(solution)/shard_map/ppermute | solution.py:26
  229.6 15.5 %collective-permute-done.32.refs_2_ = bf16[192,2048]{1,0:T(8,128)(2,1)S(1)} collective-permute-done((bf16[192,2048]{1,0:T(8,128)(2,1)S(1)}, bf16[192,2048]{1,0:T(8,128)(2,1)S(1)}, u32[]{:S(2)}, u32[]{:S(2)}) %collective-permute-start.32) | collective-permute-done | bytes 786464 | tf_op jit(solution)/shard_map/ppermute | solution.py:26
  248.3 5.5 collective-permute-done.33.refs_3_
  253.8 4.4 collective-permute-done.34.refs_4_
  260.7 24.8 %shard_map.243 = (bf16[1536,512]{1,0:T(8,128)(2,1)}, bf16[1536,1024]{1,0:T(8,128)(2,1)}, bf16[1536,2048]{1,0:T(8,128)(2,1)}, bf16[1536,2048]{1,0:T(8,128)(2,1)}) custom-call(bf16[192,2048]{1,0:T(8,128)(2,1)} %copy-done.17, bf16[192,2048]{1,0:T(8,128)(2,1)} %copy-done.20, bf16[192,2048]{1,0:T(8,128)(2,1)} %copy-done.19, bf16[96,2048]{1,0:T(8,128)(2,1)} %copy-done.43, ...), custom_call_target="tpu_custom_call" | custom-call | flops 19327352832 | bytes 36175872 | tf_op jit(solution)/shard_map/pallas_call | solution.py:619
  285.5 15.5 %shard_map.244 = bf16[2048,1536]{1,0:T(8,128)(2,1)} custom-call(bf16[1536,2048]{1,0:T(8,128)(2,1)} %get-tuple-element.178.a_ref, bf16[1536,1024]{1,0:T(8,128)(2,1)} %get-tuple-element.180.b_ref, bf16[1536,2048]{1,0:T(8,128)(2,1)} %constant_dynamic-update-slice_fusion.2.refs_10_.c_ref, bf16[1536,512]{1,0:T(8,128)(2,1)} %get-tuple-element.181.d_ref.h0_ref), custom_call_target="tpu_custom_call" | custom-call | flops 9663676416 | bytes 23592960 | tf_op jit(solution)/shard_map/pallas_call | solution.py:619
  301.1 27.5 %all-gather.8.cloned.1.call-done.w_ref.w1_ref = bf16[2048,1536]{1,0:T(8,128)(2,1)} async-done(((bf16[512,1536]{1,0:T(8,128)(2,1)}), bf16[2048,1536]{1,0:T(8,128)(2,1)}) %all-gather.8.cloned.1.call-update) | async-done | bytes 6291472 | tf_op jit(solution)/shard_map/all_gather | solution.py:51
  328.6 25.7 %shard_map.245 = (bf16[1536,512]{1,0:T(8,128)(2,1)}, bf16[1536,1024]{1,0:T(8,128)(2,1)}, bf16[768,2048]{1,0:T(8,128)(2,1)}, bf16[192,2048]{1,0:T(8,128)(2,1)}, b...) custom-call(bf16[1536,2048]{1,0:T(8,128)(2,1)} %get-tuple-element.178.a_ref, ...), custom_call_target="tpu_custom_call" | custom-call | flops 19327352832 | bytes 36175872 | tf_op jit(solution)/shard_map/pallas_call | solution.py:619
  360.2 4.2 add_convert_fusion.9
  371.1 15.0 %shard_map.246 = bf16[2048,1536]{1,0:T(8,128)(2,1)} custom-call(bf16[1536,2048]{1,0:T(8,128)(2,1)} %get-tuple-element.178.a_ref, bf16[1536,1024]{1,0:T(8,128)(2,1)} %get-tuple-element.189.b_ref, bf16[1536,2048]{1,0:T(8,128)(2,1)} %constant_dynamic-update-slice_fusion.2.refs_10_.c_ref, bf16[1536,512]{1,0:T(8,128)(2,1)} %get-tuple-element.190.d_ref.h1_ref), custom_call_target="tpu_custom_call" | custom-call | flops 9663676416 | bytes 23592960 | tf_op jit(solution)/shard_map/pallas_call | solution.py:619
  391.8 8.0 %collective-permute-done.48 = bf16[96,2048]{1,0:T(8,128)(2,1)S(1)} collective-permute-done((bf16[96,2048]{1,0:T(8,128)(2,1)S(1)}, bf16[96,2048]{1,0:T(8,128)(2,1)S(1)}, u32[]{:S(2)}, u32[]{:S(2)}) %collective-permute-start.48) | collective-permute-done | bytes 393248 | tf_op jit(solution)/shard_map/ppermute | solution.py:26
  406.2 15.3 %shard_map.247 = (bf16[768,2048]{1,0:T(8,128)(2,1)}, bf16[192,2048]{1,0:T(8,128)(2,1)}, bf16[192,2048]{1,0:T(8,128)(2,1)}, bf16[192,2048]{1,0:T(8,128)(2,1)}, bf16[192,2048]{1,0:T(8,128)(2,1)}) custom-call(bf16[1536,512]{1,0:T(8,128)(2,1)} %get-tuple-element.181.d_ref.h0_ref, bf16[1536,512]{1,0:T(8,128)(2,1)} %get-tuple-element.190.d_ref.h1_ref, ...), custom_call_target="tpu_custom_call" | custom-call | flops 6442450944 | bytes 22020096 | tf_op jit(solution)/shard_map/pallas_call | solution.py:619
  427.0 7.2 %collective-permute-done.52.refs_3_ = bf16[96,2048]{1,0:T(8,128)(2,1)S(1)} collective-permute-done((bf16[96,2048]{1,0:T(8,128)(2,1)S(1)}, bf16[96,2048]{1,0:T(8,128)(2,1)S(1)}, u32[]{:S(2)}, u32[]{:S(2)}) %collective-permute-start.52) | collective-permute-done | bytes 393248 | tf_op jit(solution)/shard_map/ppermute | solution.py:38
  434.2 2.4 collective-permute-done.53.refs_4_
  445.5 8.6 %shard_map.248 = (bf16[1536,2048]{1,0:T(8,128)(2,1)}, bf16[1536,256]{1,0:T(8,128)(2,1)}) custom-call(bf16[192,2048]{1,0:T(8,128)(2,1)} %copy-done.9, bf16[192,2048]{1,0:T(8,128)(2,1)} %collective-permute-done.50.refs_1_, bf16[192,2048]{1,0:T(8,128)(2,1)} %collective-permute-done.51.refs_2_, bf16[96,2048]{1,0:T(8,128)(2,1)} %copy-done.18, ...), custom_call_target="tpu_custom_call" | custom-call | flops 1610612736 | bytes 12582912 | tf_op jit(solution)/shard_map/pallas_call | solution.py:619
  455.0 3.6 add_convert_fusion.5
  462.9 10.8 %shard_map.249 = (f32[6144,128]{1,0:T(8,128)}, bf16[768,128]{1,0:T(8,128)(2,1)}, bf16[1536,128]{1,0:T(8,128)(2,1)}) custom-call(s32[8]{0:T(128)} %or_or_fusion.1.table, s32[8]{0:T(128)} %get-tuple-element.284.lo, s32[8]{0:T(128)} %get-tuple-element.283.hi, bf16[1536,256]{1,0:T(8,128)(2,1)} %get-tuple-element.156.q_ref, ...), custom_call_target="tpu_custom_call" | custom-call | flops 12079595520 | bytes 4718592 | tf_op jit(solution)/shard_map/pallas_call | solution.py:619
  473.7 4.4 collective-permute-done.64
  479.1 4.3 all-to-all-start.3
  486.1 30.6 %shard_map.250 = (f32[1536,256]{1,0:T(8,128)}, f32[1536,128]{1,0:T(8,128)}) custom-call(s32[8]{0:T(128)} %or_or_fusion.1.table, s32[8]{0:T(128)} %get-tuple-element.282.lo, s32[8]{0:T(128)} %get-tuple-element.281.hi, bf16[1536,256]{1,0:T(8,128)(2,1)} %get-tuple-element.156.q_ref, bf16[1536,256]{1,0:T(8,128)(2,1)} %get-tuple-element.210.do_ref, ...), custom_call_target="tpu_custom_call" | custom-call | flops 12079595520 | bytes 4718592 | tf_op jit(solution)/shard_map/pallas_call | solution.py:619
  516.8 12.4 %collective-permute-done.67.refs_0_ = bf16[1536,128]{1,0:T(8,128)(2,1)} collective-permute-done((bf16[1536,128]{1,0:T(8,128)(2,1)}, bf16[1536,128]{1,0:T(8,128)(2,1)}, u32[]{:S(2)}, u32[]{:S(2)}) %collective-permute-start.67) | collective-permute-done | bytes 393248 | tf_op jit(solution)/shard_map/ppermute | solution.py:60
  529.1 9.1 %shard_map.251 = (bf16[1536,384]{1,0:T(8,128)(2,1)}, f32[8,128]{1,0:T(8,128)}) custom-call(s32[8]{0:T(128)} %or_or_fusion.1.table, f32[1536,384]{1,0:T(8,128)} %get-tuple-element.209.raw_ref, f32[1536,128]{1,0:T(8,128)} %get-tuple-element.151.refs_9_.cos_ref, f32[1536,128]{1,0:T(8,128)} %get-tuple-element.152.refs_10_.sin_ref, ...), custom_call_target="tpu_custom_call" | custom-call | flops 9830400 | bytes 5898240 | tf_op jit(solution)/shard_map/pallas_call | solution.py:619
  538.2 8.5 %shard_map.252 = (bf16[768,2048]{1,0:T(8,128)(2,1)}, bf16[192,2048]{1,0:T(8,128)(2,1)}, bf16[192,2048]{1,0:T(8,128)(2,1)}, bf16[192,2048]{1,0:T(8,128)(2,1)}, bf16[192,2048]{1,0:T(8,128)(2,1)}) custom-call(bf16[1536,384]{1,0:T(8,128)(2,1)} %get-tuple-element.240.a_ref.b_ref, bf16[2048,384]{1,0:T(8,128)(2,1)} %slice.236.refs_8_.w_ref.refs_0_), custom_call_target="tpu_custom_call" | custom-call | flops 2415919104 | bytes 7471104 | tf_op jit(solution)/shard_map/pallas_call | solution.py:619
  547.3 11.2 %shard_map.253 = (f32[8,2048]{1,0:T(8,128)}, bf16[2048,640]{1,0:T(8,128)(2,1)}) custom-call(bf16[1536,2048]{1,0:T(8,128)(2,1)} %get-tuple-element.239.a_ref, bf16[1536,384]{1,0:T(8,128)(2,1)} %get-tuple-element.240.a_ref.b_ref, bf16[1536,2048]{1,0:T(8,128)(2,1)} %get-tuple-element.241.c_ref, bf16[1536,256]{1,0:T(8,128)(2,1)} %get-tuple-element.165.a_ref.d_ref, ...), custom_call_target="tpu_custom_call" | custom-call | flops 4026531840 | bytes 17170432 | tf_op jit(solution)/shard_map/pallas_call | solution.py:619
  558.7 3.7 add_convert_fusion
  565.9 4.6 all-to-all-start.4
  571.0 11.5 %collective-permute-done.72 = bf16[192,2048]{1,0:T(8,128)(2,1)} collective-permute-done((bf16[192,2048]{1,0:T(8,128)(2,1)}, bf16[192,2048]{1,0:T(8,128)(2,1)}, u32[]{:S(2)}, u32[]{:S(2)}) %collective-permute-start.72) | collective-permute-done | bytes 786464 | tf_op jit(solution)/shard_map/ppermute | solution.py:38
  582.5 2.9 add_convert_fusion.1
  585.4 5.2 all-to-all-done.4.refs_1_
  592.4 2.5 convert_element_type.350
  596.3 5.0 shard_map.254
  601.4 8.5 %collective-permute-done.74 = bf16[192,2048]{1,0:T(8,128)(2,1)S(1)} collective-permute-done((bf16[192,2048]{1,0:T(8,128)(2,1)}, bf16[192,2048]{1,0:T(8,128)(2,1)S(1)}, u32[]{:S(2)}, u32[]{:S(2)}) %collective-permute-start.74) | collective-permute-done | bytes 786464 | tf_op jit(solution)/shard_map/ppermute | solution.py:38
  611.1 3.0 convert_add_fusion.1
  623.2 2.1 reduce-scatter.8.cloned.1.call-done
  625.3 3.5 all-to-all-start.5
  628.8 2.0 collective-permute-start.80
  630.8 3.4 fusion.7
  634.3 6.0 collective-permute-done.80
  640.2 16.5 %collective-permute-start.81 = (f32[4224]{0:T(1024)S(1)}, f32[4224]{0:T(1024)S(1)}, u32[]{:S(2)}, u32[]{:S(2)}) collective-permute-start(f32[4224]{0:T(1024)S(1)} %add.267), channel_id=1, source_target_pairs={{0,8},{2,10},{4,12},{6,14},{8,0},{10,2},{12,4},{14,6},{16,24},{18,... | collective-permute-start | bytes 50696 | tf_op jit(solution)/shard_map/ppermute | solution.py:26
  659.9 2.2 shard_map.255
  (341 shorter events, 124.4 us)
Async XLA Ops:
  7.2 99.3 %all-gather.4.cloned.1.call-start = ((), (), s32[]{:S(2)}) async-start(), calls=%async_computation.9 | async-start | bytes 3276800 | tf_op jit(solution)/shard_map/all_gather | solution.py:51
  24.5 236.2 %all-gather.6.cloned.1.call-start = ((), (), s32[]{:S(2)}) async-start(), calls=%async_computation.10 | async-start | bytes 7864320 | tf_op jit(solution)/shard_map/all_gather | solution.py:51
  59.0 21.4 %collective-permute-start.5 = (bf16[192,2048]{1,0:T(8,128)(2,1)S(1)}, bf16[192,2048]{1,0:T(8,128)(2,1)S(1)}, u32[]{:S(2)}, u32[]{:S(2)}) collective-permute-start(bf16[192,2048]{1,0:T(8,128)(2,1)S(1)} %fusion.3.refs_0_), channel_id=1, source_target_pairs={{0,5},{1,4},{2,7},{3,6},{4,1},{5,0},{6,3},{7,2},{8,13},{9,12},{10,... | collective-permute-start | bytes 2359304 | tf_op jit(solution)/shard_map/ppermute | solution.py:73
  61.1 35.3 %collective-permute-start.4 = (bf16[192,2048]{1,0:T(8,128)(2,1)S(1)}, bf16[192,2048]{1,0:T(8,128)(2,1)S(1)}, u32[]{:S(2)}, u32[]{:S(2)}) collective-permute-start(bf16[192,2048]{1,0:T(8,128)(2,1)S(1)} %fusion.3.refs_0_), channel_id=1, source_target_pairs={{0,4},{2,6},{4,0},{6,2},{8,12},{10,14},{12,8},{14,10},{16,20},{18,... | collective-permute-start | bytes 2359304 | tf_op jit(solution)/shard_map/ppermute | solution.py:26
  62.8 33.6 %collective-permute-start.3 = (bf16[192,2048]{1,0:T(8,128)(2,1)S(1)}, bf16[192,2048]{1,0:T(8,128)(2,1)S(1)}, u32[]{:S(2)}, u32[]{:S(2)}) collective-permute-start(bf16[192,2048]{1,0:T(8,128)(2,1)S(1)} %fusion.3.refs_0_), channel_id=1, source_target_pairs={{0,1},{1,0},{2,3},{3,2},{4,5},{5,4},{6,7},{7,6},{8,9},{9,8},{10,11... | collective-permute-start | bytes 2359304 | tf_op jit(solution)/shard_map/ppermute | solution.py:38
  68.1 41.1 %collective-permute-start.6 = (bf16[192,2048]{1,0:T(8,128)(2,1)S(1)}, bf16[192,2048]{1,0:T(8,128)(2,1)}, u32[]{:S(2)}, u32[]{:S(2)}) collective-permute-start(bf16[192,2048]{1,0:T(8,128)(2,1)S(1)} %fusion.3.refs_0_), channel_id=1, source_target_pairs={{0,2},{2,0},{4,6},{6,4},{8,10},{10,8},{12,14},{14,12},{16,18},{18,... | collective-permute-start | bytes 2359304 | tf_op jit(solution)/shard_map/ppermute | solution.py:26
  97.5 25.9 %all-to-all-start.2 = ((bf16[4,128,1536]{2,1,0:T(8,128)(2,1)}), bf16[4,128,1536]{2,1,0:T(8,128)(2,1)S(1)}, u32[]{:S(2)}, u32[]{:S(2)}) async-start(bf16[4,128,1536]{2,1,0:T(8,128)(2,1)} %get-tuple-element.155), calls=%async_computation.2 | async-start | bytes 3145728 | tf_op jit(solution)/shard_map/all_to_all | solution.py:154
  101.1 227.5 %all-gather.8.cloned.1.call-start = ((), (), s32[]{:S(2)}) async-start(), calls=%async_computation.11 | async-start | bytes 7864320 | tf_op jit(solution)/shard_map/all_gather | solution.py:51
  123.4 35.1 %collective-permute-start.13 = (bf16[192,2048]{1,0:T(8,128)(2,1)S(1)}, bf16[192,2048]{1,0:T(8,128)(2,1)}, u32[]{:S(2)}, u32[]{:S(2)}) collective-permute-start(bf16[192,2048]{1,0:T(8,128)(2,1)S(1)} %copy-done.10), channel_id=1, source_target_pairs={{0,4},{2,6},{4,0},{6,2},{8,12},{10,14},{12,8},{14,10},{16,20},{18,... | collective-permute-start | bytes 2359304 | tf_op jit(solution)/shard_map/ppermute | solution.py:26
  125.2 33.4 %collective-permute-start.12 = (bf16[192,2048]{1,0:T(8,128)(2,1)S(1)}, bf16[192,2048]{1,0:T(8,128)(2,1)}, u32[]{:S(2)}, u32[]{:S(2)}) collective-permute-start(bf16[192,2048]{1,0:T(8,128)(2,1)S(1)} %copy-done.10), channel_id=1, source_target_pairs={{0,1},{1,0},{2,3},{3,2},{4,5},{5,4},{6,7},{7,6},{8,9},{9,8},{10,11... | collective-permute-start | bytes 2359304 | tf_op jit(solution)/shard_map/ppermute | solution.py:38
  128.9 29.7 %collective-permute-start.10 = (bf16[1536,128]{1,0:T(8,128)(2,1)}, bf16[1536,128]{1,0:T(8,128)(2,1)S(1)}, u32[]{:S(2)}, u32[]{:S(2)}) collective-permute-start(bf16[1536,128]{1,0:T(8,128)(2,1)} %get-tuple-element.157.kv_ref), channel_id=1, source_target_pairs={{0,8},{2,10},{4,12},{6,14},{8,16},{10,18},{12,20},{14,22},{16,24},... | collective-permute-start | bytes 1179656 | tf_op jit(solution)/shard_map/ppermute | solution.py:60
  132.4 55.1 %collective-permute-start.24 = (bf16[192,2048]{1,0:T(8,128)(2,1)S(1)}, bf16[192,2048]{1,0:T(8,128)(2,1)}, u32[]{:S(2)}, u32[]{:S(2)}) collective-permute-start(bf16[192,2048]{1,0:T(8,128)(2,1)S(1)} %copy-done.10), channel_id=1, source_target_pairs={{0,2},{2,0},{4,6},{6,4},{8,10},{10,8},{12,14},{14,12},{16,18},{18,... | collective-permute-start | bytes 2359304 | tf_op jit(solution)/shard_map/ppermute | solution.py:26
  132.5 26.1 %collective-permute-start.11 = (bf16[768,128]{1,0:T(8,128)(2,1)}, bf16[768,128]{1,0:T(8,128)(2,1)}, u32[]{:S(2)}, u32[]{:S(2)}) collective-permute-start(bf16[768,128]{1,0:T(8,128)(2,1)} %slice.180), channel_id=1, source_target_pairs={{0,16},{2,18},{4,20},{6,22},{8,24},{10,26},{12,28},{14,30},{1,17},... | collective-permute-start | bytes 589832 | tf_op jit(solution)/shard_map/ppermute | solution.py:60
  137.6 341.5 %reduce-scatter.4.cloned.1.call-start = ((), (), s32[]{:S(2)}) async-start(), calls=%async_computation.12 | async-start | bytes 7864320 | tf_op jit(solution)/shard_map/reduce_scatter | solution.py:55
  159.6 32.3 %collective-permute-start.26 = (bf16[192,2048]{1,0:T(8,128)(2,1)}, bf16[192,2048]{1,0:T(8,128)(2,1)S(1)}, u32[]{:S(2)}, u32[]{:S(2)}) collective-permute-start(bf16[192,2048]{1,0:T(8,128)(2,1)} %collective-permute-done.13), channel_id=1, source_target_pairs={{0,2},{2,0},{4,6},{6,4},{8,10},{10,8},{12,14},{14,12},{16,18},{18,... | collective-permute-start | bytes 2359304 | tf_op jit(solution)/shard_map/ppermute | solution.py:26
  160.7 26.8 %collective-permute-start.25 = (bf16[192,2048]{1,0:T(8,128)(2,1)}, bf16[192,2048]{1,0:T(8,128)(2,1)S(1)}, u32[]{:S(2)}, u32[]{:S(2)}) collective-permute-start(bf16[192,2048]{1,0:T(8,128)(2,1)} %collective-permute-done.12), channel_id=1, source_target_pairs={{0,2},{2,0},{4,6},{6,4},{8,10},{10,8},{12,14},{14,12},{16,18},{18,... | collective-permute-start | bytes 2359304 | tf_op jit(solution)/shard_map/ppermute | solution.py:26
  162.2 16.8 %collective-permute-start.15 = (bf16[96,2048]{1,0:T(8,128)(2,1)S(1)}, bf16[96,2048]{1,0:T(8,128)(2,1)S(1)}, u32[]{:S(2)}, u32[]{:S(2)}) collective-permute-start(bf16[96,2048]{1,0:T(8,128)(2,1)S(1)} %slice.182), channel_id=1, source_target_pairs={{0,4},{2,6},{4,0},{6,2},{8,12},{10,14},{12,8},{14,10},{16,20},{18,... | collective-permute-start | bytes 1179656 | tf_op jit(solution)/shard_map/ppermute | solution.py:26
  162.6 16.4 %collective-permute-start.14 = (bf16[96,2048]{1,0:T(8,128)(2,1)S(1)}, bf16[96,2048]{1,0:T(8,128)(2,1)S(1)}, u32[]{:S(2)}, u32[]{:S(2)}) collective-permute-start(bf16[96,2048]{1,0:T(8,128)(2,1)S(1)} %slice.181), channel_id=1, source_target_pairs={{0,1},{1,0},{2,3},{3,2},{4,5},{5,4},{6,7},{7,6},{8,9},{9,8},{10,11... | collective-permute-start | bytes 1179656 | tf_op jit(solution)/shard_map/ppermute | solution.py:38
  195.0 12.0 %collective-permute-start.21 = (bf16[96,2048]{1,0:T(8,128)(2,1)S(1)}, bf16[96,2048]{1,0:T(8,128)(2,1)S(1)}, u32[]{:S(2)}, u32[]{:S(2)}) collective-permute-start(bf16[96,2048]{1,0:T(8,128)(2,1)S(1)} %slice.241), channel_id=1, source_target_pairs={{0,1},{1,0},{2,3},{3,2},{4,5},{5,4},{6,7},{7,6},{8,9},{9,8},{10,11... | collective-permute-start | bytes 1179656 | tf_op jit(solution)/shard_map/ppermute | solution.py:38
  195.8 12.0 %collective-permute-start.23 = (bf16[96,2048]{1,0:T(8,128)(2,1)S(1)}, bf16[96,2048]{1,0:T(8,128)(2,1)S(1)}, u32[]{:S(2)}, u32[]{:S(2)}) collective-permute-start(bf16[96,2048]{1,0:T(8,128)(2,1)S(1)} %slice.242), channel_id=1, source_target_pairs={{0,4},{2,6},{4,0},{6,2},{8,12},{10,14},{12,8},{14,10},{16,20},{18,... | collective-permute-start | bytes 1179656 | tf_op jit(solution)/shard_map/ppermute | solution.py:26
  197.5 17.6 %collective-permute-start.19 = (bf16[96,2048]{1,0:T(8,128)(2,1)S(1)}, bf16[96,2048]{1,0:T(8,128)(2,1)S(1)}, u32[]{:S(2)}, u32[]{:S(2)}) collective-permute-start(bf16[96,2048]{1,0:T(8,128)(2,1)S(1)} %get-tuple-element.309), channel_id=1, source_target_pairs={{0,4},{2,6},{4,0},{6,2},{8,12},{10,14},{12,8},{14,10},{16,20},{18,... | collective-permute-start | bytes 1179656 | tf_op jit(solution)/shard_map/ppermute | solution.py:26
  197.8 17.2 %collective-permute-start.18 = (bf16[96,2048]{1,0:T(8,128)(2,1)S(1)}, bf16[96,2048]{1,0:T(8,128)(2,1)S(1)}, u32[]{:S(2)}, u32[]{:S(2)}) collective-permute-start(bf16[96,2048]{1,0:T(8,128)(2,1)S(1)} %get-tuple-element.310), channel_id=1, source_target_pairs={{0,1},{1,0},{2,3},{3,2},{4,5},{5,4},{6,7},{7,6},{8,9},{9,8},{10,11... | collective-permute-start | bytes 1179656 | tf_op jit(solution)/shard_map/ppermute | solution.py:38
  227.9 17.2 %collective-permute-start.32 = (bf16[192,2048]{1,0:T(8,128)(2,1)S(1)}, bf16[192,2048]{1,0:T(8,128)(2,1)S(1)}, u32[]{:S(2)}, u32[]{:S(2)}) collective-permute-start(bf16[192,2048]{1,0:T(8,128)(2,1)S(1)} %multiply_convert_fusion.refs_0_), channel_id=1, source_target_pairs={{0,4},{2,6},{4,0},{6,2},{8,12},{10,14},{12,8},{14,10},{16,20},{18,... | collective-permute-start | bytes 2359304 | tf_op jit(solution)/shard_map/ppermute | solution.py:26
  228.3 18.2 %collective-permute-start.31 = (bf16[192,2048]{1,0:T(8,128)(2,1)S(1)}, bf16[192,2048]{1,0:T(8,128)(2,1)S(1)}, u32[]{:S(2)}, u32[]{:S(2)}) collective-permute-start(bf16[192,2048]{1,0:T(8,128)(2,1)S(1)} %multiply_convert_fusion.refs_0_), channel_id=1, source_target_pairs={{0,1},{1,0},{2,3},{3,2},{4,5},{5,4},{6,7},{7,6},{8,9},{9,8},{10,11... | collective-permute-start | bytes 2359304 | tf_op jit(solution)/shard_map/ppermute | solution.py:38
  229.6 28.5 %collective-permute-start.35 = (bf16[192,2048]{1,0:T(8,128)(2,1)S(1)}, bf16[192,2048]{1,0:T(8,128)(2,1)S(1)}, u32[]{:S(2)}, u32[]{:S(2)}) collective-permute-start(bf16[192,2048]{1,0:T(8,128)(2,1)S(1)} %multiply_convert_fusion.refs_0_), channel_id=1, source_target_pairs={{0,2},{2,0},{4,6},{6,4},{8,10},{10,8},{12,14},{14,12},{16,18},{18,... | collective-permute-start | bytes 2359304 | tf_op jit(solution)/shard_map/ppermute | solution.py:26
  246.5 11.7 %collective-permute-start.37 = (bf16[192,2048]{1,0:T(8,128)(2,1)S(1)}, bf16[192,2048]{1,0:T(8,128)(2,1)S(1)}, u32[]{:S(2)}, u32[]{:S(2)}) collective-permute-start(bf16[192,2048]{1,0:T(8,128)(2,1)S(1)} %collective-permute-done.32.refs_2_), channel_id=1, source_target_pairs={{0,2},{2,0},{4,6},{6,4},{8,10},{10,8},{12,14},{14,12},{16,18},{18,... | collective-permute-start | bytes 2359304 | tf_op jit(solution)/shard_map/ppermute | solution.py:26
  246.6 11.6 %collective-permute-start.34 = (bf16[96,2048]{1,0:T(8,128)(2,1)S(1)}, bf16[96,2048]{1,0:T(8,128)(2,1)S(1)}, u32[]{:S(2)}, u32[]{:S(2)}) collective-permute-start(bf16[96,2048]{1,0:T(8,128)(2,1)S(1)} %slice.247), channel_id=1, source_target_pairs={{0,4},{2,6},{4,0},{6,2},{8,12},{10,14},{12,8},{14,10},{16,20},{18,... | collective-permute-start | bytes 1179656 | tf_op jit(solution)/shard_map/ppermute | solution.py:26
  248.3 12.4 %collective-permute-start.36 = (bf16[192,2048]{1,0:T(8,128)(2,1)S(1)}, bf16[192,2048]{1,0:T(8,128)(2,1)}, u32[]{:S(2)}, u32[]{:S(2)}) collective-permute-start(bf16[192,2048]{1,0:T(8,128)(2,1)S(1)} %collective-permute-done.31.refs_1_), channel_id=1, source_target_pairs={{0,2},{2,0},{4,6},{6,4},{8,10},{10,8},{12,14},{14,12},{16,18},{18,... | collective-permute-start | bytes 2359304 | tf_op jit(solution)/shard_map/ppermute | solution.py:26
  301.1 264.8 %reduce-scatter.6.cloned.1.call-start = ((), (), s32[]{:S(2)}) async-start(), calls=%async_computation.13 | async-start | bytes 7864320 | tf_op jit(solution)/shard_map/reduce_scatter | solution.py:55
  366.1 20.1 %collective-permute-start.45 = (bf16[96,2048]{1,0:T(8,128)(2,1)}, bf16[96,2048]{1,0:T(8,128)(2,1)S(1)}, u32[]{:S(2)}, u32[]{:S(2)}) collective-permute-start(bf16[96,2048]{1,0:T(8,128)(2,1)} %slice.251), channel_id=1, source_target_pairs={{0,1},{1,0},{2,3},{3,2},{4,5},{5,4},{6,7},{7,6},{8,9},{9,8},{10,11... | collective-permute-start | bytes 1179656 | tf_op jit(solution)/shard_map/ppermute | solution.py:38
  367.6 18.6 %collective-permute-start.47 = (bf16[96,2048]{1,0:T(8,128)(2,1)}, bf16[96,2048]{1,0:T(8,128)(2,1)}, u32[]{:S(2)}, u32[]{:S(2)}) collective-permute-start(bf16[96,2048]{1,0:T(8,128)(2,1)} %slice.252), channel_id=1, source_target_pairs={{0,4},{2,6},{4,0},{6,2},{8,12},{10,14},{12,8},{14,10},{16,20},{18,... | collective-permute-start | bytes 1179656 | tf_op jit(solution)/shard_map/ppermute | solution.py:26
  370.0 17.2 %collective-permute-start.43 = (bf16[96,2048]{1,0:T(8,128)(2,1)}, bf16[96,2048]{1,0:T(8,128)(2,1)}, u32[]{:S(2)}, u32[]{:S(2)}) collective-permute-start(bf16[96,2048]{1,0:T(8,128)(2,1)} %get-tuple-element.307), channel_id=1, source_target_pairs={{0,4},{2,6},{4,0},{6,2},{8,12},{10,14},{12,8},{14,10},{16,20},{18,... | collective-permute-start | bytes 1179656 | tf_op jit(solution)/shard_map/ppermute | solution.py:26
  370.6 16.6 %collective-permute-start.42 = (bf16[96,2048]{1,0:T(8,128)(2,1)}, bf16[96,2048]{1,0:T(8,128)(2,1)}, u32[]{:S(2)}, u32[]{:S(2)}) collective-permute-start(bf16[96,2048]{1,0:T(8,128)(2,1)} %get-tuple-element.308), channel_id=1, source_target_pairs={{0,1},{1,0},{2,3},{3,2},{4,5},{5,4},{6,7},{7,6},{8,9},{9,8},{10,11... | collective-permute-start | bytes 1179656 | tf_op jit(solution)/shard_map/ppermute | solution.py:38
  405.1 17.5 %collective-permute-start.51 = (bf16[192,2048]{1,0:T(8,128)(2,1)S(1)}, bf16[192,2048]{1,0:T(8,128)(2,1)}, u32[]{:S(2)}, u32[]{:S(2)}) collective-permute-start(bf16[192,2048]{1,0:T(8,128)(2,1)S(1)} %get-tuple-element.277.refs_0_), channel_id=1, source_target_pairs={{0,4},{2,6},{4,0},{6,2},{8,12},{10,14},{12,8},{14,10},{16,20},{18,... | collective-permute-start | bytes 2359304 | tf_op jit(solution)/shard_map/ppermute | solution.py:26
  405.6 17.2 %collective-permute-start.50 = (bf16[192,2048]{1,0:T(8,128)(2,1)S(1)}, bf16[192,2048]{1,0:T(8,128)(2,1)}, u32[]{:S(2)}, u32[]{:S(2)}) collective-permute-start(bf16[192,2048]{1,0:T(8,128)(2,1)S(1)} %get-tuple-element.277.refs_0_), channel_id=1, source_target_pairs={{0,1},{1,0},{2,3},{3,2},{4,5},{5,4},{6,7},{7,6},{8,9},{9,8},{10,11... | collective-permute-start | bytes 2359304 | tf_op jit(solution)/shard_map/ppermute | solution.py:38
  421.5 19.6 %collective-permute-start.54 = (bf16[192,2048]{1,0:T(8,128)(2,1)S(1)}, bf16[192,2048]{1,0:T(8,128)(2,1)}, u32[]{:S(2)}, u32[]{:S(2)}) collective-permute-start(bf16[192,2048]{1,0:T(8,128)(2,1)S(1)} %get-tuple-element.277.refs_0_), channel_id=1, source_target_pairs={{0,2},{2,0},{4,6},{6,4},{8,10},{10,8},{12,14},{14,12},{16,18},{18,... | collective-permute-start | bytes 2359304 | tf_op jit(solution)/shard_map/ppermute | solution.py:26
  423.9 10.4 %collective-permute-start.52 = (bf16[96,2048]{1,0:T(8,128)(2,1)S(1)}, bf16[96,2048]{1,0:T(8,128)(2,1)S(1)}, u32[]{:S(2)}, u32[]{:S(2)}) collective-permute-start(bf16[96,2048]{1,0:T(8,128)(2,1)S(1)} %slice.210), channel_id=1, source_target_pairs={{0,1},{1,0},{2,3},{3,2},{4,5},{5,4},{6,7},{7,6},{8,9},{9,8},{10,11... | collective-permute-start | bytes 1179656 | tf_op jit(solution)/shard_map/ppermute | solution.py:38
  425.5 11.1 %collective-permute-start.53 = (bf16[96,2048]{1,0:T(8,128)(2,1)S(1)}, bf16[96,2048]{1,0:T(8,128)(2,1)}, u32[]{:S(2)}, u32[]{:S(2)}) collective-permute-start(bf16[96,2048]{1,0:T(8,128)(2,1)S(1)} %slice.211), channel_id=1, source_target_pairs={{0,4},{2,6},{4,0},{6,2},{8,12},{10,14},{12,8},{14,10},{16,20},{18,... | collective-permute-start | bytes 1179656 | tf_op jit(solution)/shard_map/ppermute | solution.py:26
  427.0 14.7 %collective-permute-start.55 = (bf16[192,2048]{1,0:T(8,128)(2,1)}, bf16[192,2048]{1,0:T(8,128)(2,1)}, u32[]{:S(2)}, u32[]{:S(2)}) collective-permute-start(bf16[192,2048]{1,0:T(8,128)(2,1)} %collective-permute-done.50.refs_1_), channel_id=1, source_target_pairs={{0,2},{2,0},{4,6},{6,4},{8,10},{10,8},{12,14},{14,12},{16,18},{18,... | collective-permute-start | bytes 2359304 | tf_op jit(solution)/shard_map/ppermute | solution.py:26
  441.1 13.0 %collective-permute-start.59 = (bf16[192,2048]{1,0:T(8,128)(2,1)}, bf16[192,2048]{1,0:T(8,128)(2,1)S(1)}, u32[]{:S(2)}, u32[]{:S(2)}) collective-permute-start(bf16[192,2048]{1,0:T(8,128)(2,1)} %get-tuple-element.204), channel_id=1, source_target_pairs={{0,2},{2,0},{4,6},{6,4},{8,10},{10,8},{12,14},{14,12},{16,18},{18,... | collective-permute-start | bytes 2359304 | tf_op jit(solution)/shard_map/ppermute | solution.py:26
  441.1 13.0 %collective-permute-start.60 = (bf16[192,2048]{1,0:T(8,128)(2,1)}, bf16[192,2048]{1,0:T(8,128)(2,1)S(1)}, u32[]{:S(2)}, u32[]{:S(2)}) collective-permute-start(bf16[192,2048]{1,0:T(8,128)(2,1)} %get-tuple-element.205), channel_id=1, source_target_pairs={{0,2},{2,0},{4,6},{6,4},{8,10},{10,8},{12,14},{14,12},{16,18},{18,... | collective-permute-start | bytes 2359304 | tf_op jit(solution)/shard_map/ppermute | solution.py:26
  441.6 12.5 %collective-permute-start.61 = (bf16[192,2048]{1,0:T(8,128)(2,1)}, bf16[192,2048]{1,0:T(8,128)(2,1)S(1)}, u32[]{:S(2)}, u32[]{:S(2)}) collective-permute-start(bf16[192,2048]{1,0:T(8,128)(2,1)} %get-tuple-element.206), channel_id=1, source_target_pairs={{0,2},{2,0},{4,6},{6,4},{8,10},{10,8},{12,14},{14,12},{16,18},{18,... | collective-permute-start | bytes 2359304 | tf_op jit(solution)/shard_map/ppermute | solution.py:26
  441.7 13.3 %collective-permute-start.62 = (bf16[192,2048]{1,0:T(8,128)(2,1)}, bf16[192,2048]{1,0:T(8,128)(2,1)}, u32[]{:S(2)}, u32[]{:S(2)}) collective-permute-start(bf16[192,2048]{1,0:T(8,128)(2,1)} %get-tuple-element.207), channel_id=1, source_target_pairs={{0,2},{2,0},{4,6},{6,4},{8,10},{10,8},{12,14},{14,12},{16,18},{18,... | collective-permute-start | bytes 2359304 | tf_op jit(solution)/shard_map/ppermute | solution.py:26
  458.6 15.0 %collective-permute-start.66 = (bf16[96,2048]{1,0:T(8,128)(2,1)S(1)}, bf16[96,2048]{1,0:T(8,128)(2,1)S(1)}, u32[]{:S(2)}, u32[]{:S(2)}) collective-permute-start(bf16[96,2048]{1,0:T(8,128)(2,1)S(1)} %slice.220), channel_id=1, source_target_pairs={{0,4},{2,6},{4,0},{6,2},{8,12},{10,14},{12,8},{14,10},{16,20},{18,... | collective-permute-start | bytes 1179656 | tf_op jit(solution)/shard_map/ppermute | solution.py:26
  459.8 13.8 %collective-permute-start.65 = (bf16[96,2048]{1,0:T(8,128)(2,1)S(1)}, bf16[96,2048]{1,0:T(8,128)(2,1)}, u32[]{:S(2)}, u32[]{:S(2)}) collective-permute-start(bf16[96,2048]{1,0:T(8,128)(2,1)S(1)} %slice.219), channel_id=1, source_target_pairs={{0,1},{1,0},{2,3},{3,2},{4,5},{5,4},{6,7},{7,6},{8,9},{9,8},{10,11... | collective-permute-start | bytes 1179656 | tf_op jit(solution)/shard_map/ppermute | solution.py:38
  460.4 17.7 %collective-permute-start.64 = (bf16[96,2048]{1,0:T(8,128)(2,1)S(1)}, bf16[96,2048]{1,0:T(8,128)(2,1)}, u32[]{:S(2)}, u32[]{:S(2)}) collective-permute-start(bf16[96,2048]{1,0:T(8,128)(2,1)S(1)} %get-tuple-element.305), channel_id=1, source_target_pairs={{0,4},{2,6},{4,0},{6,2},{8,12},{10,14},{12,8},{14,10},{16,20},{18,... | collective-permute-start | bytes 1179656 | tf_op jit(solution)/shard_map/ppermute | solution.py:26
  461.0 18.1 %collective-permute-start.63 = (bf16[96,2048]{1,0:T(8,128)(2,1)S(1)}, bf16[96,2048]{1,0:T(8,128)(2,1)}, u32[]{:S(2)}, u32[]{:S(2)}) collective-permute-start(bf16[96,2048]{1,0:T(8,128)(2,1)S(1)} %get-tuple-element.306), channel_id=1, source_target_pairs={{0,1},{1,0},{2,3},{3,2},{4,5},{5,4},{6,7},{7,6},{8,9},{9,8},{10,11... | collective-permute-start | bytes 1179656 | tf_op jit(solution)/shard_map/ppermute | solution.py:38
  479.1 50.0 %all-to-all-start.3 = ((bf16[4,128,1536]{2,1,0:T(8,128)(2,1)}), bf16[4,128,1536]{2,1,0:T(8,128)(2,1)}, u32[]{:S(2)}, u32[]{:S(2)}) async-start(bf16[4,128,1536]{2,1,0:T(8,128)(2,1)} %bitcast.21), calls=%async_computation.4 | async-start | bytes 3145728 | tf_op jit(solution)/shard_map/all_to_all | solution.py:154
  483.5 141.8 %reduce-scatter.8.cloned.1.call-start = ((), (), s32[]{:S(2)}) async-start(), calls=%async_computation.14 | async-start | bytes 3276800 | tf_op jit(solution)/shard_map/reduce_scatter | solution.py:55
  483.5 33.2 %collective-permute-start.68 = (bf16[768,128]{1,0:T(8,128)(2,1)}, bf16[768,128]{1,0:T(8,128)(2,1)}, u32[]{:S(2)}, u32[]{:S(2)}) collective-permute-start(bf16[768,128]{1,0:T(8,128)(2,1)} %get-tuple-element.223), channel_id=1, source_target_pairs={{16,0},{18,2},{20,4},{22,6},{24,8},{26,10},{28,12},{30,14},{17,1},... | collective-permute-start | bytes 589832 | tf_op jit(solution)/shard_map/ppermute | solution.py:60
  484.8 44.3 %collective-permute-start.67 = (bf16[1536,128]{1,0:T(8,128)(2,1)}, bf16[1536,128]{1,0:T(8,128)(2,1)}, u32[]{:S(2)}, u32[]{:S(2)}) collective-permute-start(bf16[1536,128]{1,0:T(8,128)(2,1)} %get-tuple-element.222), channel_id=1, source_target_pairs={{8,0},{10,2},{12,4},{14,6},{16,8},{18,10},{20,12},{22,14},{24,16},... | collective-permute-start | bytes 1179656 | tf_op jit(solution)/shard_map/ppermute | solution.py:60
  546.8 12.0 %collective-permute-start.71 = (bf16[192,2048]{1,0:T(8,128)(2,1)}, bf16[192,2048]{1,0:T(8,128)(2,1)}, u32[]{:S(2)}, u32[]{:S(2)}) collective-permute-start(bf16[192,2048]{1,0:T(8,128)(2,1)} %get-tuple-element.237), channel_id=1, source_target_pairs={{0,2},{2,0},{4,6},{6,4},{8,10},{10,8},{12,14},{14,12},{16,18},{18,... | collective-permute-start | bytes 2359304 | tf_op jit(solution)/shard_map/ppermute | solution.py:26
  546.9 11.8 %collective-permute-start.73 = (bf16[192,2048]{1,0:T(8,128)(2,1)}, bf16[192,2048]{1,0:T(8,128)(2,1)}, u32[]{:S(2)}, u32[]{:S(2)}) collective-permute-start(bf16[192,2048]{1,0:T(8,128)(2,1)} %get-tuple-element.238), channel_id=1, source_target_pairs={{0,2},{2,0},{4,6},{6,4},{8,10},{10,8},{12,14},{14,12},{16,18},{18,... | collective-permute-start | bytes 2359304 | tf_op jit(solution)/shard_map/ppermute | solution.py:26
  558.5 12.5 %collective-permute-start.70 = (bf16[192,2048]{1,0:T(8,128)(2,1)}, bf16[192,2048]{1,0:T(8,128)(2,1)}, u32[]{:S(2)}, u32[]{:S(2)}) collective-permute-start(bf16[192,2048]{1,0:T(8,128)(2,1)} %get-tuple-element.236), channel_id=1, source_target_pairs={{0,2},{2,0},{4,6},{6,4},{8,10},{10,8},{12,14},{14,12},{16,18},{18,... | collective-permute-start | bytes 2359304 | tf_op jit(solution)/shard_map/ppermute | solution.py:26
  562.4 20.2 %collective-permute-start.72 = (bf16[192,2048]{1,0:T(8,128)(2,1)}, bf16[192,2048]{1,0:T(8,128)(2,1)}, u32[]{:S(2)}, u32[]{:S(2)}) collective-permute-start(bf16[192,2048]{1,0:T(8,128)(2,1)} %get-tuple-element.286), channel_id=1, source_target_pairs={{0,1},{1,0},{2,3},{3,2},{4,5},{5,4},{6,7},{7,6},{8,9},{9,8},{10,11... | collective-permute-start | bytes 2359304 | tf_op jit(solution)/shard_map/ppermute | solution.py:38
  565.9 24.7 %all-to-all-start.4 = ((bf16[4,128,1536]{2,1,0:T(8,128)(2,1)}), bf16[4,128,1536]{2,1,0:T(8,128)(2,1)}, u32[]{:S(2)}, u32[]{:S(2)}) async-start(bf16[4,128,1536]{2,1,0:T(8,128)(2,1)} %bitcast.22), calls=%async_computation.6 | async-start | bytes 3145728 | tf_op jit(solution)/shard_map/all_to_all | solution.py:154
  570.5 30.9 %collective-permute-start.69 = (bf16[192,2048]{1,0:T(8,128)(2,1)}, bf16[192,2048]{1,0:T(8,128)(2,1)}, u32[]{:S(2)}, u32[]{:S(2)}) collective-permute-start(bf16[192,2048]{1,0:T(8,128)(2,1)} %get-tuple-element.235), channel_id=1, source_target_pairs={{0,2},{2,0},{4,6},{6,4},{8,10},{10,8},{12,14},{14,12},{16,18},{18,... | collective-permute-start | bytes 2359304 | tf_op jit(solution)/shard_map/ppermute | solution.py:26
  590.6 19.3 %collective-permute-start.74 = (bf16[192,2048]{1,0:T(8,128)(2,1)}, bf16[192,2048]{1,0:T(8,128)(2,1)S(1)}, u32[]{:S(2)}, u32[]{:S(2)}) collective-permute-start(bf16[192,2048]{1,0:T(8,128)(2,1)} %get-tuple-element.245), channel_id=1, source_target_pairs={{0,1},{1,0},{2,3},{3,2},{4,5},{5,4},{6,7},{7,6},{8,9},{9,8},{10,11... | collective-permute-start | bytes 2359304 | tf_op jit(solution)/shard_map/ppermute | solution.py:38
  592.1 19.0 %collective-permute-start.75 = (bf16[192,2048]{1,0:T(8,128)(2,1)}, bf16[192,2048]{1,0:T(8,128)(2,1)S(1)}, u32[]{:S(2)}, u32[]{:S(2)}) collective-permute-start(bf16[192,2048]{1,0:T(8,128)(2,1)} %add_convert_fusion.1), channel_id=1, source_target_pairs={{0,4},{2,6},{4,0},{6,2},{8,12},{10,14},{12,8},{14,10},{16,20},{18,... | collective-permute-start | bytes 2359304 | tf_op jit(solution)/shard_map/ppermute | solution.py:26
  621.0 35.7 %collective-permute-start.76 = (bf16[96,2048]{1,0:T(8,128)(2,1)}, bf16[96,2048]{1,0:T(8,128)(2,1)}, u32[]{:S(2)}, u32[]{:S(2)}) collective-permute-start(bf16[96,2048]{1,0:T(8,128)(2,1)} %add_convert_fusion.18), channel_id=1, source_target_pairs={{0,4},{2,6},{4,0},{6,2},{8,12},{10,14},{12,8},{14,10},{16,20},{18,... | collective-permute-start | bytes 1179656 | tf_op jit(solution)/shard_map/ppermute | solution.py:26
  621.7 35.0 %collective-permute-start.77 = (bf16[96,2048]{1,0:T(8,128)(2,1)}, bf16[96,2048]{1,0:T(8,128)(2,1)}, u32[]{:S(2)}, u32[]{:S(2)}) collective-permute-start(bf16[96,2048]{1,0:T(8,128)(2,1)} %add_convert_fusion.17), channel_id=1, source_target_pairs={{0,1},{1,0},{2,3},{3,2},{4,5},{5,4},{6,7},{7,6},{8,9},{9,8},{10,11... | collective-permute-start | bytes 1179656 | tf_op jit(solution)/shard_map/ppermute | solution.py:38
  625.3 15.0 %all-to-all-start.5 = ((bf16[4,128,640]{2,1,0:T(8,128)(2,1)}), bf16[4,128,640]{2,1,0:T(8,128)(2,1)S(1)}, u32[]{:S(2)}, u32[]{:S(2)}) async-start(bf16[4,128,640]{2,1,0:T(8,128)(2,1)} %bitcast.23), calls=%async_computation.8 | async-start | bytes 1310720 | tf_op jit(solution)/shard_map/all_to_all | solution.py:154
  628.8 11.4 %collective-permute-start.80 = (f32[4224]{0:T(1024)S(1)}, f32[4224]{0:T(1024)S(1)}, u32[]{:S(2)}, u32[]{:S(2)}) collective-permute-start(f32[4224]{0:T(1024)S(1)} %add.266), channel_id=1, source_target_pairs={{0,4},{2,6},{4,0},{6,2},{8,12},{10,14},{12,8},{14,10},{16,20},{18,... | collective-permute-start | bytes 50696 | tf_op jit(solution)/shard_map/ppermute | solution.py:26
  640.2 18.5 %collective-permute-start.81 = (f32[4224]{0:T(1024)S(1)}, f32[4224]{0:T(1024)S(1)}, u32[]{:S(2)}, u32[]{:S(2)}) collective-permute-start(f32[4224]{0:T(1024)S(1)} %add.267), channel_id=1, source_target_pairs={{0,8},{2,10},{4,12},{6,14},{8,0},{10,2},{12,4},{14,6},{16,24},{18,... | collective-permute-start | bytes 50696 | tf_op jit(solution)/shard_map/ppermute | solution.py:26
  (76 other events, 521.1 us)
Sparse Core Ops, SparseCore 0:
  24.6 55.8 all-gather.3
  82.1 122.4 all-gather.5
  206.8 121.7 all-gather.7
  330.8 108.9 reduce-scatter.3
  441.9 123.8 reduce-scatter.5
  568.0 57.1 reduce-scatter.7

commit v5 on v4

--- a/solution.py
+++ b/solution.py
@@ -873,18 +873,19 @@
     gain_sums = gain_sums[0]
     attn_grad = line_scatter(attn_grad, n)
     gain_sums, ffn_grad_1 = tie(gain_sums, ffn_grad_1)
+    one.parts, gain_sums, ffn_sum.got = tie(one.parts, gain_sums, ffn_sum.got)
     one.second_x()
     back_1 = home(ffn_grad_1)
-    d_one, back_1 = one.third_x(back_1)
+    out_tokens = (resid + ffn_sum.third()).astype(BF16)
+    d_one, (back_1, out_tokens) = one.third_x((back_1, out_tokens))
     ffn_outs = unpacked((back_0, back_1), [v.shape for v in (w_gate, w_up, w_down)], (0, 0, 1), ffn_cuts)
-    d_one, ffn_outs, gain_sums, ffn_sum.got = tie(d_one, ffn_outs, gain_sums, ffn_sum.got)
+    d_one, ffn_outs, gain_sums = tie(d_one, ffn_outs, gain_sums)
     d_attn_gain = gain_sums / gain_1
     d_q_gain = d_head_gains[0, :width] + d_head_gains[0, width:]
     gains = jnp.concatenate([d_attn_gain, d_ffn_gain, d_q_gain, d_head_gains[1, :width]])
     gains = sum_over_ctx(gains + swap_x(gains), 1, QUAD)
     d_x, _ = norm_back(x_own, scale_1, gain_1, d_one)
     d_tokens = d_h + d_x
-    out_tokens = (resid + ffn_sum.third()).astype(BF16)
 
     attn_grad, back_1 = tie(attn_grad, back_1)
     attn_back = home(attn_grad)

time: 678 us -> 680 us (level)
  waiting for transfers between devices: 193 us -> 202 us
    reduce_scatter x3, waiting for transfers between devices: 2.79 us -> 23.9 us  [line_scatter(): lax.psum_scatter(partial, 'ctx', scatter_dimension=0, axis_index_groups=l...]
    unnamed x107 -> x109, local copies, waits for them, and re-layouts: 19.7 us -> 20.2 us
  transfers between devices with their start and end apart: 93 -> 93, of which waited for: 37 -> 43; matrix products, arithmetic and copies ran while one was open for 13% -> 12% of each run, Pallas kernels for 34% -> 34%
where the time goes in v5:
time: 680 us; the launch traced here: 670 us
  Pallas kernels  233 us (34%)
  waiting for transfers between devices  202 us (30%)
  starting transfers between devices  91.2 us (13%)
  other arithmetic  46 us (7%)
  local copies, waits for them, and re-layouts  42.7 us (6%)
  blocking collectives  39.6 us (6%)
  between operations  15.3 us (2%)
    pallas_call x19, Pallas kernels, call(): pl.pallas_call(kernel, out_shape=[jax.ShapeDtypeStruct(shape, dtype) for...  233 us
    ppermute x59, waiting for transfers between devices, swap_ctx(): return lax.ppermute(value, 'ctx', [(i, i ^ bit) for i in range(n)])  87 us
    ppermute x59, starting transfers between devices, swap_ctx(): return lax.ppermute(value, 'ctx', [(i, i ^ bit) for i in range(n)])  40.9 us
    ppermute x19, waiting for transfers between devices, swap_x(): return lax.ppermute(value, 'tp', [(0, 1), (1, 0)])  40.3 us
    all_to_all x2, blocking collectives, spread(): lax.all_to_all(pieces, 'ctx', axis, axis, axis_index_groups=groups, tiled...  39.6 us
    all_gather x3, waiting for transfers between devices, line_gather(): lax.all_gather(own, 'ctx', axis=0, axis_index_groups=line_groups(n), tile...  27.2 us
    reduce_scatter x3, waiting for transfers between devices, line_scatter(): lax.psum_scatter(partial, 'ctx', scatter_dimension=0, axis_index_groups=l...  23.9 us
    unnamed x109, local copies, waits for them, and re-layouts  20.2 us
  transfers between devices with their start and end apart: 93, of which 43 were waited for; matrix products, arithmetic and copies ran while one was open for 12% of the time, Pallas kernels for 34%

profile of v5, /device:TPU:0, one launch (start us, length us, event | category | flops | bytes accessed | tf_op | source)
XLA Modules:
  0.0 669.6 jit_solution(7463779479668414892)
XLA Ops:
  7.2 2.1 shard_map.237
  9.4 15.1 %all_to_all.30 = bf16[4,128,640]{2,1,0:T(8,128)(2,1)} all-to-all(bf16[4,128,640]{2,1,0:T(8,128)(2,1)} %shard_map.237), channel_id=1, replica_groups={{0,2,4,6},{8,10,12,14},{16,18,20,22},{24,26,28,30},{1,3,5,7},{9,11,13,1..., dimensions={0} | all-to-all | bytes 1310720 | tf_op jit(solution)/shard_map/all_to_all | solution.py:154
  24.6 3.9 shard_map.238
  28.4 24.5 %all_to_all.31 = bf16[4,128,1536]{2,1,0:T(8,128)(2,1)} all-to-all(bf16[4,128,1536]{2,1,0:T(8,128)(2,1)} %get-tuple-element.152), channel_id=1, replica_groups={{0,2,4,6},{8,10,12,14},{16,18,20,22},{24,26,28,30},{1,3,5,7},{9,11,13,1..., dimensions={0} | all-to-all | bytes 3145728 | tf_op jit(solution)/shard_map/all_to_all | solution.py:154
  59.5 2.1 collective-permute-start.2
  63.3 2.8 fusion.18
  66.1 2.5 pad_maximum_fusion.1
  68.6 12.3 %collective-permute-done.2.refs_3_ = bf16[192,2048]{1,0:T(8,128)(2,1)S(1)} collective-permute-done((bf16[192,2048]{1,0:T(8,128)(2,1)S(1)}, bf16[192,2048]{1,0:T(8,128)(2,1)S(1)}, u32[]{:S(2)}, u32[]{:S(2)}) %collective-permute-start.2) | collective-permute-done | bytes 786464 | tf_op jit(solution)/shard_map/ppermute | solution.py:73
  80.9 16.0 %collective-permute-done.1.refs_2_ = bf16[192,2048]{1,0:T(8,128)(2,1)S(1)} collective-permute-done((bf16[192,2048]{1,0:T(8,128)(2,1)S(1)}, bf16[192,2048]{1,0:T(8,128)(2,1)S(1)}, u32[]{:S(2)}, u32[]{:S(2)}) %collective-permute-start.1) | collective-permute-done | bytes 786464 | tf_op jit(solution)/shard_map/ppermute | solution.py:26
  98.0 3.6 all-to-all-start.2
  104.6 2.4 broadcast_subtract_fusion
  107.0 2.7 slice.236.refs_8_.w_ref.refs_0_
  109.7 14.2 %shard_map.239 = (bf16[1536,2048]{1,0:T(8,128)(2,1)}, f32[1536,384]{1,0:T(8,128)}, bf16[1536,256]{1,0:T(8,128)(2,1)}, bf16[1536,128]{1,0:T(8,128)(2,1)}) custom-call(s32[8]{0:T(128)} %or_or_fusion.table, bf16[192,2048]{1,0:T(8,128)(2,1)} %copy-done.5, bf16[192,2048]{1,0:T(8,128)(2,1)} %copy-done.17, bf16[192,2048]{1,0:T(8,128)(2,1)} %copy-done.15, ...), custom_call_target="tpu_custom_call" | custom-call | flops 2415919104 | bytes 16515072 | tf_op jit(solution)/shard_map/pallas_call | solution.py:619
  129.3 3.5 collective-permute-start.10
  132.9 5.1 collective-permute-start.11
  138.2 14.0 %shard_map.240.refs_0_ = f32[6144,128]{1,0:T(8,128)} custom-call(s32[8]{0:T(128)} %or_or_fusion.1.table, s32[8]{0:T(128)} %get-tuple-element.296.lo, s32[8]{0:T(128)} %get-tuple-element.295.hi, bf16[1536,256]{1,0:T(8,128)(2,1)} %get-tuple-element.163.q_ref, s32[1536,1]{1,0:T(8,128)} %get-tuple-element.325.start_ref, bf16[1536,128]{1,0:T(8,128)(2,1)} %get-tuple-element.164.kv_ref), custom_call_target="tpu_custom_call" | custom-call | flops 4831838208 | bytes 3932160 | tf_op jit(solution)/shard_map/pallas_call | solution.py:619
  152.2 2.3 slice.237.w_ref.refs_10_
  154.5 4.5 collective-permute-done.11
  166.9 2.5 copy-done.26
  170.3 9.2 %shard_map.241 = (bf16[1536,256]{1,0:T(8,128)(2,1)}, f32[1536,256]{1,0:T(8,128)}, f32[6144,1]{1,0:T(8,128)}) custom-call(s32[8]{0:T(128)} %or_or_fusion.1.table, s32[8]{0:T(128)} %get-tuple-element.294.lo, s32[8]{0:T(128)} %get-tuple-element.293.hi, bf16[1536,256]{1,0:T(8,128)(2,1)} %get-tuple-element.163.q_ref, s32[1536,1]{1,0:T(8,128)} %get-tuple-element.326.start_ref, ...), custom_call_target="tpu_custom_call" | custom-call | flops 4831838208 | bytes 3932160 | tf_op jit(solution)/shard_map/pallas_call | solution.py:619
  179.5 7.2 %shard_map.242 = (bf16[768,2048]{1,0:T(8,128)(2,1)}, bf16[192,2048]{1,0:T(8,128)(2,1)}, bf16[192,2048]{1,0:T(8,128)(2,1)}, bf16[192,2048]{1,0:T(8,128)(2,1)}, bf16[192,2048]{1,0:T(8,128)(2,1)}) custom-call(bf16[1536,256]{1,0:T(8,128)(2,1)} %get-tuple-element.172.a_ref.d_ref, bf16[2048,256]{1,0:T(8,128)(2,1)} %slice.237.w_ref.refs_10_), custom_call_target="tpu_custom_call" | custom-call | flops 1610612736 | bytes 7077888 | tf_op jit(solution)/shard_map/pallas_call | solution.py:619
  189.2 2.1 constant_dynamic-update-slice_fusion.6
  201.1 6.4 collective-permute-done.21
  208.2 7.2 %collective-permute-done.19 = bf16[96,2048]{1,0:T(8,128)(2,1)S(1)} collective-permute-done((bf16[96,2048]{1,0:T(8,128)(2,1)S(1)}, bf16[96,2048]{1,0:T(8,128)(2,1)S(1)}, u32[]{:S(2)}, u32[]{:S(2)}) %collective-permute-start.19) | collective-permute-done | bytes 393248 | tf_op jit(solution)/shard_map/ppermute | solution.py:26
  218.7 6.9 %collective-permute-done.29 = bf16[96,2048]{1,0:T(8,128)(2,1)S(1)} collective-permute-done((bf16[96,2048]{1,0:T(8,128)(2,1)S(1)}, bf16[96,2048]{1,0:T(8,128)(2,1)S(1)}, u32[]{:S(2)}, u32[]{:S(2)}) %collective-permute-start.29) | collective-permute-done | bytes 393248 | tf_op jit(solution)/shard_map/ppermute | solution.py:26
  230.0 15.4 %collective-permute-done.32.refs_2_ = bf16[192,2048]{1,0:T(8,128)(2,1)S(1)} collective-permute-done((bf16[192,2048]{1,0:T(8,128)(2,1)S(1)}, bf16[192,2048]{1,0:T(8,128)(2,1)S(1)}, u32[]{:S(2)}, u32[]{:S(2)}) %collective-permute-start.32) | collective-permute-done | bytes 786464 | tf_op jit(solution)/shard_map/ppermute | solution.py:26
  248.6 5.5 collective-permute-done.33.refs_3_
  254.1 4.3 collective-permute-done.34.refs_4_
  261.0 24.8 %shard_map.243 = (bf16[1536,512]{1,0:T(8,128)(2,1)}, bf16[1536,1024]{1,0:T(8,128)(2,1)}, bf16[1536,2048]{1,0:T(8,128)(2,1)}, bf16[1536,2048]{1,0:T(8,128)(2,1)}) custom-call(bf16[192,2048]{1,0:T(8,128)(2,1)} %copy-done.20, bf16[192,2048]{1,0:T(8,128)(2,1)} %copy-done.23, bf16[192,2048]{1,0:T(8,128)(2,1)} %copy-done.22, bf16[96,2048]{1,0:T(8,128)(2,1)} %copy-done.44, ...), custom_call_target="tpu_custom_call" | custom-call | flops 19327352832 | bytes 36175872 | tf_op jit(solution)/shard_map/pallas_call | solution.py:619
  285.8 15.6 %shard_map.244 = bf16[2048,1536]{1,0:T(8,128)(2,1)} custom-call(bf16[1536,2048]{1,0:T(8,128)(2,1)} %get-tuple-element.185.a_ref, bf16[1536,1024]{1,0:T(8,128)(2,1)} %get-tuple-element.187.b_ref, bf16[1536,2048]{1,0:T(8,128)(2,1)} %constant_dynamic-update-slice_fusion.2.refs_10_.c_ref, bf16[1536,512]{1,0:T(8,128)(2,1)} %get-tuple-element.188.d_ref.h0_ref), custom_call_target="tpu_custom_call" | custom-call | flops 9663676416 | bytes 23592960 | tf_op jit(solution)/shard_map/pallas_call | solution.py:619
  301.5 27.2 %all-gather.8.cloned.1.call-done.w_ref.w1_ref = bf16[2048,1536]{1,0:T(8,128)(2,1)} async-done(((bf16[512,1536]{1,0:T(8,128)(2,1)}), bf16[2048,1536]{1,0:T(8,128)(2,1)}) %all-gather.8.cloned.1.call-update) | async-done | bytes 6291472 | tf_op jit(solution)/shard_map/all_gather | solution.py:51
  328.6 25.6 %shard_map.245 = (bf16[1536,512]{1,0:T(8,128)(2,1)}, bf16[1536,1024]{1,0:T(8,128)(2,1)}, bf16[768,2048]{1,0:T(8,128)(2,1)}, bf16[192,2048]{1,0:T(8,128)(2,1)}, b...) custom-call(bf16[1536,2048]{1,0:T(8,128)(2,1)} %get-tuple-element.185.a_ref, ...), custom_call_target="tpu_custom_call" | custom-call | flops 19327352832 | bytes 36175872 | tf_op jit(solution)/shard_map/pallas_call | solution.py:619
  360.2 4.2 add_convert_fusion.9
  371.1 15.0 %shard_map.246 = bf16[2048,1536]{1,0:T(8,128)(2,1)} custom-call(bf16[1536,2048]{1,0:T(8,128)(2,1)} %get-tuple-element.185.a_ref, bf16[1536,1024]{1,0:T(8,128)(2,1)} %get-tuple-element.196.b_ref, bf16[1536,2048]{1,0:T(8,128)(2,1)} %constant_dynamic-update-slice_fusion.2.refs_10_.c_ref, bf16[1536,512]{1,0:T(8,128)(2,1)} %get-tuple-element.197.d_ref.h1_ref), custom_call_target="tpu_custom_call" | custom-call | flops 9663676416 | bytes 23592960 | tf_op jit(solution)/shard_map/pallas_call | solution.py:619
  391.7 8.0 %collective-permute-done.48 = bf16[96,2048]{1,0:T(8,128)(2,1)S(1)} collective-permute-done((bf16[96,2048]{1,0:T(8,128)(2,1)S(1)}, bf16[96,2048]{1,0:T(8,128)(2,1)S(1)}, u32[]{:S(2)}, u32[]{:S(2)}) %collective-permute-start.48) | collective-permute-done | bytes 393248 | tf_op jit(solution)/shard_map/ppermute | solution.py:26
  406.2 15.3 %shard_map.247 = (bf16[768,2048]{1,0:T(8,128)(2,1)}, bf16[192,2048]{1,0:T(8,128)(2,1)}, bf16[192,2048]{1,0:T(8,128)(2,1)}, bf16[192,2048]{1,0:T(8,128)(2,1)}, bf16[192,2048]{1,0:T(8,128)(2,1)}) custom-call(bf16[1536,512]{1,0:T(8,128)(2,1)} %get-tuple-element.188.d_ref.h0_ref, bf16[1536,512]{1,0:T(8,128)(2,1)} %get-tuple-element.197.d_ref.h1_ref, ...), custom_call_target="tpu_custom_call" | custom-call | flops 6442450944 | bytes 22020096 | tf_op jit(solution)/shard_map/pallas_call | solution.py:619
  427.1 7.1 %collective-permute-done.52.refs_3_ = bf16[96,2048]{1,0:T(8,128)(2,1)S(1)} collective-permute-done((bf16[96,2048]{1,0:T(8,128)(2,1)S(1)}, bf16[96,2048]{1,0:T(8,128)(2,1)S(1)}, u32[]{:S(2)}, u32[]{:S(2)}) %collective-permute-start.52) | collective-permute-done | bytes 393248 | tf_op jit(solution)/shard_map/ppermute | solution.py:38
  434.2 2.4 collective-permute-done.53.refs_4_
  445.5 8.1 %shard_map.248 = (bf16[1536,2048]{1,0:T(8,128)(2,1)}, bf16[1536,256]{1,0:T(8,128)(2,1)}) custom-call(bf16[192,2048]{1,0:T(8,128)(2,1)} %copy-done.10, bf16[192,2048]{1,0:T(8,128)(2,1)} %collective-permute-done.50.refs_1_, bf16[192,2048]{1,0:T(8,128)(2,1)} %collective-permute-done.51.refs_2_, bf16[96,2048]{1,0:T(8,128)(2,1)} %copy-done.21, ...), custom_call_target="tpu_custom_call" | custom-call | flops 1610612736 | bytes 12582912 | tf_op jit(solution)/shard_map/pallas_call | solution.py:619
  454.6 2.7 add_convert_fusion.5
  461.6 10.8 %shard_map.249 = (f32[6144,128]{1,0:T(8,128)}, bf16[768,128]{1,0:T(8,128)(2,1)}, bf16[1536,128]{1,0:T(8,128)(2,1)}) custom-call(s32[8]{0:T(128)} %or_or_fusion.1.table, s32[8]{0:T(128)} %get-tuple-element.294.lo, s32[8]{0:T(128)} %get-tuple-element.293.hi, bf16[1536,256]{1,0:T(8,128)(2,1)} %get-tuple-element.163.q_ref, ...), custom_call_target="tpu_custom_call" | custom-call | flops 12079595520 | bytes 4718592 | tf_op jit(solution)/shard_map/pallas_call | solution.py:619
  472.4 4.6 collective-permute-done.64
  478.2 4.4 all-to-all-start.3
  485.2 30.6 %shard_map.250 = (f32[1536,256]{1,0:T(8,128)}, f32[1536,128]{1,0:T(8,128)}) custom-call(s32[8]{0:T(128)} %or_or_fusion.1.table, s32[8]{0:T(128)} %get-tuple-element.296.lo, s32[8]{0:T(128)} %get-tuple-element.295.hi, bf16[1536,256]{1,0:T(8,128)(2,1)} %get-tuple-element.163.q_ref, bf16[1536,256]{1,0:T(8,128)(2,1)} %get-tuple-element.215.do_ref, ...), custom_call_target="tpu_custom_call" | custom-call | flops 12079595520 | bytes 4718592 | tf_op jit(solution)/shard_map/pallas_call | solution.py:619
  515.9 2.7 collective-permute-done.68.refs_1_
  518.6 4.2 collective-permute-done.67.refs_0_
  522.8 9.1 %shard_map.251 = (bf16[1536,384]{1,0:T(8,128)(2,1)}, f32[8,128]{1,0:T(8,128)}) custom-call(s32[8]{0:T(128)} %or_or_fusion.1.table, f32[1536,384]{1,0:T(8,128)} %get-tuple-element.159.raw_ref, f32[1536,128]{1,0:T(8,128)} %get-tuple-element.157.refs_9_.cos_ref, f32[1536,128]{1,0:T(8,128)} %get-tuple-element.158.refs_10_.sin_ref, ...), custom_call_target="tpu_custom_call" | custom-call | flops 9830400 | bytes 5898240 | tf_op jit(solution)/shard_map/pallas_call | solution.py:619
  531.9 8.5 %shard_map.252 = (bf16[768,2048]{1,0:T(8,128)(2,1)}, bf16[192,2048]{1,0:T(8,128)(2,1)}, bf16[192,2048]{1,0:T(8,128)(2,1)}, bf16[192,2048]{1,0:T(8,128)(2,1)}, bf16[192,2048]{1,0:T(8,128)(2,1)}) custom-call(bf16[1536,384]{1,0:T(8,128)(2,1)} %get-tuple-element.245.a_ref.b_ref, bf16[2048,384]{1,0:T(8,128)(2,1)} %slice.236.refs_8_.w_ref.refs_0_), custom_call_target="tpu_custom_call" | custom-call | flops 2415919104 | bytes 7471104 | tf_op jit(solution)/shard_map/pallas_call | solution.py:619
  540.5 11.2 %shard_map.253 = (f32[8,2048]{1,0:T(8,128)}, bf16[2048,640]{1,0:T(8,128)(2,1)}) custom-call(bf16[1536,2048]{1,0:T(8,128)(2,1)} %get-tuple-element.244.a_ref, bf16[1536,384]{1,0:T(8,128)(2,1)} %get-tuple-element.245.a_ref.b_ref, bf16[1536,2048]{1,0:T(8,128)(2,1)} %get-tuple-element.246.c_ref, bf16[1536,256]{1,0:T(8,128)(2,1)} %get-tuple-element.172.a_ref.d_ref, ...), custom_call_target="tpu_custom_call" | custom-call | flops 4026531840 | bytes 17170432 | tf_op jit(solution)/shard_map/pallas_call | solution.py:619
  557.6 4.4 add_convert_fusion.1
  562.0 6.5 reduce-scatter.6.cloned.1.call-done
  568.5 2.0 add_convert_fusion.17
  570.4 2.0 add_convert_fusion.18
  576.7 4.5 all-to-all-start.4
  585.3 2.0 fusion.13
  588.4 13.2 %collective-permute-done.73 = bf16[192,2048]{1,0:T(8,128)(2,1)S(1)} collective-permute-done((bf16[192,2048]{1,0:T(8,128)(2,1)S(1)}, bf16[192,2048]{1,0:T(8,128)(2,1)S(1)}, u32[]{:S(2)}, u32[]{:S(2)}) %collective-permute-start.73) | collective-permute-done | bytes 786464 | tf_op jit(solution)/shard_map/ppermute | solution.py:38
  604.8 5.1 shard_map.254
  609.9 17.4 %reduce-scatter.8.cloned.1.call-done = bf16[512,640]{1,0:T(8,128)(2,1)} async-done(((bf16[2048,640]{1,0:T(8,128)(2,1)}), bf16[512,640]{1,0:T(8,128)(2,1)}) %reduce-scatter.8.cloned.1.call-update) | async-done | bytes 655376 | tf_op jit(solution)/shard_map/reduce_scatter | solution.py:55
  627.4 4.2 all-to-all-start.5
  634.9 2.3 collective-permute-done.78
  638.4 2.0 collective-permute-start.80
  642.2 12.1 %collective-permute-start.81 = (f32[4224]{0:T(1024)S(1)}, f32[4224]{0:T(1024)S(1)}, u32[]{:S(2)}, u32[]{:S(2)}) collective-permute-start(f32[4224]{0:T(1024)S(1)} %add.267), channel_id=1, source_target_pairs={{0,8},{2,10},{4,12},{6,14},{8,0},{10,2},{12,4},{14,6},{16,24},{18,... | collective-permute-start | bytes 50696 | tf_op jit(solution)/shard_map/ppermute | solution.py:26
  656.1 3.0 fusion.7
  659.1 2.2 shard_map.255
  (343 shorter events, 129.0 us)
Async XLA Ops:
  7.2 99.8 %all-gather.4.cloned.1.call-start = ((), (), s32[]{:S(2)}) async-start(), calls=%async_computation.9 | async-start | bytes 3276800 | tf_op jit(solution)/shard_map/all_gather | solution.py:51
  24.5 236.5 %all-gather.6.cloned.1.call-start = ((), (), s32[]{:S(2)}) async-start(), calls=%async_computation.10 | async-start | bytes 7864320 | tf_op jit(solution)/shard_map/all_gather | solution.py:51
  59.5 21.4 %collective-permute-start.2 = (bf16[192,2048]{1,0:T(8,128)(2,1)S(1)}, bf16[192,2048]{1,0:T(8,128)(2,1)S(1)}, u32[]{:S(2)}, u32[]{:S(2)}) collective-permute-start(bf16[192,2048]{1,0:T(8,128)(2,1)S(1)} %fusion.3.refs_0_), channel_id=1, source_target_pairs={{0,5},{1,4},{2,7},{3,6},{4,1},{5,0},{6,3},{7,2},{8,13},{9,12},{10,... | collective-permute-start | bytes 2359304 | tf_op jit(solution)/shard_map/ppermute | solution.py:73
  61.6 35.3 %collective-permute-start.1 = (bf16[192,2048]{1,0:T(8,128)(2,1)S(1)}, bf16[192,2048]{1,0:T(8,128)(2,1)S(1)}, u32[]{:S(2)}, u32[]{:S(2)}) collective-permute-start(bf16[192,2048]{1,0:T(8,128)(2,1)S(1)} %fusion.3.refs_0_), channel_id=1, source_target_pairs={{0,4},{2,6},{4,0},{6,2},{8,12},{10,14},{12,8},{14,10},{16,20},{18,... | collective-permute-start | bytes 2359304 | tf_op jit(solution)/shard_map/ppermute | solution.py:26
  63.3 33.6 %collective-permute-start = (bf16[192,2048]{1,0:T(8,128)(2,1)S(1)}, bf16[192,2048]{1,0:T(8,128)(2,1)S(1)}, u32[]{:S(2)}, u32[]{:S(2)}) collective-permute-start(bf16[192,2048]{1,0:T(8,128)(2,1)S(1)} %fusion.3.refs_0_), channel_id=1, source_target_pairs={{0,1},{1,0},{2,3},{3,2},{4,5},{5,4},{6,7},{7,6},{8,9},{9,8},{10,11... | collective-permute-start | bytes 2359304 | tf_op jit(solution)/shard_map/ppermute | solution.py:38
  68.6 41.1 %collective-permute-start.6 = (bf16[192,2048]{1,0:T(8,128)(2,1)S(1)}, bf16[192,2048]{1,0:T(8,128)(2,1)}, u32[]{:S(2)}, u32[]{:S(2)}) collective-permute-start(bf16[192,2048]{1,0:T(8,128)(2,1)S(1)} %fusion.3.refs_0_), channel_id=1, source_target_pairs={{0,2},{2,0},{4,6},{6,4},{8,10},{10,8},{12,14},{14,12},{16,18},{18,... | collective-permute-start | bytes 2359304 | tf_op jit(solution)/shard_map/ppermute | solution.py:26
  98.0 25.9 %all-to-all-start.2 = ((bf16[4,128,1536]{2,1,0:T(8,128)(2,1)}), bf16[4,128,1536]{2,1,0:T(8,128)(2,1)S(1)}, u32[]{:S(2)}, u32[]{:S(2)}) async-start(bf16[4,128,1536]{2,1,0:T(8,128)(2,1)} %get-tuple-element.162), calls=%async_computation.2 | async-start | bytes 3145728 | tf_op jit(solution)/shard_map/all_to_all | solution.py:154
  101.6 227.0 %all-gather.8.cloned.1.call-start = ((), (), s32[]{:S(2)}) async-start(), calls=%async_computation.11 | async-start | bytes 7864320 | tf_op jit(solution)/shard_map/all_gather | solution.py:51
  124.0 35.1 %collective-permute-start.13 = (bf16[192,2048]{1,0:T(8,128)(2,1)S(1)}, bf16[192,2048]{1,0:T(8,128)(2,1)}, u32[]{:S(2)}, u32[]{:S(2)}) collective-permute-start(bf16[192,2048]{1,0:T(8,128)(2,1)S(1)} %copy-done.12), channel_id=1, source_target_pairs={{0,4},{2,6},{4,0},{6,2},{8,12},{10,14},{12,8},{14,10},{16,20},{18,... | collective-permute-start | bytes 2359304 | tf_op jit(solution)/shard_map/ppermute | solution.py:26
  125.7 33.3 %collective-permute-start.12 = (bf16[192,2048]{1,0:T(8,128)(2,1)S(1)}, bf16[192,2048]{1,0:T(8,128)(2,1)}, u32[]{:S(2)}, u32[]{:S(2)}) collective-permute-start(bf16[192,2048]{1,0:T(8,128)(2,1)S(1)} %copy-done.12), channel_id=1, source_target_pairs={{0,1},{1,0},{2,3},{3,2},{4,5},{5,4},{6,7},{7,6},{8,9},{9,8},{10,11... | collective-permute-start | bytes 2359304 | tf_op jit(solution)/shard_map/ppermute | solution.py:38
  129.3 29.7 %collective-permute-start.10 = (bf16[1536,128]{1,0:T(8,128)(2,1)}, bf16[1536,128]{1,0:T(8,128)(2,1)S(1)}, u32[]{:S(2)}, u32[]{:S(2)}) collective-permute-start(bf16[1536,128]{1,0:T(8,128)(2,1)} %get-tuple-element.164.kv_ref), channel_id=1, source_target_pairs={{0,8},{2,10},{4,12},{6,14},{8,16},{10,18},{12,20},{14,22},{16,24},... | collective-permute-start | bytes 1179656 | tf_op jit(solution)/shard_map/ppermute | solution.py:60
  132.8 55.1 %collective-permute-start.24 = (bf16[192,2048]{1,0:T(8,128)(2,1)S(1)}, bf16[192,2048]{1,0:T(8,128)(2,1)}, u32[]{:S(2)}, u32[]{:S(2)}) collective-permute-start(bf16[192,2048]{1,0:T(8,128)(2,1)S(1)} %copy-done.12), channel_id=1, source_target_pairs={{0,2},{2,0},{4,6},{6,4},{8,10},{10,8},{12,14},{14,12},{16,18},{18,... | collective-permute-start | bytes 2359304 | tf_op jit(solution)/shard_map/ppermute | solution.py:26
  132.9 26.1 %collective-permute-start.11 = (bf16[768,128]{1,0:T(8,128)(2,1)}, bf16[768,128]{1,0:T(8,128)(2,1)}, u32[]{:S(2)}, u32[]{:S(2)}) collective-permute-start(bf16[768,128]{1,0:T(8,128)(2,1)} %slice.180), channel_id=1, source_target_pairs={{0,16},{2,18},{4,20},{6,22},{8,24},{10,26},{12,28},{14,30},{1,17},... | collective-permute-start | bytes 589832 | tf_op jit(solution)/shard_map/ppermute | solution.py:60
  138.0 340.2 %reduce-scatter.4.cloned.1.call-start = ((), (), s32[]{:S(2)}) async-start(), calls=%async_computation.12 | async-start | bytes 7864320 | tf_op jit(solution)/shard_map/reduce_scatter | solution.py:55
  160.1 32.2 %collective-permute-start.26 = (bf16[192,2048]{1,0:T(8,128)(2,1)}, bf16[192,2048]{1,0:T(8,128)(2,1)S(1)}, u32[]{:S(2)}, u32[]{:S(2)}) collective-permute-start(bf16[192,2048]{1,0:T(8,128)(2,1)} %collective-permute-done.13), channel_id=1, source_target_pairs={{0,2},{2,0},{4,6},{6,4},{8,10},{10,8},{12,14},{14,12},{16,18},{18,... | collective-permute-start | bytes 2359304 | tf_op jit(solution)/shard_map/ppermute | solution.py:26
  161.2 26.8 %collective-permute-start.25 = (bf16[192,2048]{1,0:T(8,128)(2,1)}, bf16[192,2048]{1,0:T(8,128)(2,1)S(1)}, u32[]{:S(2)}, u32[]{:S(2)}) collective-permute-start(bf16[192,2048]{1,0:T(8,128)(2,1)} %collective-permute-done.12), channel_id=1, source_target_pairs={{0,2},{2,0},{4,6},{6,4},{8,10},{10,8},{12,14},{14,12},{16,18},{18,... | collective-permute-start | bytes 2359304 | tf_op jit(solution)/shard_map/ppermute | solution.py:26
  162.7 16.8 %collective-permute-start.15 = (bf16[96,2048]{1,0:T(8,128)(2,1)S(1)}, bf16[96,2048]{1,0:T(8,128)(2,1)S(1)}, u32[]{:S(2)}, u32[]{:S(2)}) collective-permute-start(bf16[96,2048]{1,0:T(8,128)(2,1)S(1)} %slice.182), channel_id=1, source_target_pairs={{0,4},{2,6},{4,0},{6,2},{8,12},{10,14},{12,8},{14,10},{16,20},{18,... | collective-permute-start | bytes 1179656 | tf_op jit(solution)/shard_map/ppermute | solution.py:26
  163.1 16.4 %collective-permute-start.14 = (bf16[96,2048]{1,0:T(8,128)(2,1)S(1)}, bf16[96,2048]{1,0:T(8,128)(2,1)S(1)}, u32[]{:S(2)}, u32[]{:S(2)}) collective-permute-start(bf16[96,2048]{1,0:T(8,128)(2,1)S(1)} %slice.181), channel_id=1, source_target_pairs={{0,1},{1,0},{2,3},{3,2},{4,5},{5,4},{6,7},{7,6},{8,9},{9,8},{10,11... | collective-permute-start | bytes 1179656 | tf_op jit(solution)/shard_map/ppermute | solution.py:38
  195.4 12.0 %collective-permute-start.21 = (bf16[96,2048]{1,0:T(8,128)(2,1)S(1)}, bf16[96,2048]{1,0:T(8,128)(2,1)S(1)}, u32[]{:S(2)}, u32[]{:S(2)}) collective-permute-start(bf16[96,2048]{1,0:T(8,128)(2,1)S(1)} %slice.241), channel_id=1, source_target_pairs={{0,1},{1,0},{2,3},{3,2},{4,5},{5,4},{6,7},{7,6},{8,9},{9,8},{10,11... | collective-permute-start | bytes 1179656 | tf_op jit(solution)/shard_map/ppermute | solution.py:38
  196.2 12.0 %collective-permute-start.23 = (bf16[96,2048]{1,0:T(8,128)(2,1)S(1)}, bf16[96,2048]{1,0:T(8,128)(2,1)S(1)}, u32[]{:S(2)}, u32[]{:S(2)}) collective-permute-start(bf16[96,2048]{1,0:T(8,128)(2,1)S(1)} %slice.242), channel_id=1, source_target_pairs={{0,4},{2,6},{4,0},{6,2},{8,12},{10,14},{12,8},{14,10},{16,20},{18,... | collective-permute-start | bytes 1179656 | tf_op jit(solution)/shard_map/ppermute | solution.py:26
  197.9 17.5 %collective-permute-start.19 = (bf16[96,2048]{1,0:T(8,128)(2,1)S(1)}, bf16[96,2048]{1,0:T(8,128)(2,1)S(1)}, u32[]{:S(2)}, u32[]{:S(2)}) collective-permute-start(bf16[96,2048]{1,0:T(8,128)(2,1)S(1)} %get-tuple-element.323), channel_id=1, source_target_pairs={{0,4},{2,6},{4,0},{6,2},{8,12},{10,14},{12,8},{14,10},{16,20},{18,... | collective-permute-start | bytes 1179656 | tf_op jit(solution)/shard_map/ppermute | solution.py:26
  198.2 17.2 %collective-permute-start.18 = (bf16[96,2048]{1,0:T(8,128)(2,1)S(1)}, bf16[96,2048]{1,0:T(8,128)(2,1)S(1)}, u32[]{:S(2)}, u32[]{:S(2)}) collective-permute-start(bf16[96,2048]{1,0:T(8,128)(2,1)S(1)} %get-tuple-element.324), channel_id=1, source_target_pairs={{0,1},{1,0},{2,3},{3,2},{4,5},{5,4},{6,7},{7,6},{8,9},{9,8},{10,11... | collective-permute-start | bytes 1179656 | tf_op jit(solution)/shard_map/ppermute | solution.py:38
  215.6 10.0 %collective-permute-start.29 = (bf16[96,2048]{1,0:T(8,128)(2,1)S(1)}, bf16[96,2048]{1,0:T(8,128)(2,1)S(1)}, u32[]{:S(2)}, u32[]{:S(2)}) collective-permute-start(bf16[96,2048]{1,0:T(8,128)(2,1)S(1)} %add_convert_fusion.22), channel_id=1, source_target_pairs={{0,4},{2,6},{4,0},{6,2},{8,12},{10,14},{12,8},{14,10},{16,20},{18,... | collective-permute-start | bytes 1179656 | tf_op jit(solution)/shard_map/ppermute | solution.py:26
  217.4 9.6 %collective-permute-start.30 = (bf16[96,2048]{1,0:T(8,128)(2,1)S(1)}, bf16[96,2048]{1,0:T(8,128)(2,1)S(1)}, u32[]{:S(2)}, u32[]{:S(2)}) collective-permute-start(bf16[96,2048]{1,0:T(8,128)(2,1)S(1)} %add_convert_fusion.21), channel_id=1, source_target_pairs={{0,1},{1,0},{2,3},{3,2},{4,5},{5,4},{6,7},{7,6},{8,9},{9,8},{10,11... | collective-permute-start | bytes 1179656 | tf_op jit(solution)/shard_map/ppermute | solution.py:38
  228.2 17.2 %collective-permute-start.32 = (bf16[192,2048]{1,0:T(8,128)(2,1)S(1)}, bf16[192,2048]{1,0:T(8,128)(2,1)S(1)}, u32[]{:S(2)}, u32[]{:S(2)}) collective-permute-start(bf16[192,2048]{1,0:T(8,128)(2,1)S(1)} %multiply_convert_fusion.refs_0_), channel_id=1, source_target_pairs={{0,4},{2,6},{4,0},{6,2},{8,12},{10,14},{12,8},{14,10},{16,20},{18,... | collective-permute-start | bytes 2359304 | tf_op jit(solution)/shard_map/ppermute | solution.py:26
  228.6 18.2 %collective-permute-start.31 = (bf16[192,2048]{1,0:T(8,128)(2,1)S(1)}, bf16[192,2048]{1,0:T(8,128)(2,1)S(1)}, u32[]{:S(2)}, u32[]{:S(2)}) collective-permute-start(bf16[192,2048]{1,0:T(8,128)(2,1)S(1)} %multiply_convert_fusion.refs_0_), channel_id=1, source_target_pairs={{0,1},{1,0},{2,3},{3,2},{4,5},{5,4},{6,7},{7,6},{8,9},{9,8},{10,11... | collective-permute-start | bytes 2359304 | tf_op jit(solution)/shard_map/ppermute | solution.py:38
  230.0 28.5 %collective-permute-start.35 = (bf16[192,2048]{1,0:T(8,128)(2,1)S(1)}, bf16[192,2048]{1,0:T(8,128)(2,1)S(1)}, u32[]{:S(2)}, u32[]{:S(2)}) collective-permute-start(bf16[192,2048]{1,0:T(8,128)(2,1)S(1)} %multiply_convert_fusion.refs_0_), channel_id=1, source_target_pairs={{0,2},{2,0},{4,6},{6,4},{8,10},{10,8},{12,14},{14,12},{16,18},{18,... | collective-permute-start | bytes 2359304 | tf_op jit(solution)/shard_map/ppermute | solution.py:26
  246.8 11.7 %collective-permute-start.37 = (bf16[192,2048]{1,0:T(8,128)(2,1)S(1)}, bf16[192,2048]{1,0:T(8,128)(2,1)S(1)}, u32[]{:S(2)}, u32[]{:S(2)}) collective-permute-start(bf16[192,2048]{1,0:T(8,128)(2,1)S(1)} %collective-permute-done.32.refs_2_), channel_id=1, source_target_pairs={{0,2},{2,0},{4,6},{6,4},{8,10},{10,8},{12,14},{14,12},{16,18},{18,... | collective-permute-start | bytes 2359304 | tf_op jit(solution)/shard_map/ppermute | solution.py:26
  246.9 11.6 %collective-permute-start.34 = (bf16[96,2048]{1,0:T(8,128)(2,1)S(1)}, bf16[96,2048]{1,0:T(8,128)(2,1)S(1)}, u32[]{:S(2)}, u32[]{:S(2)}) collective-permute-start(bf16[96,2048]{1,0:T(8,128)(2,1)S(1)} %slice.247), channel_id=1, source_target_pairs={{0,4},{2,6},{4,0},{6,2},{8,12},{10,14},{12,8},{14,10},{16,20},{18,... | collective-permute-start | bytes 1179656 | tf_op jit(solution)/shard_map/ppermute | solution.py:26
  248.6 12.4 %collective-permute-start.36 = (bf16[192,2048]{1,0:T(8,128)(2,1)S(1)}, bf16[192,2048]{1,0:T(8,128)(2,1)}, u32[]{:S(2)}, u32[]{:S(2)}) collective-permute-start(bf16[192,2048]{1,0:T(8,128)(2,1)S(1)} %collective-permute-done.31.refs_1_), channel_id=1, source_target_pairs={{0,2},{2,0},{4,6},{6,4},{8,10},{10,8},{12,14},{14,12},{16,18},{18,... | collective-permute-start | bytes 2359304 | tf_op jit(solution)/shard_map/ppermute | solution.py:26
  301.4 267.1 %reduce-scatter.6.cloned.1.call-start = ((), (), s32[]{:S(2)}) async-start(), calls=%async_computation.13 | async-start | bytes 7864320 | tf_op jit(solution)/shard_map/reduce_scatter | solution.py:55
  366.1 20.0 %collective-permute-start.45 = (bf16[96,2048]{1,0:T(8,128)(2,1)}, bf16[96,2048]{1,0:T(8,128)(2,1)S(1)}, u32[]{:S(2)}, u32[]{:S(2)}) collective-permute-start(bf16[96,2048]{1,0:T(8,128)(2,1)} %slice.251), channel_id=1, source_target_pairs={{0,1},{1,0},{2,3},{3,2},{4,5},{5,4},{6,7},{7,6},{8,9},{9,8},{10,11... | collective-permute-start | bytes 1179656 | tf_op jit(solution)/shard_map/ppermute | solution.py:38
  367.6 18.6 %collective-permute-start.47 = (bf16[96,2048]{1,0:T(8,128)(2,1)}, bf16[96,2048]{1,0:T(8,128)(2,1)}, u32[]{:S(2)}, u32[]{:S(2)}) collective-permute-start(bf16[96,2048]{1,0:T(8,128)(2,1)} %slice.252), channel_id=1, source_target_pairs={{0,4},{2,6},{4,0},{6,2},{8,12},{10,14},{12,8},{14,10},{16,20},{18,... | collective-permute-start | bytes 1179656 | tf_op jit(solution)/shard_map/ppermute | solution.py:26
  370.0 17.2 %collective-permute-start.43 = (bf16[96,2048]{1,0:T(8,128)(2,1)}, bf16[96,2048]{1,0:T(8,128)(2,1)}, u32[]{:S(2)}, u32[]{:S(2)}) collective-permute-start(bf16[96,2048]{1,0:T(8,128)(2,1)} %get-tuple-element.321), channel_id=1, source_target_pairs={{0,4},{2,6},{4,0},{6,2},{8,12},{10,14},{12,8},{14,10},{16,20},{18,... | collective-permute-start | bytes 1179656 | tf_op jit(solution)/shard_map/ppermute | solution.py:26
  370.5 16.7 %collective-permute-start.42 = (bf16[96,2048]{1,0:T(8,128)(2,1)}, bf16[96,2048]{1,0:T(8,128)(2,1)}, u32[]{:S(2)}, u32[]{:S(2)}) collective-permute-start(bf16[96,2048]{1,0:T(8,128)(2,1)} %get-tuple-element.322), channel_id=1, source_target_pairs={{0,1},{1,0},{2,3},{3,2},{4,5},{5,4},{6,7},{7,6},{8,9},{9,8},{10,11... | collective-permute-start | bytes 1179656 | tf_op jit(solution)/shard_map/ppermute | solution.py:38
  389.7 10.1 %collective-permute-start.48 = (bf16[96,2048]{1,0:T(8,128)(2,1)S(1)}, bf16[96,2048]{1,0:T(8,128)(2,1)S(1)}, u32[]{:S(2)}, u32[]{:S(2)}) collective-permute-start(bf16[96,2048]{1,0:T(8,128)(2,1)S(1)} %add_convert_fusion.20), channel_id=1, source_target_pairs={{0,4},{2,6},{4,0},{6,2},{8,12},{10,14},{12,8},{14,10},{16,20},{18,... | collective-permute-start | bytes 1179656 | tf_op jit(solution)/shard_map/ppermute | solution.py:26
  391.2 9.7 %collective-permute-start.49 = (bf16[96,2048]{1,0:T(8,128)(2,1)S(1)}, bf16[96,2048]{1,0:T(8,128)(2,1)S(1)}, u32[]{:S(2)}, u32[]{:S(2)}) collective-permute-start(bf16[96,2048]{1,0:T(8,128)(2,1)S(1)} %add_convert_fusion.19), channel_id=1, source_target_pairs={{0,1},{1,0},{2,3},{3,2},{4,5},{5,4},{6,7},{7,6},{8,9},{9,8},{10,11... | collective-permute-start | bytes 1179656 | tf_op jit(solution)/shard_map/ppermute | solution.py:38
  405.0 17.4 %collective-permute-start.51 = (bf16[192,2048]{1,0:T(8,128)(2,1)S(1)}, bf16[192,2048]{1,0:T(8,128)(2,1)}, u32[]{:S(2)}, u32[]{:S(2)}) collective-permute-start(bf16[192,2048]{1,0:T(8,128)(2,1)S(1)} %get-tuple-element.289.refs_0_), channel_id=1, source_target_pairs={{0,4},{2,6},{4,0},{6,2},{8,12},{10,14},{12,8},{14,10},{16,20},{18,... | collective-permute-start | bytes 2359304 | tf_op jit(solution)/shard_map/ppermute | solution.py:26
  405.6 17.2 %collective-permute-start.50 = (bf16[192,2048]{1,0:T(8,128)(2,1)S(1)}, bf16[192,2048]{1,0:T(8,128)(2,1)}, u32[]{:S(2)}, u32[]{:S(2)}) collective-permute-start(bf16[192,2048]{1,0:T(8,128)(2,1)S(1)} %get-tuple-element.289.refs_0_), channel_id=1, source_target_pairs={{0,1},{1,0},{2,3},{3,2},{4,5},{5,4},{6,7},{7,6},{8,9},{9,8},{10,11... | collective-permute-start | bytes 2359304 | tf_op jit(solution)/shard_map/ppermute | solution.py:38
  421.5 19.6 %collective-permute-start.54 = (bf16[192,2048]{1,0:T(8,128)(2,1)S(1)}, bf16[192,2048]{1,0:T(8,128)(2,1)}, u32[]{:S(2)}, u32[]{:S(2)}) collective-permute-start(bf16[192,2048]{1,0:T(8,128)(2,1)S(1)} %get-tuple-element.289.refs_0_), channel_id=1, source_target_pairs={{0,2},{2,0},{4,6},{6,4},{8,10},{10,8},{12,14},{14,12},{16,18},{18,... | collective-permute-start | bytes 2359304 | tf_op jit(solution)/shard_map/ppermute | solution.py:26
  423.8 10.4 %collective-permute-start.52 = (bf16[96,2048]{1,0:T(8,128)(2,1)S(1)}, bf16[96,2048]{1,0:T(8,128)(2,1)S(1)}, u32[]{:S(2)}, u32[]{:S(2)}) collective-permute-start(bf16[96,2048]{1,0:T(8,128)(2,1)S(1)} %slice.210), channel_id=1, source_target_pairs={{0,1},{1,0},{2,3},{3,2},{4,5},{5,4},{6,7},{7,6},{8,9},{9,8},{10,11... | collective-permute-start | bytes 1179656 | tf_op jit(solution)/shard_map/ppermute | solution.py:38
  425.5 11.1 %collective-permute-start.53 = (bf16[96,2048]{1,0:T(8,128)(2,1)S(1)}, bf16[96,2048]{1,0:T(8,128)(2,1)}, u32[]{:S(2)}, u32[]{:S(2)}) collective-permute-start(bf16[96,2048]{1,0:T(8,128)(2,1)S(1)} %slice.211), channel_id=1, source_target_pairs={{0,4},{2,6},{4,0},{6,2},{8,12},{10,14},{12,8},{14,10},{16,20},{18,... | collective-permute-start | bytes 1179656 | tf_op jit(solution)/shard_map/ppermute | solution.py:26
  427.1 14.7 %collective-permute-start.55 = (bf16[192,2048]{1,0:T(8,128)(2,1)}, bf16[192,2048]{1,0:T(8,128)(2,1)}, u32[]{:S(2)}, u32[]{:S(2)}) collective-permute-start(bf16[192,2048]{1,0:T(8,128)(2,1)} %collective-permute-done.50.refs_1_), channel_id=1, source_target_pairs={{0,2},{2,0},{4,6},{6,4},{8,10},{10,8},{12,14},{14,12},{16,18},{18,... | collective-permute-start | bytes 2359304 | tf_op jit(solution)/shard_map/ppermute | solution.py:26
  436.6 8.9 %collective-permute-start.56 = (bf16[192,2048]{1,0:T(8,128)(2,1)}, bf16[192,2048]{1,0:T(8,128)(2,1)}, u32[]{:S(2)}, u32[]{:S(2)}) collective-permute-start(bf16[192,2048]{1,0:T(8,128)(2,1)} %collective-permute-done.51.refs_2_), channel_id=1, source_target_pairs={{0,2},{2,0},{4,6},{6,4},{8,10},{10,8},{12,14},{14,12},{16,18},{18,... | collective-permute-start | bytes 2359304 | tf_op jit(solution)/shard_map/ppermute | solution.py:26
  441.1 12.5 %collective-permute-start.59 = (bf16[192,2048]{1,0:T(8,128)(2,1)}, bf16[192,2048]{1,0:T(8,128)(2,1)S(1)}, u32[]{:S(2)}, u32[]{:S(2)}) collective-permute-start(bf16[192,2048]{1,0:T(8,128)(2,1)} %get-tuple-element.211), channel_id=1, source_target_pairs={{0,2},{2,0},{4,6},{6,4},{8,10},{10,8},{12,14},{14,12},{16,18},{18,... | collective-permute-start | bytes 2359304 | tf_op jit(solution)/shard_map/ppermute | solution.py:26
  441.1 12.5 %collective-permute-start.60 = (bf16[192,2048]{1,0:T(8,128)(2,1)}, bf16[192,2048]{1,0:T(8,128)(2,1)S(1)}, u32[]{:S(2)}, u32[]{:S(2)}) collective-permute-start(bf16[192,2048]{1,0:T(8,128)(2,1)} %get-tuple-element.212), channel_id=1, source_target_pairs={{0,2},{2,0},{4,6},{6,4},{8,10},{10,8},{12,14},{14,12},{16,18},{18,... | collective-permute-start | bytes 2359304 | tf_op jit(solution)/shard_map/ppermute | solution.py:26
  441.7 12.0 %collective-permute-start.61 = (bf16[192,2048]{1,0:T(8,128)(2,1)}, bf16[192,2048]{1,0:T(8,128)(2,1)S(1)}, u32[]{:S(2)}, u32[]{:S(2)}) collective-permute-start(bf16[192,2048]{1,0:T(8,128)(2,1)} %get-tuple-element.213), channel_id=1, source_target_pairs={{0,2},{2,0},{4,6},{6,4},{8,10},{10,8},{12,14},{14,12},{16,18},{18,... | collective-permute-start | bytes 2359304 | tf_op jit(solution)/shard_map/ppermute | solution.py:26
  441.7 12.8 %collective-permute-start.62 = (bf16[192,2048]{1,0:T(8,128)(2,1)}, bf16[192,2048]{1,0:T(8,128)(2,1)}, u32[]{:S(2)}, u32[]{:S(2)}) collective-permute-start(bf16[192,2048]{1,0:T(8,128)(2,1)} %get-tuple-element.214), channel_id=1, source_target_pairs={{0,2},{2,0},{4,6},{6,4},{8,10},{10,8},{12,14},{14,12},{16,18},{18,... | collective-permute-start | bytes 2359304 | tf_op jit(solution)/shard_map/ppermute | solution.py:26
  457.3 15.1 %collective-permute-start.66 = (bf16[96,2048]{1,0:T(8,128)(2,1)S(1)}, bf16[96,2048]{1,0:T(8,128)(2,1)S(1)}, u32[]{:S(2)}, u32[]{:S(2)}) collective-permute-start(bf16[96,2048]{1,0:T(8,128)(2,1)S(1)} %slice.219), channel_id=1, source_target_pairs={{0,4},{2,6},{4,0},{6,2},{8,12},{10,14},{12,8},{14,10},{16,20},{18,... | collective-permute-start | bytes 1179656 | tf_op jit(solution)/shard_map/ppermute | solution.py:26
  458.9 13.5 %collective-permute-start.65 = (bf16[96,2048]{1,0:T(8,128)(2,1)S(1)}, bf16[96,2048]{1,0:T(8,128)(2,1)}, u32[]{:S(2)}, u32[]{:S(2)}) collective-permute-start(bf16[96,2048]{1,0:T(8,128)(2,1)S(1)} %slice.218), channel_id=1, source_target_pairs={{0,1},{1,0},{2,3},{3,2},{4,5},{5,4},{6,7},{7,6},{8,9},{9,8},{10,11... | collective-permute-start | bytes 1179656 | tf_op jit(solution)/shard_map/ppermute | solution.py:38
  459.5 17.5 %collective-permute-start.64 = (bf16[96,2048]{1,0:T(8,128)(2,1)S(1)}, bf16[96,2048]{1,0:T(8,128)(2,1)}, u32[]{:S(2)}, u32[]{:S(2)}) collective-permute-start(bf16[96,2048]{1,0:T(8,128)(2,1)S(1)} %get-tuple-element.319), channel_id=1, source_target_pairs={{0,4},{2,6},{4,0},{6,2},{8,12},{10,14},{12,8},{14,10},{16,20},{18,... | collective-permute-start | bytes 1179656 | tf_op jit(solution)/shard_map/ppermute | solution.py:26
  460.1 18.1 %collective-permute-start.63 = (bf16[96,2048]{1,0:T(8,128)(2,1)S(1)}, bf16[96,2048]{1,0:T(8,128)(2,1)}, u32[]{:S(2)}, u32[]{:S(2)}) collective-permute-start(bf16[96,2048]{1,0:T(8,128)(2,1)S(1)} %get-tuple-element.320), channel_id=1, source_target_pairs={{0,1},{1,0},{2,3},{3,2},{4,5},{5,4},{6,7},{7,6},{8,9},{9,8},{10,11... | collective-permute-start | bytes 1179656 | tf_op jit(solution)/shard_map/ppermute | solution.py:38
  478.2 44.6 %all-to-all-start.3 = ((bf16[4,128,1536]{2,1,0:T(8,128)(2,1)}), bf16[4,128,1536]{2,1,0:T(8,128)(2,1)}, u32[]{:S(2)}, u32[]{:S(2)}) async-start(bf16[4,128,1536]{2,1,0:T(8,128)(2,1)} %bitcast.22), calls=%async_computation.4 | async-start | bytes 3145728 | tf_op jit(solution)/shard_map/all_to_all | solution.py:154
  482.6 144.8 %reduce-scatter.8.cloned.1.call-start = ((), (), s32[]{:S(2)}) async-start(), calls=%async_computation.14 | async-start | bytes 3276800 | tf_op jit(solution)/shard_map/reduce_scatter | solution.py:55
  482.6 36.0 %collective-permute-start.68 = (bf16[768,128]{1,0:T(8,128)(2,1)}, bf16[768,128]{1,0:T(8,128)(2,1)}, u32[]{:S(2)}, u32[]{:S(2)}) collective-permute-start(bf16[768,128]{1,0:T(8,128)(2,1)} %get-tuple-element.228), channel_id=1, source_target_pairs={{16,0},{18,2},{20,4},{22,6},{24,8},{26,10},{28,12},{30,14},{17,1},... | collective-permute-start | bytes 589832 | tf_op jit(solution)/shard_map/ppermute | solution.py:60
  483.9 38.9 %collective-permute-start.67 = (bf16[1536,128]{1,0:T(8,128)(2,1)}, bf16[1536,128]{1,0:T(8,128)(2,1)}, u32[]{:S(2)}, u32[]{:S(2)}) collective-permute-start(bf16[1536,128]{1,0:T(8,128)(2,1)} %get-tuple-element.227), channel_id=1, source_target_pairs={{8,0},{10,2},{12,4},{14,6},{16,8},{18,10},{20,12},{22,14},{24,16},... | collective-permute-start | bytes 1179656 | tf_op jit(solution)/shard_map/ppermute | solution.py:60
  572.4 11.2 %collective-permute-start.74 = (bf16[96,2048]{1,0:T(8,128)(2,1)}, bf16[96,2048]{1,0:T(8,128)(2,1)}, u32[]{:S(2)}, u32[]{:S(2)}) collective-permute-start(bf16[96,2048]{1,0:T(8,128)(2,1)} %add_convert_fusion.18), channel_id=1, source_target_pairs={{0,4},{2,6},{4,0},{6,2},{8,12},{10,14},{12,8},{14,10},{16,20},{18,... | collective-permute-start | bytes 1179656 | tf_op jit(solution)/shard_map/ppermute | solution.py:26
  573.9 11.4 %collective-permute-start.75 = (bf16[96,2048]{1,0:T(8,128)(2,1)}, bf16[96,2048]{1,0:T(8,128)(2,1)}, u32[]{:S(2)}, u32[]{:S(2)}) collective-permute-start(bf16[96,2048]{1,0:T(8,128)(2,1)} %add_convert_fusion.17), channel_id=1, source_target_pairs={{0,1},{1,0},{2,3},{3,2},{4,5},{5,4},{6,7},{7,6},{8,9},{9,8},{10,11... | collective-permute-start | bytes 1179656 | tf_op jit(solution)/shard_map/ppermute | solution.py:38
  576.7 25.2 %all-to-all-start.4 = ((bf16[4,128,1536]{2,1,0:T(8,128)(2,1)}), bf16[4,128,1536]{2,1,0:T(8,128)(2,1)}, u32[]{:S(2)}, u32[]{:S(2)}) async-start(bf16[4,128,1536]{2,1,0:T(8,128)(2,1)} %bitcast.21), calls=%async_computation.6 | async-start | bytes 3145728 | tf_op jit(solution)/shard_map/all_to_all | solution.py:154
  581.2 20.4 %collective-permute-start.73 = (bf16[192,2048]{1,0:T(8,128)(2,1)S(1)}, bf16[192,2048]{1,0:T(8,128)(2,1)S(1)}, u32[]{:S(2)}, u32[]{:S(2)}) collective-permute-start(bf16[192,2048]{1,0:T(8,128)(2,1)S(1)} %copy-done.19), channel_id=1, source_target_pairs={{0,1},{1,0},{2,3},{3,2},{4,5},{5,4},{6,7},{7,6},{8,9},{9,8},{10,11... | collective-permute-start | bytes 2359304 | tf_op jit(solution)/shard_map/ppermute | solution.py:38
  601.9 29.7 %collective-permute-start.76 = (bf16[192,2048]{1,0:T(8,128)(2,1)S(1)}, bf16[192,2048]{1,0:T(8,128)(2,1)}, u32[]{:S(2)}, u32[]{:S(2)}) collective-permute-start(bf16[192,2048]{1,0:T(8,128)(2,1)S(1)} %copy-done.16), channel_id=1, source_target_pairs={{0,1},{1,0},{2,3},{3,2},{4,5},{5,4},{6,7},{7,6},{8,9},{9,8},{10,11... | collective-permute-start | bytes 2359304 | tf_op jit(solution)/shard_map/ppermute | solution.py:38
  603.4 28.2 %collective-permute-start.77 = (bf16[192,2048]{1,0:T(8,128)(2,1)S(1)}, bf16[192,2048]{1,0:T(8,128)(2,1)}, u32[]{:S(2)}, u32[]{:S(2)}) collective-permute-start(bf16[192,2048]{1,0:T(8,128)(2,1)S(1)} %add_convert_fusion), channel_id=1, source_target_pairs={{0,4},{2,6},{4,0},{6,2},{8,12},{10,14},{12,8},{14,10},{16,20},{18,... | collective-permute-start | bytes 2359304 | tf_op jit(solution)/shard_map/ppermute | solution.py:26
  627.4 14.8 %all-to-all-start.5 = ((bf16[4,128,640]{2,1,0:T(8,128)(2,1)}), bf16[4,128,640]{2,1,0:T(8,128)(2,1)}, u32[]{:S(2)}, u32[]{:S(2)}) async-start(bf16[4,128,640]{2,1,0:T(8,128)(2,1)} %bitcast.23), calls=%async_computation.8 | async-start | bytes 1310720 | tf_op jit(solution)/shard_map/all_to_all | solution.py:154
  642.2 13.9 %collective-permute-start.81 = (f32[4224]{0:T(1024)S(1)}, f32[4224]{0:T(1024)S(1)}, u32[]{:S(2)}, u32[]{:S(2)}) collective-permute-start(f32[4224]{0:T(1024)S(1)} %add.267), channel_id=1, source_target_pairs={{0,8},{2,10},{4,12},{6,14},{8,0},{10,2},{12,4},{14,6},{16,24},{18,... | collective-permute-start | bytes 50696 | tf_op jit(solution)/shard_map/ppermute | solution.py:26
  (77 other events, 489.7 us)
Sparse Core Ops, SparseCore 0:
  24.6 55.8 all-gather.3
  82.1 122.4 all-gather.5
  206.8 121.7 all-gather.7
  330.8 111.5 reduce-scatter.3
  444.5 123.8 reduce-scatter.5
  570.6 56.6 reduce-scatter.7

commit v6 on v4

--- a/solution.py
+++ b/solution.py
@@ -850,7 +850,8 @@
     back_0 = home(ffn_grad_0)
     returned = [line_move(g, -d, range(d, n)) for g, (d, _) in zip(halo_grads[::-1], spans)]
     dq, dkv = attend_back(own_part, 0, kv, acc)
-    dq, back_0, returned = tie(dq, back_0, returned)
+    out_tokens = (resid + ffn_sum.third()).astype(BF16)
+    dq, back_0, returned, out_tokens = tie(dq, back_0, returned, out_tokens)
     d_raw, d_head_gains = call(
         functools.partial(prep_back_kernel, heads=heads, width=width, plane=plane),
         nb,
@@ -873,18 +874,18 @@
     gain_sums = gain_sums[0]
     attn_grad = line_scatter(attn_grad, n)
     gain_sums, ffn_grad_1 = tie(gain_sums, ffn_grad_1)
+    one.parts, gain_sums = tie(one.parts, gain_sums)
     one.second_x()
     back_1 = home(ffn_grad_1)
     d_one, back_1 = one.third_x(back_1)
     ffn_outs = unpacked((back_0, back_1), [v.shape for v in (w_gate, w_up, w_down)], (0, 0, 1), ffn_cuts)
-    d_one, ffn_outs, gain_sums, ffn_sum.got = tie(d_one, ffn_outs, gain_sums, ffn_sum.got)
+    d_one, ffn_outs, gain_sums = tie(d_one, ffn_outs, gain_sums)
     d_attn_gain = gain_sums / gain_1
     d_q_gain = d_head_gains[0, :width] + d_head_gains[0, width:]
     gains = jnp.concatenate([d_attn_gain, d_ffn_gain, d_q_gain, d_head_gains[1, :width]])
     gains = sum_over_ctx(gains + swap_x(gains), 1, QUAD)
     d_x, _ = norm_back(x_own, scale_1, gain_1, d_one)
     d_tokens = d_h + d_x
-    out_tokens = (resid + ffn_sum.third()).astype(BF16)
 
     attn_grad, back_1 = tie(attn_grad, back_1)
     attn_back = home(attn_grad)

time: 678 us -> 670 us (0.988)
  starting transfers between devices: 94.1 us -> 79.9 us
  waiting for transfers between devices: 193 us -> 204 us
    reduce_scatter x3, waiting for transfers between devices: 2.79 us -> 30.4 us  [line_scatter(): lax.psum_scatter(partial, 'ctx', scatter_dimension=0, axis_index_groups=l...]
    ppermute x59, starting transfers between devices: 44.3 us -> 31.4 us  [swap_ctx(): return lax.ppermute(value, 'ctx', [(i, i ^ bit) for i in range(n)])]
    ppermute x4, waiting for transfers between devices: 16.8 us -> 6.15 us  [line_move(): return lax.ppermute(value, 'ctx', pairs)]
    unnamed x107 -> x109, local copies, waits for them, and re-layouts: 19.7 us -> 21.4 us
  transfers between devices with their start and end apart: 93 -> 93, of which waited for: 37 -> 40; matrix products, arithmetic and copies ran while one was open for 13% -> 12% of each run, Pallas kernels for 34% -> 35%
where the time goes in v6:
time: 670 us; the launch traced here: 661 us
  Pallas kernels  232 us (35%)
  waiting for transfers between devices  204 us (30%)
  starting transfers between devices  79.9 us (12%)
  other arithmetic  46.4 us (7%)
  local copies, waits for them, and re-layouts  44 us (7%)
  blocking collectives  39.6 us (6%)
  between operations  15.3 us (2%)
    pallas_call x19, Pallas kernels, call(): pl.pallas_call(kernel, out_shape=[jax.ShapeDtypeStruct(shape, dtype) for...  232 us
    ppermute x59, waiting for transfers between devices, swap_ctx(): return lax.ppermute(value, 'ctx', [(i, i ^ bit) for i in range(n)])  84.3 us
    ppermute x19, waiting for transfers between devices, swap_x(): return lax.ppermute(value, 'tp', [(0, 1), (1, 0)])  40.1 us
    all_to_all x2, blocking collectives, spread(): lax.all_to_all(pieces, 'ctx', axis, axis, axis_index_groups=groups, tiled...  39.6 us
    ppermute x59, starting transfers between devices, swap_ctx(): return lax.ppermute(value, 'ctx', [(i, i ^ bit) for i in range(n)])  31.4 us
    reduce_scatter x3, waiting for transfers between devices, line_scatter(): lax.psum_scatter(partial, 'ctx', scatter_dimension=0, axis_index_groups=l...  30.4 us
    all_gather x3, waiting for transfers between devices, line_gather(): lax.all_gather(own, 'ctx', axis=0, axis_index_groups=line_groups(n), tile...  27.1 us
    unnamed x109, local copies, waits for them, and re-layouts  21.4 us
  transfers between devices with their start and end apart: 93, of which 40 were waited for; matrix products, arithmetic and copies ran while one was open for 12% of the time, Pallas kernels for 35%

profile of v6, /device:TPU:0, one launch (start us, length us, event | category | flops | bytes accessed | tf_op | source)
XLA Modules:
  0.0 661.2 jit_solution(170109647210045119)
XLA Ops:
  7.2 2.1 shard_map.237
  9.4 15.1 %all_to_all.30 = bf16[4,128,640]{2,1,0:T(8,128)(2,1)} all-to-all(bf16[4,128,640]{2,1,0:T(8,128)(2,1)} %shard_map.237), channel_id=1, replica_groups={{0,2,4,6},{8,10,12,14},{16,18,20,22},{24,26,28,30},{1,3,5,7},{9,11,13,1..., dimensions={0} | all-to-all | bytes 1310720 | tf_op jit(solution)/shard_map/all_to_all | solution.py:154
  24.6 3.9 shard_map.238
  28.4 24.5 %all_to_all.31 = bf16[4,128,1536]{2,1,0:T(8,128)(2,1)} all-to-all(bf16[4,128,1536]{2,1,0:T(8,128)(2,1)} %get-tuple-element.148), channel_id=1, replica_groups={{0,2,4,6},{8,10,12,14},{16,18,20,22},{24,26,28,30},{1,3,5,7},{9,11,13,1..., dimensions={0} | all-to-all | bytes 3145728 | tf_op jit(solution)/shard_map/all_to_all | solution.py:154
  59.5 2.1 collective-permute-start.5
  63.3 2.8 fusion.18
  66.1 2.5 pad_maximum_fusion.1
  68.6 12.3 %collective-permute-done.5.refs_3_ = bf16[192,2048]{1,0:T(8,128)(2,1)S(1)} collective-permute-done((bf16[192,2048]{1,0:T(8,128)(2,1)S(1)}, bf16[192,2048]{1,0:T(8,128)(2,1)S(1)}, u32[]{:S(2)}, u32[]{:S(2)}) %collective-permute-start.5) | collective-permute-done | bytes 786464 | tf_op jit(solution)/shard_map/ppermute | solution.py:73
  80.9 16.0 %collective-permute-done.4.refs_2_ = bf16[192,2048]{1,0:T(8,128)(2,1)S(1)} collective-permute-done((bf16[192,2048]{1,0:T(8,128)(2,1)S(1)}, bf16[192,2048]{1,0:T(8,128)(2,1)S(1)}, u32[]{:S(2)}, u32[]{:S(2)}) %collective-permute-start.4) | collective-permute-done | bytes 786464 | tf_op jit(solution)/shard_map/ppermute | solution.py:26
  98.0 3.6 all-to-all-start.2
  104.6 2.4 broadcast_subtract_fusion
  107.0 2.7 slice.236.refs_8_.w_ref.refs_0_
  109.7 14.2 %shard_map.239 = (bf16[1536,2048]{1,0:T(8,128)(2,1)}, f32[1536,384]{1,0:T(8,128)}, bf16[1536,256]{1,0:T(8,128)(2,1)}, bf16[1536,128]{1,0:T(8,128)(2,1)}) custom-call(s32[8]{0:T(128)} %or_or_fusion.table, bf16[192,2048]{1,0:T(8,128)(2,1)} %copy-done.5, bf16[192,2048]{1,0:T(8,128)(2,1)} %copy-done.15, bf16[192,2048]{1,0:T(8,128)(2,1)} %copy-done.14, ...), custom_call_target="tpu_custom_call" | custom-call | flops 2415919104 | bytes 16515072 | tf_op jit(solution)/shard_map/pallas_call | solution.py:619
  124.0 1.8 collective-permute-start.13
  129.3 3.5 collective-permute-start.10
  132.9 5.1 collective-permute-start.11
  138.2 14.0 %shard_map.240.refs_0_ = f32[6144,128]{1,0:T(8,128)} custom-call(s32[8]{0:T(128)} %or_or_fusion.1.table, s32[8]{0:T(128)} %get-tuple-element.288.lo, s32[8]{0:T(128)} %get-tuple-element.287.hi, bf16[1536,256]{1,0:T(8,128)(2,1)} %get-tuple-element.158.q_ref, s32[1536,1]{1,0:T(8,128)} %get-tuple-element.317.start_ref, bf16[1536,128]{1,0:T(8,128)(2,1)} %get-tuple-element.159.kv_ref), custom_call_target="tpu_custom_call" | custom-call | flops 4831838208 | bytes 3932160 | tf_op jit(solution)/shard_map/pallas_call | solution.py:619
  152.2 2.3 slice.237.w_ref.refs_10_
  154.5 4.5 collective-permute-done.11
  166.9 2.5 copy-done.23
  170.3 9.2 %shard_map.241 = (bf16[1536,256]{1,0:T(8,128)(2,1)}, f32[1536,256]{1,0:T(8,128)}, f32[6144,1]{1,0:T(8,128)}) custom-call(s32[8]{0:T(128)} %or_or_fusion.1.table, s32[8]{0:T(128)} %get-tuple-element.286.lo, s32[8]{0:T(128)} %get-tuple-element.285.hi, bf16[1536,256]{1,0:T(8,128)(2,1)} %get-tuple-element.158.q_ref, s32[1536,1]{1,0:T(8,128)} %get-tuple-element.318.start_ref, ...), custom_call_target="tpu_custom_call" | custom-call | flops 4831838208 | bytes 3932160 | tf_op jit(solution)/shard_map/pallas_call | solution.py:619
  179.5 7.2 %shard_map.242 = (bf16[768,2048]{1,0:T(8,128)(2,1)}, bf16[192,2048]{1,0:T(8,128)(2,1)}, bf16[192,2048]{1,0:T(8,128)(2,1)}, bf16[192,2048]{1,0:T(8,128)(2,1)}, bf16[192,2048]{1,0:T(8,128)(2,1)}) custom-call(bf16[1536,256]{1,0:T(8,128)(2,1)} %get-tuple-element.167.a_ref.d_ref, bf16[2048,256]{1,0:T(8,128)(2,1)} %slice.237.w_ref.refs_10_), custom_call_target="tpu_custom_call" | custom-call | flops 1610612736 | bytes 7077888 | tf_op jit(solution)/shard_map/pallas_call | solution.py:619
  189.3 2.1 constant_dynamic-update-slice_fusion.6
  201.1 6.4 collective-permute-done.21
  208.2 7.2 %collective-permute-done.19 = bf16[96,2048]{1,0:T(8,128)(2,1)S(1)} collective-permute-done((bf16[96,2048]{1,0:T(8,128)(2,1)S(1)}, bf16[96,2048]{1,0:T(8,128)(2,1)S(1)}, u32[]{:S(2)}, u32[]{:S(2)}) %collective-permute-start.19) | collective-permute-done | bytes 393248 | tf_op jit(solution)/shard_map/ppermute | solution.py:26
  218.7 6.9 %collective-permute-done.29 = bf16[96,2048]{1,0:T(8,128)(2,1)S(1)} collective-permute-done((bf16[96,2048]{1,0:T(8,128)(2,1)S(1)}, bf16[96,2048]{1,0:T(8,128)(2,1)S(1)}, u32[]{:S(2)}, u32[]{:S(2)}) %collective-permute-start.29) | collective-permute-done | bytes 393248 | tf_op jit(solution)/shard_map/ppermute | solution.py:26
  230.0 15.4 %collective-permute-done.32.refs_2_ = bf16[192,2048]{1,0:T(8,128)(2,1)S(1)} collective-permute-done((bf16[192,2048]{1,0:T(8,128)(2,1)S(1)}, bf16[192,2048]{1,0:T(8,128)(2,1)S(1)}, u32[]{:S(2)}, u32[]{:S(2)}) %collective-permute-start.32) | collective-permute-done | bytes 786464 | tf_op jit(solution)/shard_map/ppermute | solution.py:26
  248.6 5.5 collective-permute-done.33.refs_3_
  254.2 4.3 collective-permute-done.34.refs_4_
  261.0 24.9 %shard_map.243 = (bf16[1536,512]{1,0:T(8,128)(2,1)}, bf16[1536,1024]{1,0:T(8,128)(2,1)}, bf16[1536,2048]{1,0:T(8,128)(2,1)}, bf16[1536,2048]{1,0:T(8,128)(2,1)}) custom-call(bf16[192,2048]{1,0:T(8,128)(2,1)} %copy-done.16, bf16[192,2048]{1,0:T(8,128)(2,1)} %copy-done.20, bf16[192,2048]{1,0:T(8,128)(2,1)} %copy-done.19, bf16[96,2048]{1,0:T(8,128)(2,1)} %copy-done.44, ...), custom_call_target="tpu_custom_call" | custom-call | flops 19327352832 | bytes 36175872 | tf_op jit(solution)/shard_map/pallas_call | solution.py:619
  285.9 15.6 %shard_map.244 = bf16[2048,1536]{1,0:T(8,128)(2,1)} custom-call(bf16[1536,2048]{1,0:T(8,128)(2,1)} %get-tuple-element.180.a_ref, bf16[1536,1024]{1,0:T(8,128)(2,1)} %get-tuple-element.182.b_ref, bf16[1536,2048]{1,0:T(8,128)(2,1)} %constant_dynamic-update-slice_fusion.2.refs_10_.c_ref, bf16[1536,512]{1,0:T(8,128)(2,1)} %get-tuple-element.183.d_ref.h0_ref), custom_call_target="tpu_custom_call" | custom-call | flops 9663676416 | bytes 23592960 | tf_op jit(solution)/shard_map/pallas_call | solution.py:619
  301.5 27.1 %all-gather.8.cloned.1.call-done.w_ref.w1_ref = bf16[2048,1536]{1,0:T(8,128)(2,1)} async-done(((bf16[512,1536]{1,0:T(8,128)(2,1)}), bf16[2048,1536]{1,0:T(8,128)(2,1)}) %all-gather.8.cloned.1.call-update) | async-done | bytes 6291472 | tf_op jit(solution)/shard_map/all_gather | solution.py:51
  328.6 25.6 %shard_map.245 = (bf16[1536,512]{1,0:T(8,128)(2,1)}, bf16[1536,1024]{1,0:T(8,128)(2,1)}, bf16[768,2048]{1,0:T(8,128)(2,1)}, bf16[192,2048]{1,0:T(8,128)(2,1)}, b...) custom-call(bf16[1536,2048]{1,0:T(8,128)(2,1)} %get-tuple-element.180.a_ref, ...), custom_call_target="tpu_custom_call" | custom-call | flops 19327352832 | bytes 36175872 | tf_op jit(solution)/shard_map/pallas_call | solution.py:619
  360.2 4.2 add_convert_fusion.9
  371.1 15.0 %shard_map.246 = bf16[2048,1536]{1,0:T(8,128)(2,1)} custom-call(bf16[1536,2048]{1,0:T(8,128)(2,1)} %get-tuple-element.180.a_ref, bf16[1536,1024]{1,0:T(8,128)(2,1)} %get-tuple-element.191.b_ref, bf16[1536,2048]{1,0:T(8,128)(2,1)} %constant_dynamic-update-slice_fusion.2.refs_10_.c_ref, bf16[1536,512]{1,0:T(8,128)(2,1)} %get-tuple-element.192.d_ref.h1_ref), custom_call_target="tpu_custom_call" | custom-call | flops 9663676416 | bytes 23592960 | tf_op jit(solution)/shard_map/pallas_call | solution.py:619
  391.7 8.0 %collective-permute-done.48 = bf16[96,2048]{1,0:T(8,128)(2,1)S(1)} collective-permute-done((bf16[96,2048]{1,0:T(8,128)(2,1)S(1)}, bf16[96,2048]{1,0:T(8,128)(2,1)S(1)}, u32[]{:S(2)}, u32[]{:S(2)}) %collective-permute-start.48) | collective-permute-done | bytes 393248 | tf_op jit(solution)/shard_map/ppermute | solution.py:26
  406.2 15.2 %shard_map.247 = (bf16[768,2048]{1,0:T(8,128)(2,1)}, bf16[192,2048]{1,0:T(8,128)(2,1)}, bf16[192,2048]{1,0:T(8,128)(2,1)}, bf16[192,2048]{1,0:T(8,128)(2,1)}, bf16[192,2048]{1,0:T(8,128)(2,1)}) custom-call(bf16[1536,512]{1,0:T(8,128)(2,1)} %get-tuple-element.183.d_ref.h0_ref, bf16[1536,512]{1,0:T(8,128)(2,1)} %get-tuple-element.192.d_ref.h1_ref, ...), custom_call_target="tpu_custom_call" | custom-call | flops 6442450944 | bytes 22020096 | tf_op jit(solution)/shard_map/pallas_call | solution.py:619
  427.1 7.1 %collective-permute-done.52.refs_3_ = bf16[96,2048]{1,0:T(8,128)(2,1)S(1)} collective-permute-done((bf16[96,2048]{1,0:T(8,128)(2,1)S(1)}, bf16[96,2048]{1,0:T(8,128)(2,1)S(1)}, u32[]{:S(2)}, u32[]{:S(2)}) %collective-permute-start.52) | collective-permute-done | bytes 393248 | tf_op jit(solution)/shard_map/ppermute | solution.py:38
  434.2 2.4 collective-permute-done.53.refs_4_
  445.5 8.0 %shard_map.248 = (bf16[1536,2048]{1,0:T(8,128)(2,1)}, bf16[1536,256]{1,0:T(8,128)(2,1)}) custom-call(bf16[192,2048]{1,0:T(8,128)(2,1)} %copy-done.9, bf16[192,2048]{1,0:T(8,128)(2,1)} %collective-permute-done.50.refs_1_, bf16[192,2048]{1,0:T(8,128)(2,1)} %collective-permute-done.51.refs_2_, bf16[96,2048]{1,0:T(8,128)(2,1)} %copy-done.18, ...), custom_call_target="tpu_custom_call" | custom-call | flops 1610612736 | bytes 12582912 | tf_op jit(solution)/shard_map/pallas_call | solution.py:619
  453.5 3.6 add_convert_fusion.5
  461.5 10.8 %shard_map.249 = (f32[6144,128]{1,0:T(8,128)}, bf16[768,128]{1,0:T(8,128)(2,1)}, bf16[1536,128]{1,0:T(8,128)(2,1)}) custom-call(s32[8]{0:T(128)} %or_or_fusion.1.table, s32[8]{0:T(128)} %get-tuple-element.286.lo, s32[8]{0:T(128)} %get-tuple-element.285.hi, bf16[1536,256]{1,0:T(8,128)(2,1)} %get-tuple-element.158.q_ref, ...), custom_call_target="tpu_custom_call" | custom-call | flops 12079595520 | bytes 4718592 | tf_op jit(solution)/shard_map/pallas_call | solution.py:619
  473.6 3.3 collective-permute-done.64
  478.1 4.4 all-to-all-start.3
  486.3 2.0 collective-permute-start.69
  490.1 30.8 %shard_map.250 = (f32[1536,256]{1,0:T(8,128)}, f32[1536,128]{1,0:T(8,128)}) custom-call(s32[8]{0:T(128)} %or_or_fusion.1.table, s32[8]{0:T(128)} %get-tuple-element.288.lo, s32[8]{0:T(128)} %get-tuple-element.287.hi, bf16[1536,256]{1,0:T(8,128)(2,1)} %get-tuple-element.158.q_ref, bf16[1536,256]{1,0:T(8,128)(2,1)} %get-tuple-element.210.do_ref, ...), custom_call_target="tpu_custom_call" | custom-call | flops 12079595520 | bytes 4718592 | tf_op jit(solution)/shard_map/pallas_call | solution.py:619
  525.0 9.1 %shard_map.251 = (bf16[1536,384]{1,0:T(8,128)(2,1)}, f32[8,128]{1,0:T(8,128)}) custom-call(s32[8]{0:T(128)} %or_or_fusion.1.table, f32[1536,384]{1,0:T(8,128)} %get-tuple-element.230.raw_ref, f32[1536,128]{1,0:T(8,128)} %get-tuple-element.153.refs_9_.cos_ref, f32[1536,128]{1,0:T(8,128)} %get-tuple-element.154.refs_10_.sin_ref, ...), custom_call_target="tpu_custom_call" | custom-call | flops 9830400 | bytes 5898240 | tf_op jit(solution)/shard_map/pallas_call | solution.py:619
  534.1 8.5 %shard_map.252 = (bf16[768,2048]{1,0:T(8,128)(2,1)}, bf16[192,2048]{1,0:T(8,128)(2,1)}, bf16[192,2048]{1,0:T(8,128)(2,1)}, bf16[192,2048]{1,0:T(8,128)(2,1)}, bf16[192,2048]{1,0:T(8,128)(2,1)}) custom-call(bf16[1536,384]{1,0:T(8,128)(2,1)} %get-tuple-element.247.a_ref.b_ref, bf16[2048,384]{1,0:T(8,128)(2,1)} %slice.236.refs_8_.w_ref.refs_0_), custom_call_target="tpu_custom_call" | custom-call | flops 2415919104 | bytes 7471104 | tf_op jit(solution)/shard_map/pallas_call | solution.py:619
  542.6 11.2 %shard_map.253 = (f32[8,2048]{1,0:T(8,128)}, bf16[2048,640]{1,0:T(8,128)(2,1)}) custom-call(bf16[1536,2048]{1,0:T(8,128)(2,1)} %get-tuple-element.246.a_ref, bf16[1536,384]{1,0:T(8,128)(2,1)} %get-tuple-element.247.a_ref.b_ref, bf16[1536,2048]{1,0:T(8,128)(2,1)} %get-tuple-element.248.c_ref, bf16[1536,256]{1,0:T(8,128)(2,1)} %get-tuple-element.167.a_ref.d_ref, ...), custom_call_target="tpu_custom_call" | custom-call | flops 4026531840 | bytes 17170432 | tf_op jit(solution)/shard_map/pallas_call | solution.py:619
  559.5 4.2 add_convert_fusion.1
  563.8 4.7 reduce-scatter.6.cloned.1.call-done
  569.9 3.6 all-to-all-start.4
  573.5 14.6 %collective-permute-done.75 = bf16[192,2048]{1,0:T(8,128)(2,1)} collective-permute-done((bf16[192,2048]{1,0:T(8,128)(2,1)}, bf16[192,2048]{1,0:T(8,128)(2,1)}, u32[]{:S(2)}, u32[]{:S(2)}) %collective-permute-start.75) | collective-permute-done | bytes 786464 | tf_op jit(solution)/shard_map/ppermute | solution.py:38
  588.2 2.3 add_convert_fusion
  590.5 3.1 all-to-all-done.4.refs_1_
  595.4 5.0 shard_map.254
  600.4 25.7 %reduce-scatter.8.cloned.1.call-done = bf16[512,640]{1,0:T(8,128)(2,1)} async-done(((bf16[2048,640]{1,0:T(8,128)(2,1)}), bf16[512,640]{1,0:T(8,128)(2,1)}) %reduce-scatter.8.cloned.1.call-update) | async-done | bytes 655376 | tf_op jit(solution)/shard_map/reduce_scatter | solution.py:55
  626.1 4.2 all-to-all-start.5
  634.5 2.3 collective-permute-done.78
  638.0 2.0 collective-permute-start.80
  642.5 3.1 collective-permute-done.81
  645.6 2.1 collective-permute-start.82
  647.7 3.0 fusion.7
  650.7 2.2 shard_map.255
  (343 shorter events, 125.0 us)
Async XLA Ops:
  7.2 99.8 %all-gather.4.cloned.1.call-start = ((), (), s32[]{:S(2)}) async-start(), calls=%async_computation.9 | async-start | bytes 3276800 | tf_op jit(solution)/shard_map/all_gather | solution.py:51
  24.5 236.5 %all-gather.6.cloned.1.call-start = ((), (), s32[]{:S(2)}) async-start(), calls=%async_computation.10 | async-start | bytes 7864320 | tf_op jit(solution)/shard_map/all_gather | solution.py:51
  59.5 21.4 %collective-permute-start.5 = (bf16[192,2048]{1,0:T(8,128)(2,1)S(1)}, bf16[192,2048]{1,0:T(8,128)(2,1)S(1)}, u32[]{:S(2)}, u32[]{:S(2)}) collective-permute-start(bf16[192,2048]{1,0:T(8,128)(2,1)S(1)} %fusion.3.refs_0_), channel_id=1, source_target_pairs={{0,5},{1,4},{2,7},{3,6},{4,1},{5,0},{6,3},{7,2},{8,13},{9,12},{10,... | collective-permute-start | bytes 2359304 | tf_op jit(solution)/shard_map/ppermute | solution.py:73
  61.6 35.3 %collective-permute-start.4 = (bf16[192,2048]{1,0:T(8,128)(2,1)S(1)}, bf16[192,2048]{1,0:T(8,128)(2,1)S(1)}, u32[]{:S(2)}, u32[]{:S(2)}) collective-permute-start(bf16[192,2048]{1,0:T(8,128)(2,1)S(1)} %fusion.3.refs_0_), channel_id=1, source_target_pairs={{0,4},{2,6},{4,0},{6,2},{8,12},{10,14},{12,8},{14,10},{16,20},{18,... | collective-permute-start | bytes 2359304 | tf_op jit(solution)/shard_map/ppermute | solution.py:26
  63.3 33.6 %collective-permute-start.3 = (bf16[192,2048]{1,0:T(8,128)(2,1)S(1)}, bf16[192,2048]{1,0:T(8,128)(2,1)S(1)}, u32[]{:S(2)}, u32[]{:S(2)}) collective-permute-start(bf16[192,2048]{1,0:T(8,128)(2,1)S(1)} %fusion.3.refs_0_), channel_id=1, source_target_pairs={{0,1},{1,0},{2,3},{3,2},{4,5},{5,4},{6,7},{7,6},{8,9},{9,8},{10,11... | collective-permute-start | bytes 2359304 | tf_op jit(solution)/shard_map/ppermute | solution.py:38
  68.6 41.1 %collective-permute-start.6 = (bf16[192,2048]{1,0:T(8,128)(2,1)S(1)}, bf16[192,2048]{1,0:T(8,128)(2,1)}, u32[]{:S(2)}, u32[]{:S(2)}) collective-permute-start(bf16[192,2048]{1,0:T(8,128)(2,1)S(1)} %fusion.3.refs_0_), channel_id=1, source_target_pairs={{0,2},{2,0},{4,6},{6,4},{8,10},{10,8},{12,14},{14,12},{16,18},{18,... | collective-permute-start | bytes 2359304 | tf_op jit(solution)/shard_map/ppermute | solution.py:26
  98.0 25.9 %all-to-all-start.2 = ((bf16[4,128,1536]{2,1,0:T(8,128)(2,1)}), bf16[4,128,1536]{2,1,0:T(8,128)(2,1)S(1)}, u32[]{:S(2)}, u32[]{:S(2)}) async-start(bf16[4,128,1536]{2,1,0:T(8,128)(2,1)} %get-tuple-element.157), calls=%async_computation.2 | async-start | bytes 3145728 | tf_op jit(solution)/shard_map/all_to_all | solution.py:154
  101.6 227.0 %all-gather.8.cloned.1.call-start = ((), (), s32[]{:S(2)}) async-start(), calls=%async_computation.11 | async-start | bytes 7864320 | tf_op jit(solution)/shard_map/all_gather | solution.py:51
  124.0 35.1 %collective-permute-start.13 = (bf16[192,2048]{1,0:T(8,128)(2,1)S(1)}, bf16[192,2048]{1,0:T(8,128)(2,1)}, u32[]{:S(2)}, u32[]{:S(2)}) collective-permute-start(bf16[192,2048]{1,0:T(8,128)(2,1)S(1)} %copy-done.11), channel_id=1, source_target_pairs={{0,4},{2,6},{4,0},{6,2},{8,12},{10,14},{12,8},{14,10},{16,20},{18,... | collective-permute-start | bytes 2359304 | tf_op jit(solution)/shard_map/ppermute | solution.py:26
  125.7 33.3 %collective-permute-start.12 = (bf16[192,2048]{1,0:T(8,128)(2,1)S(1)}, bf16[192,2048]{1,0:T(8,128)(2,1)}, u32[]{:S(2)}, u32[]{:S(2)}) collective-permute-start(bf16[192,2048]{1,0:T(8,128)(2,1)S(1)} %copy-done.11), channel_id=1, source_target_pairs={{0,1},{1,0},{2,3},{3,2},{4,5},{5,4},{6,7},{7,6},{8,9},{9,8},{10,11... | collective-permute-start | bytes 2359304 | tf_op jit(solution)/shard_map/ppermute | solution.py:38
  129.3 29.7 %collective-permute-start.10 = (bf16[1536,128]{1,0:T(8,128)(2,1)}, bf16[1536,128]{1,0:T(8,128)(2,1)S(1)}, u32[]{:S(2)}, u32[]{:S(2)}) collective-permute-start(bf16[1536,128]{1,0:T(8,128)(2,1)} %get-tuple-element.159.kv_ref), channel_id=1, source_target_pairs={{0,8},{2,10},{4,12},{6,14},{8,16},{10,18},{12,20},{14,22},{16,24},... | collective-permute-start | bytes 1179656 | tf_op jit(solution)/shard_map/ppermute | solution.py:60
  132.8 55.1 %collective-permute-start.24 = (bf16[192,2048]{1,0:T(8,128)(2,1)S(1)}, bf16[192,2048]{1,0:T(8,128)(2,1)}, u32[]{:S(2)}, u32[]{:S(2)}) collective-permute-start(bf16[192,2048]{1,0:T(8,128)(2,1)S(1)} %copy-done.11), channel_id=1, source_target_pairs={{0,2},{2,0},{4,6},{6,4},{8,10},{10,8},{12,14},{14,12},{16,18},{18,... | collective-permute-start | bytes 2359304 | tf_op jit(solution)/shard_map/ppermute | solution.py:26
  132.9 26.1 %collective-permute-start.11 = (bf16[768,128]{1,0:T(8,128)(2,1)}, bf16[768,128]{1,0:T(8,128)(2,1)}, u32[]{:S(2)}, u32[]{:S(2)}) collective-permute-start(bf16[768,128]{1,0:T(8,128)(2,1)} %slice.180), channel_id=1, source_target_pairs={{0,16},{2,18},{4,20},{6,22},{8,24},{10,26},{12,28},{14,30},{1,17},... | collective-permute-start | bytes 589832 | tf_op jit(solution)/shard_map/ppermute | solution.py:60
  138.0 340.1 %reduce-scatter.4.cloned.1.call-start = ((), (), s32[]{:S(2)}) async-start(), calls=%async_computation.12 | async-start | bytes 7864320 | tf_op jit(solution)/shard_map/reduce_scatter | solution.py:55
  160.1 32.3 %collective-permute-start.26 = (bf16[192,2048]{1,0:T(8,128)(2,1)}, bf16[192,2048]{1,0:T(8,128)(2,1)S(1)}, u32[]{:S(2)}, u32[]{:S(2)}) collective-permute-start(bf16[192,2048]{1,0:T(8,128)(2,1)} %collective-permute-done.13), channel_id=1, source_target_pairs={{0,2},{2,0},{4,6},{6,4},{8,10},{10,8},{12,14},{14,12},{16,18},{18,... | collective-permute-start | bytes 2359304 | tf_op jit(solution)/shard_map/ppermute | solution.py:26
  161.2 26.9 %collective-permute-start.25 = (bf16[192,2048]{1,0:T(8,128)(2,1)}, bf16[192,2048]{1,0:T(8,128)(2,1)S(1)}, u32[]{:S(2)}, u32[]{:S(2)}) collective-permute-start(bf16[192,2048]{1,0:T(8,128)(2,1)} %collective-permute-done.12), channel_id=1, source_target_pairs={{0,2},{2,0},{4,6},{6,4},{8,10},{10,8},{12,14},{14,12},{16,18},{18,... | collective-permute-start | bytes 2359304 | tf_op jit(solution)/shard_map/ppermute | solution.py:26
  162.7 16.8 %collective-permute-start.15 = (bf16[96,2048]{1,0:T(8,128)(2,1)S(1)}, bf16[96,2048]{1,0:T(8,128)(2,1)S(1)}, u32[]{:S(2)}, u32[]{:S(2)}) collective-permute-start(bf16[96,2048]{1,0:T(8,128)(2,1)S(1)} %slice.182), channel_id=1, source_target_pairs={{0,4},{2,6},{4,0},{6,2},{8,12},{10,14},{12,8},{14,10},{16,20},{18,... | collective-permute-start | bytes 1179656 | tf_op jit(solution)/shard_map/ppermute | solution.py:26
  163.1 16.4 %collective-permute-start.14 = (bf16[96,2048]{1,0:T(8,128)(2,1)S(1)}, bf16[96,2048]{1,0:T(8,128)(2,1)S(1)}, u32[]{:S(2)}, u32[]{:S(2)}) collective-permute-start(bf16[96,2048]{1,0:T(8,128)(2,1)S(1)} %slice.181), channel_id=1, source_target_pairs={{0,1},{1,0},{2,3},{3,2},{4,5},{5,4},{6,7},{7,6},{8,9},{9,8},{10,11... | collective-permute-start | bytes 1179656 | tf_op jit(solution)/shard_map/ppermute | solution.py:38
  195.5 12.0 %collective-permute-start.21 = (bf16[96,2048]{1,0:T(8,128)(2,1)S(1)}, bf16[96,2048]{1,0:T(8,128)(2,1)S(1)}, u32[]{:S(2)}, u32[]{:S(2)}) collective-permute-start(bf16[96,2048]{1,0:T(8,128)(2,1)S(1)} %slice.241), channel_id=1, source_target_pairs={{0,1},{1,0},{2,3},{3,2},{4,5},{5,4},{6,7},{7,6},{8,9},{9,8},{10,11... | collective-permute-start | bytes 1179656 | tf_op jit(solution)/shard_map/ppermute | solution.py:38
  196.2 12.0 %collective-permute-start.23 = (bf16[96,2048]{1,0:T(8,128)(2,1)S(1)}, bf16[96,2048]{1,0:T(8,128)(2,1)S(1)}, u32[]{:S(2)}, u32[]{:S(2)}) collective-permute-start(bf16[96,2048]{1,0:T(8,128)(2,1)S(1)} %slice.242), channel_id=1, source_target_pairs={{0,4},{2,6},{4,0},{6,2},{8,12},{10,14},{12,8},{14,10},{16,20},{18,... | collective-permute-start | bytes 1179656 | tf_op jit(solution)/shard_map/ppermute | solution.py:26
  197.9 17.5 %collective-permute-start.19 = (bf16[96,2048]{1,0:T(8,128)(2,1)S(1)}, bf16[96,2048]{1,0:T(8,128)(2,1)S(1)}, u32[]{:S(2)}, u32[]{:S(2)}) collective-permute-start(bf16[96,2048]{1,0:T(8,128)(2,1)S(1)} %get-tuple-element.315), channel_id=1, source_target_pairs={{0,4},{2,6},{4,0},{6,2},{8,12},{10,14},{12,8},{14,10},{16,20},{18,... | collective-permute-start | bytes 1179656 | tf_op jit(solution)/shard_map/ppermute | solution.py:26
  198.2 17.2 %collective-permute-start.18 = (bf16[96,2048]{1,0:T(8,128)(2,1)S(1)}, bf16[96,2048]{1,0:T(8,128)(2,1)S(1)}, u32[]{:S(2)}, u32[]{:S(2)}) collective-permute-start(bf16[96,2048]{1,0:T(8,128)(2,1)S(1)} %get-tuple-element.316), channel_id=1, source_target_pairs={{0,1},{1,0},{2,3},{3,2},{4,5},{5,4},{6,7},{7,6},{8,9},{9,8},{10,11... | collective-permute-start | bytes 1179656 | tf_op jit(solution)/shard_map/ppermute | solution.py:38
  215.7 10.0 %collective-permute-start.29 = (bf16[96,2048]{1,0:T(8,128)(2,1)S(1)}, bf16[96,2048]{1,0:T(8,128)(2,1)S(1)}, u32[]{:S(2)}, u32[]{:S(2)}) collective-permute-start(bf16[96,2048]{1,0:T(8,128)(2,1)S(1)} %add_convert_fusion.22), channel_id=1, source_target_pairs={{0,4},{2,6},{4,0},{6,2},{8,12},{10,14},{12,8},{14,10},{16,20},{18,... | collective-permute-start | bytes 1179656 | tf_op jit(solution)/shard_map/ppermute | solution.py:26
  217.4 9.6 %collective-permute-start.30 = (bf16[96,2048]{1,0:T(8,128)(2,1)S(1)}, bf16[96,2048]{1,0:T(8,128)(2,1)S(1)}, u32[]{:S(2)}, u32[]{:S(2)}) collective-permute-start(bf16[96,2048]{1,0:T(8,128)(2,1)S(1)} %add_convert_fusion.21), channel_id=1, source_target_pairs={{0,1},{1,0},{2,3},{3,2},{4,5},{5,4},{6,7},{7,6},{8,9},{9,8},{10,11... | collective-permute-start | bytes 1179656 | tf_op jit(solution)/shard_map/ppermute | solution.py:38
  228.2 17.2 %collective-permute-start.32 = (bf16[192,2048]{1,0:T(8,128)(2,1)S(1)}, bf16[192,2048]{1,0:T(8,128)(2,1)S(1)}, u32[]{:S(2)}, u32[]{:S(2)}) collective-permute-start(bf16[192,2048]{1,0:T(8,128)(2,1)S(1)} %multiply_convert_fusion.refs_0_), channel_id=1, source_target_pairs={{0,4},{2,6},{4,0},{6,2},{8,12},{10,14},{12,8},{14,10},{16,20},{18,... | collective-permute-start | bytes 2359304 | tf_op jit(solution)/shard_map/ppermute | solution.py:26
  228.7 18.2 %collective-permute-start.31 = (bf16[192,2048]{1,0:T(8,128)(2,1)S(1)}, bf16[192,2048]{1,0:T(8,128)(2,1)S(1)}, u32[]{:S(2)}, u32[]{:S(2)}) collective-permute-start(bf16[192,2048]{1,0:T(8,128)(2,1)S(1)} %multiply_convert_fusion.refs_0_), channel_id=1, source_target_pairs={{0,1},{1,0},{2,3},{3,2},{4,5},{5,4},{6,7},{7,6},{8,9},{9,8},{10,11... | collective-permute-start | bytes 2359304 | tf_op jit(solution)/shard_map/ppermute | solution.py:38
  230.0 28.5 %collective-permute-start.35 = (bf16[192,2048]{1,0:T(8,128)(2,1)S(1)}, bf16[192,2048]{1,0:T(8,128)(2,1)S(1)}, u32[]{:S(2)}, u32[]{:S(2)}) collective-permute-start(bf16[192,2048]{1,0:T(8,128)(2,1)S(1)} %multiply_convert_fusion.refs_0_), channel_id=1, source_target_pairs={{0,2},{2,0},{4,6},{6,4},{8,10},{10,8},{12,14},{14,12},{16,18},{18,... | collective-permute-start | bytes 2359304 | tf_op jit(solution)/shard_map/ppermute | solution.py:26
  245.5 8.7 %collective-permute-start.33 = (bf16[96,2048]{1,0:T(8,128)(2,1)S(1)}, bf16[96,2048]{1,0:T(8,128)(2,1)S(1)}, u32[]{:S(2)}, u32[]{:S(2)}) collective-permute-start(bf16[96,2048]{1,0:T(8,128)(2,1)S(1)} %slice.246), channel_id=1, source_target_pairs={{0,1},{1,0},{2,3},{3,2},{4,5},{5,4},{6,7},{7,6},{8,9},{9,8},{10,11... | collective-permute-start | bytes 1179656 | tf_op jit(solution)/shard_map/ppermute | solution.py:38
  246.9 11.7 %collective-permute-start.37 = (bf16[192,2048]{1,0:T(8,128)(2,1)S(1)}, bf16[192,2048]{1,0:T(8,128)(2,1)S(1)}, u32[]{:S(2)}, u32[]{:S(2)}) collective-permute-start(bf16[192,2048]{1,0:T(8,128)(2,1)S(1)} %collective-permute-done.32.refs_2_), channel_id=1, source_target_pairs={{0,2},{2,0},{4,6},{6,4},{8,10},{10,8},{12,14},{14,12},{16,18},{18,... | collective-permute-start | bytes 2359304 | tf_op jit(solution)/shard_map/ppermute | solution.py:26
  246.9 11.6 %collective-permute-start.34 = (bf16[96,2048]{1,0:T(8,128)(2,1)S(1)}, bf16[96,2048]{1,0:T(8,128)(2,1)S(1)}, u32[]{:S(2)}, u32[]{:S(2)}) collective-permute-start(bf16[96,2048]{1,0:T(8,128)(2,1)S(1)} %slice.247), channel_id=1, source_target_pairs={{0,4},{2,6},{4,0},{6,2},{8,12},{10,14},{12,8},{14,10},{16,20},{18,... | collective-permute-start | bytes 1179656 | tf_op jit(solution)/shard_map/ppermute | solution.py:26
  248.6 12.4 %collective-permute-start.36 = (bf16[192,2048]{1,0:T(8,128)(2,1)S(1)}, bf16[192,2048]{1,0:T(8,128)(2,1)}, u32[]{:S(2)}, u32[]{:S(2)}) collective-permute-start(bf16[192,2048]{1,0:T(8,128)(2,1)S(1)} %collective-permute-done.31.refs_1_), channel_id=1, source_target_pairs={{0,2},{2,0},{4,6},{6,4},{8,10},{10,8},{12,14},{14,12},{16,18},{18,... | collective-permute-start | bytes 2359304 | tf_op jit(solution)/shard_map/ppermute | solution.py:26
  301.4 267.0 %reduce-scatter.6.cloned.1.call-start = ((), (), s32[]{:S(2)}) async-start(), calls=%async_computation.13 | async-start | bytes 7864320 | tf_op jit(solution)/shard_map/reduce_scatter | solution.py:55
  366.1 20.0 %collective-permute-start.45 = (bf16[96,2048]{1,0:T(8,128)(2,1)}, bf16[96,2048]{1,0:T(8,128)(2,1)S(1)}, u32[]{:S(2)}, u32[]{:S(2)}) collective-permute-start(bf16[96,2048]{1,0:T(8,128)(2,1)} %slice.251), channel_id=1, source_target_pairs={{0,1},{1,0},{2,3},{3,2},{4,5},{5,4},{6,7},{7,6},{8,9},{9,8},{10,11... | collective-permute-start | bytes 1179656 | tf_op jit(solution)/shard_map/ppermute | solution.py:38
  367.6 18.6 %collective-permute-start.47 = (bf16[96,2048]{1,0:T(8,128)(2,1)}, bf16[96,2048]{1,0:T(8,128)(2,1)}, u32[]{:S(2)}, u32[]{:S(2)}) collective-permute-start(bf16[96,2048]{1,0:T(8,128)(2,1)} %slice.252), channel_id=1, source_target_pairs={{0,4},{2,6},{4,0},{6,2},{8,12},{10,14},{12,8},{14,10},{16,20},{18,... | collective-permute-start | bytes 1179656 | tf_op jit(solution)/shard_map/ppermute | solution.py:26
  370.0 17.2 %collective-permute-start.43 = (bf16[96,2048]{1,0:T(8,128)(2,1)}, bf16[96,2048]{1,0:T(8,128)(2,1)}, u32[]{:S(2)}, u32[]{:S(2)}) collective-permute-start(bf16[96,2048]{1,0:T(8,128)(2,1)} %get-tuple-element.313), channel_id=1, source_target_pairs={{0,4},{2,6},{4,0},{6,2},{8,12},{10,14},{12,8},{14,10},{16,20},{18,... | collective-permute-start | bytes 1179656 | tf_op jit(solution)/shard_map/ppermute | solution.py:26
  370.5 16.7 %collective-permute-start.42 = (bf16[96,2048]{1,0:T(8,128)(2,1)}, bf16[96,2048]{1,0:T(8,128)(2,1)}, u32[]{:S(2)}, u32[]{:S(2)}) collective-permute-start(bf16[96,2048]{1,0:T(8,128)(2,1)} %get-tuple-element.314), channel_id=1, source_target_pairs={{0,1},{1,0},{2,3},{3,2},{4,5},{5,4},{6,7},{7,6},{8,9},{9,8},{10,11... | collective-permute-start | bytes 1179656 | tf_op jit(solution)/shard_map/ppermute | solution.py:38
  389.7 10.1 %collective-permute-start.48 = (bf16[96,2048]{1,0:T(8,128)(2,1)S(1)}, bf16[96,2048]{1,0:T(8,128)(2,1)S(1)}, u32[]{:S(2)}, u32[]{:S(2)}) collective-permute-start(bf16[96,2048]{1,0:T(8,128)(2,1)S(1)} %add_convert_fusion.20), channel_id=1, source_target_pairs={{0,4},{2,6},{4,0},{6,2},{8,12},{10,14},{12,8},{14,10},{16,20},{18,... | collective-permute-start | bytes 1179656 | tf_op jit(solution)/shard_map/ppermute | solution.py:26
  391.2 9.7 %collective-permute-start.49 = (bf16[96,2048]{1,0:T(8,128)(2,1)S(1)}, bf16[96,2048]{1,0:T(8,128)(2,1)S(1)}, u32[]{:S(2)}, u32[]{:S(2)}) collective-permute-start(bf16[96,2048]{1,0:T(8,128)(2,1)S(1)} %add_convert_fusion.19), channel_id=1, source_target_pairs={{0,1},{1,0},{2,3},{3,2},{4,5},{5,4},{6,7},{7,6},{8,9},{9,8},{10,11... | collective-permute-start | bytes 1179656 | tf_op jit(solution)/shard_map/ppermute | solution.py:38
  405.0 17.4 %collective-permute-start.51 = (bf16[192,2048]{1,0:T(8,128)(2,1)S(1)}, bf16[192,2048]{1,0:T(8,128)(2,1)}, u32[]{:S(2)}, u32[]{:S(2)}) collective-permute-start(bf16[192,2048]{1,0:T(8,128)(2,1)S(1)} %get-tuple-element.281.refs_0_), channel_id=1, source_target_pairs={{0,4},{2,6},{4,0},{6,2},{8,12},{10,14},{12,8},{14,10},{16,20},{18,... | collective-permute-start | bytes 2359304 | tf_op jit(solution)/shard_map/ppermute | solution.py:26
  405.6 17.2 %collective-permute-start.50 = (bf16[192,2048]{1,0:T(8,128)(2,1)S(1)}, bf16[192,2048]{1,0:T(8,128)(2,1)}, u32[]{:S(2)}, u32[]{:S(2)}) collective-permute-start(bf16[192,2048]{1,0:T(8,128)(2,1)S(1)} %get-tuple-element.281.refs_0_), channel_id=1, source_target_pairs={{0,1},{1,0},{2,3},{3,2},{4,5},{5,4},{6,7},{7,6},{8,9},{9,8},{10,11... | collective-permute-start | bytes 2359304 | tf_op jit(solution)/shard_map/ppermute | solution.py:38
  421.5 19.6 %collective-permute-start.54 = (bf16[192,2048]{1,0:T(8,128)(2,1)S(1)}, bf16[192,2048]{1,0:T(8,128)(2,1)}, u32[]{:S(2)}, u32[]{:S(2)}) collective-permute-start(bf16[192,2048]{1,0:T(8,128)(2,1)S(1)} %get-tuple-element.281.refs_0_), channel_id=1, source_target_pairs={{0,2},{2,0},{4,6},{6,4},{8,10},{10,8},{12,14},{14,12},{16,18},{18,... | collective-permute-start | bytes 2359304 | tf_op jit(solution)/shard_map/ppermute | solution.py:26
  423.8 10.4 %collective-permute-start.52 = (bf16[96,2048]{1,0:T(8,128)(2,1)S(1)}, bf16[96,2048]{1,0:T(8,128)(2,1)S(1)}, u32[]{:S(2)}, u32[]{:S(2)}) collective-permute-start(bf16[96,2048]{1,0:T(8,128)(2,1)S(1)} %slice.210), channel_id=1, source_target_pairs={{0,1},{1,0},{2,3},{3,2},{4,5},{5,4},{6,7},{7,6},{8,9},{9,8},{10,11... | collective-permute-start | bytes 1179656 | tf_op jit(solution)/shard_map/ppermute | solution.py:38
  425.6 11.0 %collective-permute-start.53 = (bf16[96,2048]{1,0:T(8,128)(2,1)S(1)}, bf16[96,2048]{1,0:T(8,128)(2,1)}, u32[]{:S(2)}, u32[]{:S(2)}) collective-permute-start(bf16[96,2048]{1,0:T(8,128)(2,1)S(1)} %slice.211), channel_id=1, source_target_pairs={{0,4},{2,6},{4,0},{6,2},{8,12},{10,14},{12,8},{14,10},{16,20},{18,... | collective-permute-start | bytes 1179656 | tf_op jit(solution)/shard_map/ppermute | solution.py:26
  427.1 14.6 %collective-permute-start.55 = (bf16[192,2048]{1,0:T(8,128)(2,1)}, bf16[192,2048]{1,0:T(8,128)(2,1)}, u32[]{:S(2)}, u32[]{:S(2)}) collective-permute-start(bf16[192,2048]{1,0:T(8,128)(2,1)} %collective-permute-done.50.refs_1_), channel_id=1, source_target_pairs={{0,2},{2,0},{4,6},{6,4},{8,10},{10,8},{12,14},{14,12},{16,18},{18,... | collective-permute-start | bytes 2359304 | tf_op jit(solution)/shard_map/ppermute | solution.py:26
  436.6 8.9 %collective-permute-start.56 = (bf16[192,2048]{1,0:T(8,128)(2,1)}, bf16[192,2048]{1,0:T(8,128)(2,1)}, u32[]{:S(2)}, u32[]{:S(2)}) collective-permute-start(bf16[192,2048]{1,0:T(8,128)(2,1)} %collective-permute-done.51.refs_2_), channel_id=1, source_target_pairs={{0,2},{2,0},{4,6},{6,4},{8,10},{10,8},{12,14},{14,12},{16,18},{18,... | collective-permute-start | bytes 2359304 | tf_op jit(solution)/shard_map/ppermute | solution.py:26
  441.1 12.4 %collective-permute-start.59 = (bf16[192,2048]{1,0:T(8,128)(2,1)}, bf16[192,2048]{1,0:T(8,128)(2,1)S(1)}, u32[]{:S(2)}, u32[]{:S(2)}) collective-permute-start(bf16[192,2048]{1,0:T(8,128)(2,1)} %get-tuple-element.206), channel_id=1, source_target_pairs={{0,2},{2,0},{4,6},{6,4},{8,10},{10,8},{12,14},{14,12},{16,18},{18,... | collective-permute-start | bytes 2359304 | tf_op jit(solution)/shard_map/ppermute | solution.py:26
  441.1 12.4 %collective-permute-start.60 = (bf16[192,2048]{1,0:T(8,128)(2,1)}, bf16[192,2048]{1,0:T(8,128)(2,1)S(1)}, u32[]{:S(2)}, u32[]{:S(2)}) collective-permute-start(bf16[192,2048]{1,0:T(8,128)(2,1)} %get-tuple-element.207), channel_id=1, source_target_pairs={{0,2},{2,0},{4,6},{6,4},{8,10},{10,8},{12,14},{14,12},{16,18},{18,... | collective-permute-start | bytes 2359304 | tf_op jit(solution)/shard_map/ppermute | solution.py:26
  441.6 11.9 %collective-permute-start.61 = (bf16[192,2048]{1,0:T(8,128)(2,1)}, bf16[192,2048]{1,0:T(8,128)(2,1)S(1)}, u32[]{:S(2)}, u32[]{:S(2)}) collective-permute-start(bf16[192,2048]{1,0:T(8,128)(2,1)} %get-tuple-element.208), channel_id=1, source_target_pairs={{0,2},{2,0},{4,6},{6,4},{8,10},{10,8},{12,14},{14,12},{16,18},{18,... | collective-permute-start | bytes 2359304 | tf_op jit(solution)/shard_map/ppermute | solution.py:26
  441.7 11.8 %collective-permute-start.62 = (bf16[192,2048]{1,0:T(8,128)(2,1)}, bf16[192,2048]{1,0:T(8,128)(2,1)}, u32[]{:S(2)}, u32[]{:S(2)}) collective-permute-start(bf16[192,2048]{1,0:T(8,128)(2,1)} %get-tuple-element.209), channel_id=1, source_target_pairs={{0,2},{2,0},{4,6},{6,4},{8,10},{10,8},{12,14},{14,12},{16,18},{18,... | collective-permute-start | bytes 2359304 | tf_op jit(solution)/shard_map/ppermute | solution.py:26
  457.2 16.4 %collective-permute-start.66 = (bf16[96,2048]{1,0:T(8,128)(2,1)S(1)}, bf16[96,2048]{1,0:T(8,128)(2,1)S(1)}, u32[]{:S(2)}, u32[]{:S(2)}) collective-permute-start(bf16[96,2048]{1,0:T(8,128)(2,1)S(1)} %slice.219), channel_id=1, source_target_pairs={{0,4},{2,6},{4,0},{6,2},{8,12},{10,14},{12,8},{14,10},{16,20},{18,... | collective-permute-start | bytes 1179656 | tf_op jit(solution)/shard_map/ppermute | solution.py:26
  458.7 14.8 %collective-permute-start.65 = (bf16[96,2048]{1,0:T(8,128)(2,1)S(1)}, bf16[96,2048]{1,0:T(8,128)(2,1)}, u32[]{:S(2)}, u32[]{:S(2)}) collective-permute-start(bf16[96,2048]{1,0:T(8,128)(2,1)S(1)} %slice.218), channel_id=1, source_target_pairs={{0,1},{1,0},{2,3},{3,2},{4,5},{5,4},{6,7},{7,6},{8,9},{9,8},{10,11... | collective-permute-start | bytes 1179656 | tf_op jit(solution)/shard_map/ppermute | solution.py:38
  459.5 17.4 %collective-permute-start.64 = (bf16[96,2048]{1,0:T(8,128)(2,1)S(1)}, bf16[96,2048]{1,0:T(8,128)(2,1)}, u32[]{:S(2)}, u32[]{:S(2)}) collective-permute-start(bf16[96,2048]{1,0:T(8,128)(2,1)S(1)} %get-tuple-element.311), channel_id=1, source_target_pairs={{0,4},{2,6},{4,0},{6,2},{8,12},{10,14},{12,8},{14,10},{16,20},{18,... | collective-permute-start | bytes 1179656 | tf_op jit(solution)/shard_map/ppermute | solution.py:26
  460.1 18.0 %collective-permute-start.63 = (bf16[96,2048]{1,0:T(8,128)(2,1)S(1)}, bf16[96,2048]{1,0:T(8,128)(2,1)}, u32[]{:S(2)}, u32[]{:S(2)}) collective-permute-start(bf16[96,2048]{1,0:T(8,128)(2,1)S(1)} %get-tuple-element.312), channel_id=1, source_target_pairs={{0,1},{1,0},{2,3},{3,2},{4,5},{5,4},{6,7},{7,6},{8,9},{9,8},{10,11... | collective-permute-start | bytes 1179656 | tf_op jit(solution)/shard_map/ppermute | solution.py:38
  478.1 46.9 %all-to-all-start.3 = ((bf16[4,128,1536]{2,1,0:T(8,128)(2,1)}), bf16[4,128,1536]{2,1,0:T(8,128)(2,1)}, u32[]{:S(2)}, u32[]{:S(2)}) async-start(bf16[4,128,1536]{2,1,0:T(8,128)(2,1)} %bitcast.21), calls=%async_computation.4 | async-start | bytes 3145728 | tf_op jit(solution)/shard_map/all_to_all | solution.py:154
  482.4 143.6 %reduce-scatter.8.cloned.1.call-start = ((), (), s32[]{:S(2)}) async-start(), calls=%async_computation.14 | async-start | bytes 3276800 | tf_op jit(solution)/shard_map/reduce_scatter | solution.py:55
  482.5 40.8 %collective-permute-start.68 = (bf16[768,128]{1,0:T(8,128)(2,1)}, bf16[768,128]{1,0:T(8,128)(2,1)}, u32[]{:S(2)}, u32[]{:S(2)}) collective-permute-start(bf16[768,128]{1,0:T(8,128)(2,1)} %get-tuple-element.223), channel_id=1, source_target_pairs={{16,0},{18,2},{20,4},{22,6},{24,8},{26,10},{28,12},{30,14},{17,1},... | collective-permute-start | bytes 589832 | tf_op jit(solution)/shard_map/ppermute | solution.py:60
  483.8 41.2 %collective-permute-start.67 = (bf16[1536,128]{1,0:T(8,128)(2,1)}, bf16[1536,128]{1,0:T(8,128)(2,1)}, u32[]{:S(2)}, u32[]{:S(2)}) collective-permute-start(bf16[1536,128]{1,0:T(8,128)(2,1)} %get-tuple-element.222), channel_id=1, source_target_pairs={{8,0},{10,2},{12,4},{14,6},{16,8},{18,10},{20,12},{22,14},{24,16},... | collective-permute-start | bytes 1179656 | tf_op jit(solution)/shard_map/ppermute | solution.py:60
  486.3 34.6 %collective-permute-start.69 = (bf16[96,2048]{1,0:T(8,128)(2,1)S(1)}, bf16[96,2048]{1,0:T(8,128)(2,1)S(1)}, u32[]{:S(2)}, u32[]{:S(2)}) collective-permute-start(bf16[96,2048]{1,0:T(8,128)(2,1)S(1)} %add_convert_fusion.18), channel_id=1, source_target_pairs={{0,4},{2,6},{4,0},{6,2},{8,12},{10,14},{12,8},{14,10},{16,20},{18,... | collective-permute-start | bytes 1179656 | tf_op jit(solution)/shard_map/ppermute | solution.py:26
  489.4 31.5 %collective-permute-start.70 = (bf16[96,2048]{1,0:T(8,128)(2,1)S(1)}, bf16[96,2048]{1,0:T(8,128)(2,1)S(1)}, u32[]{:S(2)}, u32[]{:S(2)}) collective-permute-start(bf16[96,2048]{1,0:T(8,128)(2,1)S(1)} %add_convert_fusion.17), channel_id=1, source_target_pairs={{0,1},{1,0},{2,3},{3,2},{4,5},{5,4},{6,7},{7,6},{8,9},{9,8},{10,11... | collective-permute-start | bytes 1179656 | tf_op jit(solution)/shard_map/ppermute | solution.py:38
  568.5 19.7 %collective-permute-start.75 = (bf16[192,2048]{1,0:T(8,128)(2,1)}, bf16[192,2048]{1,0:T(8,128)(2,1)}, u32[]{:S(2)}, u32[]{:S(2)}) collective-permute-start(bf16[192,2048]{1,0:T(8,128)(2,1)} %get-tuple-element.254), channel_id=1, source_target_pairs={{0,1},{1,0},{2,3},{3,2},{4,5},{5,4},{6,7},{7,6},{8,9},{9,8},{10,11... | collective-permute-start | bytes 2359304 | tf_op jit(solution)/shard_map/ppermute | solution.py:38
  569.9 23.6 %all-to-all-start.4 = ((bf16[4,128,1536]{2,1,0:T(8,128)(2,1)}), bf16[4,128,1536]{2,1,0:T(8,128)(2,1)S(1)}, u32[]{:S(2)}, u32[]{:S(2)}) async-start(bf16[4,128,1536]{2,1,0:T(8,128)(2,1)} %bitcast.22), calls=%async_computation.6 | async-start | bytes 3145728 | tf_op jit(solution)/shard_map/all_to_all | solution.py:154
  593.6 36.7 %collective-permute-start.76 = (bf16[192,2048]{1,0:T(8,128)(2,1)}, bf16[192,2048]{1,0:T(8,128)(2,1)S(1)}, u32[]{:S(2)}, u32[]{:S(2)}) collective-permute-start(bf16[192,2048]{1,0:T(8,128)(2,1)} %get-tuple-element.257), channel_id=1, source_target_pairs={{0,1},{1,0},{2,3},{3,2},{4,5},{5,4},{6,7},{7,6},{8,9},{9,8},{10,11... | collective-permute-start | bytes 2359304 | tf_op jit(solution)/shard_map/ppermute | solution.py:38
  594.1 37.0 %collective-permute-start.77 = (bf16[192,2048]{1,0:T(8,128)(2,1)}, bf16[192,2048]{1,0:T(8,128)(2,1)}, u32[]{:S(2)}, u32[]{:S(2)}) collective-permute-start(bf16[192,2048]{1,0:T(8,128)(2,1)} %add_convert_fusion), channel_id=1, source_target_pairs={{0,4},{2,6},{4,0},{6,2},{8,12},{10,14},{12,8},{14,10},{16,20},{18,... | collective-permute-start | bytes 2359304 | tf_op jit(solution)/shard_map/ppermute | solution.py:26
  626.1 15.7 %all-to-all-start.5 = ((bf16[4,128,640]{2,1,0:T(8,128)(2,1)}), bf16[4,128,640]{2,1,0:T(8,128)(2,1)}, u32[]{:S(2)}, u32[]{:S(2)}) async-start(bf16[4,128,640]{2,1,0:T(8,128)(2,1)} %bitcast.23), calls=%async_computation.8 | async-start | bytes 1310720 | tf_op jit(solution)/shard_map/all_to_all | solution.py:154
  (77 other events, 483.0 us)
Sparse Core Ops, SparseCore 0:
  24.6 55.8 all-gather.3
  82.1 122.4 all-gather.5
  206.8 121.7 all-gather.7
  330.8 111.5 reduce-scatter.3
  444.5 123.8 reduce-scatter.5
  570.6 55.3 reduce-scatter.7

commit v7 on v6

--- a/solution.py
+++ b/solution.py
@@ -867,11 +867,9 @@
         plane * (qw + width) * 20,
         plane * (qw + 2 * width) * 10,
     )
-    one = split_dot(d_raw, w_qkv)
-    d_raw, one = tie(d_raw, one)
-    one = Sums(*one)
     gain_sums, attn_grad = weight_grads(a_one, d_raw, d_h_rows, o, w_qkv)
-    gain_sums = gain_sums[0]
+    gain_sums, d_raw = tie(gain_sums[0], d_raw)
+    one = Sums(*split_dot(d_raw, w_qkv))
     attn_grad = line_scatter(attn_grad, n)
     gain_sums, ffn_grad_1 = tie(gain_sums, ffn_grad_1)
     one.parts, gain_sums = tie(one.parts, gain_sums)

time: 670 us -> 669 us (level)
    unnamed x109 -> x103, local copies, waits for them, and re-layouts: 21.4 us -> 20.1 us
  transfers between devices with their start and end apart: 93 -> 93, of which waited for: 40 -> 41; matrix products, arithmetic and copies ran while one was open for 12% -> 12% of each run, Pallas kernels for 35% -> 35%
where the time goes in v7:
time: 669 us; the launch traced here: 660 us
  Pallas kernels  232 us (35%)
  waiting for transfers between devices  204 us (30%)
  starting transfers between devices  80.3 us (12%)
  other arithmetic  46.4 us (7%)
  local copies, waits for them, and re-layouts  42.7 us (6%)
  blocking collectives  39.6 us (6%)
  between operations  15.3 us (2%)
    pallas_call x19, Pallas kernels, call(): pl.pallas_call(kernel, out_shape=[jax.ShapeDtypeStruct(shape, dtype) for...  232 us
    ppermute x59, waiting for transfers between devices, swap_ctx(): return lax.ppermute(value, 'ctx', [(i, i ^ bit) for i in range(n)])  86.1 us
    ppermute x19, waiting for transfers between devices, swap_x(): return lax.ppermute(value, 'tp', [(0, 1), (1, 0)])  40.1 us
    all_to_all x2, blocking collectives, spread(): lax.all_to_all(pieces, 'ctx', axis, axis, axis_index_groups=groups, tiled...  39.6 us
    ppermute x59, starting transfers between devices, swap_ctx(): return lax.ppermute(value, 'ctx', [(i, i ^ bit) for i in range(n)])  31.9 us
    reduce_scatter x3, waiting for transfers between devices, line_scatter(): lax.psum_scatter(partial, 'ctx', scatter_dimension=0, axis_index_groups=l...  29.4 us
    all_gather x3, waiting for transfers between devices, line_gather(): lax.all_gather(own, 'ctx', axis=0, axis_index_groups=line_groups(n), tile...  27 us
    convert_element_type x11, other arithmetic, add16(): return (a.astype(F32) + b.astype(F32)).astype(BF16)  20.7 us
  transfers between devices with their start and end apart: 93, of which 41 were waited for; matrix products, arithmetic and copies ran while one was open for 12% of the time, Pallas kernels for 35%

profile of v7, /device:TPU:0, one launch (start us, length us, event | category | flops | bytes accessed | tf_op | source)
XLA Modules:
  0.0 660.3 jit_solution(14115449248231225891)
XLA Ops:
  7.2 2.1 shard_map.237
  9.4 15.1 %all_to_all.30 = bf16[4,128,640]{2,1,0:T(8,128)(2,1)} all-to-all(bf16[4,128,640]{2,1,0:T(8,128)(2,1)} %shard_map.237), channel_id=1, replica_groups={{0,2,4,6},{8,10,12,14},{16,18,20,22},{24,26,28,30},{1,3,5,7},{9,11,13,1..., dimensions={0} | all-to-all | bytes 1310720 | tf_op jit(solution)/shard_map/all_to_all | solution.py:154
  24.6 3.9 shard_map.238
  28.4 24.5 %all_to_all.31 = bf16[4,128,1536]{2,1,0:T(8,128)(2,1)} all-to-all(bf16[4,128,1536]{2,1,0:T(8,128)(2,1)} %get-tuple-element.144), channel_id=1, replica_groups={{0,2,4,6},{8,10,12,14},{16,18,20,22},{24,26,28,30},{1,3,5,7},{9,11,13,1..., dimensions={0} | all-to-all | bytes 3145728 | tf_op jit(solution)/shard_map/all_to_all | solution.py:154
  59.5 2.2 collective-permute-start.5
  63.3 2.8 fusion.18
  66.1 2.5 pad_maximum_fusion.1
  68.6 12.3 %collective-permute-done.5.refs_3_ = bf16[192,2048]{1,0:T(8,128)(2,1)S(1)} collective-permute-done((bf16[192,2048]{1,0:T(8,128)(2,1)S(1)}, bf16[192,2048]{1,0:T(8,128)(2,1)S(1)}, u32[]{:S(2)}, u32[]{:S(2)}) %collective-permute-start.5) | collective-permute-done | bytes 786464 | tf_op jit(solution)/shard_map/ppermute | solution.py:73
  80.9 16.0 %collective-permute-done.4.refs_2_ = bf16[192,2048]{1,0:T(8,128)(2,1)S(1)} collective-permute-done((bf16[192,2048]{1,0:T(8,128)(2,1)S(1)}, bf16[192,2048]{1,0:T(8,128)(2,1)S(1)}, u32[]{:S(2)}, u32[]{:S(2)}) %collective-permute-start.4) | collective-permute-done | bytes 786464 | tf_op jit(solution)/shard_map/ppermute | solution.py:26
  98.1 3.6 all-to-all-start.2
  104.5 2.4 broadcast_subtract_fusion
  106.9 2.7 slice.236.refs_8_.refs_0_.w_ref
  109.7 14.2 %shard_map.239 = (bf16[1536,2048]{1,0:T(8,128)(2,1)}, f32[1536,384]{1,0:T(8,128)}, bf16[1536,256]{1,0:T(8,128)(2,1)}, bf16[1536,128]{1,0:T(8,128)(2,1)}) custom-call(s32[8]{0:T(128)} %or_or_fusion.table, bf16[192,2048]{1,0:T(8,128)(2,1)} %copy-done.5, bf16[192,2048]{1,0:T(8,128)(2,1)} %copy-done.15, bf16[192,2048]{1,0:T(8,128)(2,1)} %copy-done.14, ...), custom_call_target="tpu_custom_call" | custom-call | flops 2415919104 | bytes 16515072 | tf_op jit(solution)/shard_map/pallas_call | solution.py:619
  129.4 3.5 collective-permute-start.10
  132.9 5.1 collective-permute-start.11
  138.3 14.0 %shard_map.240.refs_0_ = f32[6144,128]{1,0:T(8,128)} custom-call(s32[8]{0:T(128)} %or_or_fusion.1.table, s32[8]{0:T(128)} %get-tuple-element.280.lo, s32[8]{0:T(128)} %get-tuple-element.279.hi, bf16[1536,256]{1,0:T(8,128)(2,1)} %get-tuple-element.154.q_ref, s32[1536,1]{1,0:T(8,128)} %get-tuple-element.309.start_ref, bf16[1536,128]{1,0:T(8,128)(2,1)} %get-tuple-element.155.kv_ref), custom_call_target="tpu_custom_call" | custom-call | flops 4831838208 | bytes 3932160 | tf_op jit(solution)/shard_map/pallas_call | solution.py:619
  152.2 2.3 slice.237.w_ref.refs_10_
  154.6 4.5 collective-permute-done.11
  167.0 2.5 copy-done.23
  170.3 9.2 %shard_map.241 = (bf16[1536,256]{1,0:T(8,128)(2,1)}, f32[1536,256]{1,0:T(8,128)}, f32[6144,1]{1,0:T(8,128)}) custom-call(s32[8]{0:T(128)} %or_or_fusion.1.table, s32[8]{0:T(128)} %get-tuple-element.278.lo, s32[8]{0:T(128)} %get-tuple-element.277.hi, bf16[1536,256]{1,0:T(8,128)(2,1)} %get-tuple-element.154.q_ref, s32[1536,1]{1,0:T(8,128)} %get-tuple-element.310.start_ref, ...), custom_call_target="tpu_custom_call" | custom-call | flops 4831838208 | bytes 3932160 | tf_op jit(solution)/shard_map/pallas_call | solution.py:619
  179.5 7.2 %shard_map.242 = (bf16[768,2048]{1,0:T(8,128)(2,1)}, bf16[192,2048]{1,0:T(8,128)(2,1)}, bf16[192,2048]{1,0:T(8,128)(2,1)}, bf16[192,2048]{1,0:T(8,128)(2,1)}, bf16[192,2048]{1,0:T(8,128)(2,1)}) custom-call(bf16[1536,256]{1,0:T(8,128)(2,1)} %get-tuple-element.163.a_ref.d_ref, bf16[2048,256]{1,0:T(8,128)(2,1)} %slice.237.w_ref.refs_10_), custom_call_target="tpu_custom_call" | custom-call | flops 1610612736 | bytes 7077888 | tf_op jit(solution)/shard_map/pallas_call | solution.py:619
  189.3 2.1 constant_dynamic-update-slice_fusion.6
  201.2 6.4 collective-permute-done.21
  208.2 7.2 %collective-permute-done.19 = bf16[96,2048]{1,0:T(8,128)(2,1)S(1)} collective-permute-done((bf16[96,2048]{1,0:T(8,128)(2,1)S(1)}, bf16[96,2048]{1,0:T(8,128)(2,1)S(1)}, u32[]{:S(2)}, u32[]{:S(2)}) %collective-permute-start.19) | collective-permute-done | bytes 393248 | tf_op jit(solution)/shard_map/ppermute | solution.py:26
  215.7 1.8 collective-permute-start.29
  218.8 6.9 %collective-permute-done.29 = bf16[96,2048]{1,0:T(8,128)(2,1)S(1)} collective-permute-done((bf16[96,2048]{1,0:T(8,128)(2,1)S(1)}, bf16[96,2048]{1,0:T(8,128)(2,1)S(1)}, u32[]{:S(2)}, u32[]{:S(2)}) %collective-permute-start.29) | collective-permute-done | bytes 393248 | tf_op jit(solution)/shard_map/ppermute | solution.py:26
  230.1 15.5 %collective-permute-done.32.refs_2_ = bf16[192,2048]{1,0:T(8,128)(2,1)S(1)} collective-permute-done((bf16[192,2048]{1,0:T(8,128)(2,1)S(1)}, bf16[192,2048]{1,0:T(8,128)(2,1)S(1)}, u32[]{:S(2)}, u32[]{:S(2)}) %collective-permute-start.32) | collective-permute-done | bytes 786464 | tf_op jit(solution)/shard_map/ppermute | solution.py:26
  248.7 5.6 collective-permute-done.33.refs_3_
  254.3 4.4 collective-permute-done.34.refs_4_
  261.2 24.9 %shard_map.243 = (bf16[1536,512]{1,0:T(8,128)(2,1)}, bf16[1536,1024]{1,0:T(8,128)(2,1)}, bf16[1536,2048]{1,0:T(8,128)(2,1)}, bf16[1536,2048]{1,0:T(8,128)(2,1)}) custom-call(bf16[192,2048]{1,0:T(8,128)(2,1)} %copy-done.16, bf16[192,2048]{1,0:T(8,128)(2,1)} %copy-done.20, bf16[192,2048]{1,0:T(8,128)(2,1)} %copy-done.19, bf16[96,2048]{1,0:T(8,128)(2,1)} %copy-done.41, ...), custom_call_target="tpu_custom_call" | custom-call | flops 19327352832 | bytes 36175872 | tf_op jit(solution)/shard_map/pallas_call | solution.py:619
  286.0 15.6 %shard_map.244 = bf16[2048,1536]{1,0:T(8,128)(2,1)} custom-call(bf16[1536,2048]{1,0:T(8,128)(2,1)} %get-tuple-element.176.a_ref, bf16[1536,1024]{1,0:T(8,128)(2,1)} %get-tuple-element.178.b_ref, bf16[1536,2048]{1,0:T(8,128)(2,1)} %constant_dynamic-update-slice_fusion.2.refs_10_.c_ref, bf16[1536,512]{1,0:T(8,128)(2,1)} %get-tuple-element.179.d_ref.h0_ref), custom_call_target="tpu_custom_call" | custom-call | flops 9663676416 | bytes 23592960 | tf_op jit(solution)/shard_map/pallas_call | solution.py:619
  301.7 27.0 %all-gather.8.cloned.1.call-done.w_ref.w1_ref = bf16[2048,1536]{1,0:T(8,128)(2,1)} async-done(((bf16[512,1536]{1,0:T(8,128)(2,1)}), bf16[2048,1536]{1,0:T(8,128)(2,1)}) %all-gather.8.cloned.1.call-update) | async-done | bytes 6291472 | tf_op jit(solution)/shard_map/all_gather | solution.py:51
  328.6 25.6 %shard_map.245 = (bf16[1536,512]{1,0:T(8,128)(2,1)}, bf16[1536,1024]{1,0:T(8,128)(2,1)}, bf16[768,2048]{1,0:T(8,128)(2,1)}, bf16[192,2048]{1,0:T(8,128)(2,1)}, b...) custom-call(bf16[1536,2048]{1,0:T(8,128)(2,1)} %get-tuple-element.176.a_ref, ...), custom_call_target="tpu_custom_call" | custom-call | flops 19327352832 | bytes 36175872 | tf_op jit(solution)/shard_map/pallas_call | solution.py:619
  360.2 4.2 add_convert_fusion.9
  371.1 15.0 %shard_map.246 = bf16[2048,1536]{1,0:T(8,128)(2,1)} custom-call(bf16[1536,2048]{1,0:T(8,128)(2,1)} %get-tuple-element.176.a_ref, bf16[1536,1024]{1,0:T(8,128)(2,1)} %get-tuple-element.187.b_ref, bf16[1536,2048]{1,0:T(8,128)(2,1)} %constant_dynamic-update-slice_fusion.2.refs_10_.c_ref, bf16[1536,512]{1,0:T(8,128)(2,1)} %get-tuple-element.188.d_ref.h1_ref), custom_call_target="tpu_custom_call" | custom-call | flops 9663676416 | bytes 23592960 | tf_op jit(solution)/shard_map/pallas_call | solution.py:619
  391.7 8.0 %collective-permute-done.48 = bf16[96,2048]{1,0:T(8,128)(2,1)S(1)} collective-permute-done((bf16[96,2048]{1,0:T(8,128)(2,1)S(1)}, bf16[96,2048]{1,0:T(8,128)(2,1)S(1)}, u32[]{:S(2)}, u32[]{:S(2)}) %collective-permute-start.48) | collective-permute-done | bytes 393248 | tf_op jit(solution)/shard_map/ppermute | solution.py:26
  406.2 15.2 %shard_map.247 = (bf16[768,2048]{1,0:T(8,128)(2,1)}, bf16[192,2048]{1,0:T(8,128)(2,1)}, bf16[192,2048]{1,0:T(8,128)(2,1)}, bf16[192,2048]{1,0:T(8,128)(2,1)}, bf16[192,2048]{1,0:T(8,128)(2,1)}) custom-call(bf16[1536,512]{1,0:T(8,128)(2,1)} %get-tuple-element.179.d_ref.h0_ref, bf16[1536,512]{1,0:T(8,128)(2,1)} %get-tuple-element.188.d_ref.h1_ref, ...), custom_call_target="tpu_custom_call" | custom-call | flops 6442450944 | bytes 22020096 | tf_op jit(solution)/shard_map/pallas_call | solution.py:619
  427.1 7.1 %collective-permute-done.52.refs_3_ = bf16[96,2048]{1,0:T(8,128)(2,1)S(1)} collective-permute-done((bf16[96,2048]{1,0:T(8,128)(2,1)S(1)}, bf16[96,2048]{1,0:T(8,128)(2,1)S(1)}, u32[]{:S(2)}, u32[]{:S(2)}) %collective-permute-start.52) | collective-permute-done | bytes 393248 | tf_op jit(solution)/shard_map/ppermute | solution.py:38
  434.1 2.4 collective-permute-done.53.refs_4_
  445.3 8.0 %shard_map.248 = (bf16[1536,2048]{1,0:T(8,128)(2,1)}, bf16[1536,256]{1,0:T(8,128)(2,1)}) custom-call(bf16[192,2048]{1,0:T(8,128)(2,1)} %copy-done.9, bf16[192,2048]{1,0:T(8,128)(2,1)} %collective-permute-done.50.refs_1_, bf16[192,2048]{1,0:T(8,128)(2,1)} %collective-permute-done.51.refs_2_, bf16[96,2048]{1,0:T(8,128)(2,1)} %copy-done.18, ...), custom_call_target="tpu_custom_call" | custom-call | flops 1610612736 | bytes 12582912 | tf_op jit(solution)/shard_map/pallas_call | solution.py:619
  453.4 3.6 add_convert_fusion.5
  461.3 10.8 %shard_map.249 = (f32[6144,128]{1,0:T(8,128)}, bf16[768,128]{1,0:T(8,128)(2,1)}, bf16[1536,128]{1,0:T(8,128)(2,1)}) custom-call(s32[8]{0:T(128)} %or_or_fusion.1.table, s32[8]{0:T(128)} %get-tuple-element.278.lo, s32[8]{0:T(128)} %get-tuple-element.277.hi, bf16[1536,256]{1,0:T(8,128)(2,1)} %get-tuple-element.154.q_ref, ...), custom_call_target="tpu_custom_call" | custom-call | flops 12079595520 | bytes 4718592 | tf_op jit(solution)/shard_map/pallas_call | solution.py:619
  473.4 3.3 collective-permute-done.64
  477.9 4.3 all-to-all-start.3
  486.2 2.0 collective-permute-start.69
  489.9 30.8 %shard_map.250 = (f32[1536,256]{1,0:T(8,128)}, f32[1536,128]{1,0:T(8,128)}) custom-call(s32[8]{0:T(128)} %or_or_fusion.1.table, s32[8]{0:T(128)} %get-tuple-element.280.lo, s32[8]{0:T(128)} %get-tuple-element.279.hi, bf16[1536,256]{1,0:T(8,128)(2,1)} %get-tuple-element.154.q_ref, bf16[1536,256]{1,0:T(8,128)(2,1)} %get-tuple-element.206.do_ref, ...), custom_call_target="tpu_custom_call" | custom-call | flops 12079595520 | bytes 4718592 | tf_op jit(solution)/shard_map/pallas_call | solution.py:619
  524.2 9.1 %shard_map.251 = (bf16[1536,384]{1,0:T(8,128)(2,1)}, f32[8,128]{1,0:T(8,128)}) custom-call(s32[8]{0:T(128)} %or_or_fusion.1.table, f32[1536,384]{1,0:T(8,128)} %get-tuple-element.227.raw_ref, f32[1536,128]{1,0:T(8,128)} %get-tuple-element.149.refs_9_.cos_ref, f32[1536,128]{1,0:T(8,128)} %get-tuple-element.150.refs_10_.sin_ref, ...), custom_call_target="tpu_custom_call" | custom-call | flops 9830400 | bytes 5898240 | tf_op jit(solution)/shard_map/pallas_call | solution.py:619
  533.4 11.1 %shard_map.252 = (f32[8,2048]{1,0:T(8,128)}, bf16[2048,640]{1,0:T(8,128)(2,1)}) custom-call(bf16[1536,2048]{1,0:T(8,128)(2,1)} %get-tuple-element.226.a_ref, bf16[1536,384]{1,0:T(8,128)(2,1)} %get-tuple-element.235.b_ref.a_ref, bf16[1536,2048]{1,0:T(8,128)(2,1)} %get-tuple-element.233.c_ref, bf16[1536,256]{1,0:T(8,128)(2,1)} %get-tuple-element.163.a_ref.d_ref, ...), custom_call_target="tpu_custom_call" | custom-call | flops 4026531840 | bytes 17170432 | tf_op jit(solution)/shard_map/pallas_call | solution.py:619
  545.3 8.5 %shard_map.253 = (bf16[768,2048]{1,0:T(8,128)(2,1)}, bf16[192,2048]{1,0:T(8,128)(2,1)}, bf16[192,2048]{1,0:T(8,128)(2,1)}, bf16[192,2048]{1,0:T(8,128)(2,1)}, bf16[192,2048]{1,0:T(8,128)(2,1)}) custom-call(bf16[1536,384]{1,0:T(8,128)(2,1)} %get-tuple-element.235.b_ref.a_ref, bf16[2048,384]{1,0:T(8,128)(2,1)} %slice.236.refs_8_.refs_0_.w_ref), custom_call_target="tpu_custom_call" | custom-call | flops 2415919104 | bytes 7471104 | tf_op jit(solution)/shard_map/pallas_call | solution.py:619
  559.7 4.1 add_convert_fusion.1
  563.8 3.7 reduce-scatter.6.cloned.1.call-done
  569.1 3.6 all-to-all-start.4
  572.6 14.6 %collective-permute-done.75 = bf16[192,2048]{1,0:T(8,128)(2,1)} collective-permute-done((bf16[192,2048]{1,0:T(8,128)(2,1)}, bf16[192,2048]{1,0:T(8,128)(2,1)}, u32[]{:S(2)}, u32[]{:S(2)}) %collective-permute-start.75) | collective-permute-done | bytes 786464 | tf_op jit(solution)/shard_map/ppermute | solution.py:38
  587.2 2.3 add_convert_fusion
  589.5 3.1 all-to-all-done.4.refs_1_
  594.5 5.0 shard_map.254
  599.5 25.7 %reduce-scatter.8.cloned.1.call-done = bf16[512,640]{1,0:T(8,128)(2,1)} async-done(((bf16[2048,640]{1,0:T(8,128)(2,1)}), bf16[512,640]{1,0:T(8,128)(2,1)}) %reduce-scatter.8.cloned.1.call-update) | async-done | bytes 655376 | tf_op jit(solution)/shard_map/reduce_scatter | solution.py:55
  625.2 4.2 all-to-all-start.5
  633.6 2.3 collective-permute-done.78
  637.1 2.0 collective-permute-start.80
  641.6 3.1 collective-permute-done.81
  644.7 2.1 collective-permute-start.82
  646.8 3.0 fusion.7
  649.8 2.2 shard_map.255
  (337 shorter events, 125.4 us)
Async XLA Ops:
  7.2 99.7 %all-gather.4.cloned.1.call-start = ((), (), s32[]{:S(2)}) async-start(), calls=%async_computation.9 | async-start | bytes 3276800 | tf_op jit(solution)/shard_map/all_gather | solution.py:51
  24.5 236.7 %all-gather.6.cloned.1.call-start = ((), (), s32[]{:S(2)}) async-start(), calls=%async_computation.10 | async-start | bytes 7864320 | tf_op jit(solution)/shard_map/all_gather | solution.py:51
  59.5 21.4 %collective-permute-start.5 = (bf16[192,2048]{1,0:T(8,128)(2,1)S(1)}, bf16[192,2048]{1,0:T(8,128)(2,1)S(1)}, u32[]{:S(2)}, u32[]{:S(2)}) collective-permute-start(bf16[192,2048]{1,0:T(8,128)(2,1)S(1)} %fusion.3.refs_0_), channel_id=1, source_target_pairs={{0,5},{1,4},{2,7},{3,6},{4,1},{5,0},{6,3},{7,2},{8,13},{9,12},{10,... | collective-permute-start | bytes 2359304 | tf_op jit(solution)/shard_map/ppermute | solution.py:73
  61.6 35.3 %collective-permute-start.4 = (bf16[192,2048]{1,0:T(8,128)(2,1)S(1)}, bf16[192,2048]{1,0:T(8,128)(2,1)S(1)}, u32[]{:S(2)}, u32[]{:S(2)}) collective-permute-start(bf16[192,2048]{1,0:T(8,128)(2,1)S(1)} %fusion.3.refs_0_), channel_id=1, source_target_pairs={{0,4},{2,6},{4,0},{6,2},{8,12},{10,14},{12,8},{14,10},{16,20},{18,... | collective-permute-start | bytes 2359304 | tf_op jit(solution)/shard_map/ppermute | solution.py:26
  63.3 33.6 %collective-permute-start.3 = (bf16[192,2048]{1,0:T(8,128)(2,1)S(1)}, bf16[192,2048]{1,0:T(8,128)(2,1)S(1)}, u32[]{:S(2)}, u32[]{:S(2)}) collective-permute-start(bf16[192,2048]{1,0:T(8,128)(2,1)S(1)} %fusion.3.refs_0_), channel_id=1, source_target_pairs={{0,1},{1,0},{2,3},{3,2},{4,5},{5,4},{6,7},{7,6},{8,9},{9,8},{10,11... | collective-permute-start | bytes 2359304 | tf_op jit(solution)/shard_map/ppermute | solution.py:38
  68.6 41.0 %collective-permute-start.6 = (bf16[192,2048]{1,0:T(8,128)(2,1)S(1)}, bf16[192,2048]{1,0:T(8,128)(2,1)}, u32[]{:S(2)}, u32[]{:S(2)}) collective-permute-start(bf16[192,2048]{1,0:T(8,128)(2,1)S(1)} %fusion.3.refs_0_), channel_id=1, source_target_pairs={{0,2},{2,0},{4,6},{6,4},{8,10},{10,8},{12,14},{14,12},{16,18},{18,... | collective-permute-start | bytes 2359304 | tf_op jit(solution)/shard_map/ppermute | solution.py:26
  98.1 25.9 %all-to-all-start.2 = ((bf16[4,128,1536]{2,1,0:T(8,128)(2,1)}), bf16[4,128,1536]{2,1,0:T(8,128)(2,1)S(1)}, u32[]{:S(2)}, u32[]{:S(2)}) async-start(bf16[4,128,1536]{2,1,0:T(8,128)(2,1)} %get-tuple-element.153), calls=%async_computation.2 | async-start | bytes 3145728 | tf_op jit(solution)/shard_map/all_to_all | solution.py:154
  101.6 227.0 %all-gather.8.cloned.1.call-start = ((), (), s32[]{:S(2)}) async-start(), calls=%async_computation.11 | async-start | bytes 7864320 | tf_op jit(solution)/shard_map/all_gather | solution.py:51
  123.9 35.1 %collective-permute-start.13 = (bf16[192,2048]{1,0:T(8,128)(2,1)S(1)}, bf16[192,2048]{1,0:T(8,128)(2,1)}, u32[]{:S(2)}, u32[]{:S(2)}) collective-permute-start(bf16[192,2048]{1,0:T(8,128)(2,1)S(1)} %copy-done.11), channel_id=1, source_target_pairs={{0,4},{2,6},{4,0},{6,2},{8,12},{10,14},{12,8},{14,10},{16,20},{18,... | collective-permute-start | bytes 2359304 | tf_op jit(solution)/shard_map/ppermute | solution.py:26
  125.7 33.3 %collective-permute-start.12 = (bf16[192,2048]{1,0:T(8,128)(2,1)S(1)}, bf16[192,2048]{1,0:T(8,128)(2,1)}, u32[]{:S(2)}, u32[]{:S(2)}) collective-permute-start(bf16[192,2048]{1,0:T(8,128)(2,1)S(1)} %copy-done.11), channel_id=1, source_target_pairs={{0,1},{1,0},{2,3},{3,2},{4,5},{5,4},{6,7},{7,6},{8,9},{9,8},{10,11... | collective-permute-start | bytes 2359304 | tf_op jit(solution)/shard_map/ppermute | solution.py:38
  129.4 29.7 %collective-permute-start.10 = (bf16[1536,128]{1,0:T(8,128)(2,1)}, bf16[1536,128]{1,0:T(8,128)(2,1)S(1)}, u32[]{:S(2)}, u32[]{:S(2)}) collective-permute-start(bf16[1536,128]{1,0:T(8,128)(2,1)} %get-tuple-element.155.kv_ref), channel_id=1, source_target_pairs={{0,8},{2,10},{4,12},{6,14},{8,16},{10,18},{12,20},{14,22},{16,24},... | collective-permute-start | bytes 1179656 | tf_op jit(solution)/shard_map/ppermute | solution.py:60
  132.8 55.1 %collective-permute-start.24 = (bf16[192,2048]{1,0:T(8,128)(2,1)S(1)}, bf16[192,2048]{1,0:T(8,128)(2,1)}, u32[]{:S(2)}, u32[]{:S(2)}) collective-permute-start(bf16[192,2048]{1,0:T(8,128)(2,1)S(1)} %copy-done.11), channel_id=1, source_target_pairs={{0,2},{2,0},{4,6},{6,4},{8,10},{10,8},{12,14},{14,12},{16,18},{18,... | collective-permute-start | bytes 2359304 | tf_op jit(solution)/shard_map/ppermute | solution.py:26
  132.9 26.1 %collective-permute-start.11 = (bf16[768,128]{1,0:T(8,128)(2,1)}, bf16[768,128]{1,0:T(8,128)(2,1)}, u32[]{:S(2)}, u32[]{:S(2)}) collective-permute-start(bf16[768,128]{1,0:T(8,128)(2,1)} %slice.180), channel_id=1, source_target_pairs={{0,16},{2,18},{4,20},{6,22},{8,24},{10,26},{12,28},{14,30},{1,17},... | collective-permute-start | bytes 589832 | tf_op jit(solution)/shard_map/ppermute | solution.py:60
  138.1 339.9 %reduce-scatter.4.cloned.1.call-start = ((), (), s32[]{:S(2)}) async-start(), calls=%async_computation.12 | async-start | bytes 7864320 | tf_op jit(solution)/shard_map/reduce_scatter | solution.py:55
  160.1 32.3 %collective-permute-start.26 = (bf16[192,2048]{1,0:T(8,128)(2,1)}, bf16[192,2048]{1,0:T(8,128)(2,1)S(1)}, u32[]{:S(2)}, u32[]{:S(2)}) collective-permute-start(bf16[192,2048]{1,0:T(8,128)(2,1)} %collective-permute-done.13), channel_id=1, source_target_pairs={{0,2},{2,0},{4,6},{6,4},{8,10},{10,8},{12,14},{14,12},{16,18},{18,... | collective-permute-start | bytes 2359304 | tf_op jit(solution)/shard_map/ppermute | solution.py:26
  161.2 26.8 %collective-permute-start.25 = (bf16[192,2048]{1,0:T(8,128)(2,1)}, bf16[192,2048]{1,0:T(8,128)(2,1)S(1)}, u32[]{:S(2)}, u32[]{:S(2)}) collective-permute-start(bf16[192,2048]{1,0:T(8,128)(2,1)} %collective-permute-done.12), channel_id=1, source_target_pairs={{0,2},{2,0},{4,6},{6,4},{8,10},{10,8},{12,14},{14,12},{16,18},{18,... | collective-permute-start | bytes 2359304 | tf_op jit(solution)/shard_map/ppermute | solution.py:26
  162.7 16.8 %collective-permute-start.15 = (bf16[96,2048]{1,0:T(8,128)(2,1)S(1)}, bf16[96,2048]{1,0:T(8,128)(2,1)S(1)}, u32[]{:S(2)}, u32[]{:S(2)}) collective-permute-start(bf16[96,2048]{1,0:T(8,128)(2,1)S(1)} %slice.182), channel_id=1, source_target_pairs={{0,4},{2,6},{4,0},{6,2},{8,12},{10,14},{12,8},{14,10},{16,20},{18,... | collective-permute-start | bytes 1179656 | tf_op jit(solution)/shard_map/ppermute | solution.py:26
  163.1 16.4 %collective-permute-start.14 = (bf16[96,2048]{1,0:T(8,128)(2,1)S(1)}, bf16[96,2048]{1,0:T(8,128)(2,1)S(1)}, u32[]{:S(2)}, u32[]{:S(2)}) collective-permute-start(bf16[96,2048]{1,0:T(8,128)(2,1)S(1)} %slice.181), channel_id=1, source_target_pairs={{0,1},{1,0},{2,3},{3,2},{4,5},{5,4},{6,7},{7,6},{8,9},{9,8},{10,11... | collective-permute-start | bytes 1179656 | tf_op jit(solution)/shard_map/ppermute | solution.py:38
  195.5 12.0 %collective-permute-start.21 = (bf16[96,2048]{1,0:T(8,128)(2,1)S(1)}, bf16[96,2048]{1,0:T(8,128)(2,1)S(1)}, u32[]{:S(2)}, u32[]{:S(2)}) collective-permute-start(bf16[96,2048]{1,0:T(8,128)(2,1)S(1)} %slice.241), channel_id=1, source_target_pairs={{0,1},{1,0},{2,3},{3,2},{4,5},{5,4},{6,7},{7,6},{8,9},{9,8},{10,11... | collective-permute-start | bytes 1179656 | tf_op jit(solution)/shard_map/ppermute | solution.py:38
  196.2 12.0 %collective-permute-start.23 = (bf16[96,2048]{1,0:T(8,128)(2,1)S(1)}, bf16[96,2048]{1,0:T(8,128)(2,1)S(1)}, u32[]{:S(2)}, u32[]{:S(2)}) collective-permute-start(bf16[96,2048]{1,0:T(8,128)(2,1)S(1)} %slice.242), channel_id=1, source_target_pairs={{0,4},{2,6},{4,0},{6,2},{8,12},{10,14},{12,8},{14,10},{16,20},{18,... | collective-permute-start | bytes 1179656 | tf_op jit(solution)/shard_map/ppermute | solution.py:26
  198.0 17.5 %collective-permute-start.19 = (bf16[96,2048]{1,0:T(8,128)(2,1)S(1)}, bf16[96,2048]{1,0:T(8,128)(2,1)S(1)}, u32[]{:S(2)}, u32[]{:S(2)}) collective-permute-start(bf16[96,2048]{1,0:T(8,128)(2,1)S(1)} %get-tuple-element.307), channel_id=1, source_target_pairs={{0,4},{2,6},{4,0},{6,2},{8,12},{10,14},{12,8},{14,10},{16,20},{18,... | collective-permute-start | bytes 1179656 | tf_op jit(solution)/shard_map/ppermute | solution.py:26
  198.3 17.2 %collective-permute-start.18 = (bf16[96,2048]{1,0:T(8,128)(2,1)S(1)}, bf16[96,2048]{1,0:T(8,128)(2,1)S(1)}, u32[]{:S(2)}, u32[]{:S(2)}) collective-permute-start(bf16[96,2048]{1,0:T(8,128)(2,1)S(1)} %get-tuple-element.308), channel_id=1, source_target_pairs={{0,1},{1,0},{2,3},{3,2},{4,5},{5,4},{6,7},{7,6},{8,9},{9,8},{10,11... | collective-permute-start | bytes 1179656 | tf_op jit(solution)/shard_map/ppermute | solution.py:38
  215.7 10.0 %collective-permute-start.29 = (bf16[96,2048]{1,0:T(8,128)(2,1)S(1)}, bf16[96,2048]{1,0:T(8,128)(2,1)S(1)}, u32[]{:S(2)}, u32[]{:S(2)}) collective-permute-start(bf16[96,2048]{1,0:T(8,128)(2,1)S(1)} %add_convert_fusion.22), channel_id=1, source_target_pairs={{0,4},{2,6},{4,0},{6,2},{8,12},{10,14},{12,8},{14,10},{16,20},{18,... | collective-permute-start | bytes 1179656 | tf_op jit(solution)/shard_map/ppermute | solution.py:26
  217.5 9.7 %collective-permute-start.30 = (bf16[96,2048]{1,0:T(8,128)(2,1)S(1)}, bf16[96,2048]{1,0:T(8,128)(2,1)S(1)}, u32[]{:S(2)}, u32[]{:S(2)}) collective-permute-start(bf16[96,2048]{1,0:T(8,128)(2,1)S(1)} %add_convert_fusion.21), channel_id=1, source_target_pairs={{0,1},{1,0},{2,3},{3,2},{4,5},{5,4},{6,7},{7,6},{8,9},{9,8},{10,11... | collective-permute-start | bytes 1179656 | tf_op jit(solution)/shard_map/ppermute | solution.py:38
  228.4 17.2 %collective-permute-start.32 = (bf16[192,2048]{1,0:T(8,128)(2,1)S(1)}, bf16[192,2048]{1,0:T(8,128)(2,1)S(1)}, u32[]{:S(2)}, u32[]{:S(2)}) collective-permute-start(bf16[192,2048]{1,0:T(8,128)(2,1)S(1)} %multiply_convert_fusion.refs_0_), channel_id=1, source_target_pairs={{0,4},{2,6},{4,0},{6,2},{8,12},{10,14},{12,8},{14,10},{16,20},{18,... | collective-permute-start | bytes 2359304 | tf_op jit(solution)/shard_map/ppermute | solution.py:26
  228.8 18.3 %collective-permute-start.31 = (bf16[192,2048]{1,0:T(8,128)(2,1)S(1)}, bf16[192,2048]{1,0:T(8,128)(2,1)S(1)}, u32[]{:S(2)}, u32[]{:S(2)}) collective-permute-start(bf16[192,2048]{1,0:T(8,128)(2,1)S(1)} %multiply_convert_fusion.refs_0_), channel_id=1, source_target_pairs={{0,1},{1,0},{2,3},{3,2},{4,5},{5,4},{6,7},{7,6},{8,9},{9,8},{10,11... | collective-permute-start | bytes 2359304 | tf_op jit(solution)/shard_map/ppermute | solution.py:38
  230.1 28.6 %collective-permute-start.35 = (bf16[192,2048]{1,0:T(8,128)(2,1)S(1)}, bf16[192,2048]{1,0:T(8,128)(2,1)S(1)}, u32[]{:S(2)}, u32[]{:S(2)}) collective-permute-start(bf16[192,2048]{1,0:T(8,128)(2,1)S(1)} %multiply_convert_fusion.refs_0_), channel_id=1, source_target_pairs={{0,2},{2,0},{4,6},{6,4},{8,10},{10,8},{12,14},{14,12},{16,18},{18,... | collective-permute-start | bytes 2359304 | tf_op jit(solution)/shard_map/ppermute | solution.py:26
  245.6 8.7 %collective-permute-start.33 = (bf16[96,2048]{1,0:T(8,128)(2,1)S(1)}, bf16[96,2048]{1,0:T(8,128)(2,1)S(1)}, u32[]{:S(2)}, u32[]{:S(2)}) collective-permute-start(bf16[96,2048]{1,0:T(8,128)(2,1)S(1)} %slice.246), channel_id=1, source_target_pairs={{0,1},{1,0},{2,3},{3,2},{4,5},{5,4},{6,7},{7,6},{8,9},{9,8},{10,11... | collective-permute-start | bytes 1179656 | tf_op jit(solution)/shard_map/ppermute | solution.py:38
  247.0 11.7 %collective-permute-start.37 = (bf16[192,2048]{1,0:T(8,128)(2,1)S(1)}, bf16[192,2048]{1,0:T(8,128)(2,1)S(1)}, u32[]{:S(2)}, u32[]{:S(2)}) collective-permute-start(bf16[192,2048]{1,0:T(8,128)(2,1)S(1)} %collective-permute-done.32.refs_2_), channel_id=1, source_target_pairs={{0,2},{2,0},{4,6},{6,4},{8,10},{10,8},{12,14},{14,12},{16,18},{18,... | collective-permute-start | bytes 2359304 | tf_op jit(solution)/shard_map/ppermute | solution.py:26
  247.1 11.6 %collective-permute-start.34 = (bf16[96,2048]{1,0:T(8,128)(2,1)S(1)}, bf16[96,2048]{1,0:T(8,128)(2,1)S(1)}, u32[]{:S(2)}, u32[]{:S(2)}) collective-permute-start(bf16[96,2048]{1,0:T(8,128)(2,1)S(1)} %slice.247), channel_id=1, source_target_pairs={{0,4},{2,6},{4,0},{6,2},{8,12},{10,14},{12,8},{14,10},{16,20},{18,... | collective-permute-start | bytes 1179656 | tf_op jit(solution)/shard_map/ppermute | solution.py:26
  248.7 12.4 %collective-permute-start.36 = (bf16[192,2048]{1,0:T(8,128)(2,1)S(1)}, bf16[192,2048]{1,0:T(8,128)(2,1)}, u32[]{:S(2)}, u32[]{:S(2)}) collective-permute-start(bf16[192,2048]{1,0:T(8,128)(2,1)S(1)} %collective-permute-done.31.refs_1_), channel_id=1, source_target_pairs={{0,2},{2,0},{4,6},{6,4},{8,10},{10,8},{12,14},{14,12},{16,18},{18,... | collective-permute-start | bytes 2359304 | tf_op jit(solution)/shard_map/ppermute | solution.py:26
  301.6 266.0 %reduce-scatter.6.cloned.1.call-start = ((), (), s32[]{:S(2)}) async-start(), calls=%async_computation.13 | async-start | bytes 7864320 | tf_op jit(solution)/shard_map/reduce_scatter | solution.py:55
  366.1 20.0 %collective-permute-start.45 = (bf16[96,2048]{1,0:T(8,128)(2,1)}, bf16[96,2048]{1,0:T(8,128)(2,1)S(1)}, u32[]{:S(2)}, u32[]{:S(2)}) collective-permute-start(bf16[96,2048]{1,0:T(8,128)(2,1)} %slice.251), channel_id=1, source_target_pairs={{0,1},{1,0},{2,3},{3,2},{4,5},{5,4},{6,7},{7,6},{8,9},{9,8},{10,11... | collective-permute-start | bytes 1179656 | tf_op jit(solution)/shard_map/ppermute | solution.py:38
  367.5 18.6 %collective-permute-start.47 = (bf16[96,2048]{1,0:T(8,128)(2,1)}, bf16[96,2048]{1,0:T(8,128)(2,1)}, u32[]{:S(2)}, u32[]{:S(2)}) collective-permute-start(bf16[96,2048]{1,0:T(8,128)(2,1)} %slice.252), channel_id=1, source_target_pairs={{0,4},{2,6},{4,0},{6,2},{8,12},{10,14},{12,8},{14,10},{16,20},{18,... | collective-permute-start | bytes 1179656 | tf_op jit(solution)/shard_map/ppermute | solution.py:26
  370.0 17.2 %collective-permute-start.43 = (bf16[96,2048]{1,0:T(8,128)(2,1)}, bf16[96,2048]{1,0:T(8,128)(2,1)}, u32[]{:S(2)}, u32[]{:S(2)}) collective-permute-start(bf16[96,2048]{1,0:T(8,128)(2,1)} %get-tuple-element.305), channel_id=1, source_target_pairs={{0,4},{2,6},{4,0},{6,2},{8,12},{10,14},{12,8},{14,10},{16,20},{18,... | collective-permute-start | bytes 1179656 | tf_op jit(solution)/shard_map/ppermute | solution.py:26
  370.5 16.6 %collective-permute-start.42 = (bf16[96,2048]{1,0:T(8,128)(2,1)}, bf16[96,2048]{1,0:T(8,128)(2,1)}, u32[]{:S(2)}, u32[]{:S(2)}) collective-permute-start(bf16[96,2048]{1,0:T(8,128)(2,1)} %get-tuple-element.306), channel_id=1, source_target_pairs={{0,1},{1,0},{2,3},{3,2},{4,5},{5,4},{6,7},{7,6},{8,9},{9,8},{10,11... | collective-permute-start | bytes 1179656 | tf_op jit(solution)/shard_map/ppermute | solution.py:38
  389.7 10.1 %collective-permute-start.48 = (bf16[96,2048]{1,0:T(8,128)(2,1)S(1)}, bf16[96,2048]{1,0:T(8,128)(2,1)S(1)}, u32[]{:S(2)}, u32[]{:S(2)}) collective-permute-start(bf16[96,2048]{1,0:T(8,128)(2,1)S(1)} %add_convert_fusion.20), channel_id=1, source_target_pairs={{0,4},{2,6},{4,0},{6,2},{8,12},{10,14},{12,8},{14,10},{16,20},{18,... | collective-permute-start | bytes 1179656 | tf_op jit(solution)/shard_map/ppermute | solution.py:26
  391.2 9.7 %collective-permute-start.49 = (bf16[96,2048]{1,0:T(8,128)(2,1)S(1)}, bf16[96,2048]{1,0:T(8,128)(2,1)S(1)}, u32[]{:S(2)}, u32[]{:S(2)}) collective-permute-start(bf16[96,2048]{1,0:T(8,128)(2,1)S(1)} %add_convert_fusion.19), channel_id=1, source_target_pairs={{0,1},{1,0},{2,3},{3,2},{4,5},{5,4},{6,7},{7,6},{8,9},{9,8},{10,11... | collective-permute-start | bytes 1179656 | tf_op jit(solution)/shard_map/ppermute | solution.py:38
  405.0 17.4 %collective-permute-start.51 = (bf16[192,2048]{1,0:T(8,128)(2,1)S(1)}, bf16[192,2048]{1,0:T(8,128)(2,1)}, u32[]{:S(2)}, u32[]{:S(2)}) collective-permute-start(bf16[192,2048]{1,0:T(8,128)(2,1)S(1)} %get-tuple-element.273.refs_0_), channel_id=1, source_target_pairs={{0,4},{2,6},{4,0},{6,2},{8,12},{10,14},{12,8},{14,10},{16,20},{18,... | collective-permute-start | bytes 2359304 | tf_op jit(solution)/shard_map/ppermute | solution.py:26
  405.6 17.2 %collective-permute-start.50 = (bf16[192,2048]{1,0:T(8,128)(2,1)S(1)}, bf16[192,2048]{1,0:T(8,128)(2,1)}, u32[]{:S(2)}, u32[]{:S(2)}) collective-permute-start(bf16[192,2048]{1,0:T(8,128)(2,1)S(1)} %get-tuple-element.273.refs_0_), channel_id=1, source_target_pairs={{0,1},{1,0},{2,3},{3,2},{4,5},{5,4},{6,7},{7,6},{8,9},{9,8},{10,11... | collective-permute-start | bytes 2359304 | tf_op jit(solution)/shard_map/ppermute | solution.py:38
  421.4 19.5 %collective-permute-start.54 = (bf16[192,2048]{1,0:T(8,128)(2,1)S(1)}, bf16[192,2048]{1,0:T(8,128)(2,1)}, u32[]{:S(2)}, u32[]{:S(2)}) collective-permute-start(bf16[192,2048]{1,0:T(8,128)(2,1)S(1)} %get-tuple-element.273.refs_0_), channel_id=1, source_target_pairs={{0,2},{2,0},{4,6},{6,4},{8,10},{10,8},{12,14},{14,12},{16,18},{18,... | collective-permute-start | bytes 2359304 | tf_op jit(solution)/shard_map/ppermute | solution.py:26
  423.8 10.3 %collective-permute-start.52 = (bf16[96,2048]{1,0:T(8,128)(2,1)S(1)}, bf16[96,2048]{1,0:T(8,128)(2,1)S(1)}, u32[]{:S(2)}, u32[]{:S(2)}) collective-permute-start(bf16[96,2048]{1,0:T(8,128)(2,1)S(1)} %slice.210), channel_id=1, source_target_pairs={{0,1},{1,0},{2,3},{3,2},{4,5},{5,4},{6,7},{7,6},{8,9},{9,8},{10,11... | collective-permute-start | bytes 1179656 | tf_op jit(solution)/shard_map/ppermute | solution.py:38
  425.5 11.0 %collective-permute-start.53 = (bf16[96,2048]{1,0:T(8,128)(2,1)S(1)}, bf16[96,2048]{1,0:T(8,128)(2,1)}, u32[]{:S(2)}, u32[]{:S(2)}) collective-permute-start(bf16[96,2048]{1,0:T(8,128)(2,1)S(1)} %slice.211), channel_id=1, source_target_pairs={{0,4},{2,6},{4,0},{6,2},{8,12},{10,14},{12,8},{14,10},{16,20},{18,... | collective-permute-start | bytes 1179656 | tf_op jit(solution)/shard_map/ppermute | solution.py:26
  427.0 14.5 %collective-permute-start.55 = (bf16[192,2048]{1,0:T(8,128)(2,1)}, bf16[192,2048]{1,0:T(8,128)(2,1)}, u32[]{:S(2)}, u32[]{:S(2)}) collective-permute-start(bf16[192,2048]{1,0:T(8,128)(2,1)} %collective-permute-done.50.refs_1_), channel_id=1, source_target_pairs={{0,2},{2,0},{4,6},{6,4},{8,10},{10,8},{12,14},{14,12},{16,18},{18,... | collective-permute-start | bytes 2359304 | tf_op jit(solution)/shard_map/ppermute | solution.py:26
  436.5 8.9 %collective-permute-start.56 = (bf16[192,2048]{1,0:T(8,128)(2,1)}, bf16[192,2048]{1,0:T(8,128)(2,1)}, u32[]{:S(2)}, u32[]{:S(2)}) collective-permute-start(bf16[192,2048]{1,0:T(8,128)(2,1)} %collective-permute-done.51.refs_2_), channel_id=1, source_target_pairs={{0,2},{2,0},{4,6},{6,4},{8,10},{10,8},{12,14},{14,12},{16,18},{18,... | collective-permute-start | bytes 2359304 | tf_op jit(solution)/shard_map/ppermute | solution.py:26
  440.9 12.4 %collective-permute-start.59 = (bf16[192,2048]{1,0:T(8,128)(2,1)}, bf16[192,2048]{1,0:T(8,128)(2,1)S(1)}, u32[]{:S(2)}, u32[]{:S(2)}) collective-permute-start(bf16[192,2048]{1,0:T(8,128)(2,1)} %get-tuple-element.202), channel_id=1, source_target_pairs={{0,2},{2,0},{4,6},{6,4},{8,10},{10,8},{12,14},{14,12},{16,18},{18,... | collective-permute-start | bytes 2359304 | tf_op jit(solution)/shard_map/ppermute | solution.py:26
  441.0 12.4 %collective-permute-start.60 = (bf16[192,2048]{1,0:T(8,128)(2,1)}, bf16[192,2048]{1,0:T(8,128)(2,1)S(1)}, u32[]{:S(2)}, u32[]{:S(2)}) collective-permute-start(bf16[192,2048]{1,0:T(8,128)(2,1)} %get-tuple-element.203), channel_id=1, source_target_pairs={{0,2},{2,0},{4,6},{6,4},{8,10},{10,8},{12,14},{14,12},{16,18},{18,... | collective-permute-start | bytes 2359304 | tf_op jit(solution)/shard_map/ppermute | solution.py:26
  441.5 11.9 %collective-permute-start.61 = (bf16[192,2048]{1,0:T(8,128)(2,1)}, bf16[192,2048]{1,0:T(8,128)(2,1)S(1)}, u32[]{:S(2)}, u32[]{:S(2)}) collective-permute-start(bf16[192,2048]{1,0:T(8,128)(2,1)} %get-tuple-element.204), channel_id=1, source_target_pairs={{0,2},{2,0},{4,6},{6,4},{8,10},{10,8},{12,14},{14,12},{16,18},{18,... | collective-permute-start | bytes 2359304 | tf_op jit(solution)/shard_map/ppermute | solution.py:26
  441.5 11.8 %collective-permute-start.62 = (bf16[192,2048]{1,0:T(8,128)(2,1)}, bf16[192,2048]{1,0:T(8,128)(2,1)}, u32[]{:S(2)}, u32[]{:S(2)}) collective-permute-start(bf16[192,2048]{1,0:T(8,128)(2,1)} %get-tuple-element.205), channel_id=1, source_target_pairs={{0,2},{2,0},{4,6},{6,4},{8,10},{10,8},{12,14},{14,12},{16,18},{18,... | collective-permute-start | bytes 2359304 | tf_op jit(solution)/shard_map/ppermute | solution.py:26
  457.1 16.4 %collective-permute-start.66 = (bf16[96,2048]{1,0:T(8,128)(2,1)S(1)}, bf16[96,2048]{1,0:T(8,128)(2,1)S(1)}, u32[]{:S(2)}, u32[]{:S(2)}) collective-permute-start(bf16[96,2048]{1,0:T(8,128)(2,1)S(1)} %slice.219), channel_id=1, source_target_pairs={{0,4},{2,6},{4,0},{6,2},{8,12},{10,14},{12,8},{14,10},{16,20},{18,... | collective-permute-start | bytes 1179656 | tf_op jit(solution)/shard_map/ppermute | solution.py:26
  458.6 14.8 %collective-permute-start.65 = (bf16[96,2048]{1,0:T(8,128)(2,1)S(1)}, bf16[96,2048]{1,0:T(8,128)(2,1)}, u32[]{:S(2)}, u32[]{:S(2)}) collective-permute-start(bf16[96,2048]{1,0:T(8,128)(2,1)S(1)} %slice.218), channel_id=1, source_target_pairs={{0,1},{1,0},{2,3},{3,2},{4,5},{5,4},{6,7},{7,6},{8,9},{9,8},{10,11... | collective-permute-start | bytes 1179656 | tf_op jit(solution)/shard_map/ppermute | solution.py:38
  459.3 17.5 %collective-permute-start.64 = (bf16[96,2048]{1,0:T(8,128)(2,1)S(1)}, bf16[96,2048]{1,0:T(8,128)(2,1)}, u32[]{:S(2)}, u32[]{:S(2)}) collective-permute-start(bf16[96,2048]{1,0:T(8,128)(2,1)S(1)} %get-tuple-element.303), channel_id=1, source_target_pairs={{0,4},{2,6},{4,0},{6,2},{8,12},{10,14},{12,8},{14,10},{16,20},{18,... | collective-permute-start | bytes 1179656 | tf_op jit(solution)/shard_map/ppermute | solution.py:26
  459.9 18.0 %collective-permute-start.63 = (bf16[96,2048]{1,0:T(8,128)(2,1)S(1)}, bf16[96,2048]{1,0:T(8,128)(2,1)}, u32[]{:S(2)}, u32[]{:S(2)}) collective-permute-start(bf16[96,2048]{1,0:T(8,128)(2,1)S(1)} %get-tuple-element.304), channel_id=1, source_target_pairs={{0,1},{1,0},{2,3},{3,2},{4,5},{5,4},{6,7},{7,6},{8,9},{9,8},{10,11... | collective-permute-start | bytes 1179656 | tf_op jit(solution)/shard_map/ppermute | solution.py:38
  477.9 46.3 %all-to-all-start.3 = ((bf16[4,128,1536]{2,1,0:T(8,128)(2,1)}), bf16[4,128,1536]{2,1,0:T(8,128)(2,1)}, u32[]{:S(2)}, u32[]{:S(2)}) async-start(bf16[4,128,1536]{2,1,0:T(8,128)(2,1)} %bitcast.21), calls=%async_computation.4 | async-start | bytes 3145728 | tf_op jit(solution)/shard_map/all_to_all | solution.py:154
  482.3 142.9 %reduce-scatter.8.cloned.1.call-start = ((), (), s32[]{:S(2)}) async-start(), calls=%async_computation.14 | async-start | bytes 3276800 | tf_op jit(solution)/shard_map/reduce_scatter | solution.py:55
  482.3 40.7 %collective-permute-start.68 = (bf16[768,128]{1,0:T(8,128)(2,1)}, bf16[768,128]{1,0:T(8,128)(2,1)}, u32[]{:S(2)}, u32[]{:S(2)}) collective-permute-start(bf16[768,128]{1,0:T(8,128)(2,1)} %get-tuple-element.219), channel_id=1, source_target_pairs={{16,0},{18,2},{20,4},{22,6},{24,8},{26,10},{28,12},{30,14},{17,1},... | collective-permute-start | bytes 589832 | tf_op jit(solution)/shard_map/ppermute | solution.py:60
  483.6 40.6 %collective-permute-start.67 = (bf16[1536,128]{1,0:T(8,128)(2,1)}, bf16[1536,128]{1,0:T(8,128)(2,1)}, u32[]{:S(2)}, u32[]{:S(2)}) collective-permute-start(bf16[1536,128]{1,0:T(8,128)(2,1)} %get-tuple-element.218), channel_id=1, source_target_pairs={{8,0},{10,2},{12,4},{14,6},{16,8},{18,10},{20,12},{22,14},{24,16},... | collective-permute-start | bytes 1179656 | tf_op jit(solution)/shard_map/ppermute | solution.py:60
  486.2 34.5 %collective-permute-start.69 = (bf16[96,2048]{1,0:T(8,128)(2,1)S(1)}, bf16[96,2048]{1,0:T(8,128)(2,1)S(1)}, u32[]{:S(2)}, u32[]{:S(2)}) collective-permute-start(bf16[96,2048]{1,0:T(8,128)(2,1)S(1)} %add_convert_fusion.18), channel_id=1, source_target_pairs={{0,4},{2,6},{4,0},{6,2},{8,12},{10,14},{12,8},{14,10},{16,20},{18,... | collective-permute-start | bytes 1179656 | tf_op jit(solution)/shard_map/ppermute | solution.py:26
  489.2 31.5 %collective-permute-start.70 = (bf16[96,2048]{1,0:T(8,128)(2,1)S(1)}, bf16[96,2048]{1,0:T(8,128)(2,1)S(1)}, u32[]{:S(2)}, u32[]{:S(2)}) collective-permute-start(bf16[96,2048]{1,0:T(8,128)(2,1)S(1)} %add_convert_fusion.17), channel_id=1, source_target_pairs={{0,1},{1,0},{2,3},{3,2},{4,5},{5,4},{6,7},{7,6},{8,9},{9,8},{10,11... | collective-permute-start | bytes 1179656 | tf_op jit(solution)/shard_map/ppermute | solution.py:38
  567.6 19.7 %collective-permute-start.75 = (bf16[192,2048]{1,0:T(8,128)(2,1)}, bf16[192,2048]{1,0:T(8,128)(2,1)}, u32[]{:S(2)}, u32[]{:S(2)}) collective-permute-start(bf16[192,2048]{1,0:T(8,128)(2,1)} %get-tuple-element.246), channel_id=1, source_target_pairs={{0,1},{1,0},{2,3},{3,2},{4,5},{5,4},{6,7},{7,6},{8,9},{9,8},{10,11... | collective-permute-start | bytes 2359304 | tf_op jit(solution)/shard_map/ppermute | solution.py:38
  569.1 23.6 %all-to-all-start.4 = ((bf16[4,128,1536]{2,1,0:T(8,128)(2,1)}), bf16[4,128,1536]{2,1,0:T(8,128)(2,1)S(1)}, u32[]{:S(2)}, u32[]{:S(2)}) async-start(bf16[4,128,1536]{2,1,0:T(8,128)(2,1)} %bitcast.22), calls=%async_computation.6 | async-start | bytes 3145728 | tf_op jit(solution)/shard_map/all_to_all | solution.py:154
  592.7 36.7 %collective-permute-start.76 = (bf16[192,2048]{1,0:T(8,128)(2,1)}, bf16[192,2048]{1,0:T(8,128)(2,1)S(1)}, u32[]{:S(2)}, u32[]{:S(2)}) collective-permute-start(bf16[192,2048]{1,0:T(8,128)(2,1)} %get-tuple-element.249), channel_id=1, source_target_pairs={{0,1},{1,0},{2,3},{3,2},{4,5},{5,4},{6,7},{7,6},{8,9},{9,8},{10,11... | collective-permute-start | bytes 2359304 | tf_op jit(solution)/shard_map/ppermute | solution.py:38
  593.2 37.0 %collective-permute-start.77 = (bf16[192,2048]{1,0:T(8,128)(2,1)}, bf16[192,2048]{1,0:T(8,128)(2,1)}, u32[]{:S(2)}, u32[]{:S(2)}) collective-permute-start(bf16[192,2048]{1,0:T(8,128)(2,1)} %add_convert_fusion), channel_id=1, source_target_pairs={{0,4},{2,6},{4,0},{6,2},{8,12},{10,14},{12,8},{14,10},{16,20},{18,... | collective-permute-start | bytes 2359304 | tf_op jit(solution)/shard_map/ppermute | solution.py:26
  625.2 15.7 %all-to-all-start.5 = ((bf16[4,128,640]{2,1,0:T(8,128)(2,1)}), bf16[4,128,640]{2,1,0:T(8,128)(2,1)}, u32[]{:S(2)}, u32[]{:S(2)}) async-start(bf16[4,128,640]{2,1,0:T(8,128)(2,1)} %bitcast.23), calls=%async_computation.8 | async-start | bytes 1310720 | tf_op jit(solution)/shard_map/all_to_all | solution.py:154
  (74 other events, 481.6 us)
Sparse Core Ops, SparseCore 0:
  24.6 55.9 all-gather.3
  82.1 122.4 all-gather.5
  206.8 121.7 all-gather.7
  330.8 110.6 reduce-scatter.3
  443.6 123.9 reduce-scatter.5
  569.8 55.3 reduce-scatter.7
